TPU v7x, 32 devices: a whole 2x2x4 slice. The times are simulated.
32 devices in a mesh: row: 16 (over z, x, core), col: 2 (over y).
Axes of the slice: x: 2, y: 2, z: 4, core: 2. Of those that a mesh axis runs over, the one named last changes fastest.
Arguments:
- inverse_anc: float32 [8192, 8192], P('row', 'col'), as said below
- lower_panel: float32 [8192, 512], P('row', 'col'), may hold values from -0.5 to 0.5
- structure: int32 [2, 16], P('col'), may hold values from 0 to 31, as said below
- diag_inverse: float32 [512, 256], P('col'), may hold values from -6 to 6
Outputs:
- inverse_panel: float32 [8192, 512], P('row', 'col')
- diagonal_block: float32 [512, 256], P('col')
Inputs may be any that keep to these rules, and one draw needn't show every extreme that they name: inverse_anc is exactly symmetric. `structure`: each row lists 16 different ancestor block numbers in increasing order; each index of col holds exactly one row (one lower supernode).
All inputs are finite; a program needn't handle non-finite values.
Results may differ from a plain program's by a relative error of at most 0.000075.
Values sent between devices are 32-bit elements; how exact they have to be, the bound alone decides.
No kernel may reach another device: no remote copies, remote signals or barrier semaphores. Data moves between devices by JAX's collectives and lax.ppermute only.
A program may use at most 64 MiB of HBM per device.

v0:
```python
import functools

import jax
import jax.numpy as jnp
from jax import lax
from jax.experimental import pallas as pl
from jax.experimental.pallas import tpu as pltpu
from jax.sharding import PartitionSpec as P


BOTH = ("row", "col")


def keep_rows(structure, first_row, row_count, sn_width):
    block_ids = (first_row + jnp.arange(row_count, dtype=jnp.int32)) // sn_width
    listed = jnp.any(structure[None, :, :] == block_ids[:, None, None], axis=2)
    return jnp.repeat(listed, sn_width, axis=1)


def local_any(inverse_anc, lower_panel, structure, diag_inverse):
    local_rows = inverse_anc.shape[0]
    sn_width = diag_inverse.shape[1]
    local_count = structure.shape[0]
    keep = keep_rows(structure, lax.axis_index("row") * local_rows, local_rows, sn_width)
    masked = jnp.where(keep, lower_panel, jnp.float32(0.0))
    rows = lax.all_gather(masked, "row", axis=0, tiled=True)
    rows = lax.all_to_all(rows, "col", split_axis=0, concat_axis=1, tiled=True)
    part = jnp.dot(inverse_anc, rows, precision=lax.Precision.HIGHEST)
    product = lax.psum_scatter(part, "col", scatter_dimension=1, tiled=True)
    panel = jnp.where(keep, -product, jnp.float32(0.0))
    terms = jnp.einsum(
        "ika,ikb->kab",
        masked.reshape(local_rows, local_count, sn_width),
        panel.reshape(local_rows, local_count, sn_width),
        precision=lax.Precision.HIGHEST,
    )
    total = lax.psum(terms.reshape(local_count * sn_width, sn_width), "row")
    return panel, diag_inverse - total


def split(value):
    high = value.astype(jnp.bfloat16)
    low = (value - high.astype(jnp.float32)).astype(jnp.bfloat16)
    return high, low


def dot3(a, b, dims):
    dot = lambda u, v: lax.dot_general(u, v, (dims, ((), ())), preferred_element_type=jnp.float32)
    return dot(a[0], b[0]) + (dot(a[0], b[1]) + dot(a[1], b[0]))


def product_kernel(slots, blocks, width, has_acc, final, table, *refs):
    count = len(slots)
    narrays = 1 + max(s[0] for s in slots)
    refs = list(refs)
    a_hbm = refs.pop(0)
    arrays = [refs.pop(0) for _ in range(narrays)]
    acc_in = refs.pop(0) if has_acc else None
    if final:
        recv, lower = refs.pop(0), refs.pop(0)
    out = refs.pop(0)
    if final:
        terms = refs.pop(0)
    a_buf, p_buf, a_sem, p_sem = refs
    row_on = [table[2 * count + rb] > 0 for rb in range(blocks)]

    def a_copy(p, rb):
        return pltpu.make_async_copy(
            a_hbm.at[pl.ds(rb * width, width), pl.ds(pl.multiple_of(table[p] * width, width), width)],
            a_buf.at[p, rb],
            a_sem.at[p, rb],
        )

    def p_copy(p):
        array, at = slots[p]
        return pltpu.make_async_copy(arrays[array].at[pl.ds(at * width, width), :], p_buf.at[p], p_sem.at[p])

    for p in range(count):
        @pl.when(table[count + p] > 0)
        def _(p=p):
            p_copy(p).start()
            for rb in range(blocks):
                @pl.when(row_on[rb])
                def _(rb=rb):
                    a_copy(p, rb).start()

    if has_acc:
        out[...] = acc_in[...]
    else:
        out[...] = jnp.zeros_like(out)
    for p in range(count):
        @pl.when(table[count + p] > 0)
        def _(p=p):
            p_copy(p).wait()
            piece = split(p_buf[p])
            for rb in range(blocks):
                @pl.when(row_on[rb])
                def _(rb=rb):
                    a_copy(p, rb).wait()
                    out[pl.ds(rb * width, width), :] += dot3(split(a_buf[p, rb]), piece, ((1,), (0,)))

    if final:
        terms[...] = jnp.zeros_like(terms)
        for rb in range(blocks):
            rows = pl.ds(rb * width, width)

            @pl.when(row_on[rb])
            def _(rows=rows):
                panel = -(out[rows, :] + recv[rows, :])
                out[rows, :] = panel
                terms[...] += dot3(split(lower[rows, :]), split(panel), ((0,), (0,)))

            @pl.when(jnp.logical_not(row_on[rb]))
            def _(rows=rows):
                out[rows, :] = jnp.zeros((width, out.shape[1]), jnp.float32)


def product(table, inverse_anc, arrays, slots, width, acc=None, final=None):
    rows = inverse_anc.shape[0]
    blocks = rows // width
    count = len(slots)
    any_spec = pl.BlockSpec(memory_space=pl.ANY)
    vmem = pl.BlockSpec(memory_space=pltpu.VMEM)
    operands = [inverse_anc, *arrays]
    specs = [any_spec] * len(operands)
    if acc is not None:
        operands.append(acc)
        specs.append(vmem)
    if final is not None:
        operands += list(final)
        specs += [vmem, vmem]
    shapes = [jax.ShapeDtypeStruct((rows, width), jnp.float32)]
    if final is not None:
        shapes.append(jax.ShapeDtypeStruct((width, width), jnp.float32))
    return pl.pallas_call(
        functools.partial(product_kernel, slots, blocks, width, acc is not None, final is not None),
        out_shape=shapes,
        grid_spec=pltpu.PrefetchScalarGridSpec(
            num_scalar_prefetch=1,
            grid=(1,),
            in_specs=specs,
            out_specs=[vmem] * len(shapes),
            scratch_shapes=[
                pltpu.VMEM((count, blocks, width, width), jnp.float32),
                pltpu.VMEM((count, width, width), jnp.float32),
                pltpu.SemaphoreType.DMA((count, blocks)),
                pltpu.SemaphoreType.DMA((count,)),
            ],
        ),
        compiler_params=pltpu.CompilerParams(vmem_limit_bytes=20 * 1024 * 1024),
        cost_estimate=pl.CostEstimate(
            flops=6 * rows * width * width * count // 4,
            bytes_accessed=4 * rows * width * count // 2,
            transcendentals=0,
        ),
    )(table, *operands)


CORE, X, Z, FAR = 1, 2, 4, 8
FIRST = ((0, 0), (0, 1), (X, 0), (Z, 1))
SECOND = ((Z, 0), (Z | X, 0), (X, 1), (Z | X, 1))


def with_sibling(order):
    return order + tuple((m ^ CORE, h) for m, h in order)


def local_two(n_row, inverse_anc, lower_panel, structure, diag_inverse):
    n_col = 2
    rows = inverse_anc.shape[0]
    width = diag_inverse.shape[1]
    row, col = lax.axis_index("row"), lax.axis_index("col")
    near = (row // FAR) == col
    flip = [(0, 1), (1, 0)]

    def swap(value, mask):
        return lax.ppermute(value, "row", [(i, i ^ mask) for i in range(n_row)])

    def linear(r, c):
        return r * n_col + c

    every = [(r, c) for r in range(n_row) for c in range(n_col)]
    first = [
        (linear(r, c), linear(r ^ FAR, c) if r // FAR == c else linear(r, 1 - c)) for r, c in every
    ]
    second = [(linear(r, c), linear(r ^ FAR, 1 - c)) for r, c in every if r // FAR != c]
    got_first = lax.ppermute(lower_panel, BOTH, first)
    got_second = lax.ppermute(lower_panel, BOTH, second)
    other_structure = lax.ppermute(structure, "col", flip)
    q_own = jnp.where(near, lower_panel, got_first)
    q_other = jnp.where(near, got_first, got_second)

    def table(listed, order):
        order = with_sibling(order)
        block = ((row % FAR) ^ jnp.array([m for m, _ in order], jnp.int32)) * 2
        block = block + jnp.array([h for _, h in order], jnp.int32)
        ids = jnp.concatenate([block + col * 2 * FAR, row * 2 + jnp.arange(2, dtype=jnp.int32)])
        on = jnp.any(ids[:, None] == listed[0][None, :], axis=1).astype(jnp.int32)
        return jnp.concatenate([block, on])

    half = rows // 2
    s0 = jnp.concatenate([q_other[:half], q_own[:half]])
    s1 = jnp.concatenate([q_other[half:], q_own[half:]])
    x1 = swap(s0, X)
    z1 = swap(s1, Z)
    got = []
    for at in (0, 1):
        part = slice(at * half, (at + 1) * half)
        z2 = swap(jnp.concatenate([s0[part], x1[part]]), Z)
        x2 = swap(jnp.concatenate([s1[part], z1[part]]), X)
        got.append([z2, x2])
    near_arrays = [s0, s1, x1, z1]
    near_arrays += [swap(v, CORE) for v in near_arrays]
    far_arrays = [v + [swap(u, CORE) for u in v] for v in got]

    def slots1(at):
        return tuple((i, at) for i in range(8))

    slots2 = tuple((i, h) for i in range(4) for h in range(2))
    (part,) = product(table(other_structure, FIRST), inverse_anc, near_arrays, slots1(0), width)
    (part,) = product(
        table(other_structure, SECOND), inverse_anc, far_arrays[0], slots2, width, acc=part
    )
    recv = lax.ppermute(part, "col", flip)
    (acc,) = product(table(structure, FIRST), inverse_anc, near_arrays, slots1(1), width)
    panel, terms = product(
        table(structure, SECOND), inverse_anc, far_arrays[1], slots2, width,
        acc=acc, final=(recv, lower_panel),
    )

    def halve(value, mask):
        size = value.shape[0] // 2
        bit = (row & mask) > 0
        low, high = value[:size], value[size:]
        return jnp.where(bit, high, low) + swap(jnp.where(bit, low, high), mask)

    def double(value, mask):
        bit = (row & mask) > 0
        got = swap(value, mask)
        return jnp.concatenate([jnp.where(bit, got, value), jnp.where(bit, value, got)])

    total = halve(halve(terms, CORE), X)
    total = total + swap(total, Z) + swap(total, FAR) + swap(total, FAR | Z)
    total = double(double(total, X), CORE)
    return panel, diag_inverse - total


def solution(mesh):
    n_row, n_col = mesh.shape["row"], mesh.shape["col"]

    def local(inverse_anc, lower_panel, structure, diag_inverse):
        rows, columns = inverse_anc.shape
        width = diag_inverse.shape[1]
        planned = (
            n_col == 2 and n_row == 2 * FAR and rows == 2 * width
            and structure.shape[0] == 1 and columns == FAR * rows
        )
        if planned:
            return local_two(n_row, inverse_anc, lower_panel, structure, diag_inverse)
        return local_any(inverse_anc, lower_panel, structure, diag_inverse)

    return jax.shard_map(
        local,
        mesh=mesh,
        in_specs=(P("row", "col"), P("row", "col"), P("col", None), P("col", None)),
        out_specs=(P("row", "col"), P("col", None)),
        check_vma=False,
    )
```

profile of v0, /device:TPU:0, one launch (start us, length us, event | category | flops | bytes accessed | tf_op | source)
XLA Modules:
  0.0 133.8 jit_solution(12138742020300797070)
XLA Ops:
  0.6 0.0 copy-start.8
  0.6 0.0 copy-start.9
  0.7 0.0 copy-start.10
  0.7 0.0 copy-start.11
  0.7 0.0 copy-start.12
  0.7 4.1 %collective-permute-start = (f32[512,256]{1,0:T(8,128)}, f32[512,256]{1,0:T(8,128)S(1)}, u32[]{:S(2)}, u32[]{:S(2)}) collective-permute-start(f32[512,256]{1,0:T(8,128)} %refs_7_.1), channel_id=1, source_target_pairs={{0,16},{1,0},{2,18},{3,2},{4,20},{5,4},{6,22},{7,6},{8,24},{9,8},{... | collective-permute-start | bytes 1572872 | tf_op jit(solution)/shard_map/ppermute | solution.py:187
  4.8 0.7 collective-permute-start.1
  5.5 10.8 %collective-permute-done = f32[512,256]{1,0:T(8,128)S(1)} collective-permute-done((f32[512,256]{1,0:T(8,128)}, f32[512,256]{1,0:T(8,128)S(1)}, u32[]{:S(2)}, u32[]{:S(2)}) %collective-permute-start) | collective-permute-done | bytes 524320 | tf_op jit(solution)/shard_map/ppermute | solution.py:187
  16.4 0.0 collective-permute-done.1
  16.4 1.1 broadcast_select_fusion.1
  17.5 0.1 fusion.2
  17.6 0.7 copy-done.6
  18.3 12.7 %collective-permute-start.4 = (f32[512,256]{1,0:T(8,128)S(1)}, f32[512,256]{1,0:T(8,128)S(1)}, u32[]{:S(2)}, u32[]{:S(2)}) collective-permute-start(f32[512,256]{1,0:T(8,128)S(1)} %pad_maximum_fusion.3.refs_2_), channel_id=1, source_target_pairs={{0,8},{2,10},{4,12},{6,14},{8,0},{10,2},{12,4},{14,6},{16,24},{18,... | collective-permute-start | bytes 1572872 | tf_op jit(solution)/shard_map/ppermute | solution.py:177
  31.1 1.6 %collective-permute-start.2 = (f32[512,256]{1,0:T(8,128)S(1)}, f32[512,256]{1,0:T(8,128)S(1)}, u32[]{:S(2)}, u32[]{:S(2)}) collective-permute-start(f32[512,256]{1,0:T(8,128)S(1)} %pad_maximum_fusion.1.refs_1_), channel_id=1, source_target_pairs={{0,4},{2,6},{4,0},{6,2},{8,12},{10,14},{12,8},{14,10},{16,20},{18,... | collective-permute-start | bytes 1572872 | tf_op jit(solution)/shard_map/ppermute | solution.py:177
  32.6 3.6 %collective-permute-start.12 = (s32[1,16]{1,0:T(1,128)}, s32[1,16]{1,0:T(1,128)S(1)}, u32[]{:S(2)}, u32[]{:S(2)}) collective-permute-start(s32[1,16]{1,0:T(1,128)} %param.14), channel_id=1, source_target_pairs={{0,1},{1,0},{2,3},{3,2},{4,5},{5,4},{6,7},{7,6},{8,9},{9,8},{10,11... | collective-permute-start | bytes 200 | tf_op jit(solution)/shard_map/ppermute | solution.py:189
  36.2 0.0 collective-permute-start.9
  36.2 0.5 collective-permute-start.8
  36.7 6.4 %collective-permute-done.4.refs_4_ = f32[512,256]{1,0:T(8,128)S(1)} collective-permute-done((f32[512,256]{1,0:T(8,128)S(1)}, f32[512,256]{1,0:T(8,128)S(1)}, u32[]{:S(2)}, u32[]{:S(2)}) %collective-permute-start.4) | collective-permute-done | bytes 524320 | tf_op jit(solution)/shard_map/ppermute | solution.py:177
  43.2 0.7 fusion
  43.9 0.8 pad_maximum_fusion.2
  44.7 1.5 %collective-permute-start.14 = (f32[512,256]{1,0:T(8,128)}, f32[512,256]{1,0:T(8,128)}, u32[]{:S(2)}, u32[]{:S(2)}) collective-permute-start(f32[512,256]{1,0:T(8,128)} %pad_maximum_fusion.2), channel_id=1, source_target_pairs={{0,4},{2,6},{4,0},{6,2},{8,12},{10,14},{12,8},{14,10},{16,20},{18,... | collective-permute-start | bytes 1572872 | tf_op jit(solution)/shard_map/ppermute | solution.py:177
  46.2 0.0 collective-permute-done.2.refs_3_
  46.2 0.7 fusion.1
  47.0 0.8 pad_maximum_fusion
  47.8 1.7 %collective-permute-start.13 = (f32[512,256]{1,0:T(8,128)}, f32[512,256]{1,0:T(8,128)}, u32[]{:S(2)}, u32[]{:S(2)}) collective-permute-start(f32[512,256]{1,0:T(8,128)} %pad_maximum_fusion), channel_id=1, source_target_pairs={{0,8},{2,10},{4,12},{6,14},{8,0},{10,2},{12,4},{14,6},{16,24},{18,... | collective-permute-start | bytes 1572872 | tf_op jit(solution)/shard_map/ppermute | solution.py:177
  49.6 1.1 pad_maximum_fusion.5
  50.6 1.0 pad_maximum_fusion.4
  51.6 0.0 collective-permute-done.9.refs_6_
  51.7 0.6 collective-permute-start.5
  52.3 0.3 collective-permute-start.3
  52.5 7.3 %collective-permute-done.14.refs_2_ = f32[512,256]{1,0:T(8,128)} collective-permute-done((f32[512,256]{1,0:T(8,128)}, f32[512,256]{1,0:T(8,128)}, u32[]{:S(2)}, u32[]{:S(2)}) %collective-permute-start.14) | collective-permute-done | bytes 524320 | tf_op jit(solution)/shard_map/ppermute | solution.py:177
  59.9 0.0 collective-permute-start.16
  59.9 3.1 %collective-permute-done.13.refs_1_ = f32[512,256]{1,0:T(8,128)} collective-permute-done((f32[512,256]{1,0:T(8,128)}, f32[512,256]{1,0:T(8,128)}, u32[]{:S(2)}, u32[]{:S(2)}) %collective-permute-start.13) | collective-permute-done | bytes 524320 | tf_op jit(solution)/shard_map/ppermute | solution.py:177
  62.9 0.1 pad_add_fusion
  63.0 0.2 compare_reduce_fusion
  63.3 0.1 pad_add_fusion.5
  63.3 0.1 pad_add_fusion.4
  63.4 6.1 %collective-permute-done.5.refs_2_ = f32[512,256]{1,0:T(8,128)} collective-permute-done((f32[512,256]{1,0:T(8,128)S(1)}, f32[512,256]{1,0:T(8,128)}, u32[]{:S(2)}, u32[]{:S(2)}) %collective-permute-start.5) | collective-permute-done | bytes 524320 | tf_op jit(solution)/shard_map/ppermute | solution.py:177
  69.6 4.1 %collective-permute-done.3.refs_1_ = f32[512,256]{1,0:T(8,128)} collective-permute-done((f32[512,256]{1,0:T(8,128)S(1)}, f32[512,256]{1,0:T(8,128)}, u32[]{:S(2)}, u32[]{:S(2)}) %collective-permute-start.3) | collective-permute-done | bytes 524320 | tf_op jit(solution)/shard_map/ppermute | solution.py:177
  73.7 3.4 %copy-done = f32[512,4096]{1,0:T(8,128)S(1)} copy-done((f32[512,4096]{1,0:T(8,128)S(1)}, f32[512,4096]{1,0:T(8,128)}, u32[]{:S(2)}) %copy-start) | copy-done | bytes 8388632
  77.1 2.6 %shard_map.132.refs_5_ = f32[512,256]{1,0:T(8,128)S(1)} custom-call(s32[18]{0:T(128)S(1)} %get-tuple-element.28.table, f32[512,4096]{1,0:T(8,128)S(1)} %copy-done, f32[512,256]{1,0:T(8,128)S(1)} %pad_maximum_fusion.1.refs_1_, f32[512,256]{1,0:T(8,128)S(1)} %pad_maximum_fusion.3.refs_2_, f32[512,256]{1,0:T(8,128)S(1)} %collective-permute-done.2.refs_3_, ...), custom_call_target="tpu_custom_call" | custom-call | flops 402653184 | bytes 2097152 | tf_op jit(solution)/shard_map/pallas_call | solution.py:135
  79.7 0.0 copy-start.3
  79.8 0.8 copy-done.3
  80.5 3.5 %shard_map.133 = f32[512,256]{1,0:T(8,128)} custom-call(s32[18]{0:T(128)S(1)} %get-tuple-element.30.table, f32[512,4096]{1,0:T(8,128)S(1)} %copy-done, f32[512,256]{1,0:T(8,128)} %collective-permute-done.13.refs_1_, f32[512,256]{1,0:T(8,128)} %collective-permute-done.14.refs_2_, f32[512,256]{1,0:T(8,128)S(1)} %collective-permute-done.15.refs_3_, ...), custom_call_target="tpu_custom_call" | custom-call | flops 402653184 | bytes 2097152 | tf_op jit(solution)/shard_map/pallas_call | solution.py:135
  84.0 2.1 %collective-permute-start.17 = (f32[512,256]{1,0:T(8,128)}, f32[512,256]{1,0:T(8,128)}, u32[]{:S(2)}, u32[]{:S(2)}) collective-permute-start(f32[512,256]{1,0:T(8,128)} %shard_map.133), channel_id=1, source_target_pairs={{0,1},{1,0},{2,3},{3,2},{4,5},{5,4},{6,7},{7,6},{8,9},{9,8},{10,11... | collective-permute-start | bytes 1572872 | tf_op jit(solution)/shard_map/ppermute | solution.py:224
  86.2 3.4 %copy-done.1 = f32[512,4096]{1,0:T(8,128)S(1)} copy-done((f32[512,4096]{1,0:T(8,128)S(1)}, f32[512,4096]{1,0:T(8,128)}, u32[]{:S(2)}) %copy-start.1) | copy-done | bytes 8388632
  89.6 1.0 copy-done.4
  90.6 1.9 %shard_map.131.refs_5_ = f32[512,256]{1,0:T(8,128)S(1)} custom-call(s32[18]{0:T(128)S(1)} %get-tuple-element.29.table, f32[512,4096]{1,0:T(8,128)S(1)} %copy-done.1, f32[512,256]{1,0:T(8,128)S(1)} %pad_maximum_fusion.1.refs_1_, f32[512,256]{1,0:T(8,128)S(1)} %pad_maximum_fusion.3.refs_2_, f32[512,256]{1,0:T(8,128)S(1)} %collective-permute-done.2.refs_3_, ...), custom_call_target="tpu_custom_call" | custom-call | flops 402653184 | bytes 2097152 | tf_op jit(solution)/shard_map/pallas_call | solution.py:135
  92.5 3.2 %collective-permute-done.17.refs_6_ = f32[512,256]{1,0:T(8,128)} collective-permute-done((f32[512,256]{1,0:T(8,128)}, f32[512,256]{1,0:T(8,128)}, u32[]{:S(2)}, u32[]{:S(2)}) %collective-permute-start.17) | collective-permute-done | bytes 524320 | tf_op jit(solution)/shard_map/ppermute | solution.py:224
  95.7 3.4 %copy-done.2 = f32[512,4096]{1,0:T(8,128)S(1)} copy-done((f32[512,4096]{1,0:T(8,128)S(1)}, f32[512,4096]{1,0:T(8,128)}, u32[]{:S(2)}) %copy-start.2) | copy-done | bytes 8388632
  99.0 3.9 %shard_map.134 = (f32[512,256]{1,0:T(8,128)}, f32[256,256]{1,0:T(8,128)S(1)}) custom-call(s32[18]{0:T(128)S(1)} %get-tuple-element.31.table, f32[512,4096]{1,0:T(8,128)S(1)} %copy-done.2, f32[512,256]{1,0:T(8,128)} %collective-permute-done.3.refs_1_, f32[512,256]{1,0:T(8,128)} %collective-permute-done.5.refs_2_, f32[512,256]{1,0:T(8,128)} %collective-permute-done.6.refs_3_, ...), custom_call_target="tpu_custom_call" | custom-call | flops 402653184 | bytes 2097152 | tf_op jit(solution)/shard_map/pallas_call | solution.py:135
  103.0 6.7 %collective-permute-start.18 = (f32[128,256]{1,0:T(8,128)S(1)}, f32[128,256]{1,0:T(8,128)S(1)}, u32[]{:S(2)}, u32[]{:S(2)}) collective-permute-start(f32[128,256]{1,0:T(8,128)S(1)} %slice_select_fusion), channel_id=1, source_target_pairs={{0,2},{2,0},{4,6},{6,4},{8,10},{10,8},{12,14},{14,12},{16,18},{18,... | collective-permute-start | bytes 393224 | tf_op jit(solution)/shard_map/ppermute | solution.py:177
  109.7 1.0 collective-permute-done.18
  110.7 0.4 collective-permute-start.19
  111.2 4.0 %collective-permute-done.19 = f32[64,256]{1,0:T(8,128)S(1)} collective-permute-done((f32[64,256]{1,0:T(8,128)S(1)}, f32[64,256]{1,0:T(8,128)S(1)}, u32[]{:S(2)}, u32[]{:S(2)}) %collective-permute-start.19) | collective-permute-done | bytes 65568 | tf_op jit(solution)/shard_map/ppermute | solution.py:177
  115.2 0.5 collective-permute-start.20
  115.7 5.5 %collective-permute-start.21 = (f32[64,256]{1,0:T(8,128)S(1)}, f32[64,256]{1,0:T(8,128)S(1)}, u32[]{:S(2)}, u32[]{:S(2)}) collective-permute-start(f32[64,256]{1,0:T(8,128)S(1)} %select_add_fusion.1), channel_id=1, source_target_pairs={{0,16},{2,18},{4,20},{6,22},{8,24},{10,26},{12,28},{14,30},{16,0},... | collective-permute-start | bytes 196616 | tf_op jit(solution)/shard_map/ppermute | solution.py:177
  121.2 3.8 %collective-permute-done.21 = f32[64,256]{1,0:T(8,128)S(1)} collective-permute-done((f32[64,256]{1,0:T(8,128)S(1)}, f32[64,256]{1,0:T(8,128)S(1)}, u32[]{:S(2)}, u32[]{:S(2)}) %collective-permute-start.21) | collective-permute-done | bytes 65568 | tf_op jit(solution)/shard_map/ppermute | solution.py:177
  124.9 2.3 %collective-permute-done.22 = f32[64,256]{1,0:T(8,128)S(1)} collective-permute-done((f32[64,256]{1,0:T(8,128)S(1)}, f32[64,256]{1,0:T(8,128)S(1)}, u32[]{:S(2)}, u32[]{:S(2)}) %collective-permute-start.22) | collective-permute-done | bytes 65568 | tf_op jit(solution)/shard_map/ppermute | solution.py:177
  127.2 0.2 collective-permute-start.23
  127.5 4.1 %collective-permute-done.23 = f32[64,256]{1,0:T(8,128)S(1)} collective-permute-done((f32[64,256]{1,0:T(8,128)S(1)}, f32[64,256]{1,0:T(8,128)S(1)}, u32[]{:S(2)}, u32[]{:S(2)}) %collective-permute-start.23) | collective-permute-done | bytes 65568 | tf_op jit(solution)/shard_map/ppermute | solution.py:177
  131.6 0.1 collective-permute-start.24
  131.7 1.3 collective-permute-done.24
  133.0 0.7 maximum_subtract_fusion
  (45 shorter events, 0.3 us)
Async XLA Ops:
  0.6 48.9 %copy-start.8 = (s32[8]{0:T(128)S(1)}, s32[8]{0:T(128)}, u32[]{:S(2)}) copy-start(s32[8]{0:T(128)} %constant.57.clone) | copy-start | bytes 100
  0.6 48.9 %copy-start.9 = (s32[8]{0:T(128)S(1)}, s32[8]{0:T(128)}, u32[]{:S(2)}) copy-start(s32[8]{0:T(128)} %constant.58.clone) | copy-start | bytes 100
  0.7 48.9 %copy-start.10 = (s32[8]{0:T(128)S(1)}, s32[8]{0:T(128)}, u32[]{:S(2)}) copy-start(s32[8]{0:T(128)} %constant.59.clone) | copy-start | bytes 100
  0.7 48.9 %copy-start.11 = (s32[8]{0:T(128)S(1)}, s32[8]{0:T(128)}, u32[]{:S(2)}) copy-start(s32[8]{0:T(128)} %constant.60.clone) | copy-start | bytes 100
  0.7 62.3 %copy-start.12 = (s32[1,16]{1,0:T(1,128)S(1)}, s32[1,16]{1,0:T(1,128)}, u32[]{:S(2)}) copy-start(s32[1,16]{1,0:T(1,128)} %param.14) | copy-start | bytes 196
  0.7 15.7 %collective-permute-start = (f32[512,256]{1,0:T(8,128)}, f32[512,256]{1,0:T(8,128)S(1)}, u32[]{:S(2)}, u32[]{:S(2)}) collective-permute-start(f32[512,256]{1,0:T(8,128)} %refs_7_.1), channel_id=1, source_target_pairs={{0,16},{1,0},{2,18},{3,2},{4,20},{5,4},{6,22},{7,6},{8,24},{9,8},{... | collective-permute-start | bytes 1572872 | tf_op jit(solution)/shard_map/ppermute | solution.py:187
  4.8 11.5 %collective-permute-start.1 = (f32[512,256]{1,0:T(8,128)}, f32[512,256]{1,0:T(8,128)S(1)}, u32[]{:S(2)}, u32[]{:S(2)}) collective-permute-start(f32[512,256]{1,0:T(8,128)} %refs_7_.1), channel_id=1, source_target_pairs={{1,16},{3,18},{5,20},{7,22},{9,24},{11,26},{13,28},{15,30},{16,1},... | collective-permute-start | bytes 1572872 | tf_op jit(solution)/shard_map/ppermute | solution.py:188
  17.6 0.7 copy-start.6
  18.3 24.8 %collective-permute-start.4 = (f32[512,256]{1,0:T(8,128)S(1)}, f32[512,256]{1,0:T(8,128)S(1)}, u32[]{:S(2)}, u32[]{:S(2)}) collective-permute-start(f32[512,256]{1,0:T(8,128)S(1)} %pad_maximum_fusion.3.refs_2_), channel_id=1, source_target_pairs={{0,8},{2,10},{4,12},{6,14},{8,0},{10,2},{12,4},{14,6},{16,24},{18,... | collective-permute-start | bytes 1572872 | tf_op jit(solution)/shard_map/ppermute | solution.py:177
  31.1 15.1 %collective-permute-start.2 = (f32[512,256]{1,0:T(8,128)S(1)}, f32[512,256]{1,0:T(8,128)S(1)}, u32[]{:S(2)}, u32[]{:S(2)}) collective-permute-start(f32[512,256]{1,0:T(8,128)S(1)} %pad_maximum_fusion.1.refs_1_), channel_id=1, source_target_pairs={{0,4},{2,6},{4,0},{6,2},{8,12},{10,14},{12,8},{14,10},{16,20},{18,... | collective-permute-start | bytes 1572872 | tf_op jit(solution)/shard_map/ppermute | solution.py:177
  32.6 15.2 %collective-permute-start.12 = (s32[1,16]{1,0:T(1,128)}, s32[1,16]{1,0:T(1,128)S(1)}, u32[]{:S(2)}, u32[]{:S(2)}) collective-permute-start(s32[1,16]{1,0:T(1,128)} %param.14), channel_id=1, source_target_pairs={{0,1},{1,0},{2,3},{3,2},{4,5},{5,4},{6,7},{7,6},{8,9},{9,8},{10,11... | collective-permute-start | bytes 200 | tf_op jit(solution)/shard_map/ppermute | solution.py:189
  36.2 15.4 %collective-permute-start.9 = (f32[512,256]{1,0:T(8,128)S(1)}, f32[512,256]{1,0:T(8,128)S(1)}, u32[]{:S(2)}, u32[]{:S(2)}) collective-permute-start(f32[512,256]{1,0:T(8,128)S(1)} %pad_maximum_fusion.3.refs_2_), channel_id=1, source_target_pairs={{0,2},{2,0},{4,6},{6,4},{8,10},{10,8},{12,14},{14,12},{16,18},{18,... | collective-permute-start | bytes 1572872 | tf_op jit(solution)/shard_map/ppermute | solution.py:177
  36.2 16.0 %collective-permute-start.8 = (f32[512,256]{1,0:T(8,128)S(1)}, f32[512,256]{1,0:T(8,128)S(1)}, u32[]{:S(2)}, u32[]{:S(2)}) collective-permute-start(f32[512,256]{1,0:T(8,128)S(1)} %pad_maximum_fusion.1.refs_1_), channel_id=1, source_target_pairs={{0,2},{2,0},{4,6},{6,4},{8,10},{10,8},{12,14},{14,12},{16,18},{18,... | collective-permute-start | bytes 1572872 | tf_op jit(solution)/shard_map/ppermute | solution.py:177
  44.7 15.1 %collective-permute-start.14 = (f32[512,256]{1,0:T(8,128)}, f32[512,256]{1,0:T(8,128)}, u32[]{:S(2)}, u32[]{:S(2)}) collective-permute-start(f32[512,256]{1,0:T(8,128)} %pad_maximum_fusion.2), channel_id=1, source_target_pairs={{0,4},{2,6},{4,0},{6,2},{8,12},{10,14},{12,8},{14,10},{16,20},{18,... | collective-permute-start | bytes 1572872 | tf_op jit(solution)/shard_map/ppermute | solution.py:177
  46.2 6.3 %collective-permute-start.11 = (f32[512,256]{1,0:T(8,128)S(1)}, f32[512,256]{1,0:T(8,128)}, u32[]{:S(2)}, u32[]{:S(2)}) collective-permute-start(f32[512,256]{1,0:T(8,128)S(1)} %collective-permute-done.4.refs_4_), channel_id=1, source_target_pairs={{0,2},{2,0},{4,6},{6,4},{8,10},{10,8},{12,14},{14,12},{16,18},{18,... | collective-permute-start | bytes 1572872 | tf_op jit(solution)/shard_map/ppermute | solution.py:177
  47.8 15.1 %collective-permute-start.13 = (f32[512,256]{1,0:T(8,128)}, f32[512,256]{1,0:T(8,128)}, u32[]{:S(2)}, u32[]{:S(2)}) collective-permute-start(f32[512,256]{1,0:T(8,128)} %pad_maximum_fusion), channel_id=1, source_target_pairs={{0,8},{2,10},{4,12},{6,14},{8,0},{10,2},{12,4},{14,6},{16,24},{18,... | collective-permute-start | bytes 1572872 | tf_op jit(solution)/shard_map/ppermute | solution.py:177
  51.7 17.9 %collective-permute-start.5 = (f32[512,256]{1,0:T(8,128)S(1)}, f32[512,256]{1,0:T(8,128)}, u32[]{:S(2)}, u32[]{:S(2)}) collective-permute-start(f32[512,256]{1,0:T(8,128)S(1)} %pad_maximum_fusion.5), channel_id=1, source_target_pairs={{0,4},{2,6},{4,0},{6,2},{8,12},{10,14},{12,8},{14,10},{16,20},{18,... | collective-permute-start | bytes 1572872 | tf_op jit(solution)/shard_map/ppermute | solution.py:177
  52.3 21.4 %collective-permute-start.3 = (f32[512,256]{1,0:T(8,128)S(1)}, f32[512,256]{1,0:T(8,128)}, u32[]{:S(2)}, u32[]{:S(2)}) collective-permute-start(f32[512,256]{1,0:T(8,128)S(1)} %pad_maximum_fusion.4), channel_id=1, source_target_pairs={{0,8},{2,10},{4,12},{6,14},{8,0},{10,2},{12,4},{14,6},{16,24},{18,... | collective-permute-start | bytes 1572872 | tf_op jit(solution)/shard_map/ppermute | solution.py:177
  52.5 21.2 %collective-permute-start.10 = (f32[512,256]{1,0:T(8,128)S(1)}, f32[512,256]{1,0:T(8,128)S(1)}, u32[]{:S(2)}, u32[]{:S(2)}) collective-permute-start(f32[512,256]{1,0:T(8,128)S(1)} %collective-permute-done.2.refs_3_), channel_id=1, source_target_pairs={{0,2},{2,0},{4,6},{6,4},{8,10},{10,8},{12,14},{14,12},{16,18},{18,... | collective-permute-start | bytes 1572872 | tf_op jit(solution)/shard_map/ppermute | solution.py:177
  59.9 20.7 %collective-permute-start.16 = (f32[512,256]{1,0:T(8,128)}, f32[512,256]{1,0:T(8,128)S(1)}, u32[]{:S(2)}, u32[]{:S(2)}) collective-permute-start(f32[512,256]{1,0:T(8,128)} %collective-permute-done.14.refs_2_), channel_id=1, source_target_pairs={{0,2},{2,0},{4,6},{6,4},{8,10},{10,8},{12,14},{14,12},{16,18},{18,... | collective-permute-start | bytes 1572872 | tf_op jit(solution)/shard_map/ppermute | solution.py:177
  62.9 17.6 %collective-permute-start.15 = (f32[512,256]{1,0:T(8,128)}, f32[512,256]{1,0:T(8,128)S(1)}, u32[]{:S(2)}, u32[]{:S(2)}) collective-permute-start(f32[512,256]{1,0:T(8,128)} %collective-permute-done.13.refs_1_), channel_id=1, source_target_pairs={{0,2},{2,0},{4,6},{6,4},{8,10},{10,8},{12,14},{14,12},{16,18},{18,... | collective-permute-start | bytes 1572872 | tf_op jit(solution)/shard_map/ppermute | solution.py:177
  69.6 22.9 %collective-permute-start.7 = (f32[512,256]{1,0:T(8,128)}, f32[512,256]{1,0:T(8,128)}, u32[]{:S(2)}, u32[]{:S(2)}) collective-permute-start(f32[512,256]{1,0:T(8,128)} %collective-permute-done.5.refs_2_), channel_id=1, source_target_pairs={{0,2},{2,0},{4,6},{6,4},{8,10},{10,8},{12,14},{14,12},{16,18},{18,... | collective-permute-start | bytes 1572872 | tf_op jit(solution)/shard_map/ppermute | solution.py:177
  73.7 18.8 %collective-permute-start.6 = (f32[512,256]{1,0:T(8,128)}, f32[512,256]{1,0:T(8,128)}, u32[]{:S(2)}, u32[]{:S(2)}) collective-permute-start(f32[512,256]{1,0:T(8,128)} %collective-permute-done.3.refs_1_), channel_id=1, source_target_pairs={{0,2},{2,0},{4,6},{6,4},{8,10},{10,8},{12,14},{14,12},{16,18},{18,... | collective-permute-start | bytes 1572872 | tf_op jit(solution)/shard_map/ppermute | solution.py:177
  73.7 3.4 %copy-start = (f32[512,4096]{1,0:T(8,128)S(1)}, f32[512,4096]{1,0:T(8,128)}, u32[]{:S(2)}) copy-start(f32[512,4096]{1,0:T(8,128)} %refs_0_.7) | copy-start | bytes 25165828
  79.7 0.8 copy-start.3
  84.0 11.6 %collective-permute-start.17 = (f32[512,256]{1,0:T(8,128)}, f32[512,256]{1,0:T(8,128)}, u32[]{:S(2)}, u32[]{:S(2)}) collective-permute-start(f32[512,256]{1,0:T(8,128)} %shard_map.133), channel_id=1, source_target_pairs={{0,1},{1,0},{2,3},{3,2},{4,5},{5,4},{6,7},{7,6},{8,9},{9,8},{10,11... | collective-permute-start | bytes 1572872 | tf_op jit(solution)/shard_map/ppermute | solution.py:224
  86.2 3.4 %copy-start.1 = (f32[512,4096]{1,0:T(8,128)S(1)}, f32[512,4096]{1,0:T(8,128)}, u32[]{:S(2)}) copy-start(f32[512,4096]{1,0:T(8,128)} %refs_0_.7) | copy-start | bytes 25165828
  89.6 1.0 copy-start.4
  90.6 5.0 %copy-start.5 = (f32[512,256]{1,0:T(8,128)S(1)}, f32[512,256]{1,0:T(8,128)}, u32[]{:S(2)}) copy-start(f32[512,256]{1,0:T(8,128)} %refs_7_.1) | copy-start | bytes 1572868
  90.6 42.4 %copy-start.7 = (f32[256,256]{1,0:T(8,128)S(1)}, f32[256,256]{1,0:T(8,128)}, u32[]{:S(2)}) copy-start(f32[256,256]{1,0:T(8,128)} %param.15) | copy-start | bytes 786436
  95.6 3.4 %copy-start.2 = (f32[512,4096]{1,0:T(8,128)S(1)}, f32[512,4096]{1,0:T(8,128)}, u32[]{:S(2)}) copy-start(f32[512,4096]{1,0:T(8,128)} %refs_0_.7) | copy-start | bytes 25165828
  103.0 7.7 %collective-permute-start.18 = (f32[128,256]{1,0:T(8,128)S(1)}, f32[128,256]{1,0:T(8,128)S(1)}, u32[]{:S(2)}, u32[]{:S(2)}) collective-permute-start(f32[128,256]{1,0:T(8,128)S(1)} %slice_select_fusion), channel_id=1, source_target_pairs={{0,2},{2,0},{4,6},{6,4},{8,10},{10,8},{12,14},{14,12},{16,18},{18,... | collective-permute-start | bytes 393224 | tf_op jit(solution)/shard_map/ppermute | solution.py:177
  110.7 4.4 %collective-permute-start.19 = (f32[64,256]{1,0:T(8,128)S(1)}, f32[64,256]{1,0:T(8,128)S(1)}, u32[]{:S(2)}, u32[]{:S(2)}) collective-permute-start(f32[64,256]{1,0:T(8,128)S(1)} %slice_select_fusion.1), channel_id=1, source_target_pairs={{0,4},{2,6},{4,0},{6,2},{8,12},{10,14},{12,8},{14,10},{16,20},{18,... | collective-permute-start | bytes 196616 | tf_op jit(solution)/shard_map/ppermute | solution.py:177
  115.2 6.0 %collective-permute-start.20 = (f32[64,256]{1,0:T(8,128)S(1)}, f32[64,256]{1,0:T(8,128)S(1)}, u32[]{:S(2)}, u32[]{:S(2)}) collective-permute-start(f32[64,256]{1,0:T(8,128)S(1)} %select_add_fusion.1), channel_id=1, source_target_pairs={{0,8},{2,10},{4,12},{6,14},{8,0},{10,2},{12,4},{14,6},{16,24},{18,... | collective-permute-start | bytes 196616 | tf_op jit(solution)/shard_map/ppermute | solution.py:177
  115.7 9.2 %collective-permute-start.21 = (f32[64,256]{1,0:T(8,128)S(1)}, f32[64,256]{1,0:T(8,128)S(1)}, u32[]{:S(2)}, u32[]{:S(2)}) collective-permute-start(f32[64,256]{1,0:T(8,128)S(1)} %select_add_fusion.1), channel_id=1, source_target_pairs={{0,16},{2,18},{4,20},{6,22},{8,24},{10,26},{12,28},{14,30},{16,0},... | collective-permute-start | bytes 196616 | tf_op jit(solution)/shard_map/ppermute | solution.py:177
  121.2 6.1 %collective-permute-start.22 = (f32[64,256]{1,0:T(8,128)S(1)}, f32[64,256]{1,0:T(8,128)S(1)}, u32[]{:S(2)}, u32[]{:S(2)}) collective-permute-start(f32[64,256]{1,0:T(8,128)S(1)} %select_add_fusion.1), channel_id=1, source_target_pairs={{0,24},{2,26},{4,28},{6,30},{8,16},{10,18},{12,20},{14,22},{16,8},... | collective-permute-start | bytes 196616 | tf_op jit(solution)/shard_map/ppermute | solution.py:177
  127.2 4.3 %collective-permute-start.23 = (f32[64,256]{1,0:T(8,128)S(1)}, f32[64,256]{1,0:T(8,128)S(1)}, u32[]{:S(2)}, u32[]{:S(2)}) collective-permute-start(f32[64,256]{1,0:T(8,128)S(1)} %add_add_fusion), channel_id=1, source_target_pairs={{0,4},{2,6},{4,0},{6,2},{8,12},{10,14},{12,8},{14,10},{16,20},{18,... | collective-permute-start | bytes 196616 | tf_op jit(solution)/shard_map/ppermute | solution.py:177
  131.6 1.4 %collective-permute-start.24 = (f32[128,256]{1,0:T(8,128)S(1)}, f32[128,256]{1,0:T(8,128)S(1)}, u32[]{:S(2)}, u32[]{:S(2)}) collective-permute-start(f32[128,256]{1,0:T(8,128)S(1)} %pad_maximum_fusion.6), channel_id=1, source_target_pairs={{0,2},{2,0},{4,6},{6,4},{8,10},{10,8},{12,14},{14,12},{16,18},{18,... | collective-permute-start | bytes 393224 | tf_op jit(solution)/shard_map/ppermute | solution.py:177
where the time goes:
time: 134 us
  waiting for transfers between devices  57.6 us (43%)
  starting transfers between devices  42.8 us (32%)
  local copies, waits for them, and re-layouts  14.3 us (11%)
  Pallas kernels  11.9 us (9%)
  other arithmetic  6.27 us (5%)
    ppermute x21, waiting for transfers between devices, swap(): return lax.ppermute(value, 'row', [(i, i ^ mask) for i in range(n_row)])  43.6 us
    ppermute x21, starting transfers between devices, swap(): return lax.ppermute(value, 'row', [(i, i ^ mask) for i in range(n_row)])  32.3 us
    unnamed x26, local copies, waits for them, and re-layouts  12.7 us
    pallas_call x4, Pallas kernels, product(): pl.pallas_call(functools.partial(product_kernel, slots, blocks, width, ac...  11.9 us
    ppermute x1, waiting for transfers between devices, local_two(): got_first = lax.ppermute(lower_panel, BOTH, first)  10.8 us
    ppermute x1, starting transfers between devices, local_two(): got_first = lax.ppermute(lower_panel, BOTH, first)  4.12 us
    ppermute x1, starting transfers between devices, local_two(): other_structure = lax.ppermute(structure, 'col', flip)  3.59 us
    ppermute x1, waiting for transfers between devices, local_two(): recv = lax.ppermute(part, 'col', flip)  3.16 us
  transfers between devices with their start and end apart: 25, of which 13 were waited for; matrix products, arithmetic and copies ran while one was open for 4% of the time, Pallas kernels for 6%

commit v1 on v0

--- a/solution.py
+++ b/solution.py
@@ -56,11 +56,9 @@
     a_hbm = refs.pop(0)
     arrays = [refs.pop(0) for _ in range(narrays)]
     acc_in = refs.pop(0) if has_acc else None
-    if final:
-        recv, lower = refs.pop(0), refs.pop(0)
+    extra = refs.pop(0) if final else None
     out = refs.pop(0)
-    if final:
-        terms = refs.pop(0)
+    terms = refs.pop(0) if final == "terms" else None
     a_buf, p_buf, a_sem, p_sem = refs
     row_on = [table[2 * count + rb] > 0 for rb in range(blocks)]
 
@@ -99,41 +97,49 @@
                     a_copy(p, rb).wait()
                     out[pl.ds(rb * width, width), :] += dot3(split(a_buf[p, rb]), piece, ((1,), (0,)))
 
-    if final:
+    if final == "terms":
         terms[...] = jnp.zeros_like(terms)
         for rb in range(blocks):
             rows = pl.ds(rb * width, width)
 
             @pl.when(row_on[rb])
             def _(rows=rows):
-                panel = -(out[rows, :] + recv[rows, :])
-                out[rows, :] = panel
-                terms[...] += dot3(split(lower[rows, :]), split(panel), ((0,), (0,)))
+                terms[...] += dot3(split(extra[rows, :]), split(out[rows, :]), ((0,), (0,)))
+
+        @pl.when(table[2 * count + blocks] > 0)
+        def _():
+            terms[...] += terms[...].T
+
+    if final == "panel":
+        for rb in range(blocks):
+            rows = pl.ds(rb * width, width)
+
+            @pl.when(row_on[rb])
+            def _(rows=rows):
+                out[rows, :] = -(out[rows, :] + extra[rows, :])
 
             @pl.when(jnp.logical_not(row_on[rb]))
             def _(rows=rows):
                 out[rows, :] = jnp.zeros((width, out.shape[1]), jnp.float32)
 
 
-def product(table, inverse_anc, arrays, slots, width, acc=None, final=None):
+def product(table, inverse_anc, arrays, slots, width, acc=None, final=None, extra=None):
     rows = inverse_anc.shape[0]
     blocks = rows // width
     count = len(slots)
     any_spec = pl.BlockSpec(memory_space=pl.ANY)
     vmem = pl.BlockSpec(memory_space=pltpu.VMEM)
-    operands = [inverse_anc, *arrays]
-    specs = [any_spec] * len(operands)
-    if acc is not None:
-        operands.append(acc)
-        specs.append(vmem)
-    if final is not None:
-        operands += list(final)
-        specs += [vmem, vmem]
+    operands = [pltpu.with_memory_space_constraint(inverse_anc, pltpu.HBM), *arrays]
+    specs = [pl.BlockSpec(memory_space=pltpu.HBM)] + [any_spec] * len(arrays)
+    for more in (acc, extra):
+        if more is not None:
+            operands.append(more)
+            specs.append(vmem)
     shapes = [jax.ShapeDtypeStruct((rows, width), jnp.float32)]
-    if final is not None:
+    if final == "terms":
         shapes.append(jax.ShapeDtypeStruct((width, width), jnp.float32))
     return pl.pallas_call(
-        functools.partial(product_kernel, slots, blocks, width, acc is not None, final is not None),
+        functools.partial(product_kernel, slots, blocks, width, acc is not None, final),
         out_shape=shapes,
         grid_spec=pltpu.PrefetchScalarGridSpec(
             num_scalar_prefetch=1,
@@ -147,7 +153,7 @@
                 pltpu.SemaphoreType.DMA((count,)),
             ],
         ),
-        compiler_params=pltpu.CompilerParams(vmem_limit_bytes=20 * 1024 * 1024),
+        compiler_params=pltpu.CompilerParams(vmem_limit_bytes=13 * 1024 * 1024),
         cost_estimate=pl.CostEstimate(
             flops=6 * rows * width * width * count // 4,
             bytes_accessed=4 * rows * width * count // 2,
@@ -159,90 +165,109 @@
 CORE, X, Z, FAR = 1, 2, 4, 8
 FIRST = ((0, 0), (0, 1), (X, 0), (Z, 1))
 SECOND = ((Z, 0), (Z | X, 0), (X, 1), (Z | X, 1))
-
-
-def with_sibling(order):
-    return order + tuple((m ^ CORE, h) for m, h in order)
+SLOTS1 = ((0, 0), (0, 1), (1, 0), (2, 0), (3, 0), (3, 1), (4, 0), (5, 0))
+SLOTS2 = ((0, 0), (0, 1), (1, 0), (1, 1), (2, 0), (2, 1), (3, 0), (3, 1))
 
 
 def local_two(n_row, inverse_anc, lower_panel, structure, diag_inverse):
     n_col = 2
     rows = inverse_anc.shape[0]
     width = diag_inverse.shape[1]
+    half = rows // 2
     row, col = lax.axis_index("row"), lax.axis_index("col")
     near = (row // FAR) == col
-    flip = [(0, 1), (1, 0)]
-
-    def swap(value, mask):
-        return lax.ppermute(value, "row", [(i, i ^ mask) for i in range(n_row)])
-
-    def linear(r, c):
-        return r * n_col + c
-
     every = [(r, c) for r in range(n_row) for c in range(n_col)]
-    first = [
-        (linear(r, c), linear(r ^ FAR, c) if r // FAR == c else linear(r, 1 - c)) for r, c in every
-    ]
-    second = [(linear(r, c), linear(r ^ FAR, 1 - c)) for r, c in every if r // FAR != c]
-    got_first = lax.ppermute(lower_panel, BOTH, first)
-    got_second = lax.ppermute(lower_panel, BOTH, second)
-    other_structure = lax.ppermute(structure, "col", flip)
-    q_own = jnp.where(near, lower_panel, got_first)
-    q_other = jnp.where(near, got_first, got_second)
-
-    def table(listed, order):
-        order = with_sibling(order)
+
+    def is_near(r, c):
+        return r // FAR == c
+
+    def move(value, mask, across, who=None):
+        pairs = [
+            (r * n_col + c, (r ^ mask) * n_col + (c ^ across))
+            for r, c in every
+            if who is None or is_near(r, c) == who
+        ]
+        return lax.ppermute(value, BOTH, pairs)
+
+    def table(listed, order, who):
+        order = order + tuple((m ^ CORE, h) for m, h in order)
         block = ((row % FAR) ^ jnp.array([m for m, _ in order], jnp.int32)) * 2
         block = block + jnp.array([h for _, h in order], jnp.int32)
         ids = jnp.concatenate([block + col * 2 * FAR, row * 2 + jnp.arange(2, dtype=jnp.int32)])
-        on = jnp.any(ids[:, None] == listed[0][None, :], axis=1).astype(jnp.int32)
-        return jnp.concatenate([block, on])
-
-    half = rows // 2
-    s0 = jnp.concatenate([q_other[:half], q_own[:half]])
-    s1 = jnp.concatenate([q_other[half:], q_own[half:]])
-    x1 = swap(s0, X)
-    z1 = swap(s1, Z)
-    got = []
-    for at in (0, 1):
-        part = slice(at * half, (at + 1) * half)
-        z2 = swap(jnp.concatenate([s0[part], x1[part]]), Z)
-        x2 = swap(jnp.concatenate([s1[part], z1[part]]), X)
-        got.append([z2, x2])
-    near_arrays = [s0, s1, x1, z1]
-    near_arrays += [swap(v, CORE) for v in near_arrays]
-    far_arrays = [v + [swap(u, CORE) for u in v] for v in got]
-
-    def slots1(at):
-        return tuple((i, at) for i in range(8))
-
-    slots2 = tuple((i, h) for i in range(4) for h in range(2))
-    (part,) = product(table(other_structure, FIRST), inverse_anc, near_arrays, slots1(0), width)
-    (part,) = product(
-        table(other_structure, SECOND), inverse_anc, far_arrays[0], slots2, width, acc=part
-    )
-    recv = lax.ppermute(part, "col", flip)
-    (acc,) = product(table(structure, FIRST), inverse_anc, near_arrays, slots1(1), width)
-    panel, terms = product(
-        table(structure, SECOND), inverse_anc, far_arrays[1], slots2, width,
-        acc=acc, final=(recv, lower_panel),
-    )
-
-    def halve(value, mask):
+        on = jnp.any(ids[:, None] == listed[0][None, :], axis=1)
+        count = len(order)
+        if who is not None:
+            on = on & ((jnp.arange(count + 2) >= count) | (near == who))
+        far = jnp.logical_not(near) if who is None else jnp.zeros((), jnp.bool_)
+        return jnp.concatenate([block, on.astype(jnp.int32), far.astype(jnp.int32)[None]])
+
+    def step_one(q, who):
+        return move(q[:half], X, 0, who), move(q[half:], Z, 0, who)
+
+    def step_two(q, one, who):
+        z2 = move(jnp.concatenate([q[:half], one[0]]), Z, 0, who)
+        return z2, move(jnp.concatenate([q[half:], one[1]]), X, 0, who)
+
+    def with_sibling(arrays, who):
+        return list(arrays) + [move(v, CORE, 0, who) for v in arrays]
+
+    got_far = move(lower_panel, FAR, 1, False)
+    lower_other = move(lower_panel, 0, 1)
+    q_far = move(lower_panel, FAR, 0, True)
+    other_structure = move(structure, 0, 1)
+
+    n_one = step_one(lower_panel, True)
+    n_two = step_two(lower_panel, n_one, True)
+    n_first = with_sibling([lower_panel, *n_one], True)
+    n_second = with_sibling(n_two, True)
+    q_other = jnp.where(near, lower_other, got_far)
+    o_one = step_one(q_other, None)
+    o_two = step_two(q_other, o_one, None)
+    o_first = with_sibling([q_other, *o_one], None)
+    o_second = with_sibling(o_two, None)
+    f_one = step_one(q_far, False)
+    f_two = step_two(q_far, f_one, False)
+    f_first = with_sibling([q_far, *f_one], False)
+    f_second = with_sibling(f_two, False)
+
+    (own,) = product(table(structure, FIRST, True), inverse_anc, n_first, SLOTS1, width)
+    own, own_terms = product(
+        table(structure, SECOND, True), inverse_anc, n_second, SLOTS2, width,
+        acc=own, final="terms", extra=lower_panel,
+    )
+    (part,) = product(table(other_structure, FIRST, None), inverse_anc, o_first, SLOTS1, width)
+    part, other_terms = product(
+        table(other_structure, SECOND, None), inverse_anc, o_second, SLOTS2, width,
+        acc=part, final="terms", extra=lower_other,
+    )
+    recv = move(part, 0, 1)
+    (own,) = product(table(structure, FIRST, False), inverse_anc, f_first, SLOTS1, width, acc=own)
+    (panel,) = product(
+        table(structure, SECOND, False), inverse_anc, f_second, SLOTS2, width,
+        acc=own, final="panel", extra=recv,
+    )
+
+    def parts(value, mask):
         size = value.shape[0] // 2
         bit = (row & mask) > 0
         low, high = value[:size], value[size:]
-        return jnp.where(bit, high, low) + swap(jnp.where(bit, low, high), mask)
+        return jnp.where(bit, high, low), jnp.where(bit, low, high)
 
     def double(value, mask):
         bit = (row & mask) > 0
-        got = swap(value, mask)
+        got = move(value, mask, 0)
         return jnp.concatenate([jnp.where(bit, got, value), jnp.where(bit, value, got)])
 
-    total = halve(halve(terms, CORE), X)
-    total = total + swap(total, Z) + swap(total, FAR) + swap(total, FAR | Z)
+    u_keep, u_send = parts(own_terms, CORE)
+    v_keep, v_send = parts(other_terms, CORE)
+    size = u_keep.shape[0]
+    got = move(jnp.concatenate([u_send, v_send]), CORE, 0)
+    u_keep, u_send = parts(u_keep + got[:size], X)
+    v_keep, v_send = parts(v_keep + got[size:], X)
+    total = u_keep + move(u_send, X, 0) + move(v_keep, 0, 1) + move(v_send, X, 1)
+    total = total + move(total, Z, 0) + move(total, FAR, 0) + move(total, FAR | Z, 0)
     total = double(double(total, X), CORE)
-    return panel, diag_inverse - total
+    return panel, diag_inverse + total
 
 
 def solution(mesh):

time: 134 us -> 139 us (1.037)
  the two profiles are of different devices: /device:TPU:0 before, /device:TPU:24 now
where the time goes in v1:
time: 139 us
  waiting for transfers between devices  58 us (42%)
  starting transfers between devices  44.4 us (32%)
  Pallas kernels  20.8 us (15%)
  other arithmetic  10.3 us (7%)
  local copies, waits for them, and re-layouts  3.81 us (3%)
    ppermute x41, waiting for transfers between devices, move(): return lax.ppermute(value, BOTH, pairs)  58 us
    ppermute x41, starting transfers between devices, move(): return lax.ppermute(value, BOTH, pairs)  44.4 us
    pallas_call x6, Pallas kernels, product(): pl.pallas_call(functools.partial(product_kernel, slots, blocks, width, ac...  20.8 us
    concatenate x3, other arithmetic, step_two(): return (z2, move(jnp.concatenate([q[half:], one[1]]), X, 0, who))  2.96 us
    concatenate x3, other arithmetic, step_two(): z2 = move(jnp.concatenate([q[:half], one[0]]), Z, 0, who)  2.81 us
  transfers between devices with their start and end apart: 41, of which 12 were waited for; matrix products, arithmetic and copies ran while one was open for 9% of the time, Pallas kernels for 15%

profile of v1, /device:TPU:24, one launch (start us, length us, event | category | flops | bytes accessed | tf_op | source)
XLA Modules:
  0.0 138.6 jit_solution(8371500578099791555)
XLA Ops:
  0.6 1.6 %collective-permute-start.20 = (f32[512,256]{1,0:T(8,128)}, f32[512,256]{1,0:T(8,128)S(1)}, u32[]{:S(2)}, u32[]{:S(2)}) collective-permute-start(f32[512,256]{1,0:T(8,128)} %refs_6_.1), channel_id=1, source_target_pairs={{0,1},{1,0},{2,3},{3,2},{4,5},{5,4},{6,7},{7,6},{8,9},{9,8},{10,11... | collective-permute-start | bytes 1572872 | tf_op jit(solution)/shard_map/ppermute | solution.py:190
  2.2 2.2 %collective-permute-start.21 = (f32[512,256]{1,0:T(8,128)}, f32[512,256]{1,0:T(8,128)S(1)}, u32[]{:S(2)}, u32[]{:S(2)}) collective-permute-start(f32[512,256]{1,0:T(8,128)} %refs_6_.1), channel_id=1, source_target_pairs={{1,16},{3,18},{5,20},{7,22},{9,24},{11,26},{13,28},{15,30},{16,1},... | collective-permute-start | bytes 1572872 | tf_op jit(solution)/shard_map/ppermute | solution.py:190
  4.5 1.1 fusion.1
  5.6 0.7 collective-permute-start.10
  6.2 0.7 collective-permute-start.12
  7.0 0.7 multiply_add_fusion
  7.7 0.7 collective-permute-start.17
  8.4 6.3 %collective-permute-done.20.refs_6_ = f32[512,256]{1,0:T(8,128)S(1)} collective-permute-done((f32[512,256]{1,0:T(8,128)}, f32[512,256]{1,0:T(8,128)S(1)}, u32[]{:S(2)}, u32[]{:S(2)}) %collective-permute-start.20) | collective-permute-done | bytes 524320 | tf_op jit(solution)/shard_map/ppermute | solution.py:190
  14.7 16.0 %collective-permute-done.21 = f32[512,256]{1,0:T(8,128)S(1)} collective-permute-done((f32[512,256]{1,0:T(8,128)}, f32[512,256]{1,0:T(8,128)S(1)}, u32[]{:S(2)}, u32[]{:S(2)}) %collective-permute-start.21) | collective-permute-done | bytes 524320 | tf_op jit(solution)/shard_map/ppermute | solution.py:190
  30.8 0.9 fusion
  31.6 1.5 %collective-permute-start.22 = (f32[256,256]{1,0:T(8,128)}, f32[256,256]{1,0:T(8,128)S(1)}, u32[]{:S(2)}, u32[]{:S(2)}) collective-permute-start(f32[256,256]{1,0:T(8,128)} %get-tuple-element.15), channel_id=1, source_target_pairs={{0,4},{1,5},{2,6},{3,7},{4,0},{5,1},{6,2},{7,3},{8,12},{9,13},{10,... | collective-permute-start | bytes 786440 | tf_op jit(solution)/shard_map/ppermute | solution.py:190
  33.1 0.8 pad_maximum_fusion.2
  34.0 1.5 %collective-permute-start.16 = (f32[512,256]{1,0:T(8,128)}, f32[512,256]{1,0:T(8,128)}, u32[]{:S(2)}, u32[]{:S(2)}) collective-permute-start(f32[512,256]{1,0:T(8,128)} %refs_6_.1), channel_id=1, source_target_pairs={{0,2},{2,0},{4,6},{6,4},{8,10},{10,8},{12,14},{14,12},{17,19},{19,... | collective-permute-start | bytes 1572872 | tf_op jit(solution)/shard_map/ppermute | solution.py:190
  35.4 1.3 collective-permute-start
  36.7 0.7 collective-permute-start.11
  37.5 1.0 pad_maximum_fusion.3
  38.5 1.5 %collective-permute-done.22.refs_2_ = f32[256,256]{1,0:T(8,128)S(1)} collective-permute-done((f32[256,256]{1,0:T(8,128)}, f32[256,256]{1,0:T(8,128)S(1)}, u32[]{:S(2)}, u32[]{:S(2)}) %collective-permute-start.22) | collective-permute-done | bytes 262176 | tf_op jit(solution)/shard_map/ppermute | solution.py:190
  40.0 0.7 collective-permute-start.13
  40.7 1.8 %collective-permute-done.24.refs_3_ = f32[256,256]{1,0:T(8,128)S(1)} collective-permute-done((f32[256,256]{1,0:T(8,128)}, f32[256,256]{1,0:T(8,128)S(1)}, u32[]{:S(2)}, u32[]{:S(2)}) %collective-permute-start.24) | collective-permute-done | bytes 262176 | tf_op jit(solution)/shard_map/ppermute | solution.py:190
  42.5 0.7 collective-permute-start.18
  43.1 0.9 compare_reduce_fusion
  44.0 1.0 pad_maximum_fusion.4
  45.0 1.0 pad_maximum_fusion.5
  46.1 0.6 collective-permute-start.25
  46.7 16.6 %collective-permute-done.refs_1_ = f32[512,256]{1,0:T(8,128)S(1)} collective-permute-done((f32[512,256]{1,0:T(8,128)}, f32[512,256]{1,0:T(8,128)S(1)}, u32[]{:S(2)}, u32[]{:S(2)}) %collective-permute-start) | collective-permute-done | bytes 524320 | tf_op jit(solution)/shard_map/ppermute | solution.py:190
  63.3 0.5 collective-permute-start.30
  64.0 0.9 collective-permute-done.29.refs_5_
  64.9 0.7 collective-permute-start.14
  65.6 0.7 collective-permute-start.15
  66.4 1.0 copy-done
  67.5 0.9 shard_map.167.refs_5_
  68.4 0.2 collective-permute-start.26
  68.6 0.4 collective-permute-start.27
  69.0 0.8 fusion.2
  69.8 2.4 %collective-permute-start.1 = (f32[256,256]{1,0:T(8,128)}, f32[256,256]{1,0:T(8,128)S(1)}, u32[]{:S(2)}, u32[]{:S(2)}) collective-permute-start(f32[256,256]{1,0:T(8,128)} %get-tuple-element.19), channel_id=1, source_target_pairs={{1,5},{3,7},{5,1},{7,3},{9,13},{11,15},{13,9},{15,11},{16,20},{18,... | collective-permute-start | bytes 786440 | tf_op jit(solution)/shard_map/ppermute | solution.py:190
  72.2 4.1 %shard_map.170.refs_5_ = f32[512,256]{1,0:T(8,128)S(1)} custom-call(s32[19]{0:T(128)S(1)} %get-tuple-element.32.table, f32[512,4096]{1,0:T(8,128)} %refs_0_.11, f32[512,256]{1,0:T(8,128)S(1)} %broadcast_select_fusion.refs_1_, f32[256,256]{1,0:T(8,128)S(1)} %collective-permute-done.22.refs_2_, f32[256,256]{1,0:T(8,128)S(1)} %collective-permute-done.24.refs_3_, ...), custom_call_target="tpu_custom_call" | custom-call | flops 402653184 | bytes 2097152 | tf_op jit(solution)/shard_map/pallas_call | solution.py:141
  76.3 1.9 %collective-permute-start.3 = (f32[256,256]{1,0:T(8,128)}, f32[256,256]{1,0:T(8,128)S(1)}, u32[]{:S(2)}, u32[]{:S(2)}) collective-permute-start(f32[256,256]{1,0:T(8,128)} %get-tuple-element.18), channel_id=1, source_target_pairs={{1,9},{3,11},{5,13},{7,15},{9,1},{11,3},{13,5},{15,7},{16,24},{18,... | collective-permute-start | bytes 786440 | tf_op jit(solution)/shard_map/ppermute | solution.py:190
  78.3 1.8 %shard_map.168 = (f32[512,256]{1,0:T(8,128)S(1)}, f32[256,256]{1,0:T(8,128)S(1)}) custom-call(s32[19]{0:T(128)S(1)} %get-tuple-element.37.table, f32[512,4096]{1,0:T(8,128)} %refs_0_.11, f32[512,256]{1,0:T(8,128)S(1)} %collective-permute-done.11.refs_1_, f32[512,256]{1,0:T(8,128)S(1)} %collective-permute-done.13.refs_2_, ...), custom_call_target="tpu_custom_call" | custom-call | flops 402653184 | bytes 2097152 | tf_op jit(solution)/shard_map/pallas_call | solution.py:141
  80.1 4.9 %shard_map.171 = (f32[512,256]{1,0:T(8,128)S(1)}, f32[256,256]{1,0:T(8,128)S(1)}) custom-call(s32[19]{0:T(128)S(1)} %get-tuple-element.35.table, f32[512,4096]{1,0:T(8,128)} %refs_0_.11, f32[512,256]{1,0:T(8,128)S(1)} %collective-permute-done.23.refs_1_, f32[512,256]{1,0:T(8,128)S(1)} %collective-permute-done.25.refs_2_, ...), custom_call_target="tpu_custom_call" | custom-call | flops 402653184 | bytes 2097152 | tf_op jit(solution)/shard_map/pallas_call | solution.py:141
  85.0 0.7 pad_maximum_fusion.6
  85.7 1.0 pad_maximum_fusion.1
  86.7 2.8 %collective-permute-start.4 = (f32[512,256]{1,0:T(8,128)S(1)}, f32[512,256]{1,0:T(8,128)S(1)}, u32[]{:S(2)}, u32[]{:S(2)}) collective-permute-start(f32[512,256]{1,0:T(8,128)S(1)} %pad_maximum_fusion.1), channel_id=1, source_target_pairs={{1,5},{3,7},{5,1},{7,3},{9,13},{11,15},{13,9},{15,11},{16,20},{18,... | collective-permute-start | bytes 1572872 | tf_op jit(solution)/shard_map/ppermute | solution.py:190
  89.5 1.0 pad_maximum_fusion
  90.5 2.2 %collective-permute-start.2 = (f32[512,256]{1,0:T(8,128)S(1)}, f32[512,256]{1,0:T(8,128)S(1)}, u32[]{:S(2)}, u32[]{:S(2)}) collective-permute-start(f32[512,256]{1,0:T(8,128)S(1)} %pad_maximum_fusion), channel_id=1, source_target_pairs={{1,9},{3,11},{5,13},{7,15},{9,1},{11,3},{13,5},{15,7},{16,24},{18,... | collective-permute-start | bytes 1572872 | tf_op jit(solution)/shard_map/ppermute | solution.py:190
  92.7 1.0 slice_add_fusion.1
  93.8 0.9 collective-permute-start.34
  94.7 2.0 %collective-permute-start.35 = (f32[64,256]{1,0:T(8,128)S(1)}, f32[64,256]{1,0:T(8,128)S(1)}, u32[]{:S(2)}, u32[]{:S(2)}) collective-permute-start(f32[64,256]{1,0:T(8,128)S(1)} %get-tuple-element.27), channel_id=1, source_target_pairs={{0,5},{1,4},{2,7},{3,6},{4,1},{5,0},{6,3},{7,2},{8,13},{9,12},{10,... | collective-permute-start | bytes 196616 | tf_op jit(solution)/shard_map/ppermute | solution.py:190
  96.7 0.7 collective-permute-start.33
  97.4 0.7 collective-permute-done.34
  98.1 5.1 %collective-permute-done.35 = f32[64,256]{1,0:T(8,128)S(1)} collective-permute-done((f32[64,256]{1,0:T(8,128)S(1)}, f32[64,256]{1,0:T(8,128)S(1)}, u32[]{:S(2)}, u32[]{:S(2)}) %collective-permute-start.35) | collective-permute-done | bytes 65568 | tf_op jit(solution)/shard_map/ppermute | solution.py:190
  103.2 2.6 %collective-permute-done.33 = f32[64,256]{1,0:T(8,128)S(1)} collective-permute-done((f32[64,256]{1,0:T(8,128)S(1)}, f32[64,256]{1,0:T(8,128)S(1)}, u32[]{:S(2)}, u32[]{:S(2)}) %collective-permute-start.33) | collective-permute-done | bytes 65568 | tf_op jit(solution)/shard_map/ppermute | solution.py:190
  105.9 4.3 %collective-permute-start.38 = (f32[64,256]{1,0:T(8,128)S(1)}, f32[64,256]{1,0:T(8,128)S(1)}, u32[]{:S(2)}, u32[]{:S(2)}) collective-permute-start(f32[64,256]{1,0:T(8,128)S(1)} %add_add_fusion.1), channel_id=1, source_target_pairs={{0,24},{1,25},{2,26},{3,27},{4,28},{5,29},{6,30},{7,31},{8,16},{9,... | collective-permute-start | bytes 196616 | tf_op jit(solution)/shard_map/ppermute | solution.py:190
  110.2 1.9 %collective-permute-start.8 = (f32[256,256]{1,0:T(8,128)S(1)}, f32[256,256]{1,0:T(8,128)S(1)}, u32[]{:S(2)}, u32[]{:S(2)}) collective-permute-start(f32[256,256]{1,0:T(8,128)S(1)} %collective-permute-done.1.refs_2_), channel_id=1, source_target_pairs={{1,3},{3,1},{5,7},{7,5},{9,11},{11,9},{13,15},{15,13},{16,18},{18,... | collective-permute-start | bytes 786440 | tf_op jit(solution)/shard_map/ppermute | solution.py:190
  112.2 2.4 %collective-permute-start.7 = (f32[512,256]{1,0:T(8,128)S(1)}, f32[512,256]{1,0:T(8,128)S(1)}, u32[]{:S(2)}, u32[]{:S(2)}) collective-permute-start(f32[512,256]{1,0:T(8,128)S(1)} %collective-permute-done.refs_1_), channel_id=1, source_target_pairs={{1,3},{3,1},{5,7},{7,5},{9,11},{11,9},{13,15},{15,13},{16,18},{18,... | collective-permute-start | bytes 1572872 | tf_op jit(solution)/shard_map/ppermute | solution.py:190
  114.6 1.9 %collective-permute-start.6 = (f32[512,256]{1,0:T(8,128)S(1)}, f32[512,256]{1,0:T(8,128)S(1)}, u32[]{:S(2)}, u32[]{:S(2)}) collective-permute-start(f32[512,256]{1,0:T(8,128)S(1)} %collective-permute-done.4.refs_2_), channel_id=1, source_target_pairs={{1,3},{3,1},{5,7},{7,5},{9,11},{11,9},{13,15},{15,13},{16,18},{18,... | collective-permute-start | bytes 1572872 | tf_op jit(solution)/shard_map/ppermute | solution.py:190
  116.5 2.4 %collective-permute-start.5 = (f32[512,256]{1,0:T(8,128)S(1)}, f32[512,256]{1,0:T(8,128)S(1)}, u32[]{:S(2)}, u32[]{:S(2)}) collective-permute-start(f32[512,256]{1,0:T(8,128)S(1)} %collective-permute-done.2.refs_1_), channel_id=1, source_target_pairs={{1,3},{3,1},{5,7},{7,5},{9,11},{11,9},{13,15},{15,13},{16,18},{18,... | collective-permute-start | bytes 1572872 | tf_op jit(solution)/shard_map/ppermute | solution.py:190
  119.1 0.9 collective-permute-start.39
  120.0 3.4 %collective-permute-done.39 = f32[64,256]{1,0:T(8,128)S(1)} collective-permute-done((f32[64,256]{1,0:T(8,128)S(1)}, f32[64,256]{1,0:T(8,128)S(1)}, u32[]{:S(2)}, u32[]{:S(2)}) %collective-permute-start.39) | collective-permute-done | bytes 65568 | tf_op jit(solution)/shard_map/ppermute | solution.py:190
  123.4 1.9 %collective-permute-start.9 = (f32[256,256]{1,0:T(8,128)S(1)}, f32[256,256]{1,0:T(8,128)S(1)}, u32[]{:S(2)}, u32[]{:S(2)}) collective-permute-start(f32[256,256]{1,0:T(8,128)S(1)} %collective-permute-done.3.refs_3_), channel_id=1, source_target_pairs={{1,3},{3,1},{5,7},{7,5},{9,11},{11,9},{13,15},{15,13},{16,18},{18,... | collective-permute-start | bytes 786440 | tf_op jit(solution)/shard_map/ppermute | solution.py:190
  125.4 1.5 %collective-permute-done.9.refs_6_ = f32[256,256]{1,0:T(8,128)S(1)} collective-permute-done((f32[256,256]{1,0:T(8,128)S(1)}, f32[256,256]{1,0:T(8,128)S(1)}, u32[]{:S(2)}, u32[]{:S(2)}) %collective-permute-start.9) | collective-permute-done | bytes 262176 | tf_op jit(solution)/shard_map/ppermute | solution.py:190
  127.0 4.3 %shard_map.169.refs_5_ = f32[512,256]{1,0:T(8,128)S(1)} custom-call(s32[19]{0:T(128)S(1)} %get-tuple-element.33.table, f32[512,4096]{1,0:T(8,128)} %refs_0_.11, f32[512,256]{1,0:T(8,128)S(1)} %collective-permute-done.refs_1_, f32[256,256]{1,0:T(8,128)S(1)} %collective-permute-done.1.refs_2_, f32[256,256]{1,0:T(8,128)S(1)} %collective-permute-done.3.refs_3_, ...), custom_call_target="tpu_custom_call" | custom-call | flops 402653184 | bytes 2097152 | tf_op jit(solution)/shard_map/pallas_call | solution.py:141
  131.3 1.6 %collective-permute-done.31.refs_6_ = f32[512,256]{1,0:T(8,128)S(1)} collective-permute-done((f32[512,256]{1,0:T(8,128)S(1)}, f32[512,256]{1,0:T(8,128)S(1)}, u32[]{:S(2)}, u32[]{:S(2)}) %collective-permute-start.31) | collective-permute-done | bytes 524320 | tf_op jit(solution)/shard_map/ppermute | solution.py:190
  132.9 4.9 %shard_map.172 = f32[512,256]{1,0:T(8,128)} custom-call(s32[19]{0:T(128)S(1)} %get-tuple-element.36.table, f32[512,4096]{1,0:T(8,128)} %refs_0_.11, f32[512,256]{1,0:T(8,128)S(1)} %collective-permute-done.2.refs_1_, f32[512,256]{1,0:T(8,128)S(1)} %collective-permute-done.4.refs_2_, f32[512,256]{1,0:T(8,128)S(1)} %collective-permute-done.5.refs_3_, ...), custom_call_target="tpu_custom_call" | custom-call | flops 402653184 | bytes 2097152 | tf_op jit(solution)/shard_map/pallas_call | solution.py:141
  137.8 0.7 maximum_add_fusion
  (64 shorter events, 1.1 us)
Async XLA Ops:
  0.6 14.0 %collective-permute-start.20 = (f32[512,256]{1,0:T(8,128)}, f32[512,256]{1,0:T(8,128)S(1)}, u32[]{:S(2)}, u32[]{:S(2)}) collective-permute-start(f32[512,256]{1,0:T(8,128)} %refs_6_.1), channel_id=1, source_target_pairs={{0,1},{1,0},{2,3},{3,2},{4,5},{5,4},{6,7},{7,6},{8,9},{9,8},{10,11... | collective-permute-start | bytes 1572872 | tf_op jit(solution)/shard_map/ppermute | solution.py:190
  2.2 28.5 %collective-permute-start.21 = (f32[512,256]{1,0:T(8,128)}, f32[512,256]{1,0:T(8,128)S(1)}, u32[]{:S(2)}, u32[]{:S(2)}) collective-permute-start(f32[512,256]{1,0:T(8,128)} %refs_6_.1), channel_id=1, source_target_pairs={{1,16},{3,18},{5,20},{7,22},{9,24},{11,26},{13,28},{15,30},{16,1},... | collective-permute-start | bytes 1572872 | tf_op jit(solution)/shard_map/ppermute | solution.py:190
  4.4 29.6 %collective-permute-start.19 = (s32[1,16]{1,0:T(1,128)}, s32[1,16]{1,0:T(1,128)S(1)}, u32[]{:S(2)}, u32[]{:S(2)}) collective-permute-start(s32[1,16]{1,0:T(1,128)} %param.18), channel_id=1, source_target_pairs={{0,1},{1,0},{2,3},{3,2},{4,5},{5,4},{6,7},{7,6},{8,9},{9,8},{10,11... | collective-permute-start | bytes 200 | tf_op jit(solution)/shard_map/ppermute | solution.py:190
  5.6 29.9 %copy-start.2 = (f32[256,256]{1,0:T(8,128)}, f32[256,256]{1,0:T(8,128)S(1)}, u32[]{:S(2)}) copy-start(f32[256,256]{1,0:T(8,128)S(1)} %get-tuple-element.16) | copy-start | bytes 786436
  5.6 2.1 %collective-permute-start.10 = (f32[256,256]{1,0:T(8,128)S(1)}, f32[256,256]{1,0:T(8,128)S(1)}, u32[]{:S(2)}, u32[]{:S(2)}) collective-permute-start(f32[256,256]{1,0:T(8,128)S(1)} %get-tuple-element.17), channel_id=1, source_target_pairs={{0,4},{2,6},{4,0},{6,2},{8,12},{10,14},{12,8},{14,10},{17,21},{19,... | collective-permute-start | bytes 786440 | tf_op jit(solution)/shard_map/ppermute | solution.py:190
  6.2 29.2 %collective-permute-start.12 = (f32[256,256]{1,0:T(8,128)S(1)}, f32[256,256]{1,0:T(8,128)S(1)}, u32[]{:S(2)}, u32[]{:S(2)}) collective-permute-start(f32[256,256]{1,0:T(8,128)S(1)} %get-tuple-element.16), channel_id=1, source_target_pairs={{0,8},{2,10},{4,12},{6,14},{8,0},{10,2},{12,4},{14,6},{17,25},{19,... | collective-permute-start | bytes 786440 | tf_op jit(solution)/shard_map/ppermute | solution.py:190
  7.7 29.0 %collective-permute-start.17 = (f32[256,256]{1,0:T(8,128)S(1)}, f32[256,256]{1,0:T(8,128)S(1)}, u32[]{:S(2)}, u32[]{:S(2)}) collective-permute-start(f32[256,256]{1,0:T(8,128)S(1)} %collective-permute-done.10.refs_2_), channel_id=1, source_target_pairs={{0,2},{2,0},{4,6},{6,4},{8,10},{10,8},{12,14},{14,12},{17,19},{19,... | collective-permute-start | bytes 786440 | tf_op jit(solution)/shard_map/ppermute | solution.py:190
  31.6 8.4 %collective-permute-start.22 = (f32[256,256]{1,0:T(8,128)}, f32[256,256]{1,0:T(8,128)S(1)}, u32[]{:S(2)}, u32[]{:S(2)}) collective-permute-start(f32[256,256]{1,0:T(8,128)} %get-tuple-element.15), channel_id=1, source_target_pairs={{0,4},{1,5},{2,6},{3,7},{4,0},{5,1},{6,2},{7,3},{8,12},{9,13},{10,... | collective-permute-start | bytes 786440 | tf_op jit(solution)/shard_map/ppermute | solution.py:190
  33.1 9.3 %collective-permute-start.24 = (f32[256,256]{1,0:T(8,128)}, f32[256,256]{1,0:T(8,128)S(1)}, u32[]{:S(2)}, u32[]{:S(2)}) collective-permute-start(f32[256,256]{1,0:T(8,128)} %get-tuple-element.14), channel_id=1, source_target_pairs={{0,8},{1,9},{2,10},{3,11},{4,12},{5,13},{6,14},{7,15},{8,0},{9,1},... | collective-permute-start | bytes 786440 | tf_op jit(solution)/shard_map/ppermute | solution.py:190
  34.0 12.1 %collective-permute-start.16 = (f32[512,256]{1,0:T(8,128)}, f32[512,256]{1,0:T(8,128)}, u32[]{:S(2)}, u32[]{:S(2)}) collective-permute-start(f32[512,256]{1,0:T(8,128)} %refs_6_.1), channel_id=1, source_target_pairs={{0,2},{2,0},{4,6},{6,4},{8,10},{10,8},{12,14},{14,12},{17,19},{19,... | collective-permute-start | bytes 1572872 | tf_op jit(solution)/shard_map/ppermute | solution.py:190
  35.4 27.9 %collective-permute-start = (f32[512,256]{1,0:T(8,128)}, f32[512,256]{1,0:T(8,128)S(1)}, u32[]{:S(2)}, u32[]{:S(2)}) collective-permute-start(f32[512,256]{1,0:T(8,128)} %refs_6_.1), channel_id=1, source_target_pairs={{0,16},{2,18},{4,20},{6,22},{8,24},{10,26},{12,28},{14,30},{17,1},... | collective-permute-start | bytes 1572872 | tf_op jit(solution)/shard_map/ppermute | solution.py:190
  36.7 26.6 %collective-permute-start.11 = (f32[512,256]{1,0:T(8,128)}, f32[512,256]{1,0:T(8,128)S(1)}, u32[]{:S(2)}, u32[]{:S(2)}) collective-permute-start(f32[512,256]{1,0:T(8,128)} %pad_maximum_fusion.2), channel_id=1, source_target_pairs={{0,8},{2,10},{4,12},{6,14},{8,0},{10,2},{12,4},{14,6},{17,25},{19,... | collective-permute-start | bytes 1572872 | tf_op jit(solution)/shard_map/ppermute | solution.py:190
  40.0 23.8 %collective-permute-start.13 = (f32[512,256]{1,0:T(8,128)S(1)}, f32[512,256]{1,0:T(8,128)S(1)}, u32[]{:S(2)}, u32[]{:S(2)}) collective-permute-start(f32[512,256]{1,0:T(8,128)S(1)} %pad_maximum_fusion.3), channel_id=1, source_target_pairs={{0,4},{2,6},{4,0},{6,2},{8,12},{10,14},{12,8},{14,10},{17,21},{19,... | collective-permute-start | bytes 1572872 | tf_op jit(solution)/shard_map/ppermute | solution.py:190
  42.5 3.5 %collective-permute-start.18 = (f32[256,256]{1,0:T(8,128)S(1)}, f32[256,256]{1,0:T(8,128)S(1)}, u32[]{:S(2)}, u32[]{:S(2)}) collective-permute-start(f32[256,256]{1,0:T(8,128)S(1)} %collective-permute-done.12.refs_3_), channel_id=1, source_target_pairs={{0,2},{2,0},{4,6},{6,4},{8,10},{10,8},{12,14},{14,12},{17,19},{19,... | collective-permute-start | bytes 786440 | tf_op jit(solution)/shard_map/ppermute | solution.py:190
  46.0 22.4 %collective-permute-start.23 = (f32[512,256]{1,0:T(8,128)S(1)}, f32[512,256]{1,0:T(8,128)S(1)}, u32[]{:S(2)}, u32[]{:S(2)}) collective-permute-start(f32[512,256]{1,0:T(8,128)S(1)} %pad_maximum_fusion.4), channel_id=1, source_target_pairs={{0,8},{1,9},{2,10},{3,11},{4,12},{5,13},{6,14},{7,15},{8,0},{9,1},... | collective-permute-start | bytes 1572872 | tf_op jit(solution)/shard_map/ppermute | solution.py:190
  46.1 22.5 %collective-permute-start.25 = (f32[512,256]{1,0:T(8,128)S(1)}, f32[512,256]{1,0:T(8,128)S(1)}, u32[]{:S(2)}, u32[]{:S(2)}) collective-permute-start(f32[512,256]{1,0:T(8,128)S(1)} %pad_maximum_fusion.5), channel_id=1, source_target_pairs={{0,4},{1,5},{2,6},{3,7},{4,0},{5,1},{6,2},{7,3},{8,12},{9,13},{10,... | collective-permute-start | bytes 1572872 | tf_op jit(solution)/shard_map/ppermute | solution.py:190
  63.3 1.5 %collective-permute-start.29 = (f32[256,256]{1,0:T(8,128)S(1)}, f32[256,256]{1,0:T(8,128)S(1)}, u32[]{:S(2)}, u32[]{:S(2)}) collective-permute-start(f32[256,256]{1,0:T(8,128)S(1)} %collective-permute-done.22.refs_2_), channel_id=1, source_target_pairs={{0,2},{1,3},{2,0},{3,1},{4,6},{5,7},{6,4},{7,5},{8,10},{9,11},{10,... | collective-permute-start | bytes 786440 | tf_op jit(solution)/shard_map/ppermute | solution.py:190
  63.3 2.2 %collective-permute-start.30 = (f32[256,256]{1,0:T(8,128)S(1)}, f32[256,256]{1,0:T(8,128)S(1)}, u32[]{:S(2)}, u32[]{:S(2)}) collective-permute-start(f32[256,256]{1,0:T(8,128)S(1)} %collective-permute-done.24.refs_3_), channel_id=1, source_target_pairs={{0,2},{1,3},{2,0},{3,1},{4,6},{5,7},{6,4},{7,5},{8,10},{9,11},{10,... | collective-permute-start | bytes 786440 | tf_op jit(solution)/shard_map/ppermute | solution.py:190
  63.8 6.0 %collective-permute-start.28 = (f32[512,256]{1,0:T(8,128)S(1)}, f32[512,256]{1,0:T(8,128)S(1)}, u32[]{:S(2)}, u32[]{:S(2)}) collective-permute-start(f32[512,256]{1,0:T(8,128)S(1)} %broadcast_select_fusion.refs_1_), channel_id=1, source_target_pairs={{0,2},{1,3},{2,0},{3,1},{4,6},{5,7},{6,4},{7,5},{8,10},{9,11},{10,... | collective-permute-start | bytes 1572872 | tf_op jit(solution)/shard_map/ppermute | solution.py:190
  64.9 11.5 %collective-permute-start.14 = (f32[512,256]{1,0:T(8,128)S(1)}, f32[512,256]{1,0:T(8,128)S(1)}, u32[]{:S(2)}, u32[]{:S(2)}) collective-permute-start(f32[512,256]{1,0:T(8,128)S(1)} %collective-permute-done.11.refs_1_), channel_id=1, source_target_pairs={{0,2},{2,0},{4,6},{6,4},{8,10},{10,8},{12,14},{14,12},{17,19},{19,... | collective-permute-start | bytes 1572872 | tf_op jit(solution)/shard_map/ppermute | solution.py:190
  65.6 12.7 %collective-permute-start.15 = (f32[512,256]{1,0:T(8,128)S(1)}, f32[512,256]{1,0:T(8,128)S(1)}, u32[]{:S(2)}, u32[]{:S(2)}) collective-permute-start(f32[512,256]{1,0:T(8,128)S(1)} %collective-permute-done.13.refs_2_), channel_id=1, source_target_pairs={{0,2},{2,0},{4,6},{6,4},{8,10},{10,8},{12,14},{14,12},{17,19},{19,... | collective-permute-start | bytes 1572872 | tf_op jit(solution)/shard_map/ppermute | solution.py:190
  66.4 1.0 copy-start
  68.4 9.9 %copy-start.1 = (f32[512,256]{1,0:T(8,128)S(1)}, f32[512,256]{1,0:T(8,128)}, u32[]{:S(2)}) copy-start(f32[512,256]{1,0:T(8,128)} %refs_6_.1) | copy-start | bytes 1572868
  68.4 11.7 %collective-permute-start.26 = (f32[512,256]{1,0:T(8,128)S(1)}, f32[512,256]{1,0:T(8,128)S(1)}, u32[]{:S(2)}, u32[]{:S(2)}) collective-permute-start(f32[512,256]{1,0:T(8,128)S(1)} %collective-permute-done.23.refs_1_), channel_id=1, source_target_pairs={{0,2},{1,3},{2,0},{3,1},{4,6},{5,7},{6,4},{7,5},{8,10},{9,11},{10,... | collective-permute-start | bytes 1572872 | tf_op jit(solution)/shard_map/ppermute | solution.py:190
  68.6 11.5 %collective-permute-start.27 = (f32[512,256]{1,0:T(8,128)S(1)}, f32[512,256]{1,0:T(8,128)S(1)}, u32[]{:S(2)}, u32[]{:S(2)}) collective-permute-start(f32[512,256]{1,0:T(8,128)S(1)} %collective-permute-done.25.refs_2_), channel_id=1, source_target_pairs={{0,2},{1,3},{2,0},{3,1},{4,6},{5,7},{6,4},{7,5},{8,10},{9,11},{10,... | collective-permute-start | bytes 1572872 | tf_op jit(solution)/shard_map/ppermute | solution.py:190
  69.8 19.7 %collective-permute-start.1 = (f32[256,256]{1,0:T(8,128)}, f32[256,256]{1,0:T(8,128)S(1)}, u32[]{:S(2)}, u32[]{:S(2)}) collective-permute-start(f32[256,256]{1,0:T(8,128)} %get-tuple-element.19), channel_id=1, source_target_pairs={{1,5},{3,7},{5,1},{7,3},{9,13},{11,15},{13,9},{15,11},{16,20},{18,... | collective-permute-start | bytes 786440 | tf_op jit(solution)/shard_map/ppermute | solution.py:190
  76.3 9.4 %collective-permute-start.3 = (f32[256,256]{1,0:T(8,128)}, f32[256,256]{1,0:T(8,128)S(1)}, u32[]{:S(2)}, u32[]{:S(2)}) collective-permute-start(f32[256,256]{1,0:T(8,128)} %get-tuple-element.18), channel_id=1, source_target_pairs={{1,9},{3,11},{5,13},{7,15},{9,1},{11,3},{13,5},{15,7},{16,24},{18,... | collective-permute-start | bytes 786440 | tf_op jit(solution)/shard_map/ppermute | solution.py:190
  85.7 7.0 %collective-permute-start.32 = (f32[256,256]{1,0:T(8,128)}, f32[256,256]{1,0:T(8,128)}, u32[]{:S(2)}, u32[]{:S(2)}) collective-permute-start(f32[256,256]{1,0:T(8,128)} %pad_maximum_fusion.6), channel_id=1, source_target_pairs={{0,2},{1,3},{2,0},{3,1},{4,6},{5,7},{6,4},{7,5},{8,10},{9,11},{10,... | collective-permute-start | bytes 786440 | tf_op jit(solution)/shard_map/ppermute | solution.py:190
  86.7 23.5 %collective-permute-start.4 = (f32[512,256]{1,0:T(8,128)S(1)}, f32[512,256]{1,0:T(8,128)S(1)}, u32[]{:S(2)}, u32[]{:S(2)}) collective-permute-start(f32[512,256]{1,0:T(8,128)S(1)} %pad_maximum_fusion.1), channel_id=1, source_target_pairs={{1,5},{3,7},{5,1},{7,3},{9,13},{11,15},{13,9},{15,11},{16,20},{18,... | collective-permute-start | bytes 1572872 | tf_op jit(solution)/shard_map/ppermute | solution.py:190
  90.5 21.7 %collective-permute-start.2 = (f32[512,256]{1,0:T(8,128)S(1)}, f32[512,256]{1,0:T(8,128)S(1)}, u32[]{:S(2)}, u32[]{:S(2)}) collective-permute-start(f32[512,256]{1,0:T(8,128)S(1)} %pad_maximum_fusion), channel_id=1, source_target_pairs={{1,9},{3,11},{5,13},{7,15},{9,1},{11,3},{13,5},{15,7},{16,24},{18,... | collective-permute-start | bytes 1572872 | tf_op jit(solution)/shard_map/ppermute | solution.py:190
  93.8 4.3 %collective-permute-start.34 = (f32[64,256]{1,0:T(8,128)S(1)}, f32[64,256]{1,0:T(8,128)S(1)}, u32[]{:S(2)}, u32[]{:S(2)}) collective-permute-start(f32[64,256]{1,0:T(8,128)S(1)} %get-tuple-element.26), channel_id=1, source_target_pairs={{0,1},{1,0},{2,3},{3,2},{4,5},{5,4},{6,7},{7,6},{8,9},{9,8},{10,11... | collective-permute-start | bytes 196616 | tf_op jit(solution)/shard_map/ppermute | solution.py:190
  94.7 8.5 %collective-permute-start.35 = (f32[64,256]{1,0:T(8,128)S(1)}, f32[64,256]{1,0:T(8,128)S(1)}, u32[]{:S(2)}, u32[]{:S(2)}) collective-permute-start(f32[64,256]{1,0:T(8,128)S(1)} %get-tuple-element.27), channel_id=1, source_target_pairs={{0,5},{1,4},{2,7},{3,6},{4,1},{5,0},{6,3},{7,2},{8,13},{9,12},{10,... | collective-permute-start | bytes 196616 | tf_op jit(solution)/shard_map/ppermute | solution.py:190
  96.7 9.0 %collective-permute-start.33 = (f32[64,256]{1,0:T(8,128)S(1)}, f32[64,256]{1,0:T(8,128)S(1)}, u32[]{:S(2)}, u32[]{:S(2)}) collective-permute-start(f32[64,256]{1,0:T(8,128)S(1)} %slice_select_fusion.4), channel_id=1, source_target_pairs={{0,4},{1,5},{2,6},{3,7},{4,0},{5,1},{6,2},{7,3},{8,12},{9,13},{10,... | collective-permute-start | bytes 196616 | tf_op jit(solution)/shard_map/ppermute | solution.py:190
  105.8 8.8 %collective-permute-start.36 = (f32[64,256]{1,0:T(8,128)S(1)}, f32[64,256]{1,0:T(8,128)S(1)}, u32[]{:S(2)}, u32[]{:S(2)}) collective-permute-start(f32[64,256]{1,0:T(8,128)S(1)} %add_add_fusion.1), channel_id=1, source_target_pairs={{0,8},{1,9},{2,10},{3,11},{4,12},{5,13},{6,14},{7,15},{8,0},{9,1},... | collective-permute-start | bytes 196616 | tf_op jit(solution)/shard_map/ppermute | solution.py:190
  105.9 10.7 %collective-permute-start.37 = (f32[64,256]{1,0:T(8,128)S(1)}, f32[64,256]{1,0:T(8,128)S(1)}, u32[]{:S(2)}, u32[]{:S(2)}) collective-permute-start(f32[64,256]{1,0:T(8,128)S(1)} %add_add_fusion.1), channel_id=1, source_target_pairs={{0,16},{1,17},{2,18},{3,19},{4,20},{5,21},{6,22},{7,23},{8,24},{9,... | collective-permute-start | bytes 196616 | tf_op jit(solution)/shard_map/ppermute | solution.py:190
  105.9 13.0 %collective-permute-start.38 = (f32[64,256]{1,0:T(8,128)S(1)}, f32[64,256]{1,0:T(8,128)S(1)}, u32[]{:S(2)}, u32[]{:S(2)}) collective-permute-start(f32[64,256]{1,0:T(8,128)S(1)} %add_add_fusion.1), channel_id=1, source_target_pairs={{0,24},{1,25},{2,26},{3,27},{4,28},{5,29},{6,30},{7,31},{8,16},{9,... | collective-permute-start | bytes 196616 | tf_op jit(solution)/shard_map/ppermute | solution.py:190
  110.2 8.8 %collective-permute-start.8 = (f32[256,256]{1,0:T(8,128)S(1)}, f32[256,256]{1,0:T(8,128)S(1)}, u32[]{:S(2)}, u32[]{:S(2)}) collective-permute-start(f32[256,256]{1,0:T(8,128)S(1)} %collective-permute-done.1.refs_2_), channel_id=1, source_target_pairs={{1,3},{3,1},{5,7},{7,5},{9,11},{11,9},{13,15},{15,13},{16,18},{18,... | collective-permute-start | bytes 786440 | tf_op jit(solution)/shard_map/ppermute | solution.py:190
  112.2 14.8 %collective-permute-start.7 = (f32[512,256]{1,0:T(8,128)S(1)}, f32[512,256]{1,0:T(8,128)S(1)}, u32[]{:S(2)}, u32[]{:S(2)}) collective-permute-start(f32[512,256]{1,0:T(8,128)S(1)} %collective-permute-done.refs_1_), channel_id=1, source_target_pairs={{1,3},{3,1},{5,7},{7,5},{9,11},{11,9},{13,15},{15,13},{16,18},{18,... | collective-permute-start | bytes 1572872 | tf_op jit(solution)/shard_map/ppermute | solution.py:190
  114.6 16.7 %collective-permute-start.6 = (f32[512,256]{1,0:T(8,128)S(1)}, f32[512,256]{1,0:T(8,128)S(1)}, u32[]{:S(2)}, u32[]{:S(2)}) collective-permute-start(f32[512,256]{1,0:T(8,128)S(1)} %collective-permute-done.4.refs_2_), channel_id=1, source_target_pairs={{1,3},{3,1},{5,7},{7,5},{9,11},{11,9},{13,15},{15,13},{16,18},{18,... | collective-permute-start | bytes 1572872 | tf_op jit(solution)/shard_map/ppermute | solution.py:190
  116.5 14.7 %collective-permute-start.5 = (f32[512,256]{1,0:T(8,128)S(1)}, f32[512,256]{1,0:T(8,128)S(1)}, u32[]{:S(2)}, u32[]{:S(2)}) collective-permute-start(f32[512,256]{1,0:T(8,128)S(1)} %collective-permute-done.2.refs_1_), channel_id=1, source_target_pairs={{1,3},{3,1},{5,7},{7,5},{9,11},{11,9},{13,15},{15,13},{16,18},{18,... | collective-permute-start | bytes 1572872 | tf_op jit(solution)/shard_map/ppermute | solution.py:190
  118.9 13.9 %collective-permute-start.31 = (f32[512,256]{1,0:T(8,128)S(1)}, f32[512,256]{1,0:T(8,128)S(1)}, u32[]{:S(2)}, u32[]{:S(2)}) collective-permute-start(f32[512,256]{1,0:T(8,128)S(1)} %get-tuple-element.7), channel_id=1, source_target_pairs={{0,1},{1,0},{2,3},{3,2},{4,5},{5,4},{6,7},{7,6},{8,9},{9,8},{10,11... | collective-permute-start | bytes 1572872 | tf_op jit(solution)/shard_map/ppermute | solution.py:190
  119.1 4.3 %collective-permute-start.39 = (f32[64,256]{1,0:T(8,128)S(1)}, f32[64,256]{1,0:T(8,128)S(1)}, u32[]{:S(2)}, u32[]{:S(2)}) collective-permute-start(f32[64,256]{1,0:T(8,128)S(1)} %add_add_fusion), channel_id=1, source_target_pairs={{0,4},{1,5},{2,6},{3,7},{4,0},{5,1},{6,2},{7,3},{8,12},{9,13},{10,... | collective-permute-start | bytes 196616 | tf_op jit(solution)/shard_map/ppermute | solution.py:190
  123.4 3.4 %collective-permute-start.9 = (f32[256,256]{1,0:T(8,128)S(1)}, f32[256,256]{1,0:T(8,128)S(1)}, u32[]{:S(2)}, u32[]{:S(2)}) collective-permute-start(f32[256,256]{1,0:T(8,128)S(1)} %collective-permute-done.3.refs_3_), channel_id=1, source_target_pairs={{1,3},{3,1},{5,7},{7,5},{9,11},{11,9},{13,15},{15,13},{16,18},{18,... | collective-permute-start | bytes 786440 | tf_op jit(solution)/shard_map/ppermute | solution.py:190
  126.8 11.0 %collective-permute-start.40 = (f32[128,256]{1,0:T(8,128)S(1)}, f32[128,256]{1,0:T(8,128)S(1)}, u32[]{:S(2)}, u32[]{:S(2)}) collective-permute-start(f32[128,256]{1,0:T(8,128)S(1)} %pad_maximum_fusion.7), channel_id=1, source_target_pairs={{0,2},{1,3},{2,0},{3,1},{4,6},{5,7},{6,4},{7,5},{8,10},{9,11},{10,... | collective-permute-start | bytes 393224 | tf_op jit(solution)/shard_map/ppermute | solution.py:190
  131.2 6.6 %copy-start.3 = (f32[256,256]{1,0:T(8,128)S(1)}, f32[256,256]{1,0:T(8,128)}, u32[]{:S(2)}) copy-start(f32[256,256]{1,0:T(8,128)} %param.19) | copy-start | bytes 786436

commit v2 on v1

--- a/solution.py
+++ b/solution.py
@@ -56,10 +56,10 @@
     a_hbm = refs.pop(0)
     arrays = [refs.pop(0) for _ in range(narrays)]
     acc_in = refs.pop(0) if has_acc else None
-    extra = refs.pop(0) if final else None
+    extra_in = refs.pop(0) if final else None
     out = refs.pop(0)
     terms = refs.pop(0) if final == "terms" else None
-    a_buf, p_buf, a_sem, p_sem = refs
+    a_buf, p_buf, extra, a_sem, p_sem, one_sem = refs
     row_on = [table[2 * count + rb] > 0 for rb in range(blocks)]
 
     def a_copy(p, rb):
@@ -73,6 +73,9 @@
         array, at = slots[p]
         return pltpu.make_async_copy(arrays[array].at[pl.ds(at * width, width), :], p_buf.at[p], p_sem.at[p])
 
+    if has_acc:
+        acc_copy = pltpu.make_async_copy(acc_in, out, one_sem.at[0])
+        acc_copy.start()
     for p in range(count):
         @pl.when(table[count + p] > 0)
         def _(p=p):
@@ -82,8 +85,11 @@
                 def _(rb=rb):
                     a_copy(p, rb).start()
 
+    if final:
+        extra_copy = pltpu.make_async_copy(extra_in, extra, one_sem.at[1])
+        extra_copy.start()
     if has_acc:
-        out[...] = acc_in[...]
+        acc_copy.wait()
     else:
         out[...] = jnp.zeros_like(out)
     for p in range(count):
@@ -97,6 +103,8 @@
                     a_copy(p, rb).wait()
                     out[pl.ds(rb * width, width), :] += dot3(split(a_buf[p, rb]), piece, ((1,), (0,)))
 
+    if final:
+        extra_copy.wait()
     if final == "terms":
         terms[...] = jnp.zeros_like(terms)
         for rb in range(blocks):
@@ -134,7 +142,7 @@
     for more in (acc, extra):
         if more is not None:
             operands.append(more)
-            specs.append(vmem)
+            specs.append(any_spec)
     shapes = [jax.ShapeDtypeStruct((rows, width), jnp.float32)]
     if final == "terms":
         shapes.append(jax.ShapeDtypeStruct((width, width), jnp.float32))
@@ -149,8 +157,10 @@
             scratch_shapes=[
                 pltpu.VMEM((count, blocks, width, width), jnp.float32),
                 pltpu.VMEM((count, width, width), jnp.float32),
+                pltpu.VMEM((rows, width), jnp.float32),
                 pltpu.SemaphoreType.DMA((count, blocks)),
                 pltpu.SemaphoreType.DMA((count,)),
+                pltpu.SemaphoreType.DMA((2,)),
             ],
         ),
         compiler_params=pltpu.CompilerParams(vmem_limit_bytes=13 * 1024 * 1024),
@@ -205,21 +215,21 @@
         return move(q[:half], X, 0, who), move(q[half:], Z, 0, who)
 
     def step_two(q, one, who):
-        z2 = move(jnp.concatenate([q[:half], one[0]]), Z, 0, who)
-        return z2, move(jnp.concatenate([q[half:], one[1]]), X, 0, who)
+        first, second = jnp.concatenate([q[:half], one[0]]), jnp.concatenate([q[half:], one[1]])
+        return move(first, Z, 0, who), move(second, X, 0, who)
 
     def with_sibling(arrays, who):
         return list(arrays) + [move(v, CORE, 0, who) for v in arrays]
 
+    other_structure = move(structure, 0, 1)
     got_far = move(lower_panel, FAR, 1, False)
     lower_other = move(lower_panel, 0, 1)
     q_far = move(lower_panel, FAR, 0, True)
-    other_structure = move(structure, 0, 1)
 
     n_one = step_one(lower_panel, True)
     n_two = step_two(lower_panel, n_one, True)
-    n_first = with_sibling([lower_panel, *n_one], True)
-    n_second = with_sibling(n_two, True)
+    n_first = with_sibling([lower_panel, *n_one], None)
+    n_second = with_sibling(n_two, None)
     q_other = jnp.where(near, lower_other, got_far)
     o_one = step_one(q_other, None)
     o_two = step_two(q_other, o_one, None)
@@ -227,8 +237,8 @@
     o_second = with_sibling(o_two, None)
     f_one = step_one(q_far, False)
     f_two = step_two(q_far, f_one, False)
-    f_first = with_sibling([q_far, *f_one], False)
-    f_second = with_sibling(f_two, False)
+    f_first = with_sibling([q_far, *f_one], None)
+    f_second = with_sibling(f_two, None)
 
     (own,) = product(table(structure, FIRST, True), inverse_anc, n_first, SLOTS1, width)
     own, own_terms = product(

time: 139 us -> 136 us (0.978)
  the two profiles are of different devices: /device:TPU:24 before, /device:TPU:0 now
where the time goes in v2:
time: 136 us; the launch traced here: 134 us
  starting transfers between devices  63.4 us (47%)
  waiting for transfers between devices  42.9 us (32%)
  Pallas kernels  12.8 us (9%)
  other arithmetic  10.3 us (8%)
  local copies, waits for them, and re-layouts  3.8 us (3%)
    ppermute x41, starting transfers between devices, move(): return lax.ppermute(value, BOTH, pairs)  63.4 us
    ppermute x41, waiting for transfers between devices, move(): return lax.ppermute(value, BOTH, pairs)  42.9 us
    pallas_call x6, Pallas kernels, product(): pl.pallas_call(functools.partial(product_kernel, slots, blocks, width, ac...  12.8 us
    concatenate x3, other arithmetic, step_two(): jnp.concatenate([q[half:], one[1]])  2.95 us
    concatenate x3, other arithmetic, step_two(): jnp.concatenate([q[:half], one[0]])  2.81 us
    slice x3, local copies, waits for them, and re-layouts, step_two(): q[half:]  2.74 us
  transfers between devices with their start and end apart: 41, of which 13 were waited for; matrix products, arithmetic and copies ran while one was open for 9% of the time, Pallas kernels for 10%

profile of v2, /device:TPU:0, one launch (start us, length us, event | category | flops | bytes accessed | tf_op | source)
XLA Modules:
  0.0 134.3 jit_solution(5012656352082075470)
XLA Ops:
  0.6 3.1 %collective-permute-start.20 = (f32[512,256]{1,0:T(8,128)}, f32[512,256]{1,0:T(8,128)S(1)}, u32[]{:S(2)}, u32[]{:S(2)}) collective-permute-start(f32[512,256]{1,0:T(8,128)} %refs_6_.1), channel_id=1, source_target_pairs={{0,1},{1,0},{2,3},{3,2},{4,5},{5,4},{6,7},{7,6},{8,9},{9,8},{10,11... | collective-permute-start | bytes 1572872 | tf_op jit(solution)/shard_map/ppermute | solution.py:200
  3.7 0.7 collective-permute-start.21
  4.4 5.3 %collective-permute-start.19 = (s32[1,16]{1,0:T(1,128)}, s32[1,16]{1,0:T(1,128)S(1)}, u32[]{:S(2)}, u32[]{:S(2)}) collective-permute-start(s32[1,16]{1,0:T(1,128)} %param.18), channel_id=1, source_target_pairs={{0,1},{1,0},{2,3},{3,2},{4,5},{5,4},{6,7},{7,6},{8,9},{9,8},{10,11... | collective-permute-start | bytes 200 | tf_op jit(solution)/shard_map/ppermute | solution.py:200
  9.7 1.1 fusion.1
  10.8 3.4 %collective-permute-start.10 = (f32[256,256]{1,0:T(8,128)S(1)}, f32[256,256]{1,0:T(8,128)S(1)}, u32[]{:S(2)}, u32[]{:S(2)}) collective-permute-start(f32[256,256]{1,0:T(8,128)S(1)} %get-tuple-element.17), channel_id=1, source_target_pairs={{0,4},{2,6},{4,0},{6,2},{8,12},{10,14},{12,8},{14,10},{17,21},{19,... | collective-permute-start | bytes 786440 | tf_op jit(solution)/shard_map/ppermute | solution.py:200
  14.2 3.5 %collective-permute-start.12 = (f32[256,256]{1,0:T(8,128)S(1)}, f32[256,256]{1,0:T(8,128)S(1)}, u32[]{:S(2)}, u32[]{:S(2)}) collective-permute-start(f32[256,256]{1,0:T(8,128)S(1)} %get-tuple-element.16), channel_id=1, source_target_pairs={{0,8},{2,10},{4,12},{6,14},{8,0},{10,2},{12,4},{14,6},{17,25},{19,... | collective-permute-start | bytes 786440 | tf_op jit(solution)/shard_map/ppermute | solution.py:200
  17.7 0.7 multiply_add_fusion
  18.5 1.4 %collective-permute-done.10.refs_2_ = f32[256,256]{1,0:T(8,128)S(1)} collective-permute-done((f32[256,256]{1,0:T(8,128)S(1)}, f32[256,256]{1,0:T(8,128)S(1)}, u32[]{:S(2)}, u32[]{:S(2)}) %collective-permute-start.10) | collective-permute-done | bytes 262176 | tf_op jit(solution)/shard_map/ppermute | solution.py:200
  20.0 0.9 fusion
  20.8 1.5 %collective-permute-start.22 = (f32[256,256]{1,0:T(8,128)}, f32[256,256]{1,0:T(8,128)S(1)}, u32[]{:S(2)}, u32[]{:S(2)}) collective-permute-start(f32[256,256]{1,0:T(8,128)} %get-tuple-element.15), channel_id=1, source_target_pairs={{0,4},{1,5},{2,6},{3,7},{4,0},{5,1},{6,2},{7,3},{8,12},{9,13},{10,... | collective-permute-start | bytes 786440 | tf_op jit(solution)/shard_map/ppermute | solution.py:200
  22.3 8.1 %collective-permute-start.24 = (f32[256,256]{1,0:T(8,128)}, f32[256,256]{1,0:T(8,128)S(1)}, u32[]{:S(2)}, u32[]{:S(2)}) collective-permute-start(f32[256,256]{1,0:T(8,128)} %get-tuple-element.14), channel_id=1, source_target_pairs={{0,8},{1,9},{2,10},{3,11},{4,12},{5,13},{6,14},{7,15},{8,0},{9,1},... | collective-permute-start | bytes 786440 | tf_op jit(solution)/shard_map/ppermute | solution.py:200
  30.4 0.8 pad_maximum_fusion.2
  31.3 3.7 %collective-permute-done.12.refs_3_ = f32[256,256]{1,0:T(8,128)S(1)} collective-permute-done((f32[256,256]{1,0:T(8,128)S(1)}, f32[256,256]{1,0:T(8,128)S(1)}, u32[]{:S(2)}, u32[]{:S(2)}) %collective-permute-start.12) | collective-permute-done | bytes 262176 | tf_op jit(solution)/shard_map/ppermute | solution.py:200
  34.9 6.6 %collective-permute-start = (f32[512,256]{1,0:T(8,128)}, f32[512,256]{1,0:T(8,128)S(1)}, u32[]{:S(2)}, u32[]{:S(2)}) collective-permute-start(f32[512,256]{1,0:T(8,128)} %refs_6_.1), channel_id=1, source_target_pairs={{0,16},{2,18},{4,20},{6,22},{8,24},{10,26},{12,28},{14,30},{17,1},... | collective-permute-start | bytes 1572872 | tf_op jit(solution)/shard_map/ppermute | solution.py:200
  41.6 1.9 %collective-permute-start.11 = (f32[512,256]{1,0:T(8,128)}, f32[512,256]{1,0:T(8,128)S(1)}, u32[]{:S(2)}, u32[]{:S(2)}) collective-permute-start(f32[512,256]{1,0:T(8,128)} %pad_maximum_fusion.2), channel_id=1, source_target_pairs={{0,8},{2,10},{4,12},{6,14},{8,0},{10,2},{12,4},{14,6},{17,25},{19,... | collective-permute-start | bytes 1572872 | tf_op jit(solution)/shard_map/ppermute | solution.py:200
  43.6 1.0 pad_maximum_fusion.3
  44.6 2.4 %collective-permute-start.13 = (f32[512,256]{1,0:T(8,128)S(1)}, f32[512,256]{1,0:T(8,128)S(1)}, u32[]{:S(2)}, u32[]{:S(2)}) collective-permute-start(f32[512,256]{1,0:T(8,128)S(1)} %pad_maximum_fusion.3), channel_id=1, source_target_pairs={{0,4},{2,6},{4,0},{6,2},{8,12},{10,14},{12,8},{14,10},{17,21},{19,... | collective-permute-start | bytes 1572872 | tf_op jit(solution)/shard_map/ppermute | solution.py:200
  47.1 0.9 compare_reduce_fusion
  48.0 1.0 pad_maximum_fusion.4
  49.0 1.0 pad_maximum_fusion.5
  50.0 2.1 %collective-permute-start.23 = (f32[512,256]{1,0:T(8,128)S(1)}, f32[512,256]{1,0:T(8,128)S(1)}, u32[]{:S(2)}, u32[]{:S(2)}) collective-permute-start(f32[512,256]{1,0:T(8,128)S(1)} %pad_maximum_fusion.4), channel_id=1, source_target_pairs={{0,8},{1,9},{2,10},{3,11},{4,12},{5,13},{6,14},{7,15},{8,0},{9,1},... | collective-permute-start | bytes 1572872 | tf_op jit(solution)/shard_map/ppermute | solution.py:200
  52.1 1.5 %collective-permute-start.25 = (f32[512,256]{1,0:T(8,128)S(1)}, f32[512,256]{1,0:T(8,128)S(1)}, u32[]{:S(2)}, u32[]{:S(2)}) collective-permute-start(f32[512,256]{1,0:T(8,128)S(1)} %pad_maximum_fusion.5), channel_id=1, source_target_pairs={{0,4},{1,5},{2,6},{3,7},{4,0},{5,1},{6,2},{7,3},{8,12},{9,13},{10,... | collective-permute-start | bytes 1572872 | tf_op jit(solution)/shard_map/ppermute | solution.py:200
  53.6 0.6 collective-permute-done.refs_1_
  54.2 11.2 %collective-permute-done.11.refs_1_ = f32[512,256]{1,0:T(8,128)S(1)} collective-permute-done((f32[512,256]{1,0:T(8,128)}, f32[512,256]{1,0:T(8,128)S(1)}, u32[]{:S(2)}, u32[]{:S(2)}) %collective-permute-start.11) | collective-permute-done | bytes 524320 | tf_op jit(solution)/shard_map/ppermute | solution.py:200
  65.4 0.6 collective-permute-start.28
  66.0 0.1 collective-permute-start.14
  66.1 0.8 collective-permute-done.30.refs_6_
  67.0 0.1 collective-permute-start.15
  67.2 0.1 add_add_fusion.2
  67.3 1.0 copy-done
  68.3 1.9 %shard_map.167.refs_5_ = f32[512,256]{1,0:T(8,128)S(1)} custom-call(s32[19]{0:T(128)S(1)} %get-tuple-element.34.table, f32[512,4096]{1,0:T(8,128)} %refs_0_.11, f32[512,256]{1,0:T(8,128)S(1)} %copy-done, f32[256,256]{1,0:T(8,128)S(1)} %collective-permute-done.10.refs_2_, f32[256,256]{1,0:T(8,128)S(1)} %collective-permute-done.12.refs_3_, ...), custom_call_target="tpu_custom_call" | custom-call | flops 402653184 | bytes 2097152 | tf_op jit(solution)/shard_map/pallas_call | solution.py:149
  70.3 5.8 %collective-permute-done.23.refs_1_ = f32[512,256]{1,0:T(8,128)S(1)} collective-permute-done((f32[512,256]{1,0:T(8,128)S(1)}, f32[512,256]{1,0:T(8,128)S(1)}, u32[]{:S(2)}, u32[]{:S(2)}) %collective-permute-start.23) | collective-permute-done | bytes 524320 | tf_op jit(solution)/shard_map/ppermute | solution.py:200
  76.1 0.5 collective-permute-start.27
  76.6 0.8 fusion.2
  77.4 0.7 collective-permute-start.1
  78.1 3.3 %shard_map.170.refs_5_ = f32[512,256]{1,0:T(8,128)S(1)} custom-call(s32[19]{0:T(128)S(1)} %get-tuple-element.32.table, f32[512,4096]{1,0:T(8,128)} %refs_0_.11, f32[512,256]{1,0:T(8,128)S(1)} %broadcast_select_fusion.refs_1_, f32[256,256]{1,0:T(8,128)S(1)} %collective-permute-done.22.refs_2_, f32[256,256]{1,0:T(8,128)S(1)} %collective-permute-done.24.refs_3_, ...), custom_call_target="tpu_custom_call" | custom-call | flops 402653184 | bytes 2097152 | tf_op jit(solution)/shard_map/pallas_call | solution.py:149
  81.4 0.7 collective-permute-start.3
  82.1 1.5 %shard_map.168 = (f32[512,256]{1,0:T(8,128)S(1)}, f32[256,256]{1,0:T(8,128)S(1)}) custom-call(s32[19]{0:T(128)S(1)} %get-tuple-element.37.table, f32[512,4096]{1,0:T(8,128)} %refs_0_.11, f32[512,256]{1,0:T(8,128)S(1)} %collective-permute-done.11.refs_1_, f32[512,256]{1,0:T(8,128)S(1)} %collective-permute-done.13.refs_2_, ...), custom_call_target="tpu_custom_call" | custom-call | flops 402653184 | bytes 2097152 | tf_op jit(solution)/shard_map/pallas_call | solution.py:149
  83.7 3.1 %shard_map.171 = (f32[512,256]{1,0:T(8,128)S(1)}, f32[256,256]{1,0:T(8,128)S(1)}) custom-call(s32[19]{0:T(128)S(1)} %get-tuple-element.35.table, f32[512,4096]{1,0:T(8,128)} %refs_0_.11, f32[512,256]{1,0:T(8,128)S(1)} %collective-permute-done.23.refs_1_, f32[512,256]{1,0:T(8,128)S(1)} %collective-permute-done.25.refs_2_, ...), custom_call_target="tpu_custom_call" | custom-call | flops 402653184 | bytes 2097152 | tf_op jit(solution)/shard_map/pallas_call | solution.py:149
  86.8 0.7 pad_maximum_fusion.6
  87.5 6.6 %collective-permute-start.32 = (f32[256,256]{1,0:T(8,128)}, f32[256,256]{1,0:T(8,128)}, u32[]{:S(2)}, u32[]{:S(2)}) collective-permute-start(f32[256,256]{1,0:T(8,128)} %pad_maximum_fusion.6), channel_id=1, source_target_pairs={{0,2},{1,3},{2,0},{3,1},{4,6},{5,7},{6,4},{7,5},{8,10},{9,11},{10,... | collective-permute-start | bytes 786440 | tf_op jit(solution)/shard_map/ppermute | solution.py:200
  94.0 1.0 pad_maximum_fusion.1
  95.0 0.7 collective-permute-start.4
  95.7 1.0 pad_maximum_fusion
  96.7 0.7 collective-permute-start.2
  97.4 1.0 slice_add_fusion.1
  98.7 3.5 %collective-permute-start.33 = (f32[64,256]{1,0:T(8,128)S(1)}, f32[64,256]{1,0:T(8,128)S(1)}, u32[]{:S(2)}, u32[]{:S(2)}) collective-permute-start(f32[64,256]{1,0:T(8,128)S(1)} %slice_select_fusion.4), channel_id=1, source_target_pairs={{0,4},{1,5},{2,6},{3,7},{4,0},{5,1},{6,2},{7,3},{8,12},{9,13},{10,... | collective-permute-start | bytes 196616 | tf_op jit(solution)/shard_map/ppermute | solution.py:200
  102.1 0.7 collective-permute-done.34
  102.8 3.2 %collective-permute-done.35 = f32[64,256]{1,0:T(8,128)S(1)} collective-permute-done((f32[64,256]{1,0:T(8,128)S(1)}, f32[64,256]{1,0:T(8,128)S(1)}, u32[]{:S(2)}, u32[]{:S(2)}) %collective-permute-start.35) | collective-permute-done | bytes 65568 | tf_op jit(solution)/shard_map/ppermute | solution.py:200
  106.0 2.1 %collective-permute-start.36 = (f32[64,256]{1,0:T(8,128)S(1)}, f32[64,256]{1,0:T(8,128)S(1)}, u32[]{:S(2)}, u32[]{:S(2)}) collective-permute-start(f32[64,256]{1,0:T(8,128)S(1)} %add_add_fusion.1), channel_id=1, source_target_pairs={{0,8},{1,9},{2,10},{3,11},{4,12},{5,13},{6,14},{7,15},{8,0},{9,1},... | collective-permute-start | bytes 196616 | tf_op jit(solution)/shard_map/ppermute | solution.py:200
  108.1 4.8 %collective-permute-start.37 = (f32[64,256]{1,0:T(8,128)S(1)}, f32[64,256]{1,0:T(8,128)S(1)}, u32[]{:S(2)}, u32[]{:S(2)}) collective-permute-start(f32[64,256]{1,0:T(8,128)S(1)} %add_add_fusion.1), channel_id=1, source_target_pairs={{0,16},{1,17},{2,18},{3,19},{4,20},{5,21},{6,22},{7,23},{8,24},{9,... | collective-permute-start | bytes 196616 | tf_op jit(solution)/shard_map/ppermute | solution.py:200
  112.9 0.5 collective-permute-start.7
  113.4 0.1 collective-permute-start.6
  113.5 3.8 %collective-permute-done.37 = f32[64,256]{1,0:T(8,128)S(1)} collective-permute-done((f32[64,256]{1,0:T(8,128)S(1)}, f32[64,256]{1,0:T(8,128)S(1)}, u32[]{:S(2)}, u32[]{:S(2)}) %collective-permute-start.37) | collective-permute-done | bytes 65568 | tf_op jit(solution)/shard_map/ppermute | solution.py:200
  117.3 1.6 %collective-permute-done.38 = f32[64,256]{1,0:T(8,128)S(1)} collective-permute-done((f32[64,256]{1,0:T(8,128)S(1)}, f32[64,256]{1,0:T(8,128)S(1)}, u32[]{:S(2)}, u32[]{:S(2)}) %collective-permute-start.38) | collective-permute-done | bytes 65568 | tf_op jit(solution)/shard_map/ppermute | solution.py:200
  119.0 0.5 collective-permute-start.31
  119.5 0.9 collective-permute-start.39
  120.4 3.4 %collective-permute-done.39 = f32[64,256]{1,0:T(8,128)S(1)} collective-permute-done((f32[64,256]{1,0:T(8,128)S(1)}, f32[64,256]{1,0:T(8,128)S(1)}, u32[]{:S(2)}, u32[]{:S(2)}) %collective-permute-start.39) | collective-permute-done | bytes 65568 | tf_op jit(solution)/shard_map/ppermute | solution.py:200
  123.9 1.5 %collective-permute-done.9.refs_6_ = f32[256,256]{1,0:T(8,128)S(1)} collective-permute-done((f32[256,256]{1,0:T(8,128)S(1)}, f32[256,256]{1,0:T(8,128)S(1)}, u32[]{:S(2)}, u32[]{:S(2)}) %collective-permute-start.9) | collective-permute-done | bytes 262176 | tf_op jit(solution)/shard_map/ppermute | solution.py:200
  125.4 0.1 collective-permute-start.40
  125.5 1.2 shard_map.169.refs_5_
  126.7 4.9 %collective-permute-done.31.refs_6_ = f32[512,256]{1,0:T(8,128)S(1)} collective-permute-done((f32[512,256]{1,0:T(8,128)S(1)}, f32[512,256]{1,0:T(8,128)S(1)}, u32[]{:S(2)}, u32[]{:S(2)}) %collective-permute-start.31) | collective-permute-done | bytes 524320 | tf_op jit(solution)/shard_map/ppermute | solution.py:200
  131.7 1.8 %shard_map.172 = f32[512,256]{1,0:T(8,128)} custom-call(s32[19]{0:T(128)S(1)} %get-tuple-element.36.table, f32[512,4096]{1,0:T(8,128)} %refs_0_.11, f32[512,256]{1,0:T(8,128)S(1)} %collective-permute-done.2.refs_1_, f32[512,256]{1,0:T(8,128)S(1)} %collective-permute-done.4.refs_2_, f32[512,256]{1,0:T(8,128)S(1)} %collective-permute-done.5.refs_3_, ...), custom_call_target="tpu_custom_call" | custom-call | flops 402653184 | bytes 2097152 | tf_op jit(solution)/shard_map/pallas_call | solution.py:149
  133.5 0.7 maximum_add_fusion
  (64 shorter events, 0.7 us)
Async XLA Ops:
  0.6 19.3 %collective-permute-start.20 = (f32[512,256]{1,0:T(8,128)}, f32[512,256]{1,0:T(8,128)S(1)}, u32[]{:S(2)}, u32[]{:S(2)}) collective-permute-start(f32[512,256]{1,0:T(8,128)} %refs_6_.1), channel_id=1, source_target_pairs={{0,1},{1,0},{2,3},{3,2},{4,5},{5,4},{6,7},{7,6},{8,9},{9,8},{10,11... | collective-permute-start | bytes 1572872 | tf_op jit(solution)/shard_map/ppermute | solution.py:200
  3.7 16.2 %collective-permute-start.21 = (f32[512,256]{1,0:T(8,128)}, f32[512,256]{1,0:T(8,128)S(1)}, u32[]{:S(2)}, u32[]{:S(2)}) collective-permute-start(f32[512,256]{1,0:T(8,128)} %refs_6_.1), channel_id=1, source_target_pairs={{1,16},{3,18},{5,20},{7,22},{9,24},{11,26},{13,28},{15,30},{16,1},... | collective-permute-start | bytes 1572872 | tf_op jit(solution)/shard_map/ppermute | solution.py:200
  4.4 26.9 %collective-permute-start.19 = (s32[1,16]{1,0:T(1,128)}, s32[1,16]{1,0:T(1,128)S(1)}, u32[]{:S(2)}, u32[]{:S(2)}) collective-permute-start(s32[1,16]{1,0:T(1,128)} %param.18), channel_id=1, source_target_pairs={{0,1},{1,0},{2,3},{3,2},{4,5},{5,4},{6,7},{7,6},{8,9},{9,8},{10,11... | collective-permute-start | bytes 200 | tf_op jit(solution)/shard_map/ppermute | solution.py:200
  10.8 20.5 %copy-start.2 = (f32[256,256]{1,0:T(8,128)}, f32[256,256]{1,0:T(8,128)S(1)}, u32[]{:S(2)}) copy-start(f32[256,256]{1,0:T(8,128)S(1)} %get-tuple-element.16) | copy-start | bytes 786436
  10.8 9.1 %collective-permute-start.10 = (f32[256,256]{1,0:T(8,128)S(1)}, f32[256,256]{1,0:T(8,128)S(1)}, u32[]{:S(2)}, u32[]{:S(2)}) collective-permute-start(f32[256,256]{1,0:T(8,128)S(1)} %get-tuple-element.17), channel_id=1, source_target_pairs={{0,4},{2,6},{4,0},{6,2},{8,12},{10,14},{12,8},{14,10},{17,21},{19,... | collective-permute-start | bytes 786440 | tf_op jit(solution)/shard_map/ppermute | solution.py:200
  14.2 20.7 %collective-permute-start.12 = (f32[256,256]{1,0:T(8,128)S(1)}, f32[256,256]{1,0:T(8,128)S(1)}, u32[]{:S(2)}, u32[]{:S(2)}) collective-permute-start(f32[256,256]{1,0:T(8,128)S(1)} %get-tuple-element.16), channel_id=1, source_target_pairs={{0,8},{2,10},{4,12},{6,14},{8,0},{10,2},{12,4},{14,6},{17,25},{19,... | collective-permute-start | bytes 786440 | tf_op jit(solution)/shard_map/ppermute | solution.py:200
  19.9 21.7 %collective-permute-start.17 = (f32[256,256]{1,0:T(8,128)S(1)}, f32[256,256]{1,0:T(8,128)S(1)}, u32[]{:S(2)}, u32[]{:S(2)}) collective-permute-start(f32[256,256]{1,0:T(8,128)S(1)} %collective-permute-done.10.refs_2_), channel_id=1, source_target_pairs={{0,2},{1,3},{2,0},{3,1},{4,6},{5,7},{6,4},{7,5},{8,10},{9,11},{10,... | collective-permute-start | bytes 786440 | tf_op jit(solution)/shard_map/ppermute | solution.py:200
  20.8 23.7 %collective-permute-start.22 = (f32[256,256]{1,0:T(8,128)}, f32[256,256]{1,0:T(8,128)S(1)}, u32[]{:S(2)}, u32[]{:S(2)}) collective-permute-start(f32[256,256]{1,0:T(8,128)} %get-tuple-element.15), channel_id=1, source_target_pairs={{0,4},{1,5},{2,6},{3,7},{4,0},{5,1},{6,2},{7,3},{8,12},{9,13},{10,... | collective-permute-start | bytes 786440 | tf_op jit(solution)/shard_map/ppermute | solution.py:200
  22.3 24.7 %collective-permute-start.24 = (f32[256,256]{1,0:T(8,128)}, f32[256,256]{1,0:T(8,128)S(1)}, u32[]{:S(2)}, u32[]{:S(2)}) collective-permute-start(f32[256,256]{1,0:T(8,128)} %get-tuple-element.14), channel_id=1, source_target_pairs={{0,8},{1,9},{2,10},{3,11},{4,12},{5,13},{6,14},{7,15},{8,0},{9,1},... | collective-permute-start | bytes 786440 | tf_op jit(solution)/shard_map/ppermute | solution.py:200
  31.3 20.8 %collective-permute-start.16 = (f32[512,256]{1,0:T(8,128)}, f32[512,256]{1,0:T(8,128)}, u32[]{:S(2)}, u32[]{:S(2)}) collective-permute-start(f32[512,256]{1,0:T(8,128)} %refs_6_.1), channel_id=1, source_target_pairs={{0,2},{1,3},{2,0},{3,1},{4,6},{5,7},{6,4},{7,5},{8,10},{9,11},{10,... | collective-permute-start | bytes 1572872 | tf_op jit(solution)/shard_map/ppermute | solution.py:200
  34.9 19.3 %collective-permute-start = (f32[512,256]{1,0:T(8,128)}, f32[512,256]{1,0:T(8,128)S(1)}, u32[]{:S(2)}, u32[]{:S(2)}) collective-permute-start(f32[512,256]{1,0:T(8,128)} %refs_6_.1), channel_id=1, source_target_pairs={{0,16},{2,18},{4,20},{6,22},{8,24},{10,26},{12,28},{14,30},{17,1},... | collective-permute-start | bytes 1572872 | tf_op jit(solution)/shard_map/ppermute | solution.py:200
  41.6 23.8 %collective-permute-start.11 = (f32[512,256]{1,0:T(8,128)}, f32[512,256]{1,0:T(8,128)S(1)}, u32[]{:S(2)}, u32[]{:S(2)}) collective-permute-start(f32[512,256]{1,0:T(8,128)} %pad_maximum_fusion.2), channel_id=1, source_target_pairs={{0,8},{2,10},{4,12},{6,14},{8,0},{10,2},{12,4},{14,6},{17,25},{19,... | collective-permute-start | bytes 1572872 | tf_op jit(solution)/shard_map/ppermute | solution.py:200
  44.6 20.9 %collective-permute-start.13 = (f32[512,256]{1,0:T(8,128)S(1)}, f32[512,256]{1,0:T(8,128)S(1)}, u32[]{:S(2)}, u32[]{:S(2)}) collective-permute-start(f32[512,256]{1,0:T(8,128)S(1)} %pad_maximum_fusion.3), channel_id=1, source_target_pairs={{0,4},{2,6},{4,0},{6,2},{8,12},{10,14},{12,8},{14,10},{17,21},{19,... | collective-permute-start | bytes 1572872 | tf_op jit(solution)/shard_map/ppermute | solution.py:200
  47.0 2.9 %collective-permute-start.18 = (f32[256,256]{1,0:T(8,128)S(1)}, f32[256,256]{1,0:T(8,128)S(1)}, u32[]{:S(2)}, u32[]{:S(2)}) collective-permute-start(f32[256,256]{1,0:T(8,128)S(1)} %collective-permute-done.12.refs_3_), channel_id=1, source_target_pairs={{0,2},{1,3},{2,0},{3,1},{4,6},{5,7},{6,4},{7,5},{8,10},{9,11},{10,... | collective-permute-start | bytes 786440 | tf_op jit(solution)/shard_map/ppermute | solution.py:200
  50.0 26.1 %collective-permute-start.23 = (f32[512,256]{1,0:T(8,128)S(1)}, f32[512,256]{1,0:T(8,128)S(1)}, u32[]{:S(2)}, u32[]{:S(2)}) collective-permute-start(f32[512,256]{1,0:T(8,128)S(1)} %pad_maximum_fusion.4), channel_id=1, source_target_pairs={{0,8},{1,9},{2,10},{3,11},{4,12},{5,13},{6,14},{7,15},{8,0},{9,1},... | collective-permute-start | bytes 1572872 | tf_op jit(solution)/shard_map/ppermute | solution.py:200
  52.1 24.0 %collective-permute-start.25 = (f32[512,256]{1,0:T(8,128)S(1)}, f32[512,256]{1,0:T(8,128)S(1)}, u32[]{:S(2)}, u32[]{:S(2)}) collective-permute-start(f32[512,256]{1,0:T(8,128)S(1)} %pad_maximum_fusion.5), channel_id=1, source_target_pairs={{0,4},{1,5},{2,6},{3,7},{4,0},{5,1},{6,2},{7,3},{8,12},{9,13},{10,... | collective-permute-start | bytes 1572872 | tf_op jit(solution)/shard_map/ppermute | solution.py:200
  54.2 11.8 %collective-permute-start.29 = (f32[256,256]{1,0:T(8,128)S(1)}, f32[256,256]{1,0:T(8,128)S(1)}, u32[]{:S(2)}, u32[]{:S(2)}) collective-permute-start(f32[256,256]{1,0:T(8,128)S(1)} %collective-permute-done.22.refs_2_), channel_id=1, source_target_pairs={{0,2},{1,3},{2,0},{3,1},{4,6},{5,7},{6,4},{7,5},{8,10},{9,11},{10,... | collective-permute-start | bytes 786440 | tf_op jit(solution)/shard_map/ppermute | solution.py:200
  65.4 1.5 %collective-permute-start.30 = (f32[256,256]{1,0:T(8,128)S(1)}, f32[256,256]{1,0:T(8,128)S(1)}, u32[]{:S(2)}, u32[]{:S(2)}) collective-permute-start(f32[256,256]{1,0:T(8,128)S(1)} %collective-permute-done.24.refs_3_), channel_id=1, source_target_pairs={{0,2},{1,3},{2,0},{3,1},{4,6},{5,7},{6,4},{7,5},{8,10},{9,11},{10,... | collective-permute-start | bytes 786440 | tf_op jit(solution)/shard_map/ppermute | solution.py:200
  65.4 12.0 %collective-permute-start.28 = (f32[512,256]{1,0:T(8,128)S(1)}, f32[512,256]{1,0:T(8,128)S(1)}, u32[]{:S(2)}, u32[]{:S(2)}) collective-permute-start(f32[512,256]{1,0:T(8,128)S(1)} %broadcast_select_fusion.refs_1_), channel_id=1, source_target_pairs={{0,2},{1,3},{2,0},{3,1},{4,6},{5,7},{6,4},{7,5},{8,10},{9,11},{10,... | collective-permute-start | bytes 1572872 | tf_op jit(solution)/shard_map/ppermute | solution.py:200
  66.0 15.4 %collective-permute-start.14 = (f32[512,256]{1,0:T(8,128)S(1)}, f32[512,256]{1,0:T(8,128)S(1)}, u32[]{:S(2)}, u32[]{:S(2)}) collective-permute-start(f32[512,256]{1,0:T(8,128)S(1)} %collective-permute-done.11.refs_1_), channel_id=1, source_target_pairs={{0,2},{1,3},{2,0},{3,1},{4,6},{5,7},{6,4},{7,5},{8,10},{9,11},{10,... | collective-permute-start | bytes 1572872 | tf_op jit(solution)/shard_map/ppermute | solution.py:200
  67.0 15.1 %collective-permute-start.15 = (f32[512,256]{1,0:T(8,128)S(1)}, f32[512,256]{1,0:T(8,128)S(1)}, u32[]{:S(2)}, u32[]{:S(2)}) collective-permute-start(f32[512,256]{1,0:T(8,128)S(1)} %collective-permute-done.13.refs_2_), channel_id=1, source_target_pairs={{0,2},{1,3},{2,0},{3,1},{4,6},{5,7},{6,4},{7,5},{8,10},{9,11},{10,... | collective-permute-start | bytes 1572872 | tf_op jit(solution)/shard_map/ppermute | solution.py:200
  67.3 1.0 copy-start
  70.2 11.9 %copy-start.1 = (f32[512,256]{1,0:T(8,128)S(1)}, f32[512,256]{1,0:T(8,128)}, u32[]{:S(2)}) copy-start(f32[512,256]{1,0:T(8,128)} %refs_6_.1) | copy-start | bytes 1572868
  76.1 7.6 %collective-permute-start.26 = (f32[512,256]{1,0:T(8,128)S(1)}, f32[512,256]{1,0:T(8,128)S(1)}, u32[]{:S(2)}, u32[]{:S(2)}) collective-permute-start(f32[512,256]{1,0:T(8,128)S(1)} %collective-permute-done.23.refs_1_), channel_id=1, source_target_pairs={{0,2},{1,3},{2,0},{3,1},{4,6},{5,7},{6,4},{7,5},{8,10},{9,11},{10,... | collective-permute-start | bytes 1572872 | tf_op jit(solution)/shard_map/ppermute | solution.py:200
  76.1 7.6 %collective-permute-start.27 = (f32[512,256]{1,0:T(8,128)S(1)}, f32[512,256]{1,0:T(8,128)S(1)}, u32[]{:S(2)}, u32[]{:S(2)}) collective-permute-start(f32[512,256]{1,0:T(8,128)S(1)} %collective-permute-done.25.refs_2_), channel_id=1, source_target_pairs={{0,2},{1,3},{2,0},{3,1},{4,6},{5,7},{6,4},{7,5},{8,10},{9,11},{10,... | collective-permute-start | bytes 1572872 | tf_op jit(solution)/shard_map/ppermute | solution.py:200
  77.4 18.3 %collective-permute-start.1 = (f32[256,256]{1,0:T(8,128)}, f32[256,256]{1,0:T(8,128)S(1)}, u32[]{:S(2)}, u32[]{:S(2)}) collective-permute-start(f32[256,256]{1,0:T(8,128)} %get-tuple-element.19), channel_id=1, source_target_pairs={{1,5},{3,7},{5,1},{7,3},{9,13},{11,15},{13,9},{15,11},{16,20},{18,... | collective-permute-start | bytes 786440 | tf_op jit(solution)/shard_map/ppermute | solution.py:200
  81.4 12.6 %collective-permute-start.3 = (f32[256,256]{1,0:T(8,128)}, f32[256,256]{1,0:T(8,128)S(1)}, u32[]{:S(2)}, u32[]{:S(2)}) collective-permute-start(f32[256,256]{1,0:T(8,128)} %get-tuple-element.18), channel_id=1, source_target_pairs={{1,9},{3,11},{5,13},{7,15},{9,1},{11,3},{13,5},{15,7},{16,24},{18,... | collective-permute-start | bytes 786440 | tf_op jit(solution)/shard_map/ppermute | solution.py:200
  87.5 10.0 %collective-permute-start.32 = (f32[256,256]{1,0:T(8,128)}, f32[256,256]{1,0:T(8,128)}, u32[]{:S(2)}, u32[]{:S(2)}) collective-permute-start(f32[256,256]{1,0:T(8,128)} %pad_maximum_fusion.6), channel_id=1, source_target_pairs={{0,2},{1,3},{2,0},{3,1},{4,6},{5,7},{6,4},{7,5},{8,10},{9,11},{10,... | collective-permute-start | bytes 786440 | tf_op jit(solution)/shard_map/ppermute | solution.py:200
  95.0 17.9 %collective-permute-start.4 = (f32[512,256]{1,0:T(8,128)S(1)}, f32[512,256]{1,0:T(8,128)S(1)}, u32[]{:S(2)}, u32[]{:S(2)}) collective-permute-start(f32[512,256]{1,0:T(8,128)S(1)} %pad_maximum_fusion.1), channel_id=1, source_target_pairs={{1,5},{3,7},{5,1},{7,3},{9,13},{11,15},{13,9},{15,11},{16,20},{18,... | collective-permute-start | bytes 1572872 | tf_op jit(solution)/shard_map/ppermute | solution.py:200
  96.7 16.2 %collective-permute-start.2 = (f32[512,256]{1,0:T(8,128)S(1)}, f32[512,256]{1,0:T(8,128)S(1)}, u32[]{:S(2)}, u32[]{:S(2)}) collective-permute-start(f32[512,256]{1,0:T(8,128)S(1)} %pad_maximum_fusion), channel_id=1, source_target_pairs={{1,9},{3,11},{5,13},{7,15},{9,1},{11,3},{13,5},{15,7},{16,24},{18,... | collective-permute-start | bytes 1572872 | tf_op jit(solution)/shard_map/ppermute | solution.py:200
  98.5 4.3 %collective-permute-start.34 = (f32[64,256]{1,0:T(8,128)S(1)}, f32[64,256]{1,0:T(8,128)S(1)}, u32[]{:S(2)}, u32[]{:S(2)}) collective-permute-start(f32[64,256]{1,0:T(8,128)S(1)} %get-tuple-element.26), channel_id=1, source_target_pairs={{0,1},{1,0},{2,3},{3,2},{4,5},{5,4},{6,7},{7,6},{8,9},{9,8},{10,11... | collective-permute-start | bytes 196616 | tf_op jit(solution)/shard_map/ppermute | solution.py:200
  98.6 7.4 %collective-permute-start.35 = (f32[64,256]{1,0:T(8,128)S(1)}, f32[64,256]{1,0:T(8,128)S(1)}, u32[]{:S(2)}, u32[]{:S(2)}) collective-permute-start(f32[64,256]{1,0:T(8,128)S(1)} %get-tuple-element.27), channel_id=1, source_target_pairs={{0,5},{1,4},{2,7},{3,6},{4,1},{5,0},{6,3},{7,2},{8,13},{9,12},{10,... | collective-permute-start | bytes 196616 | tf_op jit(solution)/shard_map/ppermute | solution.py:200
  98.7 7.3 %collective-permute-start.33 = (f32[64,256]{1,0:T(8,128)S(1)}, f32[64,256]{1,0:T(8,128)S(1)}, u32[]{:S(2)}, u32[]{:S(2)}) collective-permute-start(f32[64,256]{1,0:T(8,128)S(1)} %slice_select_fusion.4), channel_id=1, source_target_pairs={{0,4},{1,5},{2,6},{3,7},{4,0},{5,1},{6,2},{7,3},{8,12},{9,13},{10,... | collective-permute-start | bytes 196616 | tf_op jit(solution)/shard_map/ppermute | solution.py:200
  106.0 7.4 %collective-permute-start.36 = (f32[64,256]{1,0:T(8,128)S(1)}, f32[64,256]{1,0:T(8,128)S(1)}, u32[]{:S(2)}, u32[]{:S(2)}) collective-permute-start(f32[64,256]{1,0:T(8,128)S(1)} %add_add_fusion.1), channel_id=1, source_target_pairs={{0,8},{1,9},{2,10},{3,11},{4,12},{5,13},{6,14},{7,15},{8,0},{9,1},... | collective-permute-start | bytes 196616 | tf_op jit(solution)/shard_map/ppermute | solution.py:200
  108.1 9.2 %collective-permute-start.37 = (f32[64,256]{1,0:T(8,128)S(1)}, f32[64,256]{1,0:T(8,128)S(1)}, u32[]{:S(2)}, u32[]{:S(2)}) collective-permute-start(f32[64,256]{1,0:T(8,128)S(1)} %add_add_fusion.1), channel_id=1, source_target_pairs={{0,16},{1,17},{2,18},{3,19},{4,20},{5,21},{6,22},{7,23},{8,24},{9,... | collective-permute-start | bytes 196616 | tf_op jit(solution)/shard_map/ppermute | solution.py:200
  112.9 6.1 %collective-permute-start.38 = (f32[64,256]{1,0:T(8,128)S(1)}, f32[64,256]{1,0:T(8,128)S(1)}, u32[]{:S(2)}, u32[]{:S(2)}) collective-permute-start(f32[64,256]{1,0:T(8,128)S(1)} %add_add_fusion.1), channel_id=1, source_target_pairs={{0,24},{1,25},{2,26},{3,27},{4,28},{5,29},{6,30},{7,31},{8,16},{9,... | collective-permute-start | bytes 196616 | tf_op jit(solution)/shard_map/ppermute | solution.py:200
  112.9 6.6 %collective-permute-start.8 = (f32[256,256]{1,0:T(8,128)S(1)}, f32[256,256]{1,0:T(8,128)S(1)}, u32[]{:S(2)}, u32[]{:S(2)}) collective-permute-start(f32[256,256]{1,0:T(8,128)S(1)} %collective-permute-done.1.refs_2_), channel_id=1, source_target_pairs={{0,2},{1,3},{2,0},{3,1},{4,6},{5,7},{6,4},{7,5},{8,10},{9,11},{10,... | collective-permute-start | bytes 786440 | tf_op jit(solution)/shard_map/ppermute | solution.py:200
  112.9 12.6 %collective-permute-start.7 = (f32[512,256]{1,0:T(8,128)S(1)}, f32[512,256]{1,0:T(8,128)S(1)}, u32[]{:S(2)}, u32[]{:S(2)}) collective-permute-start(f32[512,256]{1,0:T(8,128)S(1)} %collective-permute-done.refs_1_), channel_id=1, source_target_pairs={{0,2},{1,3},{2,0},{3,1},{4,6},{5,7},{6,4},{7,5},{8,10},{9,11},{10,... | collective-permute-start | bytes 1572872 | tf_op jit(solution)/shard_map/ppermute | solution.py:200
  113.4 13.3 %collective-permute-start.6 = (f32[512,256]{1,0:T(8,128)S(1)}, f32[512,256]{1,0:T(8,128)S(1)}, u32[]{:S(2)}, u32[]{:S(2)}) collective-permute-start(f32[512,256]{1,0:T(8,128)S(1)} %collective-permute-done.4.refs_2_), channel_id=1, source_target_pairs={{0,2},{1,3},{2,0},{3,1},{4,6},{5,7},{6,4},{7,5},{8,10},{9,11},{10,... | collective-permute-start | bytes 1572872 | tf_op jit(solution)/shard_map/ppermute | solution.py:200
  117.3 9.4 %collective-permute-start.5 = (f32[512,256]{1,0:T(8,128)S(1)}, f32[512,256]{1,0:T(8,128)S(1)}, u32[]{:S(2)}, u32[]{:S(2)}) collective-permute-start(f32[512,256]{1,0:T(8,128)S(1)} %collective-permute-done.2.refs_1_), channel_id=1, source_target_pairs={{0,2},{1,3},{2,0},{3,1},{4,6},{5,7},{6,4},{7,5},{8,10},{9,11},{10,... | collective-permute-start | bytes 1572872 | tf_op jit(solution)/shard_map/ppermute | solution.py:200
  119.0 12.7 %collective-permute-start.31 = (f32[512,256]{1,0:T(8,128)S(1)}, f32[512,256]{1,0:T(8,128)S(1)}, u32[]{:S(2)}, u32[]{:S(2)}) collective-permute-start(f32[512,256]{1,0:T(8,128)S(1)} %get-tuple-element.7), channel_id=1, source_target_pairs={{0,1},{1,0},{2,3},{3,2},{4,5},{5,4},{6,7},{7,6},{8,9},{9,8},{10,11... | collective-permute-start | bytes 1572872 | tf_op jit(solution)/shard_map/ppermute | solution.py:200
  119.5 4.3 %collective-permute-start.39 = (f32[64,256]{1,0:T(8,128)S(1)}, f32[64,256]{1,0:T(8,128)S(1)}, u32[]{:S(2)}, u32[]{:S(2)}) collective-permute-start(f32[64,256]{1,0:T(8,128)S(1)} %add_add_fusion), channel_id=1, source_target_pairs={{0,4},{1,5},{2,6},{3,7},{4,0},{5,1},{6,2},{7,3},{8,12},{9,13},{10,... | collective-permute-start | bytes 196616 | tf_op jit(solution)/shard_map/ppermute | solution.py:200
  123.8 1.5 %collective-permute-start.9 = (f32[256,256]{1,0:T(8,128)S(1)}, f32[256,256]{1,0:T(8,128)S(1)}, u32[]{:S(2)}, u32[]{:S(2)}) collective-permute-start(f32[256,256]{1,0:T(8,128)S(1)} %collective-permute-done.3.refs_3_), channel_id=1, source_target_pairs={{0,2},{1,3},{2,0},{3,1},{4,6},{5,7},{6,4},{7,5},{8,10},{9,11},{10,... | collective-permute-start | bytes 786440 | tf_op jit(solution)/shard_map/ppermute | solution.py:200
  125.4 8.1 %collective-permute-start.40 = (f32[128,256]{1,0:T(8,128)S(1)}, f32[128,256]{1,0:T(8,128)S(1)}, u32[]{:S(2)}, u32[]{:S(2)}) collective-permute-start(f32[128,256]{1,0:T(8,128)S(1)} %pad_maximum_fusion.7), channel_id=1, source_target_pairs={{0,2},{1,3},{2,0},{3,1},{4,6},{5,7},{6,4},{7,5},{8,10},{9,11},{10,... | collective-permute-start | bytes 393224 | tf_op jit(solution)/shard_map/ppermute | solution.py:200
  126.7 6.8 %copy-start.3 = (f32[256,256]{1,0:T(8,128)S(1)}, f32[256,256]{1,0:T(8,128)}, u32[]{:S(2)}) copy-start(f32[256,256]{1,0:T(8,128)} %param.19) | copy-start | bytes 786436

commit v3 on v2

--- a/solution.py
+++ b/solution.py
@@ -58,9 +58,11 @@
     acc_in = refs.pop(0) if has_acc else None
     extra_in = refs.pop(0) if final else None
     out = refs.pop(0)
-    terms = refs.pop(0) if final == "terms" else None
+    terms = refs.pop(0) if final else None
     a_buf, p_buf, extra, a_sem, p_sem, one_sem = refs
     row_on = [table[2 * count + rb] > 0 for rb in range(blocks)]
+    all_on = functools.reduce(jnp.logical_and, row_on)
+    dot = functools.partial(jnp.dot, preferred_element_type=jnp.float32)
 
     def a_copy(p, rb):
         return pltpu.make_async_copy(
@@ -92,20 +94,35 @@
         acc_copy.wait()
     else:
         out[...] = jnp.zeros_like(out)
-    for p in range(count):
+
+    def step(p, carry):
         @pl.when(table[count + p] > 0)
-        def _(p=p):
-            p_copy(p).wait()
-            piece = split(p_buf[p])
+        def _():
+            pltpu.make_async_copy(p_buf.at[p], p_buf.at[p], p_sem.at[p]).wait()
+            high, low = split(p_buf[p])
+
+            def add(first, size):
+                for rb in range(first, first + size):
+                    a_copy(p, rb).wait()
+                a_high, a_low = split(a_buf[p, first : first + size].reshape(size * width, width))
+                both = dot(jnp.concatenate([a_high, a_low]), high)
+                total = both[: size * width] + (both[size * width :] + dot(a_high, low))
+                out[pl.ds(first * width, size * width), :] += total
+
+            @pl.when(all_on)
+            def _():
+                add(0, blocks)
+
             for rb in range(blocks):
-                @pl.when(row_on[rb])
+                @pl.when(jnp.logical_not(all_on) & row_on[rb])
                 def _(rb=rb):
-                    a_copy(p, rb).wait()
-                    out[pl.ds(rb * width, width), :] += dot3(split(a_buf[p, rb]), piece, ((1,), (0,)))
-
+                    add(rb, 1)
+
+        return carry
+
+    lax.fori_loop(0, count, step, 0)
     if final:
         extra_copy.wait()
-    if final == "terms":
         terms[...] = jnp.zeros_like(terms)
         for rb in range(blocks):
             rows = pl.ds(rb * width, width)
@@ -118,20 +135,8 @@
         def _():
             terms[...] += terms[...].T
 
-    if final == "panel":
-        for rb in range(blocks):
-            rows = pl.ds(rb * width, width)
-
-            @pl.when(row_on[rb])
-            def _(rows=rows):
-                out[rows, :] = -(out[rows, :] + extra[rows, :])
-
-            @pl.when(jnp.logical_not(row_on[rb]))
-            def _(rows=rows):
-                out[rows, :] = jnp.zeros((width, out.shape[1]), jnp.float32)
-
-
-def product(table, inverse_anc, arrays, slots, width, acc=None, final=None, extra=None):
+
+def product(table, inverse_anc, arrays, slots, width, acc=None, extra=None):
     rows = inverse_anc.shape[0]
     blocks = rows // width
     count = len(slots)
@@ -143,11 +148,11 @@
         if more is not None:
             operands.append(more)
             specs.append(any_spec)
-    shapes = [jax.ShapeDtypeStruct((rows, width), jnp.float32)]
-    if final == "terms":
+    shapes = [pltpu.HBM((rows, width), jnp.float32)]
+    if extra is not None:
         shapes.append(jax.ShapeDtypeStruct((width, width), jnp.float32))
     return pl.pallas_call(
-        functools.partial(product_kernel, slots, blocks, width, acc is not None, final),
+        functools.partial(product_kernel, slots, blocks, width, acc is not None, extra is not None),
         out_shape=shapes,
         grid_spec=pltpu.PrefetchScalarGridSpec(
             num_scalar_prefetch=1,
@@ -163,7 +168,7 @@
                 pltpu.SemaphoreType.DMA((2,)),
             ],
         ),
-        compiler_params=pltpu.CompilerParams(vmem_limit_bytes=13 * 1024 * 1024),
+        compiler_params=pltpu.CompilerParams(vmem_limit_bytes=20 * 1024 * 1024),
         cost_estimate=pl.CostEstimate(
             flops=6 * rows * width * width * count // 4,
             bytes_accessed=4 * rows * width * count // 2,
@@ -173,10 +178,13 @@
 
 
 CORE, X, Z, FAR = 1, 2, 4, 8
-FIRST = ((0, 0), (0, 1), (X, 0), (Z, 1))
-SECOND = ((Z, 0), (Z | X, 0), (X, 1), (Z | X, 1))
+FIRST = ((0, 0), (0, 1), (X, 0), (Z, 1), (1, 0), (1, 1), (X | 1, 0), (Z | 1, 1))
+SECOND = tuple((m | c, h) for c in (0, 1) for m, h in ((Z, 0), (Z | X, 0), (X, 1), (Z | X, 1)))
+WHOLE = tuple((m | c, h) for c in (0, 1) for m in (0, X, Z, Z | X) for h in (0, 1))
 SLOTS1 = ((0, 0), (0, 1), (1, 0), (2, 0), (3, 0), (3, 1), (4, 0), (5, 0))
 SLOTS2 = ((0, 0), (0, 1), (1, 0), (1, 1), (2, 0), (2, 1), (3, 0), (3, 1))
+SLOTSW = tuple((i, h) for i in range(8) for h in (0, 1))
+SLOTS12 = SLOTS1 + tuple((6 + i, h) for i, h in SLOTS2)
 
 
 def local_two(n_row, inverse_anc, lower_panel, structure, diag_inverse):
@@ -200,7 +208,6 @@
         return lax.ppermute(value, BOTH, pairs)
 
     def table(listed, order, who):
-        order = order + tuple((m ^ CORE, h) for m, h in order)
         block = ((row % FAR) ^ jnp.array([m for m, _ in order], jnp.int32)) * 2
         block = block + jnp.array([h for _, h in order], jnp.int32)
         ids = jnp.concatenate([block + col * 2 * FAR, row * 2 + jnp.arange(2, dtype=jnp.int32)])
@@ -224,12 +231,13 @@
     other_structure = move(structure, 0, 1)
     got_far = move(lower_panel, FAR, 1, False)
     lower_other = move(lower_panel, 0, 1)
+    n_z = move(lower_panel, Z, 0, True)
+    n_x = move(lower_panel, X, 0, True)
     q_far = move(lower_panel, FAR, 0, True)
-
-    n_one = step_one(lower_panel, True)
-    n_two = step_two(lower_panel, n_one, True)
-    n_first = with_sibling([lower_panel, *n_one], None)
-    n_second = with_sibling(n_two, None)
+    n_zx = move(n_z, X, 0, True)
+    n_all = with_sibling([lower_panel, n_x, n_z, n_zx], None)
+    in_hbm = lambda v: pltpu.with_memory_space_constraint(v, pltpu.HBM)
+    n_all[0] = in_hbm(lower_panel)
     q_other = jnp.where(near, lower_other, got_far)
     o_one = step_one(q_other, None)
     o_two = step_two(q_other, o_one, None)
@@ -240,22 +248,21 @@
     f_first = with_sibling([q_far, *f_one], None)
     f_second = with_sibling(f_two, None)
 
-    (own,) = product(table(structure, FIRST, True), inverse_anc, n_first, SLOTS1, width)
     own, own_terms = product(
-        table(structure, SECOND, True), inverse_anc, n_second, SLOTS2, width,
-        acc=own, final="terms", extra=lower_panel,
+        table(structure, WHOLE, True), inverse_anc, n_all, SLOTSW, width, extra=n_all[0]
     )
     (part,) = product(table(other_structure, FIRST, None), inverse_anc, o_first, SLOTS1, width)
     part, other_terms = product(
         table(other_structure, SECOND, None), inverse_anc, o_second, SLOTS2, width,
-        acc=part, final="terms", extra=lower_other,
+        acc=in_hbm(part), extra=lower_other,
     )
     recv = move(part, 0, 1)
-    (own,) = product(table(structure, FIRST, False), inverse_anc, f_first, SLOTS1, width, acc=own)
-    (panel,) = product(
-        table(structure, SECOND, False), inverse_anc, f_second, SLOTS2, width,
-        acc=own, final="panel", extra=recv,
-    )
+    (own,) = product(
+        table(structure, FIRST + SECOND, False), inverse_anc, f_first + f_second, SLOTS12, width,
+        acc=in_hbm(own),
+    )
+    keep = keep_rows(structure, row * rows, rows, width)
+    panel = jnp.where(keep, -(own + recv), jnp.float32(0.0))
 
     def parts(value, mask):
         size = value.shape[0] // 2

time: 136 us -> 146 us (1.074)
  waiting for transfers between devices: 42.9 us -> 51.1 us
  starting transfers between devices: 63.4 us -> 67.3 us
  local copies, waits for them, and re-layouts: 3.8 us -> 1.58 us
  Pallas kernels: 12.8 us -> 14.3 us
    ppermute x41 -> x39, waiting for transfers between devices: 42.9 us -> 51.1 us  [move(): return lax.ppermute(value, BOTH, pairs)]
    ppermute x41 -> x39, starting transfers between devices: 63.4 us -> 67.3 us  [move(): return lax.ppermute(value, BOTH, pairs)]
    slice x3 -> x1, local copies, waits for them, and re-layouts: 2.74 us -> 0.74 us  [step_two(): q[half:]]
    select_n x0 -> x2, other arithmetic: none -> 2 us  [the longest x1 1.99 us: local_two(): panel = jnp.where(keep, -(own + recv), jnp.float32(0.0))]
    pallas_call x6 -> x4, Pallas kernels: 12.8 us -> 14.3 us  [product(): pl.pallas_call(functools.partial(product_kernel, slots, blocks, width, ac...]
    concatenate x3 -> x2, other arithmetic: 2.95 us -> 1.97 us  [step_two(): jnp.concatenate([q[half:], one[1]])]
  transfers between devices with their start and end apart: 41 -> 39, of which waited for: 13 -> 10; matrix products, arithmetic and copies ran while one was open for 9% -> 7% of each run, Pallas kernels for 10% -> 10%
where the time goes in v3:
time: 146 us; the launch traced here: 145 us
  starting transfers between devices  67.3 us (46%)
  waiting for transfers between devices  51.1 us (35%)
  Pallas kernels  14.3 us (10%)
  other arithmetic  9.89 us (7%)
  local copies, waits for them, and re-layouts  1.58 us (1%)
    ppermute x39, starting transfers between devices, move(): return lax.ppermute(value, BOTH, pairs)  67.3 us
    ppermute x39, waiting for transfers between devices, move(): return lax.ppermute(value, BOTH, pairs)  51.1 us
    pallas_call x4, Pallas kernels, product(): pl.pallas_call(functools.partial(product_kernel, slots, blocks, width, ac...  14.3 us
  transfers between devices with their start and end apart: 39, of which 10 were waited for; matrix products, arithmetic and copies ran while one was open for 7% of the time, Pallas kernels for 10%

profile of v3, /device:TPU:0, one launch (start us, length us, event | category | flops | bytes accessed | tf_op | source)
XLA Modules:
  0.0 145.4 jit_solution(18250960391591947375)
XLA Ops:
  0.6 3.1 %collective-permute-start.18 = (f32[512,256]{1,0:T(8,128)}, f32[512,256]{1,0:T(8,128)S(1)}, u32[]{:S(2)}, u32[]{:S(2)}) collective-permute-start(f32[512,256]{1,0:T(8,128)} %refs_9_.1), channel_id=1, source_target_pairs={{0,1},{1,0},{2,3},{3,2},{4,5},{5,4},{6,7},{7,6},{8,9},{9,8},{10,11... | collective-permute-start | bytes 1572872 | tf_op jit(solution)/shard_map/ppermute | solution.py:208
  3.7 0.7 collective-permute-start.19
  4.4 3.5 %collective-permute-start.11 = (f32[512,256]{1,0:T(8,128)}, f32[512,256]{1,0:T(8,128)S(1)}, u32[]{:S(2)}, u32[]{:S(2)}) collective-permute-start(f32[512,256]{1,0:T(8,128)} %refs_9_.1), channel_id=1, source_target_pairs={{0,8},{2,10},{4,12},{6,14},{8,0},{10,2},{12,4},{14,6},{17,25},{19,... | collective-permute-start | bytes 1572872 | tf_op jit(solution)/shard_map/ppermute | solution.py:208
  7.9 3.4 %collective-permute-start.10 = (f32[512,256]{1,0:T(8,128)}, f32[512,256]{1,0:T(8,128)S(1)}, u32[]{:S(2)}, u32[]{:S(2)}) collective-permute-start(f32[512,256]{1,0:T(8,128)} %refs_9_.1), channel_id=1, source_target_pairs={{0,4},{2,6},{4,0},{6,2},{8,12},{10,14},{12,8},{14,10},{17,21},{19,... | collective-permute-start | bytes 1572872 | tf_op jit(solution)/shard_map/ppermute | solution.py:208
  11.3 0.1 collective-permute-start.13
  11.4 0.7 multiply_add_fusion
  12.1 0.7 multiply_add_fusion.2
  12.8 3.4 %collective-permute-done.18.refs_6_ = f32[512,256]{1,0:T(8,128)S(1)} collective-permute-done((f32[512,256]{1,0:T(8,128)}, f32[512,256]{1,0:T(8,128)S(1)}, u32[]{:S(2)}, u32[]{:S(2)}) %collective-permute-start.18) | collective-permute-done | bytes 524320 | tf_op jit(solution)/shard_map/ppermute | solution.py:208
  16.3 2.4 %collective-permute-start.17 = (s32[1,16]{1,0:T(1,128)}, s32[1,16]{1,0:T(1,128)S(1)}, u32[]{:S(2)}, u32[]{:S(2)}) collective-permute-start(s32[1,16]{1,0:T(1,128)} %param.14), channel_id=1, source_target_pairs={{0,1},{1,0},{2,3},{3,2},{4,5},{5,4},{6,7},{7,6},{8,9},{9,8},{10,11... | collective-permute-start | bytes 200 | tf_op jit(solution)/shard_map/ppermute | solution.py:208
  18.7 0.7 fusion.3
  19.4 1.5 %collective-permute-start.20 = (f32[256,256]{1,0:T(8,128)S(1)}, f32[256,256]{1,0:T(8,128)S(1)}, u32[]{:S(2)}, u32[]{:S(2)}) collective-permute-start(f32[256,256]{1,0:T(8,128)S(1)} %get-tuple-element.15), channel_id=1, source_target_pairs={{0,4},{1,5},{2,6},{3,7},{4,0},{5,1},{6,2},{7,3},{8,12},{9,13},{10,... | collective-permute-start | bytes 786440 | tf_op jit(solution)/shard_map/ppermute | solution.py:208
  20.9 0.1 pad_add_fusion.2
  21.0 14.5 %collective-permute-start = (f32[512,256]{1,0:T(8,128)}, f32[512,256]{1,0:T(8,128)S(1)}, u32[]{:S(2)}, u32[]{:S(2)}) collective-permute-start(f32[512,256]{1,0:T(8,128)} %refs_9_.1), channel_id=1, source_target_pairs={{0,16},{2,18},{4,20},{6,22},{8,24},{10,26},{12,28},{14,30},{17,1},... | collective-permute-start | bytes 1572872 | tf_op jit(solution)/shard_map/ppermute | solution.py:208
  35.5 0.7 compare_reduce_fusion.3
  36.3 0.1 collective-permute-start.26
  36.3 5.1 %collective-permute-start.22 = (f32[256,256]{1,0:T(8,128)}, f32[256,256]{1,0:T(8,128)S(1)}, u32[]{:S(2)}, u32[]{:S(2)}) collective-permute-start(f32[256,256]{1,0:T(8,128)} %get-tuple-element.14), channel_id=1, source_target_pairs={{0,8},{1,9},{2,10},{3,11},{4,12},{5,13},{6,14},{7,15},{8,0},{9,1},... | collective-permute-start | bytes 786440 | tf_op jit(solution)/shard_map/ppermute | solution.py:208
  41.5 2.4 %collective-permute-start.12 = (f32[512,256]{1,0:T(8,128)S(1)}, f32[512,256]{1,0:T(8,128)}, u32[]{:S(2)}, u32[]{:S(2)}) collective-permute-start(f32[512,256]{1,0:T(8,128)S(1)} %collective-permute-done.11.refs_3_), channel_id=1, source_target_pairs={{0,4},{2,6},{4,0},{6,2},{8,12},{10,14},{12,8},{14,10},{17,21},{19,... | collective-permute-start | bytes 1572872 | tf_op jit(solution)/shard_map/ppermute | solution.py:208
  43.9 0.1 collective-permute-start.27
  44.1 1.0 pad_maximum_fusion.2
  45.0 6.3 %collective-permute-done.22.refs_3_ = f32[256,256]{1,0:T(8,128)S(1)} collective-permute-done((f32[256,256]{1,0:T(8,128)}, f32[256,256]{1,0:T(8,128)S(1)}, u32[]{:S(2)}, u32[]{:S(2)}) %collective-permute-start.22) | collective-permute-done | bytes 262176 | tf_op jit(solution)/shard_map/ppermute | solution.py:208
  51.3 1.0 pad_maximum_fusion.3
  52.3 6.0 %collective-permute-start.21 = (f32[512,256]{1,0:T(8,128)S(1)}, f32[512,256]{1,0:T(8,128)S(1)}, u32[]{:S(2)}, u32[]{:S(2)}) collective-permute-start(f32[512,256]{1,0:T(8,128)S(1)} %pad_maximum_fusion.2), channel_id=1, source_target_pairs={{0,8},{1,9},{2,10},{3,11},{4,12},{5,13},{6,14},{7,15},{8,0},{9,1},... | collective-permute-start | bytes 1572872 | tf_op jit(solution)/shard_map/ppermute | solution.py:208
  58.4 0.8 collective-permute-start.23
  59.1 0.1 pad_add_fusion.table
  59.2 0.1 pad_add_fusion.4
  59.3 0.5 collective-permute-start.14
  59.8 0.1 collective-permute-start.16
  59.9 0.2 compare_reduce_fusion.1
  60.1 0.1 add_add_fusion.3.table
  60.2 0.1 add_add_fusion.2.table
  60.3 10.2 %collective-permute-done.21.refs_1_ = f32[512,256]{1,0:T(8,128)S(1)} collective-permute-done((f32[512,256]{1,0:T(8,128)S(1)}, f32[512,256]{1,0:T(8,128)S(1)}, u32[]{:S(2)}, u32[]{:S(2)}) %collective-permute-start.21) | collective-permute-done | bytes 524320 | tf_op jit(solution)/shard_map/ppermute | solution.py:208
  70.5 1.5 %collective-permute-done.23.refs_2_ = f32[512,256]{1,0:T(8,128)S(1)} collective-permute-done((f32[512,256]{1,0:T(8,128)S(1)}, f32[512,256]{1,0:T(8,128)S(1)}, u32[]{:S(2)}, u32[]{:S(2)}) %collective-permute-start.23) | collective-permute-done | bytes 524320 | tf_op jit(solution)/shard_map/ppermute | solution.py:208
  71.9 0.8 fusion.4
  72.8 4.2 %shard_map.136.refs_5_ = f32[512,256]{1,0:T(8,128)} custom-call(s32[19]{0:T(128)S(1)} %add_add_fusion.3.table, f32[512,4096]{1,0:T(8,128)} %refs_0_.7, f32[512,256]{1,0:T(8,128)S(1)} %broadcast_select_fusion.refs_1_, f32[256,256]{1,0:T(8,128)S(1)} %collective-permute-done.20.refs_2_, f32[256,256]{1,0:T(8,128)S(1)} %collective-permute-done.22.refs_3_, ...), custom_call_target="tpu_custom_call" | custom-call | flops 402653184 | bytes 2097152 | tf_op jit(solution)/shard_map/pallas_call | solution.py:154
  76.9 0.7 collective-permute-start.1
  77.6 0.7 collective-permute-start.2
  78.3 3.3 %shard_map.134 = (f32[512,256]{1,0:T(8,128)}, f32[256,256]{1,0:T(8,128)S(1)}) custom-call(s32[35]{0:T(128)S(1)} %pad_add_fusion.table, f32[512,4096]{1,0:T(8,128)} %refs_0_.7, f32[512,256]{1,0:T(8,128)} %refs_9_.1, f32[512,256]{1,0:T(8,128)S(1)} %collective-permute-done.10.refs_2_, f32[512,256]{1,0:T(8,128)S(1)} %collective-permute-done.11.refs_3_, ...), custom_call_target="tpu_custom_call" | custom-call | flops 805306368 | bytes 4194304 | tf_op jit(solution)/shard_map/pallas_call | solution.py:154
  81.7 4.0 %shard_map.137 = (f32[512,256]{1,0:T(8,128)}, f32[256,256]{1,0:T(8,128)S(1)}) custom-call(s32[19]{0:T(128)S(1)} %add_add_fusion.2.table, f32[512,4096]{1,0:T(8,128)} %refs_0_.7, f32[512,256]{1,0:T(8,128)S(1)} %collective-permute-done.21.refs_1_, f32[512,256]{1,0:T(8,128)S(1)} %collective-permute-done.23.refs_2_, ...), custom_call_target="tpu_custom_call" | custom-call | flops 402653184 | bytes 2097152 | tf_op jit(solution)/shard_map/pallas_call | solution.py:154
  85.7 5.8 %collective-permute-start.30 = (f32[256,256]{1,0:T(8,128)S(1)}, f32[256,256]{1,0:T(8,128)S(1)}, u32[]{:S(2)}, u32[]{:S(2)}) collective-permute-start(f32[256,256]{1,0:T(8,128)S(1)} %pad_maximum_fusion.4), channel_id=1, source_target_pairs={{0,2},{1,3},{2,0},{3,1},{4,6},{5,7},{6,4},{7,5},{8,10},{9,11},{10,... | collective-permute-start | bytes 786440 | tf_op jit(solution)/shard_map/ppermute | solution.py:208
  91.5 1.0 pad_maximum_fusion
  92.5 0.7 collective-permute-start.6
  93.2 1.0 pad_maximum_fusion.1
  94.2 0.7 collective-permute-start.7
  94.9 0.1 collective-permute-start.4
  95.1 7.3 %collective-permute-start.32 = (f32[64,256]{1,0:T(8,128)S(1)}, f32[64,256]{1,0:T(8,128)S(1)}, u32[]{:S(2)}, u32[]{:S(2)}) collective-permute-start(f32[64,256]{1,0:T(8,128)S(1)} %get-tuple-element.24), channel_id=1, source_target_pairs={{0,1},{1,0},{2,3},{3,2},{4,5},{5,4},{6,7},{7,6},{8,9},{9,8},{10,11... | collective-permute-start | bytes 196616 | tf_op jit(solution)/shard_map/ppermute | solution.py:208
  102.4 0.3 collective-permute-start.33
  102.8 1.3 collective-permute-start.31
  104.1 0.1 collective-permute-start.3
  104.2 1.5 %collective-permute-done.32 = f32[64,256]{1,0:T(8,128)S(1)} collective-permute-done((f32[64,256]{1,0:T(8,128)S(1)}, f32[64,256]{1,0:T(8,128)S(1)}, u32[]{:S(2)}, u32[]{:S(2)}) %collective-permute-start.32) | collective-permute-done | bytes 65568 | tf_op jit(solution)/shard_map/ppermute | solution.py:208
  105.6 10.5 %collective-permute-done.33 = f32[64,256]{1,0:T(8,128)S(1)} collective-permute-done((f32[64,256]{1,0:T(8,128)S(1)}, f32[64,256]{1,0:T(8,128)S(1)}, u32[]{:S(2)}, u32[]{:S(2)}) %collective-permute-start.33) | collective-permute-done | bytes 65568 | tf_op jit(solution)/shard_map/ppermute | solution.py:208
  116.1 1.2 collective-permute-start.34
  117.4 0.5 collective-permute-start.35
  117.9 0.1 compare_reduce_fusion
  118.0 2.7 %collective-permute-done.34 = f32[64,256]{1,0:T(8,128)S(1)} collective-permute-done((f32[64,256]{1,0:T(8,128)S(1)}, f32[64,256]{1,0:T(8,128)S(1)}, u32[]{:S(2)}, u32[]{:S(2)}) %collective-permute-start.34) | collective-permute-done | bytes 65568 | tf_op jit(solution)/shard_map/ppermute | solution.py:208
  120.7 3.2 %collective-permute-done.35 = f32[64,256]{1,0:T(8,128)S(1)} collective-permute-done((f32[64,256]{1,0:T(8,128)S(1)}, f32[64,256]{1,0:T(8,128)S(1)}, u32[]{:S(2)}, u32[]{:S(2)}) %collective-permute-start.35) | collective-permute-done | bytes 65568 | tf_op jit(solution)/shard_map/ppermute | solution.py:208
  123.9 1.5 %collective-permute-start.36 = (f32[64,256]{1,0:T(8,128)S(1)}, f32[64,256]{1,0:T(8,128)S(1)}, u32[]{:S(2)}, u32[]{:S(2)}) collective-permute-start(f32[64,256]{1,0:T(8,128)S(1)} %add_add_fusion.1), channel_id=1, source_target_pairs={{0,24},{1,25},{2,26},{3,27},{4,28},{5,29},{6,30},{7,31},{8,16},{9,... | collective-permute-start | bytes 196616 | tf_op jit(solution)/shard_map/ppermute | solution.py:208
  125.4 0.1 pad_add_fusion.1.table
  125.5 4.5 %collective-permute-done.36 = f32[64,256]{1,0:T(8,128)S(1)} collective-permute-done((f32[64,256]{1,0:T(8,128)S(1)}, f32[64,256]{1,0:T(8,128)S(1)}, u32[]{:S(2)}, u32[]{:S(2)}) %collective-permute-start.36) | collective-permute-done | bytes 65568 | tf_op jit(solution)/shard_map/ppermute | solution.py:208
  130.0 0.6 collective-permute-start.29
  130.6 1.6 %collective-permute-start.37 = (f32[64,256]{1,0:T(8,128)S(1)}, f32[64,256]{1,0:T(8,128)S(1)}, u32[]{:S(2)}, u32[]{:S(2)}) collective-permute-start(f32[64,256]{1,0:T(8,128)S(1)} %add_add_fusion), channel_id=1, source_target_pairs={{0,4},{1,5},{2,6},{3,7},{4,0},{5,1},{6,2},{7,3},{8,12},{9,13},{10,... | collective-permute-start | bytes 196616 | tf_op jit(solution)/shard_map/ppermute | solution.py:208
  132.2 2.9 %shard_map.135 = f32[512,256]{1,0:T(8,128)} custom-call(s32[35]{0:T(128)S(1)} %pad_add_fusion.1.table, f32[512,4096]{1,0:T(8,128)} %refs_0_.7, f32[512,256]{1,0:T(8,128)S(1)} %collective-permute-done.refs_1_, f32[256,256]{1,0:T(8,128)S(1)} %collective-permute-done.1.refs_2_, f32[256,256]{1,0:T(8,128)S(1)} %collective-permute-done.2.refs_3_, ...), custom_call_target="tpu_custom_call" | custom-call | flops 805306368 | bytes 4194304 | tf_op jit(solution)/shard_map/pallas_call | solution.py:154
  135.2 7.4 %collective-permute-done.29 = f32[512,256]{1,0:T(8,128)S(1)} collective-permute-done((f32[512,256]{1,0:T(8,128)}, f32[512,256]{1,0:T(8,128)S(1)}, u32[]{:S(2)}, u32[]{:S(2)}) %collective-permute-start.29) | collective-permute-done | bytes 524320 | tf_op jit(solution)/shard_map/ppermute | solution.py:208
  142.6 2.0 %negate_select_fusion = f32[512,256]{1,0:T(8,128)} fusion(f32[512,256]{1,0:T(8,128)} %shard_map.135, f32[512,256]{1,0:T(8,128)S(1)} %collective-permute-done.29, pred[512]{0:T(512)(128)(4,1)S(1)} %compare_reduce_fusion), kind=kLoop, calls=%fused_computation.4 | loop fusion | flops 393216 | bytes 1573376 | tf_op jit(solution)/shard_map/jit(_where)/select_n | solution.py:265
  144.6 0.7 maximum_add_fusion
  (61 shorter events, 0.5 us)
Async XLA Ops:
  0.6 15.6 %collective-permute-start.18 = (f32[512,256]{1,0:T(8,128)}, f32[512,256]{1,0:T(8,128)S(1)}, u32[]{:S(2)}, u32[]{:S(2)}) collective-permute-start(f32[512,256]{1,0:T(8,128)} %refs_9_.1), channel_id=1, source_target_pairs={{0,1},{1,0},{2,3},{3,2},{4,5},{5,4},{6,7},{7,6},{8,9},{9,8},{10,11... | collective-permute-start | bytes 1572872 | tf_op jit(solution)/shard_map/ppermute | solution.py:208
  3.7 14.9 %collective-permute-start.19 = (f32[512,256]{1,0:T(8,128)}, f32[512,256]{1,0:T(8,128)S(1)}, u32[]{:S(2)}, u32[]{:S(2)}) collective-permute-start(f32[512,256]{1,0:T(8,128)} %refs_9_.1), channel_id=1, source_target_pairs={{1,16},{3,18},{5,20},{7,22},{9,24},{11,26},{13,28},{15,30},{16,1},... | collective-permute-start | bytes 1572872 | tf_op jit(solution)/shard_map/ppermute | solution.py:208
  4.4 31.9 %collective-permute-start.11 = (f32[512,256]{1,0:T(8,128)}, f32[512,256]{1,0:T(8,128)S(1)}, u32[]{:S(2)}, u32[]{:S(2)}) collective-permute-start(f32[512,256]{1,0:T(8,128)} %refs_9_.1), channel_id=1, source_target_pairs={{0,8},{2,10},{4,12},{6,14},{8,0},{10,2},{12,4},{14,6},{17,25},{19,... | collective-permute-start | bytes 1572872 | tf_op jit(solution)/shard_map/ppermute | solution.py:208
  7.9 28.5 %collective-permute-start.10 = (f32[512,256]{1,0:T(8,128)}, f32[512,256]{1,0:T(8,128)S(1)}, u32[]{:S(2)}, u32[]{:S(2)}) collective-permute-start(f32[512,256]{1,0:T(8,128)} %refs_9_.1), channel_id=1, source_target_pairs={{0,4},{2,6},{4,0},{6,2},{8,12},{10,14},{12,8},{14,10},{17,21},{19,... | collective-permute-start | bytes 1572872 | tf_op jit(solution)/shard_map/ppermute | solution.py:208
  11.3 30.2 %collective-permute-start.13 = (f32[512,256]{1,0:T(8,128)}, f32[512,256]{1,0:T(8,128)}, u32[]{:S(2)}, u32[]{:S(2)}) collective-permute-start(f32[512,256]{1,0:T(8,128)} %refs_9_.1), channel_id=1, source_target_pairs={{0,2},{1,3},{2,0},{3,1},{4,6},{5,7},{6,4},{7,5},{8,10},{9,11},{10,... | collective-permute-start | bytes 1572872 | tf_op jit(solution)/shard_map/ppermute | solution.py:208
  16.3 4.8 %collective-permute-start.17 = (s32[1,16]{1,0:T(1,128)}, s32[1,16]{1,0:T(1,128)S(1)}, u32[]{:S(2)}, u32[]{:S(2)}) collective-permute-start(s32[1,16]{1,0:T(1,128)} %param.14), channel_id=1, source_target_pairs={{0,1},{1,0},{2,3},{3,2},{4,5},{5,4},{6,7},{7,6},{8,9},{9,8},{10,11... | collective-permute-start | bytes 200 | tf_op jit(solution)/shard_map/ppermute | solution.py:208
  19.4 24.5 %copy-start = (f32[256,256]{1,0:T(8,128)}, f32[256,256]{1,0:T(8,128)S(1)}, u32[]{:S(2)}) copy-start(f32[256,256]{1,0:T(8,128)S(1)} %get-tuple-element.15) | copy-start | bytes 786436
  19.4 24.5 %collective-permute-start.20 = (f32[256,256]{1,0:T(8,128)S(1)}, f32[256,256]{1,0:T(8,128)S(1)}, u32[]{:S(2)}, u32[]{:S(2)}) collective-permute-start(f32[256,256]{1,0:T(8,128)S(1)} %get-tuple-element.15), channel_id=1, source_target_pairs={{0,4},{1,5},{2,6},{3,7},{4,0},{5,1},{6,2},{7,3},{8,12},{9,13},{10,... | collective-permute-start | bytes 786440 | tf_op jit(solution)/shard_map/ppermute | solution.py:208
  21.0 31.3 %collective-permute-start = (f32[512,256]{1,0:T(8,128)}, f32[512,256]{1,0:T(8,128)S(1)}, u32[]{:S(2)}, u32[]{:S(2)}) collective-permute-start(f32[512,256]{1,0:T(8,128)} %refs_9_.1), channel_id=1, source_target_pairs={{0,16},{2,18},{4,20},{6,22},{8,24},{10,26},{12,28},{14,30},{17,1},... | collective-permute-start | bytes 1572872 | tf_op jit(solution)/shard_map/ppermute | solution.py:208
  36.3 23.1 %collective-permute-start.26 = (f32[512,256]{1,0:T(8,128)S(1)}, f32[512,256]{1,0:T(8,128)}, u32[]{:S(2)}, u32[]{:S(2)}) collective-permute-start(f32[512,256]{1,0:T(8,128)S(1)} %broadcast_select_fusion.refs_1_), channel_id=1, source_target_pairs={{0,2},{1,3},{2,0},{3,1},{4,6},{5,7},{6,4},{7,5},{8,10},{9,11},{10,... | collective-permute-start | bytes 1572872 | tf_op jit(solution)/shard_map/ppermute | solution.py:208
  36.3 15.0 %collective-permute-start.22 = (f32[256,256]{1,0:T(8,128)}, f32[256,256]{1,0:T(8,128)S(1)}, u32[]{:S(2)}, u32[]{:S(2)}) collective-permute-start(f32[256,256]{1,0:T(8,128)} %get-tuple-element.14), channel_id=1, source_target_pairs={{0,8},{1,9},{2,10},{3,11},{4,12},{5,13},{6,14},{7,15},{8,0},{9,1},... | collective-permute-start | bytes 786440 | tf_op jit(solution)/shard_map/ppermute | solution.py:208
  41.5 18.3 %collective-permute-start.12 = (f32[512,256]{1,0:T(8,128)S(1)}, f32[512,256]{1,0:T(8,128)}, u32[]{:S(2)}, u32[]{:S(2)}) collective-permute-start(f32[512,256]{1,0:T(8,128)S(1)} %collective-permute-done.11.refs_3_), channel_id=1, source_target_pairs={{0,4},{2,6},{4,0},{6,2},{8,12},{10,14},{12,8},{14,10},{17,21},{19,... | collective-permute-start | bytes 1572872 | tf_op jit(solution)/shard_map/ppermute | solution.py:208
  43.9 14.4 %collective-permute-start.27 = (f32[256,256]{1,0:T(8,128)S(1)}, f32[256,256]{1,0:T(8,128)S(1)}, u32[]{:S(2)}, u32[]{:S(2)}) collective-permute-start(f32[256,256]{1,0:T(8,128)S(1)} %collective-permute-done.20.refs_2_), channel_id=1, source_target_pairs={{0,2},{1,3},{2,0},{3,1},{4,6},{5,7},{6,4},{7,5},{8,10},{9,11},{10,... | collective-permute-start | bytes 786440 | tf_op jit(solution)/shard_map/ppermute | solution.py:208
  51.3 8.0 %collective-permute-start.28 = (f32[256,256]{1,0:T(8,128)S(1)}, f32[256,256]{1,0:T(8,128)S(1)}, u32[]{:S(2)}, u32[]{:S(2)}) collective-permute-start(f32[256,256]{1,0:T(8,128)S(1)} %collective-permute-done.22.refs_3_), channel_id=1, source_target_pairs={{0,2},{1,3},{2,0},{3,1},{4,6},{5,7},{6,4},{7,5},{8,10},{9,11},{10,... | collective-permute-start | bytes 786440 | tf_op jit(solution)/shard_map/ppermute | solution.py:208
  52.3 18.1 %collective-permute-start.21 = (f32[512,256]{1,0:T(8,128)S(1)}, f32[512,256]{1,0:T(8,128)S(1)}, u32[]{:S(2)}, u32[]{:S(2)}) collective-permute-start(f32[512,256]{1,0:T(8,128)S(1)} %pad_maximum_fusion.2), channel_id=1, source_target_pairs={{0,8},{1,9},{2,10},{3,11},{4,12},{5,13},{6,14},{7,15},{8,0},{9,1},... | collective-permute-start | bytes 1572872 | tf_op jit(solution)/shard_map/ppermute | solution.py:208
  58.4 13.6 %collective-permute-start.23 = (f32[512,256]{1,0:T(8,128)S(1)}, f32[512,256]{1,0:T(8,128)S(1)}, u32[]{:S(2)}, u32[]{:S(2)}) collective-permute-start(f32[512,256]{1,0:T(8,128)S(1)} %pad_maximum_fusion.3), channel_id=1, source_target_pairs={{0,4},{1,5},{2,6},{3,7},{4,0},{5,1},{6,2},{7,3},{8,12},{9,13},{10,... | collective-permute-start | bytes 1572872 | tf_op jit(solution)/shard_map/ppermute | solution.py:208
  59.3 17.6 %collective-permute-start.15 = (f32[512,256]{1,0:T(8,128)S(1)}, f32[512,256]{1,0:T(8,128)S(1)}, u32[]{:S(2)}, u32[]{:S(2)}) collective-permute-start(f32[512,256]{1,0:T(8,128)S(1)} %collective-permute-done.11.refs_3_), channel_id=1, source_target_pairs={{0,2},{1,3},{2,0},{3,1},{4,6},{5,7},{6,4},{7,5},{8,10},{9,11},{10,... | collective-permute-start | bytes 1572872 | tf_op jit(solution)/shard_map/ppermute | solution.py:208
  59.3 18.3 %collective-permute-start.14 = (f32[512,256]{1,0:T(8,128)S(1)}, f32[512,256]{1,0:T(8,128)S(1)}, u32[]{:S(2)}, u32[]{:S(2)}) collective-permute-start(f32[512,256]{1,0:T(8,128)S(1)} %collective-permute-done.10.refs_2_), channel_id=1, source_target_pairs={{0,2},{1,3},{2,0},{3,1},{4,6},{5,7},{6,4},{7,5},{8,10},{9,11},{10,... | collective-permute-start | bytes 1572872 | tf_op jit(solution)/shard_map/ppermute | solution.py:208
  59.8 18.5 %collective-permute-start.16 = (f32[512,256]{1,0:T(8,128)}, f32[512,256]{1,0:T(8,128)S(1)}, u32[]{:S(2)}, u32[]{:S(2)}) collective-permute-start(f32[512,256]{1,0:T(8,128)} %collective-permute-done.12.refs_4_), channel_id=1, source_target_pairs={{0,2},{1,3},{2,0},{3,1},{4,6},{5,7},{6,4},{7,5},{8,10},{9,11},{10,... | collective-permute-start | bytes 1572872 | tf_op jit(solution)/shard_map/ppermute | solution.py:208
  70.5 11.3 %collective-permute-start.24 = (f32[512,256]{1,0:T(8,128)S(1)}, f32[512,256]{1,0:T(8,128)S(1)}, u32[]{:S(2)}, u32[]{:S(2)}) collective-permute-start(f32[512,256]{1,0:T(8,128)S(1)} %collective-permute-done.21.refs_1_), channel_id=1, source_target_pairs={{0,2},{1,3},{2,0},{3,1},{4,6},{5,7},{6,4},{7,5},{8,10},{9,11},{10,... | collective-permute-start | bytes 1572872 | tf_op jit(solution)/shard_map/ppermute | solution.py:208
  71.9 9.8 %collective-permute-start.25 = (f32[512,256]{1,0:T(8,128)S(1)}, f32[512,256]{1,0:T(8,128)S(1)}, u32[]{:S(2)}, u32[]{:S(2)}) collective-permute-start(f32[512,256]{1,0:T(8,128)S(1)} %collective-permute-done.23.refs_2_), channel_id=1, source_target_pairs={{0,2},{1,3},{2,0},{3,1},{4,6},{5,7},{6,4},{7,5},{8,10},{9,11},{10,... | collective-permute-start | bytes 1572872 | tf_op jit(solution)/shard_map/ppermute | solution.py:208
  76.9 14.6 %collective-permute-start.1 = (f32[256,256]{1,0:T(8,128)}, f32[256,256]{1,0:T(8,128)S(1)}, u32[]{:S(2)}, u32[]{:S(2)}) collective-permute-start(f32[256,256]{1,0:T(8,128)} %get-tuple-element.17), channel_id=1, source_target_pairs={{1,5},{3,7},{5,1},{7,3},{9,13},{11,15},{13,9},{15,11},{16,20},{18,... | collective-permute-start | bytes 786440 | tf_op jit(solution)/shard_map/ppermute | solution.py:208
  77.6 15.6 %collective-permute-start.2 = (f32[256,256]{1,0:T(8,128)}, f32[256,256]{1,0:T(8,128)S(1)}, u32[]{:S(2)}, u32[]{:S(2)}) collective-permute-start(f32[256,256]{1,0:T(8,128)} %get-tuple-element.16), channel_id=1, source_target_pairs={{1,9},{3,11},{5,13},{7,15},{9,1},{11,3},{13,5},{15,7},{16,24},{18,... | collective-permute-start | bytes 786440 | tf_op jit(solution)/shard_map/ppermute | solution.py:208
  81.7 36.2 %copy-start.2 = (s32[1,16]{1,0:T(1,128)S(1)}, s32[1,16]{1,0:T(1,128)}, u32[]{:S(2)}) copy-start(s32[1,16]{1,0:T(1,128)} %param.14) | copy-start | bytes 196
  85.7 9.3 %collective-permute-start.30 = (f32[256,256]{1,0:T(8,128)S(1)}, f32[256,256]{1,0:T(8,128)S(1)}, u32[]{:S(2)}, u32[]{:S(2)}) collective-permute-start(f32[256,256]{1,0:T(8,128)S(1)} %pad_maximum_fusion.4), channel_id=1, source_target_pairs={{0,2},{1,3},{2,0},{3,1},{4,6},{5,7},{6,4},{7,5},{8,10},{9,11},{10,... | collective-permute-start | bytes 786440 | tf_op jit(solution)/shard_map/ppermute | solution.py:208
  92.5 10.3 %collective-permute-start.6 = (f32[512,256]{1,0:T(8,128)S(1)}, f32[512,256]{1,0:T(8,128)S(1)}, u32[]{:S(2)}, u32[]{:S(2)}) collective-permute-start(f32[512,256]{1,0:T(8,128)S(1)} %pad_maximum_fusion), channel_id=1, source_target_pairs={{1,9},{3,11},{5,13},{7,15},{9,1},{11,3},{13,5},{15,7},{16,24},{18,... | collective-permute-start | bytes 1572872 | tf_op jit(solution)/shard_map/ppermute | solution.py:208
  94.2 9.9 %collective-permute-start.7 = (f32[512,256]{1,0:T(8,128)S(1)}, f32[512,256]{1,0:T(8,128)S(1)}, u32[]{:S(2)}, u32[]{:S(2)}) collective-permute-start(f32[512,256]{1,0:T(8,128)S(1)} %pad_maximum_fusion.1), channel_id=1, source_target_pairs={{1,5},{3,7},{5,1},{7,3},{9,13},{11,15},{13,9},{15,11},{16,20},{18,... | collective-permute-start | bytes 1572872 | tf_op jit(solution)/shard_map/ppermute | solution.py:208
  94.9 22.5 %collective-permute-start.4 = (f32[256,256]{1,0:T(8,128)S(1)}, f32[256,256]{1,0:T(8,128)S(1)}, u32[]{:S(2)}, u32[]{:S(2)}) collective-permute-start(f32[256,256]{1,0:T(8,128)S(1)} %collective-permute-done.1.refs_2_), channel_id=1, source_target_pairs={{0,2},{1,3},{2,0},{3,1},{4,6},{5,7},{6,4},{7,5},{8,10},{9,11},{10,... | collective-permute-start | bytes 786440 | tf_op jit(solution)/shard_map/ppermute | solution.py:208
  95.1 10.5 %collective-permute-start.32 = (f32[64,256]{1,0:T(8,128)S(1)}, f32[64,256]{1,0:T(8,128)S(1)}, u32[]{:S(2)}, u32[]{:S(2)}) collective-permute-start(f32[64,256]{1,0:T(8,128)S(1)} %get-tuple-element.24), channel_id=1, source_target_pairs={{0,1},{1,0},{2,3},{3,2},{4,5},{5,4},{6,7},{7,6},{8,9},{9,8},{10,11... | collective-permute-start | bytes 196616 | tf_op jit(solution)/shard_map/ppermute | solution.py:208
  102.4 13.7 %collective-permute-start.33 = (f32[64,256]{1,0:T(8,128)S(1)}, f32[64,256]{1,0:T(8,128)S(1)}, u32[]{:S(2)}, u32[]{:S(2)}) collective-permute-start(f32[64,256]{1,0:T(8,128)S(1)} %get-tuple-element.25), channel_id=1, source_target_pairs={{0,5},{1,4},{2,7},{3,6},{4,1},{5,0},{6,3},{7,2},{8,13},{9,12},{10,... | collective-permute-start | bytes 196616 | tf_op jit(solution)/shard_map/ppermute | solution.py:208
  102.8 13.3 %collective-permute-start.31 = (f32[64,256]{1,0:T(8,128)S(1)}, f32[64,256]{1,0:T(8,128)S(1)}, u32[]{:S(2)}, u32[]{:S(2)}) collective-permute-start(f32[64,256]{1,0:T(8,128)S(1)} %slice_select_fusion.4), channel_id=1, source_target_pairs={{0,4},{1,5},{2,6},{3,7},{4,0},{5,1},{6,2},{7,3},{8,12},{9,13},{10,... | collective-permute-start | bytes 196616 | tf_op jit(solution)/shard_map/ppermute | solution.py:208
  104.1 28.1 %collective-permute-start.3 = (f32[512,256]{1,0:T(8,128)S(1)}, f32[512,256]{1,0:T(8,128)S(1)}, u32[]{:S(2)}, u32[]{:S(2)}) collective-permute-start(f32[512,256]{1,0:T(8,128)S(1)} %collective-permute-done.refs_1_), channel_id=1, source_target_pairs={{0,2},{1,3},{2,0},{3,1},{4,6},{5,7},{6,4},{7,5},{8,10},{9,11},{10,... | collective-permute-start | bytes 1572872 | tf_op jit(solution)/shard_map/ppermute | solution.py:208
  105.6 26.6 %collective-permute-start.8 = (f32[512,256]{1,0:T(8,128)S(1)}, f32[512,256]{1,0:T(8,128)S(1)}, u32[]{:S(2)}, u32[]{:S(2)}) collective-permute-start(f32[512,256]{1,0:T(8,128)S(1)} %collective-permute-done.6.refs_7_), channel_id=1, source_target_pairs={{0,2},{1,3},{2,0},{3,1},{4,6},{5,7},{6,4},{7,5},{8,10},{9,11},{10,... | collective-permute-start | bytes 1572872 | tf_op jit(solution)/shard_map/ppermute | solution.py:208
  116.1 16.1 %collective-permute-start.9 = (f32[512,256]{1,0:T(8,128)S(1)}, f32[512,256]{1,0:T(8,128)S(1)}, u32[]{:S(2)}, u32[]{:S(2)}) collective-permute-start(f32[512,256]{1,0:T(8,128)S(1)} %collective-permute-done.7.refs_8_), channel_id=1, source_target_pairs={{0,2},{1,3},{2,0},{3,1},{4,6},{5,7},{6,4},{7,5},{8,10},{9,11},{10,... | collective-permute-start | bytes 1572872 | tf_op jit(solution)/shard_map/ppermute | solution.py:208
  116.1 28.5 %copy-start.1 = (f32[256,256]{1,0:T(8,128)S(1)}, f32[256,256]{1,0:T(8,128)}, u32[]{:S(2)}) copy-start(f32[256,256]{1,0:T(8,128)} %param.15) | copy-start | bytes 786436
  116.1 4.6 %collective-permute-start.34 = (f32[64,256]{1,0:T(8,128)S(1)}, f32[64,256]{1,0:T(8,128)S(1)}, u32[]{:S(2)}, u32[]{:S(2)}) collective-permute-start(f32[64,256]{1,0:T(8,128)S(1)} %add_add_fusion.1), channel_id=1, source_target_pairs={{0,8},{1,9},{2,10},{3,11},{4,12},{5,13},{6,14},{7,15},{8,0},{9,1},... | collective-permute-start | bytes 196616 | tf_op jit(solution)/shard_map/ppermute | solution.py:208
  117.4 6.5 %collective-permute-start.35 = (f32[64,256]{1,0:T(8,128)S(1)}, f32[64,256]{1,0:T(8,128)S(1)}, u32[]{:S(2)}, u32[]{:S(2)}) collective-permute-start(f32[64,256]{1,0:T(8,128)S(1)} %add_add_fusion.1), channel_id=1, source_target_pairs={{0,16},{1,17},{2,18},{3,19},{4,20},{5,21},{6,22},{7,23},{8,24},{9,... | collective-permute-start | bytes 196616 | tf_op jit(solution)/shard_map/ppermute | solution.py:208
  120.7 9.9 %collective-permute-start.5 = (f32[256,256]{1,0:T(8,128)S(1)}, f32[256,256]{1,0:T(8,128)S(1)}, u32[]{:S(2)}, u32[]{:S(2)}) collective-permute-start(f32[256,256]{1,0:T(8,128)S(1)} %collective-permute-done.2.refs_3_), channel_id=1, source_target_pairs={{0,2},{1,3},{2,0},{3,1},{4,6},{5,7},{6,4},{7,5},{8,10},{9,11},{10,... | collective-permute-start | bytes 786440 | tf_op jit(solution)/shard_map/ppermute | solution.py:208
  123.9 6.1 %collective-permute-start.36 = (f32[64,256]{1,0:T(8,128)S(1)}, f32[64,256]{1,0:T(8,128)S(1)}, u32[]{:S(2)}, u32[]{:S(2)}) collective-permute-start(f32[64,256]{1,0:T(8,128)S(1)} %add_add_fusion.1), channel_id=1, source_target_pairs={{0,24},{1,25},{2,26},{3,27},{4,28},{5,29},{6,30},{7,31},{8,16},{9,... | collective-permute-start | bytes 196616 | tf_op jit(solution)/shard_map/ppermute | solution.py:208
  130.0 12.6 %collective-permute-start.29 = (f32[512,256]{1,0:T(8,128)}, f32[512,256]{1,0:T(8,128)S(1)}, u32[]{:S(2)}, u32[]{:S(2)}) collective-permute-start(f32[512,256]{1,0:T(8,128)} %get-tuple-element.7), channel_id=1, source_target_pairs={{0,1},{1,0},{2,3},{3,2},{4,5},{5,4},{6,7},{7,6},{8,9},{9,8},{10,11... | collective-permute-start | bytes 1572872 | tf_op jit(solution)/shard_map/ppermute | solution.py:208
  130.6 4.5 %collective-permute-start.37 = (f32[64,256]{1,0:T(8,128)S(1)}, f32[64,256]{1,0:T(8,128)S(1)}, u32[]{:S(2)}, u32[]{:S(2)}) collective-permute-start(f32[64,256]{1,0:T(8,128)S(1)} %add_add_fusion), channel_id=1, source_target_pairs={{0,4},{1,5},{2,6},{3,7},{4,0},{5,1},{6,2},{7,3},{8,12},{9,13},{10,... | collective-permute-start | bytes 196616 | tf_op jit(solution)/shard_map/ppermute | solution.py:208
  135.1 9.5 %collective-permute-start.38 = (f32[128,256]{1,0:T(8,128)S(1)}, f32[128,256]{1,0:T(8,128)S(1)}, u32[]{:S(2)}, u32[]{:S(2)}) collective-permute-start(f32[128,256]{1,0:T(8,128)S(1)} %pad_maximum_fusion.5), channel_id=1, source_target_pairs={{0,2},{1,3},{2,0},{3,1},{4,6},{5,7},{6,4},{7,5},{8,10},{9,11},{10,... | collective-permute-start | bytes 393224 | tf_op jit(solution)/shard_map/ppermute | solution.py:208

commit v4 on v3

--- a/solution.py
+++ b/solution.py
@@ -213,9 +213,8 @@
         ids = jnp.concatenate([block + col * 2 * FAR, row * 2 + jnp.arange(2, dtype=jnp.int32)])
         on = jnp.any(ids[:, None] == listed[0][None, :], axis=1)
         count = len(order)
-        if who is not None:
-            on = on & ((jnp.arange(count + 2) >= count) | (near == who))
-        far = jnp.logical_not(near) if who is None else jnp.zeros((), jnp.bool_)
+        on = on & ((jnp.arange(count + 2) >= count) | (near == who))
+        far = jnp.logical_not(near) & jnp.bool_(order == SECOND)
         return jnp.concatenate([block, on.astype(jnp.int32), far.astype(jnp.int32)[None]])
 
     def step_one(q, who):
@@ -228,20 +227,25 @@
     def with_sibling(arrays, who):
         return list(arrays) + [move(v, CORE, 0, who) for v in arrays]
 
-    other_structure = move(structure, 0, 1)
+    in_hbm = lambda v: pltpu.with_memory_space_constraint(v, pltpu.HBM)
+    n_z = move(lower_panel, Z, 0, True)
+    n_x = move(lower_panel, X, 0, True)
     got_far = move(lower_panel, FAR, 1, False)
     lower_other = move(lower_panel, 0, 1)
-    n_z = move(lower_panel, Z, 0, True)
-    n_x = move(lower_panel, X, 0, True)
     q_far = move(lower_panel, FAR, 0, True)
+    other_structure = move(structure, 0, 1)
+    m_x = move(lower_other, X, 0, True)
+    m_z = move(lower_other, Z, 0, True)
     n_zx = move(n_z, X, 0, True)
+    m_xz = move(m_x, Z, 0, True)
     n_all = with_sibling([lower_panel, n_x, n_z, n_zx], None)
-    in_hbm = lambda v: pltpu.with_memory_space_constraint(v, pltpu.HBM)
     n_all[0] = in_hbm(lower_panel)
-    q_other = jnp.where(near, lower_other, got_far)
-    o_one = step_one(q_other, None)
-    o_two = step_two(q_other, o_one, None)
-    o_first = with_sibling([q_other, *o_one], None)
+    m_all = with_sibling([lower_other, m_x, m_z], None)
+    m_xzs = move(m_xz, CORE, 0, None)
+    m_all = m_all[:3] + [m_xz] + m_all[3:] + [m_xzs]
+    o_one = step_one(got_far, False)
+    o_two = step_two(got_far, o_one, False)
+    o_first = with_sibling([got_far, *o_one], None)
     o_second = with_sibling(o_two, None)
     f_one = step_one(q_far, False)
     f_two = step_two(q_far, f_one, False)
@@ -251,9 +255,13 @@
     own, own_terms = product(
         table(structure, WHOLE, True), inverse_anc, n_all, SLOTSW, width, extra=n_all[0]
     )
-    (part,) = product(table(other_structure, FIRST, None), inverse_anc, o_first, SLOTS1, width)
+    (part,) = product(table(other_structure, WHOLE, True), inverse_anc, m_all, SLOTSW, width)
+    (part,) = product(
+        table(other_structure, FIRST, False), inverse_anc, o_first, SLOTS1, width,
+        acc=in_hbm(part),
+    )
     part, other_terms = product(
-        table(other_structure, SECOND, None), inverse_anc, o_second, SLOTS2, width,
+        table(other_structure, SECOND, False), inverse_anc, o_second, SLOTS2, width,
         acc=in_hbm(part), extra=lower_other,
     )
     recv = move(part, 0, 1)

time: 146 us -> 152 us (1.041)
  waiting for transfers between devices: 51.1 us -> 54.2 us
  Pallas kernels: 14.3 us -> 17 us
    ppermute x39 -> x46, waiting for transfers between devices: 51.1 us -> 54.2 us  [move(): return lax.ppermute(value, BOTH, pairs)]
    pallas_call x4 -> x5, Pallas kernels: 14.3 us -> 17 us  [product(): pl.pallas_call(functools.partial(product_kernel, slots, blocks, width, ac...]
    ppermute x39 -> x46, starting transfers between devices: 67.3 us -> 68.8 us  [move(): return lax.ppermute(value, BOTH, pairs)]
  transfers between devices with their start and end apart: 39 -> 46, of which waited for: 10 -> 13; matrix products, arithmetic and copies ran while one was open for 7% -> 6% of each run, Pallas kernels for 10% -> 11%
where the time goes in v4:
time: 152 us
  starting transfers between devices  68.8 us (45%)
  waiting for transfers between devices  54.2 us (36%)
  Pallas kernels  17 us (11%)
  other arithmetic  9.61 us (6%)
    ppermute x46, starting transfers between devices, move(): return lax.ppermute(value, BOTH, pairs)  68.8 us
    ppermute x46, waiting for transfers between devices, move(): return lax.ppermute(value, BOTH, pairs)  54.2 us
    pallas_call x5, Pallas kernels, product(): pl.pallas_call(functools.partial(product_kernel, slots, blocks, width, ac...  17 us
  transfers between devices with their start and end apart: 46, of which 13 were waited for; matrix products, arithmetic and copies ran while one was open for 6% of the time, Pallas kernels for 11%

profile of v4, /device:TPU:0, one launch (start us, length us, event | category | flops | bytes accessed | tf_op | source)
XLA Modules:
  0.0 151.7 jit_solution(10252263160890678579)
XLA Ops:
  0.6 3.1 %collective-permute-start.28 = (f32[512,256]{1,0:T(8,128)}, f32[512,256]{1,0:T(8,128)S(1)}, u32[]{:S(2)}, u32[]{:S(2)}) collective-permute-start(f32[512,256]{1,0:T(8,128)} %refs_9_.1), channel_id=1, source_target_pairs={{0,1},{1,0},{2,3},{3,2},{4,5},{5,4},{6,7},{7,6},{8,9},{9,8},{10,11... | collective-permute-start | bytes 1572872 | tf_op jit(solution)/shard_map/ppermute | solution.py:208
  3.7 0.7 collective-permute-start.18
  4.4 3.5 %collective-permute-start.11 = (f32[512,256]{1,0:T(8,128)}, f32[512,256]{1,0:T(8,128)S(1)}, u32[]{:S(2)}, u32[]{:S(2)}) collective-permute-start(f32[512,256]{1,0:T(8,128)} %refs_9_.1), channel_id=1, source_target_pairs={{0,8},{2,10},{4,12},{6,14},{8,0},{10,2},{12,4},{14,6},{17,25},{19,... | collective-permute-start | bytes 1572872 | tf_op jit(solution)/shard_map/ppermute | solution.py:208
  7.9 3.4 %collective-permute-start.10 = (f32[512,256]{1,0:T(8,128)}, f32[512,256]{1,0:T(8,128)S(1)}, u32[]{:S(2)}, u32[]{:S(2)}) collective-permute-start(f32[512,256]{1,0:T(8,128)} %refs_9_.1), channel_id=1, source_target_pairs={{0,4},{2,6},{4,0},{6,2},{8,12},{10,14},{12,8},{14,10},{17,21},{19,... | collective-permute-start | bytes 1572872 | tf_op jit(solution)/shard_map/ppermute | solution.py:208
  11.4 0.7 multiply_add_fusion.2
  12.1 0.7 multiply_add_fusion
  12.8 3.5 %collective-permute-done.17 = s32[1,16]{1,0:T(1,128)S(1)} collective-permute-done((s32[1,16]{1,0:T(1,128)}, s32[1,16]{1,0:T(1,128)S(1)}, u32[]{:S(2)}, u32[]{:S(2)}) %collective-permute-start.17) | collective-permute-done | bytes 96 | tf_op jit(solution)/shard_map/ppermute | solution.py:208
  16.3 15.6 %collective-permute-start = (f32[512,256]{1,0:T(8,128)}, f32[512,256]{1,0:T(8,128)S(1)}, u32[]{:S(2)}, u32[]{:S(2)}) collective-permute-start(f32[512,256]{1,0:T(8,128)} %refs_9_.1), channel_id=1, source_target_pairs={{0,16},{2,18},{4,20},{6,22},{8,24},{10,26},{12,28},{14,30},{17,1},... | collective-permute-start | bytes 1572872 | tf_op jit(solution)/shard_map/ppermute | solution.py:208
  32.1 0.7 compare_reduce_fusion.1
  32.8 3.4 %collective-permute-start.29 = (f32[512,256]{1,0:T(8,128)S(1)}, f32[512,256]{1,0:T(8,128)S(1)}, u32[]{:S(2)}, u32[]{:S(2)}) collective-permute-start(f32[512,256]{1,0:T(8,128)S(1)} %collective-permute-done.28.refs_1_.refs_6_), channel_id=1, source_target_pairs={{0,4},{2,6},{4,0},{6,2},{8,12},{10,14},{12,8},{14,10},{17,21},{19,... | collective-permute-start | bytes 1572872 | tf_op jit(solution)/shard_map/ppermute | solution.py:208
  36.3 0.7 collective-permute-start.19
  37.0 0.7 collective-permute-start.21
  37.7 1.9 %collective-permute-start.30 = (f32[512,256]{1,0:T(8,128)S(1)}, f32[512,256]{1,0:T(8,128)S(1)}, u32[]{:S(2)}, u32[]{:S(2)}) collective-permute-start(f32[512,256]{1,0:T(8,128)S(1)} %collective-permute-done.28.refs_1_.refs_6_), channel_id=1, source_target_pairs={{0,8},{2,10},{4,12},{6,14},{8,0},{10,2},{12,4},{14,6},{17,25},{19,... | collective-permute-start | bytes 1572872 | tf_op jit(solution)/shard_map/ppermute | solution.py:208
  39.6 4.9 %collective-permute-done.refs_1_ = f32[512,256]{1,0:T(8,128)S(1)} collective-permute-done((f32[512,256]{1,0:T(8,128)}, f32[512,256]{1,0:T(8,128)S(1)}, u32[]{:S(2)}, u32[]{:S(2)}) %collective-permute-start) | collective-permute-done | bytes 524320 | tf_op jit(solution)/shard_map/ppermute | solution.py:208
  44.6 3.4 %collective-permute-start.12 = (f32[512,256]{1,0:T(8,128)S(1)}, f32[512,256]{1,0:T(8,128)S(1)}, u32[]{:S(2)}, u32[]{:S(2)}) collective-permute-start(f32[512,256]{1,0:T(8,128)S(1)} %collective-permute-done.11.refs_3_), channel_id=1, source_target_pairs={{0,4},{2,6},{4,0},{6,2},{8,12},{10,14},{12,8},{14,10},{17,21},{19,... | collective-permute-start | bytes 1572872 | tf_op jit(solution)/shard_map/ppermute | solution.py:208
  48.0 0.3 collective-permute-start.15
  48.3 0.5 collective-permute-done.29.refs_2_
  48.8 0.2 compare_reduce_fusion.2
  49.0 6.2 %collective-permute-done.30.refs_3_ = f32[512,256]{1,0:T(8,128)S(1)} collective-permute-done((f32[512,256]{1,0:T(8,128)S(1)}, f32[512,256]{1,0:T(8,128)S(1)}, u32[]{:S(2)}, u32[]{:S(2)}) %collective-permute-start.30) | collective-permute-done | bytes 524320 | tf_op jit(solution)/shard_map/ppermute | solution.py:208
  55.2 0.7 collective-permute-start.20
  55.9 4.4 %collective-permute-start.31 = (f32[512,256]{1,0:T(8,128)S(1)}, f32[512,256]{1,0:T(8,128)S(1)}, u32[]{:S(2)}, u32[]{:S(2)}) collective-permute-start(f32[512,256]{1,0:T(8,128)S(1)} %collective-permute-done.29.refs_2_), channel_id=1, source_target_pairs={{0,8},{2,10},{4,12},{6,14},{8,0},{10,2},{12,4},{14,6},{17,25},{19,... | collective-permute-start | bytes 1572872 | tf_op jit(solution)/shard_map/ppermute | solution.py:208
  60.4 0.4 collective-permute-done.12.refs_4_
  60.8 0.7 collective-permute-start.22
  61.6 0.5 collective-permute-start.16
  62.2 0.2 collective-permute-start.34
  62.3 9.9 %collective-permute-done.31.refs_4_ = f32[512,256]{1,0:T(8,128)S(1)} collective-permute-done((f32[512,256]{1,0:T(8,128)S(1)}, f32[512,256]{1,0:T(8,128)S(1)}, u32[]{:S(2)}, u32[]{:S(2)}) %collective-permute-start.31) | collective-permute-done | bytes 524320 | tf_op jit(solution)/shard_map/ppermute | solution.py:208
  72.4 0.5 collective-permute-start.25
  72.9 0.1 collective-permute-start.23
  73.0 0.4 collective-permute-start.24
  73.4 0.8 fusion.4
  74.2 3.1 %shard_map.152 = (f32[512,256]{1,0:T(8,128)}, f32[256,256]{1,0:T(8,128)S(1)}) custom-call(s32[35]{0:T(128)S(1)} %get-tuple-element.36.table, f32[512,4096]{1,0:T(8,128)} %refs_0_.9, f32[512,256]{1,0:T(8,128)} %refs_9_.1, f32[512,256]{1,0:T(8,128)S(1)} %collective-permute-done.10.refs_2_, f32[512,256]{1,0:T(8,128)S(1)} %collective-permute-done.11.refs_3_, ...), custom_call_target="tpu_custom_call" | custom-call | flops 805306368 | bytes 4194304 | tf_op jit(solution)/shard_map/pallas_call | solution.py:154
  77.4 4.1 %collective-permute-start.26 = (f32[256,256]{1,0:T(8,128)S(1)}, f32[256,256]{1,0:T(8,128)S(1)}, u32[]{:S(2)}, u32[]{:S(2)}) collective-permute-start(f32[256,256]{1,0:T(8,128)S(1)} %collective-permute-done.19.refs_2_), channel_id=1, source_target_pairs={{0,2},{1,3},{2,0},{3,1},{4,6},{5,7},{6,4},{7,5},{8,10},{9,11},{10,... | collective-permute-start | bytes 786440 | tf_op jit(solution)/shard_map/ppermute | solution.py:208
  81.5 0.1 collective-permute-start.27
  81.6 5.4 %shard_map.154.refs_7_ = f32[512,256]{1,0:T(8,128)} custom-call(s32[35]{0:T(128)S(1)} %get-tuple-element.35.table, f32[512,4096]{1,0:T(8,128)} %refs_0_.9, f32[512,256]{1,0:T(8,128)S(1)} %collective-permute-done.28.refs_1_.refs_6_, f32[512,256]{1,0:T(8,128)S(1)} %collective-permute-done.29.refs_2_, f32[512,256]{1,0:T(8,128)S(1)} %collective-permute-done.30.refs_3_, ...), custom_call_target="tpu_custom_call" | custom-call | flops 805306368 | bytes 4194304 | tf_op jit(solution)/shard_map/pallas_call | solution.py:154
  87.1 0.7 collective-permute-start.1
  87.8 0.7 collective-permute-start.2
  88.5 2.6 %shard_map.155.refs_5_ = f32[512,256]{1,0:T(8,128)} custom-call(s32[19]{0:T(128)S(1)} %pad_add_fusion.8.table, f32[512,4096]{1,0:T(8,128)} %refs_0_.9, f32[512,256]{1,0:T(8,128)S(1)} %collective-permute-done.18.refs_1_, f32[256,256]{1,0:T(8,128)S(1)} %collective-permute-done.19.refs_2_, f32[256,256]{1,0:T(8,128)S(1)} %collective-permute-done.21.refs_3_, ...), custom_call_target="tpu_custom_call" | custom-call | flops 402653184 | bytes 2097152 | tf_op jit(solution)/shard_map/pallas_call | solution.py:154
  91.2 2.9 %shard_map.156 = (f32[512,256]{1,0:T(8,128)}, f32[256,256]{1,0:T(8,128)S(1)}) custom-call(s32[19]{0:T(128)S(1)} %pad_add_fusion.6.table, f32[512,4096]{1,0:T(8,128)} %refs_0_.9, f32[512,256]{1,0:T(8,128)S(1)} %collective-permute-done.20.refs_1_, f32[512,256]{1,0:T(8,128)S(1)} %collective-permute-done.22.refs_2_, ...), custom_call_target="tpu_custom_call" | custom-call | flops 402653184 | bytes 2097152 | tf_op jit(solution)/shard_map/pallas_call | solution.py:154
  94.1 0.7 pad_maximum_fusion.4
  94.9 1.7 %collective-permute-start.37 = (f32[256,256]{1,0:T(8,128)}, f32[256,256]{1,0:T(8,128)}, u32[]{:S(2)}, u32[]{:S(2)}) collective-permute-start(f32[256,256]{1,0:T(8,128)} %pad_maximum_fusion.4), channel_id=1, source_target_pairs={{0,2},{1,3},{2,0},{3,1},{4,6},{5,7},{6,4},{7,5},{8,10},{9,11},{10,... | collective-permute-start | bytes 786440 | tf_op jit(solution)/shard_map/ppermute | solution.py:208
  96.6 1.0 pad_maximum_fusion
  97.6 0.7 collective-permute-start.6
  98.3 1.0 pad_maximum_fusion.1
  99.3 0.7 collective-permute-start.7
  100.1 1.0 slice_add_fusion.1
  101.1 7.0 %collective-permute-start.39 = (f32[64,256]{1,0:T(8,128)S(1)}, f32[64,256]{1,0:T(8,128)S(1)}, u32[]{:S(2)}, u32[]{:S(2)}) collective-permute-start(f32[64,256]{1,0:T(8,128)S(1)} %get-tuple-element.25), channel_id=1, source_target_pairs={{0,1},{1,0},{2,3},{3,2},{4,5},{5,4},{6,7},{7,6},{8,9},{9,8},{10,11... | collective-permute-start | bytes 196616 | tf_op jit(solution)/shard_map/ppermute | solution.py:208
  108.1 1.5 %collective-permute-start.40 = (f32[64,256]{1,0:T(8,128)S(1)}, f32[64,256]{1,0:T(8,128)S(1)}, u32[]{:S(2)}, u32[]{:S(2)}) collective-permute-start(f32[64,256]{1,0:T(8,128)S(1)} %get-tuple-element.26), channel_id=1, source_target_pairs={{0,5},{1,4},{2,7},{3,6},{4,1},{5,0},{6,3},{7,2},{8,13},{9,12},{10,... | collective-permute-start | bytes 196616 | tf_op jit(solution)/shard_map/ppermute | solution.py:208
  109.6 0.6 collective-permute-start.38
  110.2 0.1 compare_reduce_fusion
  110.4 0.5 collective-permute-done.39
  110.9 11.1 %collective-permute-done.40 = f32[64,256]{1,0:T(8,128)S(1)} collective-permute-done((f32[64,256]{1,0:T(8,128)S(1)}, f32[64,256]{1,0:T(8,128)S(1)}, u32[]{:S(2)}, u32[]{:S(2)}) %collective-permute-start.40) | collective-permute-done | bytes 65568 | tf_op jit(solution)/shard_map/ppermute | solution.py:208
  122.0 1.5 collective-permute-start.41
  123.5 1.7 %collective-permute-start.42 = (f32[64,256]{1,0:T(8,128)S(1)}, f32[64,256]{1,0:T(8,128)S(1)}, u32[]{:S(2)}, u32[]{:S(2)}) collective-permute-start(f32[64,256]{1,0:T(8,128)S(1)} %add_add_fusion.1), channel_id=1, source_target_pairs={{0,16},{1,17},{2,18},{3,19},{4,20},{5,21},{6,22},{7,23},{8,24},{9,... | collective-permute-start | bytes 196616 | tf_op jit(solution)/shard_map/ppermute | solution.py:208
  125.1 1.4 collective-permute-done.41
  126.6 3.4 %collective-permute-done.42 = f32[64,256]{1,0:T(8,128)S(1)} collective-permute-done((f32[64,256]{1,0:T(8,128)S(1)}, f32[64,256]{1,0:T(8,128)S(1)}, u32[]{:S(2)}, u32[]{:S(2)}) %collective-permute-start.42) | collective-permute-done | bytes 65568 | tf_op jit(solution)/shard_map/ppermute | solution.py:208
  130.0 1.9 %collective-permute-start.43 = (f32[64,256]{1,0:T(8,128)S(1)}, f32[64,256]{1,0:T(8,128)S(1)}, u32[]{:S(2)}, u32[]{:S(2)}) collective-permute-start(f32[64,256]{1,0:T(8,128)S(1)} %add_add_fusion.1), channel_id=1, source_target_pairs={{0,24},{1,25},{2,26},{3,27},{4,28},{5,29},{6,30},{7,31},{8,16},{9,... | collective-permute-start | bytes 196616 | tf_op jit(solution)/shard_map/ppermute | solution.py:208
  132.0 4.1 %collective-permute-done.43 = f32[64,256]{1,0:T(8,128)S(1)} collective-permute-done((f32[64,256]{1,0:T(8,128)S(1)}, f32[64,256]{1,0:T(8,128)S(1)}, u32[]{:S(2)}, u32[]{:S(2)}) %collective-permute-start.43) | collective-permute-done | bytes 65568 | tf_op jit(solution)/shard_map/ppermute | solution.py:208
  136.1 1.2 collective-permute-start.36
  137.3 0.4 collective-permute-start.44
  137.8 2.9 %shard_map.153 = f32[512,256]{1,0:T(8,128)} custom-call(s32[35]{0:T(128)S(1)} %pad_add_fusion.2.table, f32[512,4096]{1,0:T(8,128)} %refs_0_.9, f32[512,256]{1,0:T(8,128)S(1)} %collective-permute-done.refs_1_, f32[256,256]{1,0:T(8,128)S(1)} %collective-permute-done.1.refs_2_, f32[256,256]{1,0:T(8,128)S(1)} %collective-permute-done.2.refs_3_, ...), custom_call_target="tpu_custom_call" | custom-call | flops 805306368 | bytes 4194304 | tf_op jit(solution)/shard_map/pallas_call | solution.py:154
  140.6 1.0 collective-permute-done.44
  141.8 7.1 %collective-permute-done.36 = f32[512,256]{1,0:T(8,128)S(1)} collective-permute-done((f32[512,256]{1,0:T(8,128)}, f32[512,256]{1,0:T(8,128)S(1)}, u32[]{:S(2)}, u32[]{:S(2)}) %collective-permute-start.36) | collective-permute-done | bytes 524320 | tf_op jit(solution)/shard_map/ppermute | solution.py:208
  148.9 2.0 %negate_select_fusion = f32[512,256]{1,0:T(8,128)} fusion(f32[512,256]{1,0:T(8,128)} %shard_map.153, f32[512,256]{1,0:T(8,128)S(1)} %collective-permute-done.36, pred[512]{0:T(512)(128)(4,1)S(1)} %compare_reduce_fusion), kind=kLoop, calls=%fused_computation.4 | loop fusion | flops 393216 | bytes 1573376 | tf_op jit(solution)/shard_map/jit(_where)/select_n | solution.py:273
  150.9 0.7 maximum_add_fusion
  (74 shorter events, 1.3 us)
Async XLA Ops:
  0.6 15.6 %collective-permute-start.28 = (f32[512,256]{1,0:T(8,128)}, f32[512,256]{1,0:T(8,128)S(1)}, u32[]{:S(2)}, u32[]{:S(2)}) collective-permute-start(f32[512,256]{1,0:T(8,128)} %refs_9_.1), channel_id=1, source_target_pairs={{0,1},{1,0},{2,3},{3,2},{4,5},{5,4},{6,7},{7,6},{8,9},{9,8},{10,11... | collective-permute-start | bytes 1572872 | tf_op jit(solution)/shard_map/ppermute | solution.py:208
  3.7 29.1 %collective-permute-start.18 = (f32[512,256]{1,0:T(8,128)}, f32[512,256]{1,0:T(8,128)S(1)}, u32[]{:S(2)}, u32[]{:S(2)}) collective-permute-start(f32[512,256]{1,0:T(8,128)} %refs_9_.1), channel_id=1, source_target_pairs={{1,16},{3,18},{5,20},{7,22},{9,24},{11,26},{13,28},{15,30},{16,1},... | collective-permute-start | bytes 1572872 | tf_op jit(solution)/shard_map/ppermute | solution.py:208
  4.4 31.9 %collective-permute-start.11 = (f32[512,256]{1,0:T(8,128)}, f32[512,256]{1,0:T(8,128)S(1)}, u32[]{:S(2)}, u32[]{:S(2)}) collective-permute-start(f32[512,256]{1,0:T(8,128)} %refs_9_.1), channel_id=1, source_target_pairs={{0,8},{2,10},{4,12},{6,14},{8,0},{10,2},{12,4},{14,6},{17,25},{19,... | collective-permute-start | bytes 1572872 | tf_op jit(solution)/shard_map/ppermute | solution.py:208
  7.9 29.1 %collective-permute-start.10 = (f32[512,256]{1,0:T(8,128)}, f32[512,256]{1,0:T(8,128)S(1)}, u32[]{:S(2)}, u32[]{:S(2)}) collective-permute-start(f32[512,256]{1,0:T(8,128)} %refs_9_.1), channel_id=1, source_target_pairs={{0,4},{2,6},{4,0},{6,2},{8,12},{10,14},{12,8},{14,10},{17,21},{19,... | collective-permute-start | bytes 1572872 | tf_op jit(solution)/shard_map/ppermute | solution.py:208
  11.3 5.0 %collective-permute-start.17 = (s32[1,16]{1,0:T(1,128)}, s32[1,16]{1,0:T(1,128)S(1)}, u32[]{:S(2)}, u32[]{:S(2)}) collective-permute-start(s32[1,16]{1,0:T(1,128)} %param.16), channel_id=1, source_target_pairs={{0,1},{1,0},{2,3},{3,2},{4,5},{5,4},{6,7},{7,6},{8,9},{9,8},{10,11... | collective-permute-start | bytes 200 | tf_op jit(solution)/shard_map/ppermute | solution.py:208
  16.3 21.4 %collective-permute-start.13 = (f32[512,256]{1,0:T(8,128)}, f32[512,256]{1,0:T(8,128)S(1)}, u32[]{:S(2)}, u32[]{:S(2)}) collective-permute-start(f32[512,256]{1,0:T(8,128)} %refs_9_.1), channel_id=1, source_target_pairs={{0,2},{1,3},{2,0},{3,1},{4,6},{5,7},{6,4},{7,5},{8,10},{9,11},{10,... | collective-permute-start | bytes 1572872 | tf_op jit(solution)/shard_map/ppermute | solution.py:208
  16.3 28.3 %collective-permute-start = (f32[512,256]{1,0:T(8,128)}, f32[512,256]{1,0:T(8,128)S(1)}, u32[]{:S(2)}, u32[]{:S(2)}) collective-permute-start(f32[512,256]{1,0:T(8,128)} %refs_9_.1), channel_id=1, source_target_pairs={{0,16},{2,18},{4,20},{6,22},{8,24},{10,26},{12,28},{14,30},{17,1},... | collective-permute-start | bytes 1572872 | tf_op jit(solution)/shard_map/ppermute | solution.py:208
  32.8 15.9 %collective-permute-start.29 = (f32[512,256]{1,0:T(8,128)S(1)}, f32[512,256]{1,0:T(8,128)S(1)}, u32[]{:S(2)}, u32[]{:S(2)}) collective-permute-start(f32[512,256]{1,0:T(8,128)S(1)} %collective-permute-done.28.refs_1_.refs_6_), channel_id=1, source_target_pairs={{0,4},{2,6},{4,0},{6,2},{8,12},{10,14},{12,8},{14,10},{17,21},{19,... | collective-permute-start | bytes 1572872 | tf_op jit(solution)/shard_map/ppermute | solution.py:208
  36.3 8.3 %collective-permute-start.19 = (f32[256,256]{1,0:T(8,128)S(1)}, f32[256,256]{1,0:T(8,128)S(1)}, u32[]{:S(2)}, u32[]{:S(2)}) collective-permute-start(f32[256,256]{1,0:T(8,128)S(1)} %get-tuple-element.16), channel_id=1, source_target_pairs={{1,5},{3,7},{5,1},{7,3},{9,13},{11,15},{13,9},{15,11},{16,20},{18,... | collective-permute-start | bytes 786440 | tf_op jit(solution)/shard_map/ppermute | solution.py:208
  37.0 11.0 %collective-permute-start.21 = (f32[256,256]{1,0:T(8,128)S(1)}, f32[256,256]{1,0:T(8,128)S(1)}, u32[]{:S(2)}, u32[]{:S(2)}) collective-permute-start(f32[256,256]{1,0:T(8,128)S(1)} %get-tuple-element.15), channel_id=1, source_target_pairs={{1,9},{3,11},{5,13},{7,15},{9,1},{11,3},{13,5},{15,7},{16,24},{18,... | collective-permute-start | bytes 786440 | tf_op jit(solution)/shard_map/ppermute | solution.py:208
  37.7 17.5 %collective-permute-start.30 = (f32[512,256]{1,0:T(8,128)S(1)}, f32[512,256]{1,0:T(8,128)S(1)}, u32[]{:S(2)}, u32[]{:S(2)}) collective-permute-start(f32[512,256]{1,0:T(8,128)S(1)} %collective-permute-done.28.refs_1_.refs_6_), channel_id=1, source_target_pairs={{0,8},{2,10},{4,12},{6,14},{8,0},{10,2},{12,4},{14,6},{17,25},{19,... | collective-permute-start | bytes 1572872 | tf_op jit(solution)/shard_map/ppermute | solution.py:208
  44.5 11.4 %collective-permute-start.32 = (f32[512,256]{1,0:T(8,128)S(1)}, f32[512,256]{1,0:T(8,128)S(1)}, u32[]{:S(2)}, u32[]{:S(2)}) collective-permute-start(f32[512,256]{1,0:T(8,128)S(1)} %collective-permute-done.28.refs_1_.refs_6_), channel_id=1, source_target_pairs={{0,2},{1,3},{2,0},{3,1},{4,6},{5,7},{6,4},{7,5},{8,10},{9,11},{10,... | collective-permute-start | bytes 1572872 | tf_op jit(solution)/shard_map/ppermute | solution.py:208
  44.6 16.2 %collective-permute-start.12 = (f32[512,256]{1,0:T(8,128)S(1)}, f32[512,256]{1,0:T(8,128)S(1)}, u32[]{:S(2)}, u32[]{:S(2)}) collective-permute-start(f32[512,256]{1,0:T(8,128)S(1)} %collective-permute-done.11.refs_3_), channel_id=1, source_target_pairs={{0,4},{2,6},{4,0},{6,2},{8,12},{10,14},{12,8},{14,10},{17,21},{19,... | collective-permute-start | bytes 1572872 | tf_op jit(solution)/shard_map/ppermute | solution.py:208
  48.0 13.5 %collective-permute-start.15 = (f32[512,256]{1,0:T(8,128)S(1)}, f32[512,256]{1,0:T(8,128)S(1)}, u32[]{:S(2)}, u32[]{:S(2)}) collective-permute-start(f32[512,256]{1,0:T(8,128)S(1)} %collective-permute-done.11.refs_3_), channel_id=1, source_target_pairs={{0,2},{1,3},{2,0},{3,1},{4,6},{5,7},{6,4},{7,5},{8,10},{9,11},{10,... | collective-permute-start | bytes 1572872 | tf_op jit(solution)/shard_map/ppermute | solution.py:208
  48.8 12.8 %collective-permute-start.14 = (f32[512,256]{1,0:T(8,128)S(1)}, f32[512,256]{1,0:T(8,128)S(1)}, u32[]{:S(2)}, u32[]{:S(2)}) collective-permute-start(f32[512,256]{1,0:T(8,128)S(1)} %collective-permute-done.10.refs_2_), channel_id=1, source_target_pairs={{0,2},{1,3},{2,0},{3,1},{4,6},{5,7},{6,4},{7,5},{8,10},{9,11},{10,... | collective-permute-start | bytes 1572872 | tf_op jit(solution)/shard_map/ppermute | solution.py:208
  55.2 7.0 %collective-permute-start.20 = (f32[512,256]{1,0:T(8,128)S(1)}, f32[512,256]{1,0:T(8,128)S(1)}, u32[]{:S(2)}, u32[]{:S(2)}) collective-permute-start(f32[512,256]{1,0:T(8,128)S(1)} %pad_maximum_fusion.2), channel_id=1, source_target_pairs={{1,9},{3,11},{5,13},{7,15},{9,1},{11,3},{13,5},{15,7},{16,24},{18,... | collective-permute-start | bytes 1572872 | tf_op jit(solution)/shard_map/ppermute | solution.py:208
  55.9 16.3 %collective-permute-start.31 = (f32[512,256]{1,0:T(8,128)S(1)}, f32[512,256]{1,0:T(8,128)S(1)}, u32[]{:S(2)}, u32[]{:S(2)}) collective-permute-start(f32[512,256]{1,0:T(8,128)S(1)} %collective-permute-done.29.refs_2_), channel_id=1, source_target_pairs={{0,8},{2,10},{4,12},{6,14},{8,0},{10,2},{12,4},{14,6},{17,25},{19,... | collective-permute-start | bytes 1572872 | tf_op jit(solution)/shard_map/ppermute | solution.py:208
  60.8 11.6 %collective-permute-start.22 = (f32[512,256]{1,0:T(8,128)S(1)}, f32[512,256]{1,0:T(8,128)S(1)}, u32[]{:S(2)}, u32[]{:S(2)}) collective-permute-start(f32[512,256]{1,0:T(8,128)S(1)} %pad_maximum_fusion.3), channel_id=1, source_target_pairs={{1,5},{3,7},{5,1},{7,3},{9,13},{11,15},{13,9},{15,11},{16,20},{18,... | collective-permute-start | bytes 1572872 | tf_op jit(solution)/shard_map/ppermute | solution.py:208
  61.5 11.4 %collective-permute-start.33 = (f32[512,256]{1,0:T(8,128)S(1)}, f32[512,256]{1,0:T(8,128)S(1)}, u32[]{:S(2)}, u32[]{:S(2)}) collective-permute-start(f32[512,256]{1,0:T(8,128)S(1)} %collective-permute-done.29.refs_2_), channel_id=1, source_target_pairs={{0,2},{1,3},{2,0},{3,1},{4,6},{5,7},{6,4},{7,5},{8,10},{9,11},{10,... | collective-permute-start | bytes 1572872 | tf_op jit(solution)/shard_map/ppermute | solution.py:208
  61.6 11.4 %collective-permute-start.16 = (f32[512,256]{1,0:T(8,128)S(1)}, f32[512,256]{1,0:T(8,128)S(1)}, u32[]{:S(2)}, u32[]{:S(2)}) collective-permute-start(f32[512,256]{1,0:T(8,128)S(1)} %collective-permute-done.12.refs_4_), channel_id=1, source_target_pairs={{0,2},{1,3},{2,0},{3,1},{4,6},{5,7},{6,4},{7,5},{8,10},{9,11},{10,... | collective-permute-start | bytes 1572872 | tf_op jit(solution)/shard_map/ppermute | solution.py:208
  62.2 15.2 %collective-permute-start.34 = (f32[512,256]{1,0:T(8,128)S(1)}, f32[512,256]{1,0:T(8,128)S(1)}, u32[]{:S(2)}, u32[]{:S(2)}) collective-permute-start(f32[512,256]{1,0:T(8,128)S(1)} %collective-permute-done.30.refs_3_), channel_id=1, source_target_pairs={{0,2},{1,3},{2,0},{3,1},{4,6},{5,7},{6,4},{7,5},{8,10},{9,11},{10,... | collective-permute-start | bytes 1572872 | tf_op jit(solution)/shard_map/ppermute | solution.py:208
  72.2 9.3 %collective-permute-start.35 = (f32[512,256]{1,0:T(8,128)S(1)}, f32[512,256]{1,0:T(8,128)S(1)}, u32[]{:S(2)}, u32[]{:S(2)}) collective-permute-start(f32[512,256]{1,0:T(8,128)S(1)} %collective-permute-done.31.refs_4_), channel_id=1, source_target_pairs={{0,2},{1,3},{2,0},{3,1},{4,6},{5,7},{6,4},{7,5},{8,10},{9,11},{10,... | collective-permute-start | bytes 1572872 | tf_op jit(solution)/shard_map/ppermute | solution.py:208
  72.4 16.1 %collective-permute-start.25 = (f32[512,256]{1,0:T(8,128)S(1)}, f32[512,256]{1,0:T(8,128)S(1)}, u32[]{:S(2)}, u32[]{:S(2)}) collective-permute-start(f32[512,256]{1,0:T(8,128)S(1)} %collective-permute-done.18.refs_1_), channel_id=1, source_target_pairs={{0,2},{1,3},{2,0},{3,1},{4,6},{5,7},{6,4},{7,5},{8,10},{9,11},{10,... | collective-permute-start | bytes 1572872 | tf_op jit(solution)/shard_map/ppermute | solution.py:208
  72.9 18.3 %collective-permute-start.23 = (f32[512,256]{1,0:T(8,128)S(1)}, f32[512,256]{1,0:T(8,128)S(1)}, u32[]{:S(2)}, u32[]{:S(2)}) collective-permute-start(f32[512,256]{1,0:T(8,128)S(1)} %collective-permute-done.20.refs_1_), channel_id=1, source_target_pairs={{0,2},{1,3},{2,0},{3,1},{4,6},{5,7},{6,4},{7,5},{8,10},{9,11},{10,... | collective-permute-start | bytes 1572872 | tf_op jit(solution)/shard_map/ppermute | solution.py:208
  73.0 18.2 %collective-permute-start.24 = (f32[512,256]{1,0:T(8,128)S(1)}, f32[512,256]{1,0:T(8,128)S(1)}, u32[]{:S(2)}, u32[]{:S(2)}) collective-permute-start(f32[512,256]{1,0:T(8,128)S(1)} %collective-permute-done.22.refs_2_), channel_id=1, source_target_pairs={{0,2},{1,3},{2,0},{3,1},{4,6},{5,7},{6,4},{7,5},{8,10},{9,11},{10,... | collective-permute-start | bytes 1572872 | tf_op jit(solution)/shard_map/ppermute | solution.py:208
  77.4 9.7 %collective-permute-start.26 = (f32[256,256]{1,0:T(8,128)S(1)}, f32[256,256]{1,0:T(8,128)S(1)}, u32[]{:S(2)}, u32[]{:S(2)}) collective-permute-start(f32[256,256]{1,0:T(8,128)S(1)} %collective-permute-done.19.refs_2_), channel_id=1, source_target_pairs={{0,2},{1,3},{2,0},{3,1},{4,6},{5,7},{6,4},{7,5},{8,10},{9,11},{10,... | collective-permute-start | bytes 786440 | tf_op jit(solution)/shard_map/ppermute | solution.py:208
  81.5 6.2 %collective-permute-start.27 = (f32[256,256]{1,0:T(8,128)S(1)}, f32[256,256]{1,0:T(8,128)S(1)}, u32[]{:S(2)}, u32[]{:S(2)}) collective-permute-start(f32[256,256]{1,0:T(8,128)S(1)} %collective-permute-done.21.refs_3_), channel_id=1, source_target_pairs={{0,2},{1,3},{2,0},{3,1},{4,6},{5,7},{6,4},{7,5},{8,10},{9,11},{10,... | collective-permute-start | bytes 786440 | tf_op jit(solution)/shard_map/ppermute | solution.py:208
  87.1 9.5 %collective-permute-start.1 = (f32[256,256]{1,0:T(8,128)}, f32[256,256]{1,0:T(8,128)S(1)}, u32[]{:S(2)}, u32[]{:S(2)}) collective-permute-start(f32[256,256]{1,0:T(8,128)} %get-tuple-element.18), channel_id=1, source_target_pairs={{1,5},{3,7},{5,1},{7,3},{9,13},{11,15},{13,9},{15,11},{16,20},{18,... | collective-permute-start | bytes 786440 | tf_op jit(solution)/shard_map/ppermute | solution.py:208
  87.8 10.5 %collective-permute-start.2 = (f32[256,256]{1,0:T(8,128)}, f32[256,256]{1,0:T(8,128)S(1)}, u32[]{:S(2)}, u32[]{:S(2)}) collective-permute-start(f32[256,256]{1,0:T(8,128)} %get-tuple-element.17), channel_id=1, source_target_pairs={{1,9},{3,11},{5,13},{7,15},{9,1},{11,3},{13,5},{15,7},{16,24},{18,... | collective-permute-start | bytes 786440 | tf_op jit(solution)/shard_map/ppermute | solution.py:208
  91.1 19.1 %copy-start.1 = (s32[1,16]{1,0:T(1,128)S(1)}, s32[1,16]{1,0:T(1,128)}, u32[]{:S(2)}) copy-start(s32[1,16]{1,0:T(1,128)} %param.16) | copy-start | bytes 196
  94.9 5.2 %collective-permute-start.37 = (f32[256,256]{1,0:T(8,128)}, f32[256,256]{1,0:T(8,128)}, u32[]{:S(2)}, u32[]{:S(2)}) collective-permute-start(f32[256,256]{1,0:T(8,128)} %pad_maximum_fusion.4), channel_id=1, source_target_pairs={{0,2},{1,3},{2,0},{3,1},{4,6},{5,7},{6,4},{7,5},{8,10},{9,11},{10,... | collective-permute-start | bytes 786440 | tf_op jit(solution)/shard_map/ppermute | solution.py:208
  97.6 12.0 %collective-permute-start.6 = (f32[512,256]{1,0:T(8,128)S(1)}, f32[512,256]{1,0:T(8,128)S(1)}, u32[]{:S(2)}, u32[]{:S(2)}) collective-permute-start(f32[512,256]{1,0:T(8,128)S(1)} %pad_maximum_fusion), channel_id=1, source_target_pairs={{1,9},{3,11},{5,13},{7,15},{9,1},{11,3},{13,5},{15,7},{16,24},{18,... | collective-permute-start | bytes 1572872 | tf_op jit(solution)/shard_map/ppermute | solution.py:208
  99.3 11.0 %collective-permute-start.7 = (f32[512,256]{1,0:T(8,128)S(1)}, f32[512,256]{1,0:T(8,128)S(1)}, u32[]{:S(2)}, u32[]{:S(2)}) collective-permute-start(f32[512,256]{1,0:T(8,128)S(1)} %pad_maximum_fusion.1), channel_id=1, source_target_pairs={{1,5},{3,7},{5,1},{7,3},{9,13},{11,15},{13,9},{15,11},{16,20},{18,... | collective-permute-start | bytes 1572872 | tf_op jit(solution)/shard_map/ppermute | solution.py:208
  100.0 23.5 %collective-permute-start.4 = (f32[256,256]{1,0:T(8,128)S(1)}, f32[256,256]{1,0:T(8,128)S(1)}, u32[]{:S(2)}, u32[]{:S(2)}) collective-permute-start(f32[256,256]{1,0:T(8,128)S(1)} %collective-permute-done.1.refs_2_), channel_id=1, source_target_pairs={{0,2},{1,3},{2,0},{3,1},{4,6},{5,7},{6,4},{7,5},{8,10},{9,11},{10,... | collective-permute-start | bytes 786440 | tf_op jit(solution)/shard_map/ppermute | solution.py:208
  101.1 9.7 %collective-permute-start.39 = (f32[64,256]{1,0:T(8,128)S(1)}, f32[64,256]{1,0:T(8,128)S(1)}, u32[]{:S(2)}, u32[]{:S(2)}) collective-permute-start(f32[64,256]{1,0:T(8,128)S(1)} %get-tuple-element.25), channel_id=1, source_target_pairs={{0,1},{1,0},{2,3},{3,2},{4,5},{5,4},{6,7},{7,6},{8,9},{9,8},{10,11... | collective-permute-start | bytes 196616 | tf_op jit(solution)/shard_map/ppermute | solution.py:208
  108.1 13.9 %collective-permute-start.40 = (f32[64,256]{1,0:T(8,128)S(1)}, f32[64,256]{1,0:T(8,128)S(1)}, u32[]{:S(2)}, u32[]{:S(2)}) collective-permute-start(f32[64,256]{1,0:T(8,128)S(1)} %get-tuple-element.26), channel_id=1, source_target_pairs={{0,5},{1,4},{2,7},{3,6},{4,1},{5,0},{6,3},{7,2},{8,13},{9,12},{10,... | collective-permute-start | bytes 196616 | tf_op jit(solution)/shard_map/ppermute | solution.py:208
  109.6 12.3 %collective-permute-start.38 = (f32[64,256]{1,0:T(8,128)S(1)}, f32[64,256]{1,0:T(8,128)S(1)}, u32[]{:S(2)}, u32[]{:S(2)}) collective-permute-start(f32[64,256]{1,0:T(8,128)S(1)} %slice_select_fusion.4), channel_id=1, source_target_pairs={{0,4},{1,5},{2,6},{3,7},{4,0},{5,1},{6,2},{7,3},{8,12},{9,13},{10,... | collective-permute-start | bytes 196616 | tf_op jit(solution)/shard_map/ppermute | solution.py:208
  110.3 27.5 %collective-permute-start.3 = (f32[512,256]{1,0:T(8,128)S(1)}, f32[512,256]{1,0:T(8,128)S(1)}, u32[]{:S(2)}, u32[]{:S(2)}) collective-permute-start(f32[512,256]{1,0:T(8,128)S(1)} %collective-permute-done.refs_1_), channel_id=1, source_target_pairs={{0,2},{1,3},{2,0},{3,1},{4,6},{5,7},{6,4},{7,5},{8,10},{9,11},{10,... | collective-permute-start | bytes 1572872 | tf_op jit(solution)/shard_map/ppermute | solution.py:208
  110.8 26.9 %collective-permute-start.8 = (f32[512,256]{1,0:T(8,128)S(1)}, f32[512,256]{1,0:T(8,128)S(1)}, u32[]{:S(2)}, u32[]{:S(2)}) collective-permute-start(f32[512,256]{1,0:T(8,128)S(1)} %collective-permute-done.6.refs_7_), channel_id=1, source_target_pairs={{0,2},{1,3},{2,0},{3,1},{4,6},{5,7},{6,4},{7,5},{8,10},{9,11},{10,... | collective-permute-start | bytes 1572872 | tf_op jit(solution)/shard_map/ppermute | solution.py:208
  122.0 15.8 %collective-permute-start.9 = (f32[512,256]{1,0:T(8,128)S(1)}, f32[512,256]{1,0:T(8,128)S(1)}, u32[]{:S(2)}, u32[]{:S(2)}) collective-permute-start(f32[512,256]{1,0:T(8,128)S(1)} %collective-permute-done.7.refs_8_), channel_id=1, source_target_pairs={{0,2},{1,3},{2,0},{3,1},{4,6},{5,7},{6,4},{7,5},{8,10},{9,11},{10,... | collective-permute-start | bytes 1572872 | tf_op jit(solution)/shard_map/ppermute | solution.py:208
  122.0 28.9 %copy-start = (f32[256,256]{1,0:T(8,128)S(1)}, f32[256,256]{1,0:T(8,128)}, u32[]{:S(2)}) copy-start(f32[256,256]{1,0:T(8,128)} %param.17) | copy-start | bytes 786436
  122.0 4.6 %collective-permute-start.41 = (f32[64,256]{1,0:T(8,128)S(1)}, f32[64,256]{1,0:T(8,128)S(1)}, u32[]{:S(2)}, u32[]{:S(2)}) collective-permute-start(f32[64,256]{1,0:T(8,128)S(1)} %add_add_fusion.1), channel_id=1, source_target_pairs={{0,8},{1,9},{2,10},{3,11},{4,12},{5,13},{6,14},{7,15},{8,0},{9,1},... | collective-permute-start | bytes 196616 | tf_op jit(solution)/shard_map/ppermute | solution.py:208
  123.5 6.5 %collective-permute-start.42 = (f32[64,256]{1,0:T(8,128)S(1)}, f32[64,256]{1,0:T(8,128)S(1)}, u32[]{:S(2)}, u32[]{:S(2)}) collective-permute-start(f32[64,256]{1,0:T(8,128)S(1)} %add_add_fusion.1), channel_id=1, source_target_pairs={{0,16},{1,17},{2,18},{3,19},{4,20},{5,21},{6,22},{7,23},{8,24},{9,... | collective-permute-start | bytes 196616 | tf_op jit(solution)/shard_map/ppermute | solution.py:208
  126.6 10.8 %collective-permute-start.5 = (f32[256,256]{1,0:T(8,128)S(1)}, f32[256,256]{1,0:T(8,128)S(1)}, u32[]{:S(2)}, u32[]{:S(2)}) collective-permute-start(f32[256,256]{1,0:T(8,128)S(1)} %collective-permute-done.2.refs_3_), channel_id=1, source_target_pairs={{0,2},{1,3},{2,0},{3,1},{4,6},{5,7},{6,4},{7,5},{8,10},{9,11},{10,... | collective-permute-start | bytes 786440 | tf_op jit(solution)/shard_map/ppermute | solution.py:208
  130.0 6.1 %collective-permute-start.43 = (f32[64,256]{1,0:T(8,128)S(1)}, f32[64,256]{1,0:T(8,128)S(1)}, u32[]{:S(2)}, u32[]{:S(2)}) collective-permute-start(f32[64,256]{1,0:T(8,128)S(1)} %add_add_fusion.1), channel_id=1, source_target_pairs={{0,24},{1,25},{2,26},{3,27},{4,28},{5,29},{6,30},{7,31},{8,16},{9,... | collective-permute-start | bytes 196616 | tf_op jit(solution)/shard_map/ppermute | solution.py:208
  136.1 12.8 %collective-permute-start.36 = (f32[512,256]{1,0:T(8,128)}, f32[512,256]{1,0:T(8,128)S(1)}, u32[]{:S(2)}, u32[]{:S(2)}) collective-permute-start(f32[512,256]{1,0:T(8,128)} %get-tuple-element.7), channel_id=1, source_target_pairs={{0,1},{1,0},{2,3},{3,2},{4,5},{5,4},{6,7},{7,6},{8,9},{9,8},{10,11... | collective-permute-start | bytes 1572872 | tf_op jit(solution)/shard_map/ppermute | solution.py:208
  137.3 4.3 %collective-permute-start.44 = (f32[64,256]{1,0:T(8,128)S(1)}, f32[64,256]{1,0:T(8,128)S(1)}, u32[]{:S(2)}, u32[]{:S(2)}) collective-permute-start(f32[64,256]{1,0:T(8,128)S(1)} %add_add_fusion), channel_id=1, source_target_pairs={{0,4},{1,5},{2,6},{3,7},{4,0},{5,1},{6,2},{7,3},{8,12},{9,13},{10,... | collective-permute-start | bytes 196616 | tf_op jit(solution)/shard_map/ppermute | solution.py:208
  141.7 9.2 %collective-permute-start.45 = (f32[128,256]{1,0:T(8,128)S(1)}, f32[128,256]{1,0:T(8,128)S(1)}, u32[]{:S(2)}, u32[]{:S(2)}) collective-permute-start(f32[128,256]{1,0:T(8,128)S(1)} %pad_maximum_fusion.5), channel_id=1, source_target_pairs={{0,2},{1,3},{2,0},{3,1},{4,6},{5,7},{6,4},{7,5},{8,10},{9,11},{10,... | collective-permute-start | bytes 393224 | tf_op jit(solution)/shard_map/ppermute | solution.py:208

commit v5 on v3

--- a/solution.py
+++ b/solution.py
@@ -180,10 +180,8 @@
 CORE, X, Z, FAR = 1, 2, 4, 8
 FIRST = ((0, 0), (0, 1), (X, 0), (Z, 1), (1, 0), (1, 1), (X | 1, 0), (Z | 1, 1))
 SECOND = tuple((m | c, h) for c in (0, 1) for m, h in ((Z, 0), (Z | X, 0), (X, 1), (Z | X, 1)))
-WHOLE = tuple((m | c, h) for c in (0, 1) for m in (0, X, Z, Z | X) for h in (0, 1))
 SLOTS1 = ((0, 0), (0, 1), (1, 0), (2, 0), (3, 0), (3, 1), (4, 0), (5, 0))
 SLOTS2 = ((0, 0), (0, 1), (1, 0), (1, 1), (2, 0), (2, 1), (3, 0), (3, 1))
-SLOTSW = tuple((i, h) for i in range(8) for h in (0, 1))
 SLOTS12 = SLOTS1 + tuple((6 + i, h) for i, h in SLOTS2)
 
 
@@ -231,13 +229,13 @@
     other_structure = move(structure, 0, 1)
     got_far = move(lower_panel, FAR, 1, False)
     lower_other = move(lower_panel, 0, 1)
-    n_z = move(lower_panel, Z, 0, True)
-    n_x = move(lower_panel, X, 0, True)
+    n_one = step_one(lower_panel, True)
     q_far = move(lower_panel, FAR, 0, True)
-    n_zx = move(n_z, X, 0, True)
-    n_all = with_sibling([lower_panel, n_x, n_z, n_zx], None)
+    n_two = step_two(lower_panel, n_one, True)
     in_hbm = lambda v: pltpu.with_memory_space_constraint(v, pltpu.HBM)
-    n_all[0] = in_hbm(lower_panel)
+    n_first = with_sibling([lower_panel, *n_one], None)
+    n_first[0] = in_hbm(lower_panel)
+    n_second = with_sibling(n_two, None)
     q_other = jnp.where(near, lower_other, got_far)
     o_one = step_one(q_other, None)
     o_two = step_two(q_other, o_one, None)
@@ -249,7 +247,8 @@
     f_second = with_sibling(f_two, None)
 
     own, own_terms = product(
-        table(structure, WHOLE, True), inverse_anc, n_all, SLOTSW, width, extra=n_all[0]
+        table(structure, FIRST + SECOND, True), inverse_anc, n_first + n_second, SLOTS12, width,
+        extra=n_first[0],
     )
     (part,) = product(table(other_structure, FIRST, None), inverse_anc, o_first, SLOTS1, width)
     part, other_terms = product(

time: 146 us -> 138 us (0.945)
  starting transfers between devices: 67.3 us -> 51.5 us
  waiting for transfers between devices: 51.1 us -> 55 us
  other arithmetic: 9.89 us -> 12.4 us
  local copies, waits for them, and re-layouts: 1.58 us -> 3.46 us
    ppermute x39 -> x41, starting transfers between devices: 67.3 us -> 51.5 us  [move(): return lax.ppermute(value, BOTH, pairs)]
    ppermute x39 -> x41, waiting for transfers between devices: 51.1 us -> 55 us  [move(): return lax.ppermute(value, BOTH, pairs)]
  transfers between devices with their start and end apart: 39 -> 41, of which waited for: 10 -> 12; matrix products, arithmetic and copies ran while one was open for 7% -> 10% of each run, Pallas kernels for 10% -> 10%
where the time goes in v5:
time: 138 us
  waiting for transfers between devices  55 us (40%)
  starting transfers between devices  51.5 us (37%)
  Pallas kernels  14.2 us (10%)
  other arithmetic  12.4 us (9%)
  local copies, waits for them, and re-layouts  3.46 us (3%)
    ppermute x41, waiting for transfers between devices, move(): return lax.ppermute(value, BOTH, pairs)  55 us
    ppermute x41, starting transfers between devices, move(): return lax.ppermute(value, BOTH, pairs)  51.5 us
    pallas_call x4, Pallas kernels, product(): pl.pallas_call(functools.partial(product_kernel, slots, blocks, width, ac...  14.2 us
    concatenate x3, other arithmetic, step_two(): jnp.concatenate([q[:half], one[0]])  2.84 us
    concatenate x3, other arithmetic, step_two(): jnp.concatenate([q[half:], one[1]])  2.83 us
  transfers between devices with their start and end apart: 41, of which 12 were waited for; matrix products, arithmetic and copies ran while one was open for 10% of the time, Pallas kernels for 10%

profile of v5, /device:TPU:0, one launch (start us, length us, event | category | flops | bytes accessed | tf_op | source)
XLA Modules:
  0.0 137.7 jit_solution(6958033987443628664)
XLA Ops:
  0.6 3.1 %collective-permute-start.20 = (f32[512,256]{1,0:T(8,128)}, f32[512,256]{1,0:T(8,128)S(1)}, u32[]{:S(2)}, u32[]{:S(2)}) collective-permute-start(f32[512,256]{1,0:T(8,128)} %refs_11_.1), channel_id=1, source_target_pairs={{0,1},{1,0},{2,3},{3,2},{4,5},{5,4},{6,7},{7,6},{8,9},{9,8},{10,11... | collective-permute-start | bytes 1572872 | tf_op jit(solution)/shard_map/ppermute | solution.py:206
  3.7 1.5 %collective-permute-start.21 = (f32[512,256]{1,0:T(8,128)}, f32[512,256]{1,0:T(8,128)}, u32[]{:S(2)}, u32[]{:S(2)}) collective-permute-start(f32[512,256]{1,0:T(8,128)} %refs_11_.1), channel_id=1, source_target_pairs={{1,16},{3,18},{5,20},{7,22},{9,24},{11,26},{13,28},{15,30},{16,1},... | collective-permute-start | bytes 1572872 | tf_op jit(solution)/shard_map/ppermute | solution.py:206
  5.1 5.0 %collective-permute-start = (f32[512,256]{1,0:T(8,128)}, f32[512,256]{1,0:T(8,128)S(1)}, u32[]{:S(2)}, u32[]{:S(2)}) collective-permute-start(f32[512,256]{1,0:T(8,128)} %refs_11_.1), channel_id=1, source_target_pairs={{0,16},{2,18},{4,20},{6,22},{8,24},{10,26},{12,28},{14,30},{17,1},... | collective-permute-start | bytes 1572872 | tf_op jit(solution)/shard_map/ppermute | solution.py:206
  10.1 1.1 fusion.4
  11.2 3.7 %collective-permute-start.10 = (f32[256,256]{1,0:T(8,128)S(1)}, f32[256,256]{1,0:T(8,128)S(1)}, u32[]{:S(2)}, u32[]{:S(2)}) collective-permute-start(f32[256,256]{1,0:T(8,128)S(1)} %get-tuple-element.15), channel_id=1, source_target_pairs={{0,4},{2,6},{4,0},{6,2},{8,12},{10,14},{12,8},{14,10},{17,21},{19,... | collective-permute-start | bytes 786440 | tf_op jit(solution)/shard_map/ppermute | solution.py:206
  14.9 3.5 %collective-permute-start.11 = (f32[256,256]{1,0:T(8,128)S(1)}, f32[256,256]{1,0:T(8,128)S(1)}, u32[]{:S(2)}, u32[]{:S(2)}) collective-permute-start(f32[256,256]{1,0:T(8,128)S(1)} %get-tuple-element.14), channel_id=1, source_target_pairs={{0,8},{2,10},{4,12},{6,14},{8,0},{10,2},{12,4},{14,6},{17,25},{19,... | collective-permute-start | bytes 786440 | tf_op jit(solution)/shard_map/ppermute | solution.py:206
  18.4 0.7 multiply_add_fusion.2
  19.2 0.7 multiply_add_fusion
  19.9 0.7 collective-permute-done.10.refs_2_
  20.6 13.2 %collective-permute-done.11.refs_3_ = f32[256,256]{1,0:T(8,128)S(1)} collective-permute-done((f32[256,256]{1,0:T(8,128)S(1)}, f32[256,256]{1,0:T(8,128)S(1)}, u32[]{:S(2)}, u32[]{:S(2)}) %collective-permute-start.11) | collective-permute-done | bytes 262176 | tf_op jit(solution)/shard_map/ppermute | solution.py:206
  33.9 0.5 collective-permute-start.14
  34.4 0.8 fusion.3
  35.3 0.5 collective-permute-start.22
  35.8 0.8 pad_maximum_fusion.2
  36.6 0.9 pad_maximum_fusion.3
  37.5 1.9 %collective-permute-start.15 = (f32[512,256]{1,0:T(8,128)}, f32[512,256]{1,0:T(8,128)S(1)}, u32[]{:S(2)}, u32[]{:S(2)}) collective-permute-start(f32[512,256]{1,0:T(8,128)} %pad_maximum_fusion.2), channel_id=1, source_target_pairs={{0,8},{2,10},{4,12},{6,14},{8,0},{10,2},{12,4},{14,6},{17,25},{19,... | collective-permute-start | bytes 1572872 | tf_op jit(solution)/shard_map/ppermute | solution.py:206
  39.4 3.4 %collective-permute-start.16 = (f32[512,256]{1,0:T(8,128)}, f32[512,256]{1,0:T(8,128)}, u32[]{:S(2)}, u32[]{:S(2)}) collective-permute-start(f32[512,256]{1,0:T(8,128)} %pad_maximum_fusion.3), channel_id=1, source_target_pairs={{0,4},{2,6},{4,0},{6,2},{8,12},{10,14},{12,8},{14,10},{17,21},{19,... | collective-permute-start | bytes 1572872 | tf_op jit(solution)/shard_map/ppermute | solution.py:206
  42.8 0.7 compare_reduce_fusion.3
  43.6 0.7 copy-done
  44.3 2.0 %collective-permute-start.24 = (f32[256,256]{1,0:T(8,128)}, f32[256,256]{1,0:T(8,128)S(1)}, u32[]{:S(2)}, u32[]{:S(2)}) collective-permute-start(f32[256,256]{1,0:T(8,128)} %get-tuple-element.12), channel_id=1, source_target_pairs={{0,8},{1,9},{2,10},{3,11},{4,12},{5,13},{6,14},{7,15},{8,0},{9,1},... | collective-permute-start | bytes 786440 | tf_op jit(solution)/shard_map/ppermute | solution.py:206
  46.3 1.0 pad_maximum_fusion.4
  47.4 0.3 collective-permute-start.29
  47.7 11.1 %collective-permute-done.24.refs_3_ = f32[256,256]{1,0:T(8,128)S(1)} collective-permute-done((f32[256,256]{1,0:T(8,128)}, f32[256,256]{1,0:T(8,128)S(1)}, u32[]{:S(2)}, u32[]{:S(2)}) %collective-permute-start.24) | collective-permute-done | bytes 262176 | tf_op jit(solution)/shard_map/ppermute | solution.py:206
  58.8 1.0 pad_maximum_fusion.5
  59.8 0.4 collective-permute-start.23
  60.1 1.5 %collective-permute-start.25 = (f32[512,256]{1,0:T(8,128)S(1)}, f32[512,256]{1,0:T(8,128)S(1)}, u32[]{:S(2)}, u32[]{:S(2)}) collective-permute-start(f32[512,256]{1,0:T(8,128)S(1)} %pad_maximum_fusion.5), channel_id=1, source_target_pairs={{0,4},{1,5},{2,6},{3,7},{4,0},{5,1},{6,2},{7,3},{8,12},{9,13},{10,... | collective-permute-start | bytes 1572872 | tf_op jit(solution)/shard_map/ppermute | solution.py:206
  61.8 0.5 collective-permute-start.17
  62.3 0.1 collective-permute-start.18
  62.4 0.2 compare_reduce_fusion.1
  62.6 0.1 add_add_fusion.3.table
  62.8 11.4 %collective-permute-done.23.refs_1_ = f32[512,256]{1,0:T(8,128)S(1)} collective-permute-done((f32[512,256]{1,0:T(8,128)S(1)}, f32[512,256]{1,0:T(8,128)S(1)}, u32[]{:S(2)}, u32[]{:S(2)}) %collective-permute-start.23) | collective-permute-done | bytes 524320 | tf_op jit(solution)/shard_map/ppermute | solution.py:206
  74.2 0.1 collective-permute-done.25.refs_2_
  74.3 0.4 collective-permute-start.27
  74.7 0.8 fusion.5
  75.5 4.2 %shard_map.136.refs_5_ = f32[512,256]{1,0:T(8,128)} custom-call(s32[19]{0:T(128)S(1)} %add_add_fusion.3.table, f32[512,4096]{1,0:T(8,128)} %refs_0_.7, f32[512,256]{1,0:T(8,128)S(1)} %broadcast_select_fusion.refs_1_, f32[256,256]{1,0:T(8,128)S(1)} %collective-permute-done.22.refs_2_, f32[256,256]{1,0:T(8,128)S(1)} %collective-permute-done.24.refs_3_, ...), custom_call_target="tpu_custom_call" | custom-call | flops 402653184 | bytes 2097152 | tf_op jit(solution)/shard_map/pallas_call | solution.py:154
  79.7 0.7 collective-permute-start.1
  80.4 0.7 collective-permute-start.2
  81.1 3.2 %shard_map.134 = (f32[512,256]{1,0:T(8,128)}, f32[256,256]{1,0:T(8,128)S(1)}) custom-call(s32[35]{0:T(128)S(1)} %get-tuple-element.34.table, f32[512,4096]{1,0:T(8,128)} %refs_0_.7, f32[512,256]{1,0:T(8,128)} %refs_11_.1, f32[256,256]{1,0:T(8,128)S(1)} %collective-permute-done.10.refs_2_, f32[256,256]{1,0:T(8,128)S(1)} %collective-permute-done.11.refs_3_, ...), custom_call_target="tpu_custom_call" | custom-call | flops 805306368 | bytes 4194304 | tf_op jit(solution)/shard_map/pallas_call | solution.py:154
  84.4 4.0 %shard_map.137 = (f32[512,256]{1,0:T(8,128)}, f32[256,256]{1,0:T(8,128)S(1)}) custom-call(s32[19]{0:T(128)S(1)} %add_add_fusion.2.table, f32[512,4096]{1,0:T(8,128)} %refs_0_.7, f32[512,256]{1,0:T(8,128)S(1)} %collective-permute-done.23.refs_1_, f32[512,256]{1,0:T(8,128)S(1)} %collective-permute-done.25.refs_2_, ...), custom_call_target="tpu_custom_call" | custom-call | flops 402653184 | bytes 2097152 | tf_op jit(solution)/shard_map/pallas_call | solution.py:154
  88.4 5.5 %collective-permute-start.32 = (f32[256,256]{1,0:T(8,128)S(1)}, f32[256,256]{1,0:T(8,128)}, u32[]{:S(2)}, u32[]{:S(2)}) collective-permute-start(f32[256,256]{1,0:T(8,128)S(1)} %pad_maximum_fusion.6), channel_id=1, source_target_pairs={{0,2},{1,3},{2,0},{3,1},{4,6},{5,7},{6,4},{7,5},{8,10},{9,11},{10,... | collective-permute-start | bytes 786440 | tf_op jit(solution)/shard_map/ppermute | solution.py:206
  93.9 1.0 pad_maximum_fusion
  94.9 0.7 collective-permute-start.6
  95.6 1.0 pad_maximum_fusion.1
  96.6 0.7 collective-permute-start.7
  97.3 1.0 slice_add_fusion.1
  98.5 1.6 %collective-permute-start.35 = (f32[64,256]{1,0:T(8,128)S(1)}, f32[64,256]{1,0:T(8,128)S(1)}, u32[]{:S(2)}, u32[]{:S(2)}) collective-permute-start(f32[64,256]{1,0:T(8,128)S(1)} %get-tuple-element.25), channel_id=1, source_target_pairs={{0,5},{1,4},{2,7},{3,6},{4,1},{5,0},{6,3},{7,2},{8,13},{9,12},{10,... | collective-permute-start | bytes 196616 | tf_op jit(solution)/shard_map/ppermute | solution.py:206
  100.1 1.9 %collective-permute-start.33 = (f32[64,256]{1,0:T(8,128)S(1)}, f32[64,256]{1,0:T(8,128)S(1)}, u32[]{:S(2)}, u32[]{:S(2)}) collective-permute-start(f32[64,256]{1,0:T(8,128)S(1)} %slice_select_fusion.4), channel_id=1, source_target_pairs={{0,4},{1,5},{2,6},{3,7},{4,0},{5,1},{6,2},{7,3},{8,12},{9,13},{10,... | collective-permute-start | bytes 196616 | tf_op jit(solution)/shard_map/ppermute | solution.py:206
  102.0 0.5 collective-permute-start.3
  102.5 0.2 collective-permute-done.34
  102.7 5.7 %collective-permute-done.35 = f32[64,256]{1,0:T(8,128)S(1)} collective-permute-done((f32[64,256]{1,0:T(8,128)S(1)}, f32[64,256]{1,0:T(8,128)S(1)}, u32[]{:S(2)}, u32[]{:S(2)}) %collective-permute-start.35) | collective-permute-done | bytes 65568 | tf_op jit(solution)/shard_map/ppermute | solution.py:206
  108.5 0.4 collective-permute-start.36
  108.9 3.8 %collective-permute-start.37 = (f32[64,256]{1,0:T(8,128)S(1)}, f32[64,256]{1,0:T(8,128)S(1)}, u32[]{:S(2)}, u32[]{:S(2)}) collective-permute-start(f32[64,256]{1,0:T(8,128)S(1)} %add_add_fusion.1), channel_id=1, source_target_pairs={{0,16},{1,17},{2,18},{3,19},{4,20},{5,21},{6,22},{7,23},{8,24},{9,... | collective-permute-start | bytes 196616 | tf_op jit(solution)/shard_map/ppermute | solution.py:206
  112.6 1.1 collective-permute-done.36
  113.8 1.7 %collective-permute-done.37 = f32[64,256]{1,0:T(8,128)S(1)} collective-permute-done((f32[64,256]{1,0:T(8,128)S(1)}, f32[64,256]{1,0:T(8,128)S(1)}, u32[]{:S(2)}, u32[]{:S(2)}) %collective-permute-start.37) | collective-permute-done | bytes 65568 | tf_op jit(solution)/shard_map/ppermute | solution.py:206
  115.5 3.9 %collective-permute-start.38 = (f32[64,256]{1,0:T(8,128)S(1)}, f32[64,256]{1,0:T(8,128)S(1)}, u32[]{:S(2)}, u32[]{:S(2)}) collective-permute-start(f32[64,256]{1,0:T(8,128)S(1)} %add_add_fusion.1), channel_id=1, source_target_pairs={{0,24},{1,25},{2,26},{3,27},{4,28},{5,29},{6,30},{7,31},{8,16},{9,... | collective-permute-start | bytes 196616 | tf_op jit(solution)/shard_map/ppermute | solution.py:206
  119.4 0.1 compare_reduce_fusion
  119.5 2.2 %collective-permute-done.38 = f32[64,256]{1,0:T(8,128)S(1)} collective-permute-done((f32[64,256]{1,0:T(8,128)S(1)}, f32[64,256]{1,0:T(8,128)S(1)}, u32[]{:S(2)}, u32[]{:S(2)}) %collective-permute-start.38) | collective-permute-done | bytes 65568 | tf_op jit(solution)/shard_map/ppermute | solution.py:206
  121.7 1.6 %collective-permute-start.31 = (f32[512,256]{1,0:T(8,128)}, f32[512,256]{1,0:T(8,128)S(1)}, u32[]{:S(2)}, u32[]{:S(2)}) collective-permute-start(f32[512,256]{1,0:T(8,128)} %get-tuple-element.7), channel_id=1, source_target_pairs={{0,1},{1,0},{2,3},{3,2},{4,5},{5,4},{6,7},{7,6},{8,9},{9,8},{10,11... | collective-permute-start | bytes 1572872 | tf_op jit(solution)/shard_map/ppermute | solution.py:206
  123.3 1.3 collective-permute-start.39
  124.6 2.9 %shard_map.135 = f32[512,256]{1,0:T(8,128)} custom-call(s32[35]{0:T(128)S(1)} %get-tuple-element.35.table, f32[512,4096]{1,0:T(8,128)} %refs_0_.7, f32[512,256]{1,0:T(8,128)S(1)} %collective-permute-done.refs_1_, f32[256,256]{1,0:T(8,128)S(1)} %collective-permute-done.1.refs_2_, f32[256,256]{1,0:T(8,128)S(1)} %collective-permute-done.2.refs_3_, ...), custom_call_target="tpu_custom_call" | custom-call | flops 805306368 | bytes 4194304 | tf_op jit(solution)/shard_map/pallas_call | solution.py:154
  127.5 0.2 collective-permute-done.39
  127.8 7.2 %collective-permute-done.31 = f32[512,256]{1,0:T(8,128)S(1)} collective-permute-done((f32[512,256]{1,0:T(8,128)}, f32[512,256]{1,0:T(8,128)S(1)}, u32[]{:S(2)}, u32[]{:S(2)}) %collective-permute-start.31) | collective-permute-done | bytes 524320 | tf_op jit(solution)/shard_map/ppermute | solution.py:206
  135.0 2.0 %negate_select_fusion = f32[512,256]{1,0:T(8,128)} fusion(f32[512,256]{1,0:T(8,128)} %shard_map.135, f32[512,256]{1,0:T(8,128)S(1)} %collective-permute-done.31, pred[512]{0:T(512)(128)(4,1)S(1)} %compare_reduce_fusion), kind=kLoop, calls=%fused_computation.6 | loop fusion | flops 393216 | bytes 1573376 | tf_op jit(solution)/shard_map/jit(_where)/select_n | solution.py:264
  137.0 0.7 maximum_add_fusion
  (68 shorter events, 0.8 us)
Async XLA Ops:
  0.6 33.2 %collective-permute-start.20 = (f32[512,256]{1,0:T(8,128)}, f32[512,256]{1,0:T(8,128)S(1)}, u32[]{:S(2)}, u32[]{:S(2)}) collective-permute-start(f32[512,256]{1,0:T(8,128)} %refs_11_.1), channel_id=1, source_target_pairs={{0,1},{1,0},{2,3},{3,2},{4,5},{5,4},{6,7},{7,6},{8,9},{9,8},{10,11... | collective-permute-start | bytes 1572872 | tf_op jit(solution)/shard_map/ppermute | solution.py:206
  3.7 30.7 %collective-permute-start.21 = (f32[512,256]{1,0:T(8,128)}, f32[512,256]{1,0:T(8,128)}, u32[]{:S(2)}, u32[]{:S(2)}) collective-permute-start(f32[512,256]{1,0:T(8,128)} %refs_11_.1), channel_id=1, source_target_pairs={{1,16},{3,18},{5,20},{7,22},{9,24},{11,26},{13,28},{15,30},{16,1},... | collective-permute-start | bytes 1572872 | tf_op jit(solution)/shard_map/ppermute | solution.py:206
  5.1 42.2 %collective-permute-start = (f32[512,256]{1,0:T(8,128)}, f32[512,256]{1,0:T(8,128)S(1)}, u32[]{:S(2)}, u32[]{:S(2)}) collective-permute-start(f32[512,256]{1,0:T(8,128)} %refs_11_.1), channel_id=1, source_target_pairs={{0,16},{2,18},{4,20},{6,22},{8,24},{10,26},{12,28},{14,30},{17,1},... | collective-permute-start | bytes 1572872 | tf_op jit(solution)/shard_map/ppermute | solution.py:206
  11.2 9.4 %collective-permute-start.10 = (f32[256,256]{1,0:T(8,128)S(1)}, f32[256,256]{1,0:T(8,128)S(1)}, u32[]{:S(2)}, u32[]{:S(2)}) collective-permute-start(f32[256,256]{1,0:T(8,128)S(1)} %get-tuple-element.15), channel_id=1, source_target_pairs={{0,4},{2,6},{4,0},{6,2},{8,12},{10,14},{12,8},{14,10},{17,21},{19,... | collective-permute-start | bytes 786440 | tf_op jit(solution)/shard_map/ppermute | solution.py:206
  14.9 19.0 %collective-permute-start.11 = (f32[256,256]{1,0:T(8,128)S(1)}, f32[256,256]{1,0:T(8,128)S(1)}, u32[]{:S(2)}, u32[]{:S(2)}) collective-permute-start(f32[256,256]{1,0:T(8,128)S(1)} %get-tuple-element.14), channel_id=1, source_target_pairs={{0,8},{2,10},{4,12},{6,14},{8,0},{10,2},{12,4},{14,6},{17,25},{19,... | collective-permute-start | bytes 786440 | tf_op jit(solution)/shard_map/ppermute | solution.py:206
  20.6 16.9 %collective-permute-start.19 = (s32[1,16]{1,0:T(1,128)}, s32[1,16]{1,0:T(1,128)S(1)}, u32[]{:S(2)}, u32[]{:S(2)}) collective-permute-start(s32[1,16]{1,0:T(1,128)} %param.14), channel_id=1, source_target_pairs={{0,1},{1,0},{2,3},{3,2},{4,5},{5,4},{6,7},{7,6},{8,9},{9,8},{10,11... | collective-permute-start | bytes 200 | tf_op jit(solution)/shard_map/ppermute | solution.py:206
  33.8 5.6 %collective-permute-start.13 = (f32[256,256]{1,0:T(8,128)S(1)}, f32[256,256]{1,0:T(8,128)S(1)}, u32[]{:S(2)}, u32[]{:S(2)}) collective-permute-start(f32[256,256]{1,0:T(8,128)S(1)} %collective-permute-done.10.refs_2_), channel_id=1, source_target_pairs={{0,2},{1,3},{2,0},{3,1},{4,6},{5,7},{6,4},{7,5},{8,10},{9,11},{10,... | collective-permute-start | bytes 786440 | tf_op jit(solution)/shard_map/ppermute | solution.py:206
  33.9 9.7 %collective-permute-start.14 = (f32[256,256]{1,0:T(8,128)S(1)}, f32[256,256]{1,0:T(8,128)S(1)}, u32[]{:S(2)}, u32[]{:S(2)}) collective-permute-start(f32[256,256]{1,0:T(8,128)S(1)} %collective-permute-done.11.refs_3_), channel_id=1, source_target_pairs={{0,2},{1,3},{2,0},{3,1},{4,6},{5,7},{6,4},{7,5},{8,10},{9,11},{10,... | collective-permute-start | bytes 786440 | tf_op jit(solution)/shard_map/ppermute | solution.py:206
  35.3 9.0 %collective-permute-start.22 = (f32[256,256]{1,0:T(8,128)}, f32[256,256]{1,0:T(8,128)S(1)}, u32[]{:S(2)}, u32[]{:S(2)}) collective-permute-start(f32[256,256]{1,0:T(8,128)} %get-tuple-element.13), channel_id=1, source_target_pairs={{0,4},{1,5},{2,6},{3,7},{4,0},{5,1},{6,2},{7,3},{8,12},{9,13},{10,... | collective-permute-start | bytes 786440 | tf_op jit(solution)/shard_map/ppermute | solution.py:206
  37.5 22.3 %collective-permute-start.15 = (f32[512,256]{1,0:T(8,128)}, f32[512,256]{1,0:T(8,128)S(1)}, u32[]{:S(2)}, u32[]{:S(2)}) collective-permute-start(f32[512,256]{1,0:T(8,128)} %pad_maximum_fusion.2), channel_id=1, source_target_pairs={{0,8},{2,10},{4,12},{6,14},{8,0},{10,2},{12,4},{14,6},{17,25},{19,... | collective-permute-start | bytes 1572872 | tf_op jit(solution)/shard_map/ppermute | solution.py:206
  39.4 20.7 %collective-permute-start.16 = (f32[512,256]{1,0:T(8,128)}, f32[512,256]{1,0:T(8,128)}, u32[]{:S(2)}, u32[]{:S(2)}) collective-permute-start(f32[512,256]{1,0:T(8,128)} %pad_maximum_fusion.3), channel_id=1, source_target_pairs={{0,4},{2,6},{4,0},{6,2},{8,12},{10,14},{12,8},{14,10},{17,21},{19,... | collective-permute-start | bytes 1572872 | tf_op jit(solution)/shard_map/ppermute | solution.py:206
  43.6 0.7 copy-start
  44.3 18.0 %collective-permute-start.28 = (f32[512,256]{1,0:T(8,128)S(1)}, f32[512,256]{1,0:T(8,128)}, u32[]{:S(2)}, u32[]{:S(2)}) collective-permute-start(f32[512,256]{1,0:T(8,128)S(1)} %broadcast_select_fusion.refs_1_), channel_id=1, source_target_pairs={{0,2},{1,3},{2,0},{3,1},{4,6},{5,7},{6,4},{7,5},{8,10},{9,11},{10,... | collective-permute-start | bytes 1572872 | tf_op jit(solution)/shard_map/ppermute | solution.py:206
  44.3 14.5 %collective-permute-start.24 = (f32[256,256]{1,0:T(8,128)}, f32[256,256]{1,0:T(8,128)S(1)}, u32[]{:S(2)}, u32[]{:S(2)}) collective-permute-start(f32[256,256]{1,0:T(8,128)} %get-tuple-element.12), channel_id=1, source_target_pairs={{0,8},{1,9},{2,10},{3,11},{4,12},{5,13},{6,14},{7,15},{8,0},{9,1},... | collective-permute-start | bytes 786440 | tf_op jit(solution)/shard_map/ppermute | solution.py:206
  46.3 34.8 %copy-start.1 = (f32[256,256]{1,0:T(8,128)S(1)}, f32[256,256]{1,0:T(8,128)}, u32[]{:S(2)}) copy-start(f32[256,256]{1,0:T(8,128)} %copy-done) | copy-start | bytes 786436
  47.4 14.4 %collective-permute-start.29 = (f32[256,256]{1,0:T(8,128)S(1)}, f32[256,256]{1,0:T(8,128)S(1)}, u32[]{:S(2)}, u32[]{:S(2)}) collective-permute-start(f32[256,256]{1,0:T(8,128)S(1)} %collective-permute-done.22.refs_2_), channel_id=1, source_target_pairs={{0,2},{1,3},{2,0},{3,1},{4,6},{5,7},{6,4},{7,5},{8,10},{9,11},{10,... | collective-permute-start | bytes 786440 | tf_op jit(solution)/shard_map/ppermute | solution.py:206
  58.8 3.0 %collective-permute-start.30 = (f32[256,256]{1,0:T(8,128)S(1)}, f32[256,256]{1,0:T(8,128)S(1)}, u32[]{:S(2)}, u32[]{:S(2)}) collective-permute-start(f32[256,256]{1,0:T(8,128)S(1)} %collective-permute-done.24.refs_3_), channel_id=1, source_target_pairs={{0,2},{1,3},{2,0},{3,1},{4,6},{5,7},{6,4},{7,5},{8,10},{9,11},{10,... | collective-permute-start | bytes 786440 | tf_op jit(solution)/shard_map/ppermute | solution.py:206
  59.8 14.4 %collective-permute-start.23 = (f32[512,256]{1,0:T(8,128)S(1)}, f32[512,256]{1,0:T(8,128)S(1)}, u32[]{:S(2)}, u32[]{:S(2)}) collective-permute-start(f32[512,256]{1,0:T(8,128)S(1)} %pad_maximum_fusion.4), channel_id=1, source_target_pairs={{0,8},{1,9},{2,10},{3,11},{4,12},{5,13},{6,14},{7,15},{8,0},{9,1},... | collective-permute-start | bytes 1572872 | tf_op jit(solution)/shard_map/ppermute | solution.py:206
  60.1 14.1 %collective-permute-start.25 = (f32[512,256]{1,0:T(8,128)S(1)}, f32[512,256]{1,0:T(8,128)S(1)}, u32[]{:S(2)}, u32[]{:S(2)}) collective-permute-start(f32[512,256]{1,0:T(8,128)S(1)} %pad_maximum_fusion.5), channel_id=1, source_target_pairs={{0,4},{1,5},{2,6},{3,7},{4,0},{5,1},{6,2},{7,3},{8,12},{9,13},{10,... | collective-permute-start | bytes 1572872 | tf_op jit(solution)/shard_map/ppermute | solution.py:206
  61.8 17.9 %collective-permute-start.12 = (f32[512,256]{1,0:T(8,128)}, f32[512,256]{1,0:T(8,128)S(1)}, u32[]{:S(2)}, u32[]{:S(2)}) collective-permute-start(f32[512,256]{1,0:T(8,128)} %refs_11_.1), channel_id=1, source_target_pairs={{0,2},{1,3},{2,0},{3,1},{4,6},{5,7},{6,4},{7,5},{8,10},{9,11},{10,... | collective-permute-start | bytes 1572872 | tf_op jit(solution)/shard_map/ppermute | solution.py:206
  61.8 18.6 %collective-permute-start.17 = (f32[512,256]{1,0:T(8,128)S(1)}, f32[512,256]{1,0:T(8,128)S(1)}, u32[]{:S(2)}, u32[]{:S(2)}) collective-permute-start(f32[512,256]{1,0:T(8,128)S(1)} %collective-permute-done.15.refs_7_), channel_id=1, source_target_pairs={{0,2},{1,3},{2,0},{3,1},{4,6},{5,7},{6,4},{7,5},{8,10},{9,11},{10,... | collective-permute-start | bytes 1572872 | tf_op jit(solution)/shard_map/ppermute | solution.py:206
  62.3 18.8 %collective-permute-start.18 = (f32[512,256]{1,0:T(8,128)}, f32[512,256]{1,0:T(8,128)S(1)}, u32[]{:S(2)}, u32[]{:S(2)}) collective-permute-start(f32[512,256]{1,0:T(8,128)} %collective-permute-done.16.refs_8_), channel_id=1, source_target_pairs={{0,2},{1,3},{2,0},{3,1},{4,6},{5,7},{6,4},{7,5},{8,10},{9,11},{10,... | collective-permute-start | bytes 1572872 | tf_op jit(solution)/shard_map/ppermute | solution.py:206
  74.2 10.2 %collective-permute-start.26 = (f32[512,256]{1,0:T(8,128)S(1)}, f32[512,256]{1,0:T(8,128)S(1)}, u32[]{:S(2)}, u32[]{:S(2)}) collective-permute-start(f32[512,256]{1,0:T(8,128)S(1)} %collective-permute-done.23.refs_1_), channel_id=1, source_target_pairs={{0,2},{1,3},{2,0},{3,1},{4,6},{5,7},{6,4},{7,5},{8,10},{9,11},{10,... | collective-permute-start | bytes 1572872 | tf_op jit(solution)/shard_map/ppermute | solution.py:206
  74.3 10.1 %collective-permute-start.27 = (f32[512,256]{1,0:T(8,128)S(1)}, f32[512,256]{1,0:T(8,128)S(1)}, u32[]{:S(2)}, u32[]{:S(2)}) collective-permute-start(f32[512,256]{1,0:T(8,128)S(1)} %collective-permute-done.25.refs_2_), channel_id=1, source_target_pairs={{0,2},{1,3},{2,0},{3,1},{4,6},{5,7},{6,4},{7,5},{8,10},{9,11},{10,... | collective-permute-start | bytes 1572872 | tf_op jit(solution)/shard_map/ppermute | solution.py:206
  79.7 14.2 %collective-permute-start.1 = (f32[256,256]{1,0:T(8,128)}, f32[256,256]{1,0:T(8,128)S(1)}, u32[]{:S(2)}, u32[]{:S(2)}) collective-permute-start(f32[256,256]{1,0:T(8,128)} %get-tuple-element.17), channel_id=1, source_target_pairs={{1,5},{3,7},{5,1},{7,3},{9,13},{11,15},{13,9},{15,11},{16,20},{18,... | collective-permute-start | bytes 786440 | tf_op jit(solution)/shard_map/ppermute | solution.py:206
  80.4 15.2 %collective-permute-start.2 = (f32[256,256]{1,0:T(8,128)}, f32[256,256]{1,0:T(8,128)S(1)}, u32[]{:S(2)}, u32[]{:S(2)}) collective-permute-start(f32[256,256]{1,0:T(8,128)} %get-tuple-element.16), channel_id=1, source_target_pairs={{1,9},{3,11},{5,13},{7,15},{9,1},{11,3},{13,5},{15,7},{16,24},{18,... | collective-permute-start | bytes 786440 | tf_op jit(solution)/shard_map/ppermute | solution.py:206
  84.3 35.0 %copy-start.3 = (s32[1,16]{1,0:T(1,128)S(1)}, s32[1,16]{1,0:T(1,128)}, u32[]{:S(2)}) copy-start(s32[1,16]{1,0:T(1,128)} %param.14) | copy-start | bytes 196
  88.4 8.9 %collective-permute-start.32 = (f32[256,256]{1,0:T(8,128)S(1)}, f32[256,256]{1,0:T(8,128)}, u32[]{:S(2)}, u32[]{:S(2)}) collective-permute-start(f32[256,256]{1,0:T(8,128)S(1)} %pad_maximum_fusion.6), channel_id=1, source_target_pairs={{0,2},{1,3},{2,0},{3,1},{4,6},{5,7},{6,4},{7,5},{8,10},{9,11},{10,... | collective-permute-start | bytes 786440 | tf_op jit(solution)/shard_map/ppermute | solution.py:206
  94.9 7.1 %collective-permute-start.6 = (f32[512,256]{1,0:T(8,128)S(1)}, f32[512,256]{1,0:T(8,128)S(1)}, u32[]{:S(2)}, u32[]{:S(2)}) collective-permute-start(f32[512,256]{1,0:T(8,128)S(1)} %pad_maximum_fusion), channel_id=1, source_target_pairs={{1,9},{3,11},{5,13},{7,15},{9,1},{11,3},{13,5},{15,7},{16,24},{18,... | collective-permute-start | bytes 1572872 | tf_op jit(solution)/shard_map/ppermute | solution.py:206
  96.6 5.4 %collective-permute-start.7 = (f32[512,256]{1,0:T(8,128)S(1)}, f32[512,256]{1,0:T(8,128)S(1)}, u32[]{:S(2)}, u32[]{:S(2)}) collective-permute-start(f32[512,256]{1,0:T(8,128)S(1)} %pad_maximum_fusion.1), channel_id=1, source_target_pairs={{1,5},{3,7},{5,1},{7,3},{9,13},{11,15},{13,9},{15,11},{16,20},{18,... | collective-permute-start | bytes 1572872 | tf_op jit(solution)/shard_map/ppermute | solution.py:206
  98.4 4.3 %collective-permute-start.34 = (f32[64,256]{1,0:T(8,128)S(1)}, f32[64,256]{1,0:T(8,128)S(1)}, u32[]{:S(2)}, u32[]{:S(2)}) collective-permute-start(f32[64,256]{1,0:T(8,128)S(1)} %get-tuple-element.24), channel_id=1, source_target_pairs={{0,1},{1,0},{2,3},{3,2},{4,5},{5,4},{6,7},{7,6},{8,9},{9,8},{10,11... | collective-permute-start | bytes 196616 | tf_op jit(solution)/shard_map/ppermute | solution.py:206
  98.5 10.0 %collective-permute-start.35 = (f32[64,256]{1,0:T(8,128)S(1)}, f32[64,256]{1,0:T(8,128)S(1)}, u32[]{:S(2)}, u32[]{:S(2)}) collective-permute-start(f32[64,256]{1,0:T(8,128)S(1)} %get-tuple-element.25), channel_id=1, source_target_pairs={{0,5},{1,4},{2,7},{3,6},{4,1},{5,0},{6,3},{7,2},{8,13},{9,12},{10,... | collective-permute-start | bytes 196616 | tf_op jit(solution)/shard_map/ppermute | solution.py:206
  100.1 8.4 %collective-permute-start.33 = (f32[64,256]{1,0:T(8,128)S(1)}, f32[64,256]{1,0:T(8,128)S(1)}, u32[]{:S(2)}, u32[]{:S(2)}) collective-permute-start(f32[64,256]{1,0:T(8,128)S(1)} %slice_select_fusion.4), channel_id=1, source_target_pairs={{0,4},{1,5},{2,6},{3,7},{4,0},{5,1},{6,2},{7,3},{8,12},{9,13},{10,... | collective-permute-start | bytes 196616 | tf_op jit(solution)/shard_map/ppermute | solution.py:206
  102.0 6.8 %collective-permute-start.4 = (f32[256,256]{1,0:T(8,128)S(1)}, f32[256,256]{1,0:T(8,128)S(1)}, u32[]{:S(2)}, u32[]{:S(2)}) collective-permute-start(f32[256,256]{1,0:T(8,128)S(1)} %collective-permute-done.1.refs_2_), channel_id=1, source_target_pairs={{0,2},{1,3},{2,0},{3,1},{4,6},{5,7},{6,4},{7,5},{8,10},{9,11},{10,... | collective-permute-start | bytes 786440 | tf_op jit(solution)/shard_map/ppermute | solution.py:206
  102.0 22.6 %collective-permute-start.3 = (f32[512,256]{1,0:T(8,128)S(1)}, f32[512,256]{1,0:T(8,128)S(1)}, u32[]{:S(2)}, u32[]{:S(2)}) collective-permute-start(f32[512,256]{1,0:T(8,128)S(1)} %collective-permute-done.refs_1_), channel_id=1, source_target_pairs={{0,2},{1,3},{2,0},{3,1},{4,6},{5,7},{6,4},{7,5},{8,10},{9,11},{10,... | collective-permute-start | bytes 1572872 | tf_op jit(solution)/shard_map/ppermute | solution.py:206
  102.7 21.9 %collective-permute-start.8 = (f32[512,256]{1,0:T(8,128)S(1)}, f32[512,256]{1,0:T(8,128)S(1)}, u32[]{:S(2)}, u32[]{:S(2)}) collective-permute-start(f32[512,256]{1,0:T(8,128)S(1)} %collective-permute-done.6.refs_7_), channel_id=1, source_target_pairs={{0,2},{1,3},{2,0},{3,1},{4,6},{5,7},{6,4},{7,5},{8,10},{9,11},{10,... | collective-permute-start | bytes 1572872 | tf_op jit(solution)/shard_map/ppermute | solution.py:206
  108.5 16.1 %collective-permute-start.9 = (f32[512,256]{1,0:T(8,128)S(1)}, f32[512,256]{1,0:T(8,128)S(1)}, u32[]{:S(2)}, u32[]{:S(2)}) collective-permute-start(f32[512,256]{1,0:T(8,128)S(1)} %collective-permute-done.7.refs_8_), channel_id=1, source_target_pairs={{0,2},{1,3},{2,0},{3,1},{4,6},{5,7},{6,4},{7,5},{8,10},{9,11},{10,... | collective-permute-start | bytes 1572872 | tf_op jit(solution)/shard_map/ppermute | solution.py:206
  108.5 28.5 %copy-start.2 = (f32[256,256]{1,0:T(8,128)S(1)}, f32[256,256]{1,0:T(8,128)}, u32[]{:S(2)}) copy-start(f32[256,256]{1,0:T(8,128)} %param.15) | copy-start | bytes 786436
  108.5 5.3 %collective-permute-start.36 = (f32[64,256]{1,0:T(8,128)S(1)}, f32[64,256]{1,0:T(8,128)S(1)}, u32[]{:S(2)}, u32[]{:S(2)}) collective-permute-start(f32[64,256]{1,0:T(8,128)S(1)} %add_add_fusion.1), channel_id=1, source_target_pairs={{0,8},{1,9},{2,10},{3,11},{4,12},{5,13},{6,14},{7,15},{8,0},{9,1},... | collective-permute-start | bytes 196616 | tf_op jit(solution)/shard_map/ppermute | solution.py:206
  108.9 6.7 %collective-permute-start.37 = (f32[64,256]{1,0:T(8,128)S(1)}, f32[64,256]{1,0:T(8,128)S(1)}, u32[]{:S(2)}, u32[]{:S(2)}) collective-permute-start(f32[64,256]{1,0:T(8,128)S(1)} %add_add_fusion.1), channel_id=1, source_target_pairs={{0,16},{1,17},{2,18},{3,19},{4,20},{5,21},{6,22},{7,23},{8,24},{9,... | collective-permute-start | bytes 196616 | tf_op jit(solution)/shard_map/ppermute | solution.py:206
  113.8 9.5 %collective-permute-start.5 = (f32[256,256]{1,0:T(8,128)S(1)}, f32[256,256]{1,0:T(8,128)S(1)}, u32[]{:S(2)}, u32[]{:S(2)}) collective-permute-start(f32[256,256]{1,0:T(8,128)S(1)} %collective-permute-done.2.refs_3_), channel_id=1, source_target_pairs={{0,2},{1,3},{2,0},{3,1},{4,6},{5,7},{6,4},{7,5},{8,10},{9,11},{10,... | collective-permute-start | bytes 786440 | tf_op jit(solution)/shard_map/ppermute | solution.py:206
  115.5 6.2 %collective-permute-start.38 = (f32[64,256]{1,0:T(8,128)S(1)}, f32[64,256]{1,0:T(8,128)S(1)}, u32[]{:S(2)}, u32[]{:S(2)}) collective-permute-start(f32[64,256]{1,0:T(8,128)S(1)} %add_add_fusion.1), channel_id=1, source_target_pairs={{0,24},{1,25},{2,26},{3,27},{4,28},{5,29},{6,30},{7,31},{8,16},{9,... | collective-permute-start | bytes 196616 | tf_op jit(solution)/shard_map/ppermute | solution.py:206
  121.7 13.3 %collective-permute-start.31 = (f32[512,256]{1,0:T(8,128)}, f32[512,256]{1,0:T(8,128)S(1)}, u32[]{:S(2)}, u32[]{:S(2)}) collective-permute-start(f32[512,256]{1,0:T(8,128)} %get-tuple-element.7), channel_id=1, source_target_pairs={{0,1},{1,0},{2,3},{3,2},{4,5},{5,4},{6,7},{7,6},{8,9},{9,8},{10,11... | collective-permute-start | bytes 1572872 | tf_op jit(solution)/shard_map/ppermute | solution.py:206
  123.3 4.3 %collective-permute-start.39 = (f32[64,256]{1,0:T(8,128)S(1)}, f32[64,256]{1,0:T(8,128)S(1)}, u32[]{:S(2)}, u32[]{:S(2)}) collective-permute-start(f32[64,256]{1,0:T(8,128)S(1)} %add_add_fusion), channel_id=1, source_target_pairs={{0,4},{1,5},{2,6},{3,7},{4,0},{5,1},{6,2},{7,3},{8,12},{9,13},{10,... | collective-permute-start | bytes 196616 | tf_op jit(solution)/shard_map/ppermute | solution.py:206
  127.7 9.2 %collective-permute-start.40 = (f32[128,256]{1,0:T(8,128)S(1)}, f32[128,256]{1,0:T(8,128)S(1)}, u32[]{:S(2)}, u32[]{:S(2)}) collective-permute-start(f32[128,256]{1,0:T(8,128)S(1)} %pad_maximum_fusion.7), channel_id=1, source_target_pairs={{0,2},{1,3},{2,0},{3,1},{4,6},{5,7},{6,4},{7,5},{8,10},{9,11},{10,... | collective-permute-start | bytes 393224 | tf_op jit(solution)/shard_map/ppermute | solution.py:206

commit v6 on v5

--- a/solution.py
+++ b/solution.py
@@ -64,29 +64,33 @@
     all_on = functools.reduce(jnp.logical_and, row_on)
     dot = functools.partial(jnp.dot, preferred_element_type=jnp.float32)
 
+    held = a_buf.shape[0]
+
     def a_copy(p, rb):
         return pltpu.make_async_copy(
             a_hbm.at[pl.ds(rb * width, width), pl.ds(pl.multiple_of(table[p] * width, width), width)],
-            a_buf.at[p, rb],
-            a_sem.at[p, rb],
+            a_buf.at[lax.rem(p, held), rb],
+            a_sem.at[lax.rem(p, held), rb],
         )
 
-    def p_copy(p):
+    def start(p):
         array, at = slots[p]
-        return pltpu.make_async_copy(arrays[array].at[pl.ds(at * width, width), :], p_buf.at[p], p_sem.at[p])
-
-    if has_acc:
-        acc_copy = pltpu.make_async_copy(acc_in, out, one_sem.at[0])
-        acc_copy.start()
-    for p in range(count):
+
         @pl.when(table[count + p] > 0)
-        def _(p=p):
-            p_copy(p).start()
+        def _():
+            pltpu.make_async_copy(
+                arrays[array].at[pl.ds(at * width, width), :], p_buf.at[p % held], p_sem.at[p % held]
+            ).start()
             for rb in range(blocks):
                 @pl.when(row_on[rb])
                 def _(rb=rb):
                     a_copy(p, rb).start()
 
+    if has_acc:
+        acc_copy = pltpu.make_async_copy(acc_in, out, one_sem.at[0])
+        acc_copy.start()
+    for p in range(held):
+        start(p)
     if final:
         extra_copy = pltpu.make_async_copy(extra_in, extra, one_sem.at[1])
         extra_copy.start()
@@ -98,13 +102,14 @@
     def step(p, carry):
         @pl.when(table[count + p] > 0)
         def _():
-            pltpu.make_async_copy(p_buf.at[p], p_buf.at[p], p_sem.at[p]).wait()
-            high, low = split(p_buf[p])
+            slot = lax.rem(p, held)
+            pltpu.make_async_copy(p_buf.at[slot], p_buf.at[slot], p_sem.at[slot]).wait()
+            high, low = split(p_buf[slot])
 
             def add(first, size):
                 for rb in range(first, first + size):
                     a_copy(p, rb).wait()
-                a_high, a_low = split(a_buf[p, first : first + size].reshape(size * width, width))
+                a_high, a_low = split(a_buf[slot, first : first + size].reshape(size * width, width))
                 both = dot(jnp.concatenate([a_high, a_low]), high)
                 total = both[: size * width] + (both[size * width :] + dot(a_high, low))
                 out[pl.ds(first * width, size * width), :] += total
@@ -117,6 +122,11 @@
                 @pl.when(jnp.logical_not(all_on) & row_on[rb])
                 def _(rb=rb):
                     add(rb, 1)
+
+        for later in range(held, count):
+            @pl.when(p == later - held)
+            def _(later=later):
+                start(later)
 
         return carry
 
@@ -140,6 +150,7 @@
     rows = inverse_anc.shape[0]
     blocks = rows // width
     count = len(slots)
+    held = min(count, 8)
     any_spec = pl.BlockSpec(memory_space=pl.ANY)
     vmem = pl.BlockSpec(memory_space=pltpu.VMEM)
     operands = [pltpu.with_memory_space_constraint(inverse_anc, pltpu.HBM), *arrays]
@@ -160,15 +171,15 @@
             in_specs=specs,
             out_specs=[vmem] * len(shapes),
             scratch_shapes=[
-                pltpu.VMEM((count, blocks, width, width), jnp.float32),
-                pltpu.VMEM((count, width, width), jnp.float32),
+                pltpu.VMEM((held, blocks, width, width), jnp.float32),
+                pltpu.VMEM((held, width, width), jnp.float32),
                 pltpu.VMEM((rows, width), jnp.float32),
-                pltpu.SemaphoreType.DMA((count, blocks)),
-                pltpu.SemaphoreType.DMA((count,)),
+                pltpu.SemaphoreType.DMA((held, blocks)),
+                pltpu.SemaphoreType.DMA((held,)),
                 pltpu.SemaphoreType.DMA((2,)),
             ],
         ),
-        compiler_params=pltpu.CompilerParams(vmem_limit_bytes=20 * 1024 * 1024),
+        compiler_params=pltpu.CompilerParams(vmem_limit_bytes=12 * 1024 * 1024),
         cost_estimate=pl.CostEstimate(
             flops=6 * rows * width * width * count // 4,
             bytes_accessed=4 * rows * width * count // 2,
@@ -210,9 +221,8 @@
         block = block + jnp.array([h for _, h in order], jnp.int32)
         ids = jnp.concatenate([block + col * 2 * FAR, row * 2 + jnp.arange(2, dtype=jnp.int32)])
         on = jnp.any(ids[:, None] == listed[0][None, :], axis=1)
-        count = len(order)
         if who is not None:
-            on = on & ((jnp.arange(count + 2) >= count) | (near == who))
+            on = on & (near == who)
         far = jnp.logical_not(near) if who is None else jnp.zeros((), jnp.bool_)
         return jnp.concatenate([block, on.astype(jnp.int32), far.astype(jnp.int32)[None]])
 

time: 138 us -> 137 us (level)
  waiting for transfers between devices: 55 us -> 53.5 us
    ppermute x41, waiting for transfers between devices: 55 us -> 53.5 us  [move(): return lax.ppermute(value, BOTH, pairs)]
  transfers between devices with their start and end apart: 41 -> 41, of which waited for: 12 -> 11; matrix products, arithmetic and copies ran while one was open for 10% -> 11% of each run, Pallas kernels for 10% -> 10%
where the time goes in v6:
time: 137 us; the launch traced here: 136 us
  waiting for transfers between devices  53.5 us (39%)
  starting transfers between devices  51.5 us (38%)
  Pallas kernels  14.3 us (10%)
  other arithmetic  12.4 us (9%)
  local copies, waits for them, and re-layouts  3.46 us (3%)
    ppermute x41, waiting for transfers between devices, move(): return lax.ppermute(value, BOTH, pairs)  53.5 us
    ppermute x41, starting transfers between devices, move(): return lax.ppermute(value, BOTH, pairs)  51.5 us
    pallas_call x4, Pallas kernels, product(): pl.pallas_call(functools.partial(product_kernel, slots, blocks, width, ac...  14.3 us
    concatenate x3, other arithmetic, step_two(): jnp.concatenate([q[:half], one[0]])  2.84 us
    concatenate x3, other arithmetic, step_two(): jnp.concatenate([q[half:], one[1]])  2.83 us
  transfers between devices with their start and end apart: 41, of which 11 were waited for; matrix products, arithmetic and copies ran while one was open for 11% of the time, Pallas kernels for 10%

profile of v6, /device:TPU:0, one launch (start us, length us, event | category | flops | bytes accessed | tf_op | source)
XLA Modules:
  0.0 136.3 jit_solution(16057004425937218061)
XLA Ops:
  0.6 3.1 %collective-permute-start.20 = (f32[512,256]{1,0:T(8,128)}, f32[512,256]{1,0:T(8,128)S(1)}, u32[]{:S(2)}, u32[]{:S(2)}) collective-permute-start(f32[512,256]{1,0:T(8,128)} %refs_11_.1), channel_id=1, source_target_pairs={{0,1},{1,0},{2,3},{3,2},{4,5},{5,4},{6,7},{7,6},{8,9},{9,8},{10,11... | collective-permute-start | bytes 1572872 | tf_op jit(solution)/shard_map/ppermute | solution.py:217
  3.7 1.5 %collective-permute-start.21 = (f32[512,256]{1,0:T(8,128)}, f32[512,256]{1,0:T(8,128)}, u32[]{:S(2)}, u32[]{:S(2)}) collective-permute-start(f32[512,256]{1,0:T(8,128)} %refs_11_.1), channel_id=1, source_target_pairs={{1,16},{3,18},{5,20},{7,22},{9,24},{11,26},{13,28},{15,30},{16,1},... | collective-permute-start | bytes 1572872 | tf_op jit(solution)/shard_map/ppermute | solution.py:217
  5.1 5.0 %collective-permute-start = (f32[512,256]{1,0:T(8,128)}, f32[512,256]{1,0:T(8,128)S(1)}, u32[]{:S(2)}, u32[]{:S(2)}) collective-permute-start(f32[512,256]{1,0:T(8,128)} %refs_11_.1), channel_id=1, source_target_pairs={{0,16},{2,18},{4,20},{6,22},{8,24},{10,26},{12,28},{14,30},{17,1},... | collective-permute-start | bytes 1572872 | tf_op jit(solution)/shard_map/ppermute | solution.py:217
  10.1 1.1 fusion.4
  11.2 3.7 %collective-permute-start.10 = (f32[256,256]{1,0:T(8,128)S(1)}, f32[256,256]{1,0:T(8,128)S(1)}, u32[]{:S(2)}, u32[]{:S(2)}) collective-permute-start(f32[256,256]{1,0:T(8,128)S(1)} %get-tuple-element.15), channel_id=1, source_target_pairs={{0,4},{2,6},{4,0},{6,2},{8,12},{10,14},{12,8},{14,10},{17,21},{19,... | collective-permute-start | bytes 786440 | tf_op jit(solution)/shard_map/ppermute | solution.py:217
  14.9 3.5 %collective-permute-start.11 = (f32[256,256]{1,0:T(8,128)S(1)}, f32[256,256]{1,0:T(8,128)S(1)}, u32[]{:S(2)}, u32[]{:S(2)}) collective-permute-start(f32[256,256]{1,0:T(8,128)S(1)} %get-tuple-element.14), channel_id=1, source_target_pairs={{0,8},{2,10},{4,12},{6,14},{8,0},{10,2},{12,4},{14,6},{17,25},{19,... | collective-permute-start | bytes 786440 | tf_op jit(solution)/shard_map/ppermute | solution.py:217
  18.4 0.7 multiply_add_fusion.2
  19.1 0.1 pad_add_fusion.2
  19.2 0.7 multiply_add_fusion
  19.9 0.7 collective-permute-done.10.refs_2_
  20.6 13.2 %collective-permute-done.11.refs_3_ = f32[256,256]{1,0:T(8,128)S(1)} collective-permute-done((f32[256,256]{1,0:T(8,128)S(1)}, f32[256,256]{1,0:T(8,128)S(1)}, u32[]{:S(2)}, u32[]{:S(2)}) %collective-permute-start.11) | collective-permute-done | bytes 262176 | tf_op jit(solution)/shard_map/ppermute | solution.py:217
  33.9 0.5 collective-permute-start.14
  34.4 0.8 fusion.3
  35.3 0.5 collective-permute-start.22
  35.8 0.8 pad_maximum_fusion.2
  36.6 0.9 pad_maximum_fusion.3
  37.5 1.9 %collective-permute-start.15 = (f32[512,256]{1,0:T(8,128)}, f32[512,256]{1,0:T(8,128)S(1)}, u32[]{:S(2)}, u32[]{:S(2)}) collective-permute-start(f32[512,256]{1,0:T(8,128)} %pad_maximum_fusion.2), channel_id=1, source_target_pairs={{0,8},{2,10},{4,12},{6,14},{8,0},{10,2},{12,4},{14,6},{17,25},{19,... | collective-permute-start | bytes 1572872 | tf_op jit(solution)/shard_map/ppermute | solution.py:217
  39.4 3.4 %collective-permute-start.16 = (f32[512,256]{1,0:T(8,128)}, f32[512,256]{1,0:T(8,128)}, u32[]{:S(2)}, u32[]{:S(2)}) collective-permute-start(f32[512,256]{1,0:T(8,128)} %pad_maximum_fusion.3), channel_id=1, source_target_pairs={{0,4},{2,6},{4,0},{6,2},{8,12},{10,14},{12,8},{14,10},{17,21},{19,... | collective-permute-start | bytes 1572872 | tf_op jit(solution)/shard_map/ppermute | solution.py:217
  42.8 0.7 compare_reduce_fusion.3
  43.6 0.7 copy-done
  44.3 2.0 %collective-permute-start.24 = (f32[256,256]{1,0:T(8,128)}, f32[256,256]{1,0:T(8,128)S(1)}, u32[]{:S(2)}, u32[]{:S(2)}) collective-permute-start(f32[256,256]{1,0:T(8,128)} %get-tuple-element.12), channel_id=1, source_target_pairs={{0,8},{1,9},{2,10},{3,11},{4,12},{5,13},{6,14},{7,15},{8,0},{9,1},... | collective-permute-start | bytes 786440 | tf_op jit(solution)/shard_map/ppermute | solution.py:217
  46.3 1.0 pad_maximum_fusion.4
  47.4 0.3 collective-permute-start.29
  47.7 11.1 %collective-permute-done.24.refs_3_ = f32[256,256]{1,0:T(8,128)S(1)} collective-permute-done((f32[256,256]{1,0:T(8,128)}, f32[256,256]{1,0:T(8,128)S(1)}, u32[]{:S(2)}, u32[]{:S(2)}) %collective-permute-start.24) | collective-permute-done | bytes 262176 | tf_op jit(solution)/shard_map/ppermute | solution.py:217
  58.8 1.0 pad_maximum_fusion.5
  59.8 0.4 collective-permute-start.23
  60.1 1.5 %collective-permute-start.25 = (f32[512,256]{1,0:T(8,128)S(1)}, f32[512,256]{1,0:T(8,128)S(1)}, u32[]{:S(2)}, u32[]{:S(2)}) collective-permute-start(f32[512,256]{1,0:T(8,128)S(1)} %pad_maximum_fusion.5), channel_id=1, source_target_pairs={{0,4},{1,5},{2,6},{3,7},{4,0},{5,1},{6,2},{7,3},{8,12},{9,13},{10,... | collective-permute-start | bytes 1572872 | tf_op jit(solution)/shard_map/ppermute | solution.py:217
  61.8 0.5 collective-permute-start.17
  62.3 0.1 collective-permute-start.18
  62.4 0.2 compare_reduce_fusion.1
  62.6 0.1 add_add_fusion.3.table
  62.8 11.4 %collective-permute-done.23.refs_1_ = f32[512,256]{1,0:T(8,128)S(1)} collective-permute-done((f32[512,256]{1,0:T(8,128)S(1)}, f32[512,256]{1,0:T(8,128)S(1)}, u32[]{:S(2)}, u32[]{:S(2)}) %collective-permute-start.23) | collective-permute-done | bytes 524320 | tf_op jit(solution)/shard_map/ppermute | solution.py:217
  74.2 0.1 collective-permute-done.25.refs_2_
  74.3 0.4 collective-permute-start.27
  74.7 0.8 fusion.5
  75.5 4.2 %shard_map.136.refs_5_ = f32[512,256]{1,0:T(8,128)} custom-call(s32[19]{0:T(128)S(1)} %add_add_fusion.3.table, f32[512,4096]{1,0:T(8,128)} %refs_0_.7, f32[512,256]{1,0:T(8,128)S(1)} %broadcast_select_fusion.refs_1_, f32[256,256]{1,0:T(8,128)S(1)} %collective-permute-done.22.refs_2_, f32[256,256]{1,0:T(8,128)S(1)} %collective-permute-done.24.refs_3_, ...), custom_call_target="tpu_custom_call" | custom-call | flops 402653184 | bytes 2097152 | tf_op jit(solution)/shard_map/pallas_call | solution.py:165
  79.7 0.7 collective-permute-start.1
  80.4 0.7 collective-permute-start.2
  81.1 3.5 %shard_map.134 = (f32[512,256]{1,0:T(8,128)}, f32[256,256]{1,0:T(8,128)S(1)}) custom-call(s32[35]{0:T(128)S(1)} %get-tuple-element.34.table, f32[512,4096]{1,0:T(8,128)} %refs_0_.7, f32[512,256]{1,0:T(8,128)} %refs_11_.1, f32[256,256]{1,0:T(8,128)S(1)} %collective-permute-done.10.refs_2_, f32[256,256]{1,0:T(8,128)S(1)} %collective-permute-done.11.refs_3_, ...), custom_call_target="tpu_custom_call" | custom-call | flops 805306368 | bytes 4194304 | tf_op jit(solution)/shard_map/pallas_call | solution.py:165
  84.7 4.0 %shard_map.137 = (f32[512,256]{1,0:T(8,128)}, f32[256,256]{1,0:T(8,128)S(1)}) custom-call(s32[19]{0:T(128)S(1)} %add_add_fusion.2.table, f32[512,4096]{1,0:T(8,128)} %refs_0_.7, f32[512,256]{1,0:T(8,128)S(1)} %collective-permute-done.23.refs_1_, f32[512,256]{1,0:T(8,128)S(1)} %collective-permute-done.25.refs_2_, ...), custom_call_target="tpu_custom_call" | custom-call | flops 402653184 | bytes 2097152 | tf_op jit(solution)/shard_map/pallas_call | solution.py:165
  88.7 5.8 %collective-permute-start.32 = (f32[256,256]{1,0:T(8,128)S(1)}, f32[256,256]{1,0:T(8,128)}, u32[]{:S(2)}, u32[]{:S(2)}) collective-permute-start(f32[256,256]{1,0:T(8,128)S(1)} %pad_maximum_fusion.6), channel_id=1, source_target_pairs={{0,2},{1,3},{2,0},{3,1},{4,6},{5,7},{6,4},{7,5},{8,10},{9,11},{10,... | collective-permute-start | bytes 786440 | tf_op jit(solution)/shard_map/ppermute | solution.py:217
  94.6 1.0 pad_maximum_fusion
  95.5 0.7 collective-permute-start.6
  96.3 1.0 pad_maximum_fusion.1
  97.2 0.7 collective-permute-start.7
  98.0 1.0 slice_add_fusion.1
  99.1 1.6 %collective-permute-start.35 = (f32[64,256]{1,0:T(8,128)S(1)}, f32[64,256]{1,0:T(8,128)S(1)}, u32[]{:S(2)}, u32[]{:S(2)}) collective-permute-start(f32[64,256]{1,0:T(8,128)S(1)} %get-tuple-element.25), channel_id=1, source_target_pairs={{0,5},{1,4},{2,7},{3,6},{4,1},{5,0},{6,3},{7,2},{8,13},{9,12},{10,... | collective-permute-start | bytes 196616 | tf_op jit(solution)/shard_map/ppermute | solution.py:217
  100.7 2.0 %collective-permute-start.33 = (f32[64,256]{1,0:T(8,128)S(1)}, f32[64,256]{1,0:T(8,128)S(1)}, u32[]{:S(2)}, u32[]{:S(2)}) collective-permute-start(f32[64,256]{1,0:T(8,128)S(1)} %slice_select_fusion.4), channel_id=1, source_target_pairs={{0,4},{1,5},{2,6},{3,7},{4,0},{5,1},{6,2},{7,3},{8,12},{9,13},{10,... | collective-permute-start | bytes 196616 | tf_op jit(solution)/shard_map/ppermute | solution.py:217
  102.6 0.5 collective-permute-start.3
  103.2 0.2 collective-permute-done.34
  103.3 4.5 %collective-permute-done.35 = f32[64,256]{1,0:T(8,128)S(1)} collective-permute-done((f32[64,256]{1,0:T(8,128)S(1)}, f32[64,256]{1,0:T(8,128)S(1)}, u32[]{:S(2)}, u32[]{:S(2)}) %collective-permute-start.35) | collective-permute-done | bytes 65568 | tf_op jit(solution)/shard_map/ppermute | solution.py:217
  107.9 0.4 collective-permute-start.36
  108.3 3.6 %collective-permute-start.37 = (f32[64,256]{1,0:T(8,128)S(1)}, f32[64,256]{1,0:T(8,128)S(1)}, u32[]{:S(2)}, u32[]{:S(2)}) collective-permute-start(f32[64,256]{1,0:T(8,128)S(1)} %add_add_fusion.1), channel_id=1, source_target_pairs={{0,16},{1,17},{2,18},{3,19},{4,20},{5,21},{6,22},{7,23},{8,24},{9,... | collective-permute-start | bytes 196616 | tf_op jit(solution)/shard_map/ppermute | solution.py:217
  111.9 0.6 collective-permute-done.36
  112.5 2.4 %collective-permute-done.37 = f32[64,256]{1,0:T(8,128)S(1)} collective-permute-done((f32[64,256]{1,0:T(8,128)S(1)}, f32[64,256]{1,0:T(8,128)S(1)}, u32[]{:S(2)}, u32[]{:S(2)}) %collective-permute-start.37) | collective-permute-done | bytes 65568 | tf_op jit(solution)/shard_map/ppermute | solution.py:217
  114.9 3.7 %collective-permute-start.38 = (f32[64,256]{1,0:T(8,128)S(1)}, f32[64,256]{1,0:T(8,128)S(1)}, u32[]{:S(2)}, u32[]{:S(2)}) collective-permute-start(f32[64,256]{1,0:T(8,128)S(1)} %add_add_fusion.1), channel_id=1, source_target_pairs={{0,24},{1,25},{2,26},{3,27},{4,28},{5,29},{6,30},{7,31},{8,16},{9,... | collective-permute-start | bytes 196616 | tf_op jit(solution)/shard_map/ppermute | solution.py:217
  118.6 0.1 compare_reduce_fusion
  118.7 2.3 %collective-permute-done.38 = f32[64,256]{1,0:T(8,128)S(1)} collective-permute-done((f32[64,256]{1,0:T(8,128)S(1)}, f32[64,256]{1,0:T(8,128)S(1)}, u32[]{:S(2)}, u32[]{:S(2)}) %collective-permute-start.38) | collective-permute-done | bytes 65568 | tf_op jit(solution)/shard_map/ppermute | solution.py:217
  121.0 1.2 collective-permute-start.31
  122.3 1.7 %collective-permute-start.39 = (f32[64,256]{1,0:T(8,128)S(1)}, f32[64,256]{1,0:T(8,128)S(1)}, u32[]{:S(2)}, u32[]{:S(2)}) collective-permute-start(f32[64,256]{1,0:T(8,128)S(1)} %add_add_fusion), channel_id=1, source_target_pairs={{0,4},{1,5},{2,6},{3,7},{4,0},{5,1},{6,2},{7,3},{8,12},{9,13},{10,... | collective-permute-start | bytes 196616 | tf_op jit(solution)/shard_map/ppermute | solution.py:217
  124.0 2.6 %shard_map.135 = f32[512,256]{1,0:T(8,128)} custom-call(s32[35]{0:T(128)S(1)} %get-tuple-element.35.table, f32[512,4096]{1,0:T(8,128)} %refs_0_.7, f32[512,256]{1,0:T(8,128)S(1)} %collective-permute-done.refs_1_, f32[256,256]{1,0:T(8,128)S(1)} %collective-permute-done.1.refs_2_, f32[256,256]{1,0:T(8,128)S(1)} %collective-permute-done.2.refs_3_, ...), custom_call_target="tpu_custom_call" | custom-call | flops 805306368 | bytes 4194304 | tf_op jit(solution)/shard_map/pallas_call | solution.py:165
  126.8 6.8 %collective-permute-done.31 = f32[512,256]{1,0:T(8,128)S(1)} collective-permute-done((f32[512,256]{1,0:T(8,128)}, f32[512,256]{1,0:T(8,128)S(1)}, u32[]{:S(2)}, u32[]{:S(2)}) %collective-permute-start.31) | collective-permute-done | bytes 524320 | tf_op jit(solution)/shard_map/ppermute | solution.py:217
  133.6 2.0 %negate_select_fusion = f32[512,256]{1,0:T(8,128)} fusion(f32[512,256]{1,0:T(8,128)} %shard_map.135, f32[512,256]{1,0:T(8,128)S(1)} %collective-permute-done.31, pred[512]{0:T(512)(128)(4,1)S(1)} %compare_reduce_fusion), kind=kLoop, calls=%fused_computation.6 | loop fusion | flops 393216 | bytes 1573376 | tf_op jit(solution)/shard_map/jit(_where)/select_n | solution.py:274
  135.6 0.7 maximum_add_fusion
  (68 shorter events, 0.8 us)
Async XLA Ops:
  0.6 33.2 %collective-permute-start.20 = (f32[512,256]{1,0:T(8,128)}, f32[512,256]{1,0:T(8,128)S(1)}, u32[]{:S(2)}, u32[]{:S(2)}) collective-permute-start(f32[512,256]{1,0:T(8,128)} %refs_11_.1), channel_id=1, source_target_pairs={{0,1},{1,0},{2,3},{3,2},{4,5},{5,4},{6,7},{7,6},{8,9},{9,8},{10,11... | collective-permute-start | bytes 1572872 | tf_op jit(solution)/shard_map/ppermute | solution.py:217
  3.7 30.7 %collective-permute-start.21 = (f32[512,256]{1,0:T(8,128)}, f32[512,256]{1,0:T(8,128)}, u32[]{:S(2)}, u32[]{:S(2)}) collective-permute-start(f32[512,256]{1,0:T(8,128)} %refs_11_.1), channel_id=1, source_target_pairs={{1,16},{3,18},{5,20},{7,22},{9,24},{11,26},{13,28},{15,30},{16,1},... | collective-permute-start | bytes 1572872 | tf_op jit(solution)/shard_map/ppermute | solution.py:217
  5.1 42.2 %collective-permute-start = (f32[512,256]{1,0:T(8,128)}, f32[512,256]{1,0:T(8,128)S(1)}, u32[]{:S(2)}, u32[]{:S(2)}) collective-permute-start(f32[512,256]{1,0:T(8,128)} %refs_11_.1), channel_id=1, source_target_pairs={{0,16},{2,18},{4,20},{6,22},{8,24},{10,26},{12,28},{14,30},{17,1},... | collective-permute-start | bytes 1572872 | tf_op jit(solution)/shard_map/ppermute | solution.py:217
  11.2 9.4 %collective-permute-start.10 = (f32[256,256]{1,0:T(8,128)S(1)}, f32[256,256]{1,0:T(8,128)S(1)}, u32[]{:S(2)}, u32[]{:S(2)}) collective-permute-start(f32[256,256]{1,0:T(8,128)S(1)} %get-tuple-element.15), channel_id=1, source_target_pairs={{0,4},{2,6},{4,0},{6,2},{8,12},{10,14},{12,8},{14,10},{17,21},{19,... | collective-permute-start | bytes 786440 | tf_op jit(solution)/shard_map/ppermute | solution.py:217
  14.9 19.0 %collective-permute-start.11 = (f32[256,256]{1,0:T(8,128)S(1)}, f32[256,256]{1,0:T(8,128)S(1)}, u32[]{:S(2)}, u32[]{:S(2)}) collective-permute-start(f32[256,256]{1,0:T(8,128)S(1)} %get-tuple-element.14), channel_id=1, source_target_pairs={{0,8},{2,10},{4,12},{6,14},{8,0},{10,2},{12,4},{14,6},{17,25},{19,... | collective-permute-start | bytes 786440 | tf_op jit(solution)/shard_map/ppermute | solution.py:217
  20.6 16.9 %collective-permute-start.19 = (s32[1,16]{1,0:T(1,128)}, s32[1,16]{1,0:T(1,128)S(1)}, u32[]{:S(2)}, u32[]{:S(2)}) collective-permute-start(s32[1,16]{1,0:T(1,128)} %param.14), channel_id=1, source_target_pairs={{0,1},{1,0},{2,3},{3,2},{4,5},{5,4},{6,7},{7,6},{8,9},{9,8},{10,11... | collective-permute-start | bytes 200 | tf_op jit(solution)/shard_map/ppermute | solution.py:217
  33.8 5.6 %collective-permute-start.13 = (f32[256,256]{1,0:T(8,128)S(1)}, f32[256,256]{1,0:T(8,128)S(1)}, u32[]{:S(2)}, u32[]{:S(2)}) collective-permute-start(f32[256,256]{1,0:T(8,128)S(1)} %collective-permute-done.10.refs_2_), channel_id=1, source_target_pairs={{0,2},{1,3},{2,0},{3,1},{4,6},{5,7},{6,4},{7,5},{8,10},{9,11},{10,... | collective-permute-start | bytes 786440 | tf_op jit(solution)/shard_map/ppermute | solution.py:217
  33.9 9.7 %collective-permute-start.14 = (f32[256,256]{1,0:T(8,128)S(1)}, f32[256,256]{1,0:T(8,128)S(1)}, u32[]{:S(2)}, u32[]{:S(2)}) collective-permute-start(f32[256,256]{1,0:T(8,128)S(1)} %collective-permute-done.11.refs_3_), channel_id=1, source_target_pairs={{0,2},{1,3},{2,0},{3,1},{4,6},{5,7},{6,4},{7,5},{8,10},{9,11},{10,... | collective-permute-start | bytes 786440 | tf_op jit(solution)/shard_map/ppermute | solution.py:217
  35.3 9.0 %collective-permute-start.22 = (f32[256,256]{1,0:T(8,128)}, f32[256,256]{1,0:T(8,128)S(1)}, u32[]{:S(2)}, u32[]{:S(2)}) collective-permute-start(f32[256,256]{1,0:T(8,128)} %get-tuple-element.13), channel_id=1, source_target_pairs={{0,4},{1,5},{2,6},{3,7},{4,0},{5,1},{6,2},{7,3},{8,12},{9,13},{10,... | collective-permute-start | bytes 786440 | tf_op jit(solution)/shard_map/ppermute | solution.py:217
  37.5 22.3 %collective-permute-start.15 = (f32[512,256]{1,0:T(8,128)}, f32[512,256]{1,0:T(8,128)S(1)}, u32[]{:S(2)}, u32[]{:S(2)}) collective-permute-start(f32[512,256]{1,0:T(8,128)} %pad_maximum_fusion.2), channel_id=1, source_target_pairs={{0,8},{2,10},{4,12},{6,14},{8,0},{10,2},{12,4},{14,6},{17,25},{19,... | collective-permute-start | bytes 1572872 | tf_op jit(solution)/shard_map/ppermute | solution.py:217
  39.4 20.7 %collective-permute-start.16 = (f32[512,256]{1,0:T(8,128)}, f32[512,256]{1,0:T(8,128)}, u32[]{:S(2)}, u32[]{:S(2)}) collective-permute-start(f32[512,256]{1,0:T(8,128)} %pad_maximum_fusion.3), channel_id=1, source_target_pairs={{0,4},{2,6},{4,0},{6,2},{8,12},{10,14},{12,8},{14,10},{17,21},{19,... | collective-permute-start | bytes 1572872 | tf_op jit(solution)/shard_map/ppermute | solution.py:217
  43.6 0.7 copy-start
  44.3 18.0 %collective-permute-start.28 = (f32[512,256]{1,0:T(8,128)S(1)}, f32[512,256]{1,0:T(8,128)}, u32[]{:S(2)}, u32[]{:S(2)}) collective-permute-start(f32[512,256]{1,0:T(8,128)S(1)} %broadcast_select_fusion.refs_1_), channel_id=1, source_target_pairs={{0,2},{1,3},{2,0},{3,1},{4,6},{5,7},{6,4},{7,5},{8,10},{9,11},{10,... | collective-permute-start | bytes 1572872 | tf_op jit(solution)/shard_map/ppermute | solution.py:217
  44.3 14.5 %collective-permute-start.24 = (f32[256,256]{1,0:T(8,128)}, f32[256,256]{1,0:T(8,128)S(1)}, u32[]{:S(2)}, u32[]{:S(2)}) collective-permute-start(f32[256,256]{1,0:T(8,128)} %get-tuple-element.12), channel_id=1, source_target_pairs={{0,8},{1,9},{2,10},{3,11},{4,12},{5,13},{6,14},{7,15},{8,0},{9,1},... | collective-permute-start | bytes 786440 | tf_op jit(solution)/shard_map/ppermute | solution.py:217
  46.3 34.8 %copy-start.1 = (f32[256,256]{1,0:T(8,128)S(1)}, f32[256,256]{1,0:T(8,128)}, u32[]{:S(2)}) copy-start(f32[256,256]{1,0:T(8,128)} %copy-done) | copy-start | bytes 786436
  47.4 14.4 %collective-permute-start.29 = (f32[256,256]{1,0:T(8,128)S(1)}, f32[256,256]{1,0:T(8,128)S(1)}, u32[]{:S(2)}, u32[]{:S(2)}) collective-permute-start(f32[256,256]{1,0:T(8,128)S(1)} %collective-permute-done.22.refs_2_), channel_id=1, source_target_pairs={{0,2},{1,3},{2,0},{3,1},{4,6},{5,7},{6,4},{7,5},{8,10},{9,11},{10,... | collective-permute-start | bytes 786440 | tf_op jit(solution)/shard_map/ppermute | solution.py:217
  58.8 3.0 %collective-permute-start.30 = (f32[256,256]{1,0:T(8,128)S(1)}, f32[256,256]{1,0:T(8,128)S(1)}, u32[]{:S(2)}, u32[]{:S(2)}) collective-permute-start(f32[256,256]{1,0:T(8,128)S(1)} %collective-permute-done.24.refs_3_), channel_id=1, source_target_pairs={{0,2},{1,3},{2,0},{3,1},{4,6},{5,7},{6,4},{7,5},{8,10},{9,11},{10,... | collective-permute-start | bytes 786440 | tf_op jit(solution)/shard_map/ppermute | solution.py:217
  59.8 14.4 %collective-permute-start.23 = (f32[512,256]{1,0:T(8,128)S(1)}, f32[512,256]{1,0:T(8,128)S(1)}, u32[]{:S(2)}, u32[]{:S(2)}) collective-permute-start(f32[512,256]{1,0:T(8,128)S(1)} %pad_maximum_fusion.4), channel_id=1, source_target_pairs={{0,8},{1,9},{2,10},{3,11},{4,12},{5,13},{6,14},{7,15},{8,0},{9,1},... | collective-permute-start | bytes 1572872 | tf_op jit(solution)/shard_map/ppermute | solution.py:217
  60.1 14.1 %collective-permute-start.25 = (f32[512,256]{1,0:T(8,128)S(1)}, f32[512,256]{1,0:T(8,128)S(1)}, u32[]{:S(2)}, u32[]{:S(2)}) collective-permute-start(f32[512,256]{1,0:T(8,128)S(1)} %pad_maximum_fusion.5), channel_id=1, source_target_pairs={{0,4},{1,5},{2,6},{3,7},{4,0},{5,1},{6,2},{7,3},{8,12},{9,13},{10,... | collective-permute-start | bytes 1572872 | tf_op jit(solution)/shard_map/ppermute | solution.py:217
  61.8 17.9 %collective-permute-start.12 = (f32[512,256]{1,0:T(8,128)}, f32[512,256]{1,0:T(8,128)S(1)}, u32[]{:S(2)}, u32[]{:S(2)}) collective-permute-start(f32[512,256]{1,0:T(8,128)} %refs_11_.1), channel_id=1, source_target_pairs={{0,2},{1,3},{2,0},{3,1},{4,6},{5,7},{6,4},{7,5},{8,10},{9,11},{10,... | collective-permute-start | bytes 1572872 | tf_op jit(solution)/shard_map/ppermute | solution.py:217
  61.8 18.6 %collective-permute-start.17 = (f32[512,256]{1,0:T(8,128)S(1)}, f32[512,256]{1,0:T(8,128)S(1)}, u32[]{:S(2)}, u32[]{:S(2)}) collective-permute-start(f32[512,256]{1,0:T(8,128)S(1)} %collective-permute-done.15.refs_7_), channel_id=1, source_target_pairs={{0,2},{1,3},{2,0},{3,1},{4,6},{5,7},{6,4},{7,5},{8,10},{9,11},{10,... | collective-permute-start | bytes 1572872 | tf_op jit(solution)/shard_map/ppermute | solution.py:217
  62.3 18.8 %collective-permute-start.18 = (f32[512,256]{1,0:T(8,128)}, f32[512,256]{1,0:T(8,128)S(1)}, u32[]{:S(2)}, u32[]{:S(2)}) collective-permute-start(f32[512,256]{1,0:T(8,128)} %collective-permute-done.16.refs_8_), channel_id=1, source_target_pairs={{0,2},{1,3},{2,0},{3,1},{4,6},{5,7},{6,4},{7,5},{8,10},{9,11},{10,... | collective-permute-start | bytes 1572872 | tf_op jit(solution)/shard_map/ppermute | solution.py:217
  74.2 10.5 %collective-permute-start.26 = (f32[512,256]{1,0:T(8,128)S(1)}, f32[512,256]{1,0:T(8,128)S(1)}, u32[]{:S(2)}, u32[]{:S(2)}) collective-permute-start(f32[512,256]{1,0:T(8,128)S(1)} %collective-permute-done.23.refs_1_), channel_id=1, source_target_pairs={{0,2},{1,3},{2,0},{3,1},{4,6},{5,7},{6,4},{7,5},{8,10},{9,11},{10,... | collective-permute-start | bytes 1572872 | tf_op jit(solution)/shard_map/ppermute | solution.py:217
  74.3 10.4 %collective-permute-start.27 = (f32[512,256]{1,0:T(8,128)S(1)}, f32[512,256]{1,0:T(8,128)S(1)}, u32[]{:S(2)}, u32[]{:S(2)}) collective-permute-start(f32[512,256]{1,0:T(8,128)S(1)} %collective-permute-done.25.refs_2_), channel_id=1, source_target_pairs={{0,2},{1,3},{2,0},{3,1},{4,6},{5,7},{6,4},{7,5},{8,10},{9,11},{10,... | collective-permute-start | bytes 1572872 | tf_op jit(solution)/shard_map/ppermute | solution.py:217
  79.7 14.8 %collective-permute-start.1 = (f32[256,256]{1,0:T(8,128)}, f32[256,256]{1,0:T(8,128)S(1)}, u32[]{:S(2)}, u32[]{:S(2)}) collective-permute-start(f32[256,256]{1,0:T(8,128)} %get-tuple-element.17), channel_id=1, source_target_pairs={{1,5},{3,7},{5,1},{7,3},{9,13},{11,15},{13,9},{15,11},{16,20},{18,... | collective-permute-start | bytes 786440 | tf_op jit(solution)/shard_map/ppermute | solution.py:217
  80.4 15.8 %collective-permute-start.2 = (f32[256,256]{1,0:T(8,128)}, f32[256,256]{1,0:T(8,128)S(1)}, u32[]{:S(2)}, u32[]{:S(2)}) collective-permute-start(f32[256,256]{1,0:T(8,128)} %get-tuple-element.16), channel_id=1, source_target_pairs={{1,9},{3,11},{5,13},{7,15},{9,1},{11,3},{13,5},{15,7},{16,24},{18,... | collective-permute-start | bytes 786440 | tf_op jit(solution)/shard_map/ppermute | solution.py:217
  84.6 34.0 %copy-start.3 = (s32[1,16]{1,0:T(1,128)S(1)}, s32[1,16]{1,0:T(1,128)}, u32[]{:S(2)}) copy-start(s32[1,16]{1,0:T(1,128)} %param.14) | copy-start | bytes 196
  88.7 9.2 %collective-permute-start.32 = (f32[256,256]{1,0:T(8,128)S(1)}, f32[256,256]{1,0:T(8,128)}, u32[]{:S(2)}, u32[]{:S(2)}) collective-permute-start(f32[256,256]{1,0:T(8,128)S(1)} %pad_maximum_fusion.6), channel_id=1, source_target_pairs={{0,2},{1,3},{2,0},{3,1},{4,6},{5,7},{6,4},{7,5},{8,10},{9,11},{10,... | collective-permute-start | bytes 786440 | tf_op jit(solution)/shard_map/ppermute | solution.py:217
  95.5 7.1 %collective-permute-start.6 = (f32[512,256]{1,0:T(8,128)S(1)}, f32[512,256]{1,0:T(8,128)S(1)}, u32[]{:S(2)}, u32[]{:S(2)}) collective-permute-start(f32[512,256]{1,0:T(8,128)S(1)} %pad_maximum_fusion), channel_id=1, source_target_pairs={{1,9},{3,11},{5,13},{7,15},{9,1},{11,3},{13,5},{15,7},{16,24},{18,... | collective-permute-start | bytes 1572872 | tf_op jit(solution)/shard_map/ppermute | solution.py:217
  97.2 5.4 %collective-permute-start.7 = (f32[512,256]{1,0:T(8,128)S(1)}, f32[512,256]{1,0:T(8,128)S(1)}, u32[]{:S(2)}, u32[]{:S(2)}) collective-permute-start(f32[512,256]{1,0:T(8,128)S(1)} %pad_maximum_fusion.1), channel_id=1, source_target_pairs={{1,5},{3,7},{5,1},{7,3},{9,13},{11,15},{13,9},{15,11},{16,20},{18,... | collective-permute-start | bytes 1572872 | tf_op jit(solution)/shard_map/ppermute | solution.py:217
  99.0 4.3 %collective-permute-start.34 = (f32[64,256]{1,0:T(8,128)S(1)}, f32[64,256]{1,0:T(8,128)S(1)}, u32[]{:S(2)}, u32[]{:S(2)}) collective-permute-start(f32[64,256]{1,0:T(8,128)S(1)} %get-tuple-element.24), channel_id=1, source_target_pairs={{0,1},{1,0},{2,3},{3,2},{4,5},{5,4},{6,7},{7,6},{8,9},{9,8},{10,11... | collective-permute-start | bytes 196616 | tf_op jit(solution)/shard_map/ppermute | solution.py:217
  99.1 8.8 %collective-permute-start.35 = (f32[64,256]{1,0:T(8,128)S(1)}, f32[64,256]{1,0:T(8,128)S(1)}, u32[]{:S(2)}, u32[]{:S(2)}) collective-permute-start(f32[64,256]{1,0:T(8,128)S(1)} %get-tuple-element.25), channel_id=1, source_target_pairs={{0,5},{1,4},{2,7},{3,6},{4,1},{5,0},{6,3},{7,2},{8,13},{9,12},{10,... | collective-permute-start | bytes 196616 | tf_op jit(solution)/shard_map/ppermute | solution.py:217
  100.7 7.2 %collective-permute-start.33 = (f32[64,256]{1,0:T(8,128)S(1)}, f32[64,256]{1,0:T(8,128)S(1)}, u32[]{:S(2)}, u32[]{:S(2)}) collective-permute-start(f32[64,256]{1,0:T(8,128)S(1)} %slice_select_fusion.4), channel_id=1, source_target_pairs={{0,4},{1,5},{2,6},{3,7},{4,0},{5,1},{6,2},{7,3},{8,12},{9,13},{10,... | collective-permute-start | bytes 196616 | tf_op jit(solution)/shard_map/ppermute | solution.py:217
  102.6 5.6 %collective-permute-start.4 = (f32[256,256]{1,0:T(8,128)S(1)}, f32[256,256]{1,0:T(8,128)S(1)}, u32[]{:S(2)}, u32[]{:S(2)}) collective-permute-start(f32[256,256]{1,0:T(8,128)S(1)} %collective-permute-done.1.refs_2_), channel_id=1, source_target_pairs={{0,2},{1,3},{2,0},{3,1},{4,6},{5,7},{6,4},{7,5},{8,10},{9,11},{10,... | collective-permute-start | bytes 786440 | tf_op jit(solution)/shard_map/ppermute | solution.py:217
  102.6 21.4 %collective-permute-start.3 = (f32[512,256]{1,0:T(8,128)S(1)}, f32[512,256]{1,0:T(8,128)S(1)}, u32[]{:S(2)}, u32[]{:S(2)}) collective-permute-start(f32[512,256]{1,0:T(8,128)S(1)} %collective-permute-done.refs_1_), channel_id=1, source_target_pairs={{0,2},{1,3},{2,0},{3,1},{4,6},{5,7},{6,4},{7,5},{8,10},{9,11},{10,... | collective-permute-start | bytes 1572872 | tf_op jit(solution)/shard_map/ppermute | solution.py:217
  103.3 20.7 %collective-permute-start.8 = (f32[512,256]{1,0:T(8,128)S(1)}, f32[512,256]{1,0:T(8,128)S(1)}, u32[]{:S(2)}, u32[]{:S(2)}) collective-permute-start(f32[512,256]{1,0:T(8,128)S(1)} %collective-permute-done.6.refs_7_), channel_id=1, source_target_pairs={{0,2},{1,3},{2,0},{3,1},{4,6},{5,7},{6,4},{7,5},{8,10},{9,11},{10,... | collective-permute-start | bytes 1572872 | tf_op jit(solution)/shard_map/ppermute | solution.py:217
  107.9 16.1 %collective-permute-start.9 = (f32[512,256]{1,0:T(8,128)S(1)}, f32[512,256]{1,0:T(8,128)S(1)}, u32[]{:S(2)}, u32[]{:S(2)}) collective-permute-start(f32[512,256]{1,0:T(8,128)S(1)} %collective-permute-done.7.refs_8_), channel_id=1, source_target_pairs={{0,2},{1,3},{2,0},{3,1},{4,6},{5,7},{6,4},{7,5},{8,10},{9,11},{10,... | collective-permute-start | bytes 1572872 | tf_op jit(solution)/shard_map/ppermute | solution.py:217
  107.9 27.7 %copy-start.2 = (f32[256,256]{1,0:T(8,128)S(1)}, f32[256,256]{1,0:T(8,128)}, u32[]{:S(2)}) copy-start(f32[256,256]{1,0:T(8,128)} %param.15) | copy-start | bytes 786436
  107.9 4.6 %collective-permute-start.36 = (f32[64,256]{1,0:T(8,128)S(1)}, f32[64,256]{1,0:T(8,128)S(1)}, u32[]{:S(2)}, u32[]{:S(2)}) collective-permute-start(f32[64,256]{1,0:T(8,128)S(1)} %add_add_fusion.1), channel_id=1, source_target_pairs={{0,8},{1,9},{2,10},{3,11},{4,12},{5,13},{6,14},{7,15},{8,0},{9,1},... | collective-permute-start | bytes 196616 | tf_op jit(solution)/shard_map/ppermute | solution.py:217
  108.3 6.7 %collective-permute-start.37 = (f32[64,256]{1,0:T(8,128)S(1)}, f32[64,256]{1,0:T(8,128)S(1)}, u32[]{:S(2)}, u32[]{:S(2)}) collective-permute-start(f32[64,256]{1,0:T(8,128)S(1)} %add_add_fusion.1), channel_id=1, source_target_pairs={{0,16},{1,17},{2,18},{3,19},{4,20},{5,21},{6,22},{7,23},{8,24},{9,... | collective-permute-start | bytes 196616 | tf_op jit(solution)/shard_map/ppermute | solution.py:217
  112.5 9.8 %collective-permute-start.5 = (f32[256,256]{1,0:T(8,128)S(1)}, f32[256,256]{1,0:T(8,128)S(1)}, u32[]{:S(2)}, u32[]{:S(2)}) collective-permute-start(f32[256,256]{1,0:T(8,128)S(1)} %collective-permute-done.2.refs_3_), channel_id=1, source_target_pairs={{0,2},{1,3},{2,0},{3,1},{4,6},{5,7},{6,4},{7,5},{8,10},{9,11},{10,... | collective-permute-start | bytes 786440 | tf_op jit(solution)/shard_map/ppermute | solution.py:217
  114.9 6.1 %collective-permute-start.38 = (f32[64,256]{1,0:T(8,128)S(1)}, f32[64,256]{1,0:T(8,128)S(1)}, u32[]{:S(2)}, u32[]{:S(2)}) collective-permute-start(f32[64,256]{1,0:T(8,128)S(1)} %add_add_fusion.1), channel_id=1, source_target_pairs={{0,24},{1,25},{2,26},{3,27},{4,28},{5,29},{6,30},{7,31},{8,16},{9,... | collective-permute-start | bytes 196616 | tf_op jit(solution)/shard_map/ppermute | solution.py:217
  121.0 12.5 %collective-permute-start.31 = (f32[512,256]{1,0:T(8,128)}, f32[512,256]{1,0:T(8,128)S(1)}, u32[]{:S(2)}, u32[]{:S(2)}) collective-permute-start(f32[512,256]{1,0:T(8,128)} %get-tuple-element.7), channel_id=1, source_target_pairs={{0,1},{1,0},{2,3},{3,2},{4,5},{5,4},{6,7},{7,6},{8,9},{9,8},{10,11... | collective-permute-start | bytes 1572872 | tf_op jit(solution)/shard_map/ppermute | solution.py:217
  122.3 4.4 %collective-permute-start.39 = (f32[64,256]{1,0:T(8,128)S(1)}, f32[64,256]{1,0:T(8,128)S(1)}, u32[]{:S(2)}, u32[]{:S(2)}) collective-permute-start(f32[64,256]{1,0:T(8,128)S(1)} %add_add_fusion), channel_id=1, source_target_pairs={{0,4},{1,5},{2,6},{3,7},{4,0},{5,1},{6,2},{7,3},{8,12},{9,13},{10,... | collective-permute-start | bytes 196616 | tf_op jit(solution)/shard_map/ppermute | solution.py:217
  126.7 8.8 %collective-permute-start.40 = (f32[128,256]{1,0:T(8,128)S(1)}, f32[128,256]{1,0:T(8,128)S(1)}, u32[]{:S(2)}, u32[]{:S(2)}) collective-permute-start(f32[128,256]{1,0:T(8,128)S(1)} %pad_maximum_fusion.7), channel_id=1, source_target_pairs={{0,2},{1,3},{2,0},{3,1},{4,6},{5,7},{6,4},{7,5},{8,10},{9,11},{10,... | collective-permute-start | bytes 393224 | tf_op jit(solution)/shard_map/ppermute | solution.py:217

commit v7 on v6

--- a/solution.py
+++ b/solution.py
@@ -69,8 +69,8 @@
     def a_copy(p, rb):
         return pltpu.make_async_copy(
             a_hbm.at[pl.ds(rb * width, width), pl.ds(pl.multiple_of(table[p] * width, width), width)],
-            a_buf.at[lax.rem(p, held), rb],
-            a_sem.at[lax.rem(p, held), rb],
+            a_buf.at[p % held, rb],
+            a_sem.at[p % held, rb],
         )
 
     def start(p):
@@ -102,7 +102,7 @@
     def step(p, carry):
         @pl.when(table[count + p] > 0)
         def _():
-            slot = lax.rem(p, held)
+            slot = p % held
             pltpu.make_async_copy(p_buf.at[slot], p_buf.at[slot], p_sem.at[slot]).wait()
             high, low = split(p_buf[slot])
 
@@ -130,7 +130,11 @@
 
         return carry
 
-    lax.fori_loop(0, count, step, 0)
+    if count > 4:
+        lax.fori_loop(0, count, step, 0)
+    else:
+        for p in range(count):
+            step(p, 0)
     if final:
         extra_copy.wait()
         terms[...] = jnp.zeros_like(terms)
@@ -146,11 +150,11 @@
             terms[...] += terms[...].T
 
 
-def product(table, inverse_anc, arrays, slots, width, acc=None, extra=None):
+def product(table, inverse_anc, arrays, slots, width, acc=None, extra=None, kind=jax.ShapeDtypeStruct):
     rows = inverse_anc.shape[0]
     blocks = rows // width
     count = len(slots)
-    held = min(count, 8)
+    held = count
     any_spec = pl.BlockSpec(memory_space=pl.ANY)
     vmem = pl.BlockSpec(memory_space=pltpu.VMEM)
     operands = [pltpu.with_memory_space_constraint(inverse_anc, pltpu.HBM), *arrays]
@@ -159,7 +163,7 @@
         if more is not None:
             operands.append(more)
             specs.append(any_spec)
-    shapes = [pltpu.HBM((rows, width), jnp.float32)]
+    shapes = [kind((rows, width), jnp.float32)]
     if extra is not None:
         shapes.append(jax.ShapeDtypeStruct((width, width), jnp.float32))
     return pl.pallas_call(
@@ -179,7 +183,7 @@
                 pltpu.SemaphoreType.DMA((2,)),
             ],
         ),
-        compiler_params=pltpu.CompilerParams(vmem_limit_bytes=12 * 1024 * 1024),
+        compiler_params=pltpu.CompilerParams(vmem_limit_bytes=20 * 1024 * 1024),
         cost_estimate=pl.CostEstimate(
             flops=6 * rows * width * width * count // 4,
             bytes_accessed=4 * rows * width * count // 2,
@@ -189,11 +193,11 @@
 
 
 CORE, X, Z, FAR = 1, 2, 4, 8
-FIRST = ((0, 0), (0, 1), (X, 0), (Z, 1), (1, 0), (1, 1), (X | 1, 0), (Z | 1, 1))
-SECOND = tuple((m | c, h) for c in (0, 1) for m, h in ((Z, 0), (Z | X, 0), (X, 1), (Z | X, 1)))
-SLOTS1 = ((0, 0), (0, 1), (1, 0), (2, 0), (3, 0), (3, 1), (4, 0), (5, 0))
-SLOTS2 = ((0, 0), (0, 1), (1, 0), (1, 1), (2, 0), (2, 1), (3, 0), (3, 1))
-SLOTS12 = SLOTS1 + tuple((6 + i, h) for i, h in SLOTS2)
+FIRST = tuple((m | c, h) for c in (0, 1) for m in (0, X, Z) for h in (0, 1))
+SECOND = tuple((Z | X | c, h) for c in (0, 1) for h in (0, 1))
+SLOTS1 = tuple((i, h) for i in range(6) for h in (0, 1))
+SLOTS2 = tuple((i, 0) for i in range(4))
+SLOTS12 = SLOTS1 + tuple((6 + i, 0) for i in range(4))
 
 
 def local_two(n_row, inverse_anc, lower_panel, structure, diag_inverse):
@@ -227,11 +231,11 @@
         return jnp.concatenate([block, on.astype(jnp.int32), far.astype(jnp.int32)[None]])
 
     def step_one(q, who):
-        return move(q[:half], X, 0, who), move(q[half:], Z, 0, who)
-
-    def step_two(q, one, who):
-        first, second = jnp.concatenate([q[:half], one[0]]), jnp.concatenate([q[half:], one[1]])
-        return move(first, Z, 0, who), move(second, X, 0, who)
+        return move(q, X, 0, who), move(q, Z, 0, who)
+
+    def step_two(one, who):
+        z2 = move(one[0][:half], Z, 0, who)
+        return z2, move(one[1][half:], X, 0, who)
 
     def with_sibling(arrays, who):
         return list(arrays) + [move(v, CORE, 0, who) for v in arrays]
@@ -241,29 +245,29 @@
     lower_other = move(lower_panel, 0, 1)
     n_one = step_one(lower_panel, True)
     q_far = move(lower_panel, FAR, 0, True)
-    n_two = step_two(lower_panel, n_one, True)
+    n_two = step_two(n_one, True)
     in_hbm = lambda v: pltpu.with_memory_space_constraint(v, pltpu.HBM)
     n_first = with_sibling([lower_panel, *n_one], None)
     n_first[0] = in_hbm(lower_panel)
     n_second = with_sibling(n_two, None)
     q_other = jnp.where(near, lower_other, got_far)
     o_one = step_one(q_other, None)
-    o_two = step_two(q_other, o_one, None)
+    o_two = step_two(o_one, None)
     o_first = with_sibling([q_other, *o_one], None)
     o_second = with_sibling(o_two, None)
     f_one = step_one(q_far, False)
-    f_two = step_two(q_far, f_one, False)
+    f_two = step_two(f_one, False)
     f_first = with_sibling([q_far, *f_one], None)
     f_second = with_sibling(f_two, None)
 
     own, own_terms = product(
         table(structure, FIRST + SECOND, True), inverse_anc, n_first + n_second, SLOTS12, width,
-        extra=n_first[0],
+        extra=n_first[0], kind=pltpu.HBM,
     )
     (part,) = product(table(other_structure, FIRST, None), inverse_anc, o_first, SLOTS1, width)
     part, other_terms = product(
         table(other_structure, SECOND, None), inverse_anc, o_second, SLOTS2, width,
-        acc=in_hbm(part), extra=lower_other,
+        acc=part, extra=lower_other, kind=pltpu.HBM,
     )
     recv = move(part, 0, 1)
     (own,) = product(

time: 137 us -> 143 us (1.044)
  starting transfers between devices: 51.5 us -> 78.4 us
  waiting for transfers between devices: 53.5 us -> 43.8 us
  other arithmetic: 12.4 us -> 5.68 us
  local copies, waits for them, and re-layouts: 3.46 us -> 1.08 us
  Pallas kernels: 14.3 us -> 12.8 us
    ppermute x41, starting transfers between devices: 51.5 us -> 78.4 us  [move(): return lax.ppermute(value, BOTH, pairs)]
    ppermute x41, waiting for transfers between devices: 53.5 us -> 43.8 us  [move(): return lax.ppermute(value, BOTH, pairs)]
    concatenate x6 -> x0, other arithmetic: 5.67 us -> none  [the longest x3 2.84 us: step_two(): jnp.concatenate([q[:half], one[0]])]
    slice x3 -> x6, local copies, waits for them, and re-layouts: 2.74 us -> 0.11 us  [the longest x3 0.06 us: step_two(): return (z2, move(one[1][half:], X, 0, who))]
    pallas_call x4, Pallas kernels: 14.3 us -> 12.8 us  [product(): pl.pallas_call(functools.partial(product_kernel, slots, blocks, width, ac...]
  transfers between devices with their start and end apart: 41 -> 41, of which waited for: 11 -> 13; matrix products, arithmetic and copies ran while one was open for 11% -> 4% of each run, Pallas kernels for 10% -> 9%
where the time goes in v7:
time: 143 us
  starting transfers between devices  78.4 us (55%)
  waiting for transfers between devices  43.8 us (31%)
  Pallas kernels  12.8 us (9%)
  other arithmetic  5.68 us (4%)
    ppermute x41, starting transfers between devices, move(): return lax.ppermute(value, BOTH, pairs)  78.4 us
    ppermute x41, waiting for transfers between devices, move(): return lax.ppermute(value, BOTH, pairs)  43.8 us
    pallas_call x4, Pallas kernels, product(): pl.pallas_call(functools.partial(product_kernel, slots, blocks, width, ac...  12.8 us
  transfers between devices with their start and end apart: 41, of which 13 were waited for; matrix products, arithmetic and copies ran while one was open for 4% of the time, Pallas kernels for 9%

profile of v7, /device:TPU:0, one launch (start us, length us, event | category | flops | bytes accessed | tf_op | source)
XLA Modules:
  0.0 142.8 jit_solution(5594655958913139146)
XLA Ops:
  0.6 3.1 %collective-permute-start.20 = (f32[512,256]{1,0:T(8,128)}, f32[512,256]{1,0:T(8,128)S(1)}, u32[]{:S(2)}, u32[]{:S(2)}) collective-permute-start(f32[512,256]{1,0:T(8,128)} %refs_11_.1), channel_id=1, source_target_pairs={{0,1},{1,0},{2,3},{3,2},{4,5},{5,4},{6,7},{7,6},{8,9},{9,8},{10,11... | collective-permute-start | bytes 1572872 | tf_op jit(solution)/shard_map/ppermute | solution.py:221
  3.7 0.7 collective-permute-start.21
  4.4 3.4 %collective-permute-start.10 = (f32[512,256]{1,0:T(8,128)}, f32[512,256]{1,0:T(8,128)S(1)}, u32[]{:S(2)}, u32[]{:S(2)}) collective-permute-start(f32[512,256]{1,0:T(8,128)} %refs_11_.1), channel_id=1, source_target_pairs={{0,4},{2,6},{4,0},{6,2},{8,12},{10,14},{12,8},{14,10},{17,21},{19,... | collective-permute-start | bytes 1572872 | tf_op jit(solution)/shard_map/ppermute | solution.py:221
  7.8 3.5 %collective-permute-start.11 = (f32[512,256]{1,0:T(8,128)}, f32[512,256]{1,0:T(8,128)S(1)}, u32[]{:S(2)}, u32[]{:S(2)}) collective-permute-start(f32[512,256]{1,0:T(8,128)} %refs_11_.1), channel_id=1, source_target_pairs={{0,8},{2,10},{4,12},{6,14},{8,0},{10,2},{12,4},{14,6},{17,25},{19,... | collective-permute-start | bytes 1572872 | tf_op jit(solution)/shard_map/ppermute | solution.py:221
  11.3 0.1 collective-permute-start.19
  11.4 0.7 multiply_add_fusion.2
  12.1 0.1 pad_add_fusion.2
  12.1 0.7 compare_reduce_fusion.2
  12.9 0.7 multiply_add_fusion
  13.6 2.7 %collective-permute-done.20.refs_6_ = f32[512,256]{1,0:T(8,128)S(1)} collective-permute-done((f32[512,256]{1,0:T(8,128)}, f32[512,256]{1,0:T(8,128)S(1)}, u32[]{:S(2)}, u32[]{:S(2)}) %collective-permute-start.20) | collective-permute-done | bytes 524320 | tf_op jit(solution)/shard_map/ppermute | solution.py:221
  16.4 1.6 %collective-permute-start.22 = (f32[512,256]{1,0:T(8,128)S(1)}, f32[512,256]{1,0:T(8,128)S(1)}, u32[]{:S(2)}, u32[]{:S(2)}) collective-permute-start(f32[512,256]{1,0:T(8,128)S(1)} %broadcast_select_fusion.refs_1_), channel_id=1, source_target_pairs={{0,4},{1,5},{2,6},{3,7},{4,0},{5,1},{6,2},{7,3},{8,12},{9,13},{10,... | collective-permute-start | bytes 1572872 | tf_op jit(solution)/shard_map/ppermute | solution.py:221
  17.9 11.7 %collective-permute-start.24 = (f32[512,256]{1,0:T(8,128)S(1)}, f32[512,256]{1,0:T(8,128)S(1)}, u32[]{:S(2)}, u32[]{:S(2)}) collective-permute-start(f32[512,256]{1,0:T(8,128)S(1)} %broadcast_select_fusion.refs_1_), channel_id=1, source_target_pairs={{0,8},{1,9},{2,10},{3,11},{4,12},{5,13},{6,14},{7,15},{8,0},{9,1},... | collective-permute-start | bytes 1572872 | tf_op jit(solution)/shard_map/ppermute | solution.py:221
  29.7 1.9 %collective-permute-start.15 = (f32[256,256]{1,0:T(8,128)S(1)}, f32[256,256]{1,0:T(8,128)S(1)}, u32[]{:S(2)}, u32[]{:S(2)}) collective-permute-start(f32[256,256]{1,0:T(8,128)S(1)} %slice.66), channel_id=1, source_target_pairs={{0,8},{2,10},{4,12},{6,14},{8,0},{10,2},{12,4},{14,6},{17,25},{19,... | collective-permute-start | bytes 786440 | tf_op jit(solution)/shard_map/ppermute | solution.py:221
  31.6 3.2 %collective-permute-done.11.refs_3_ = f32[512,256]{1,0:T(8,128)S(1)} collective-permute-done((f32[512,256]{1,0:T(8,128)}, f32[512,256]{1,0:T(8,128)S(1)}, u32[]{:S(2)}, u32[]{:S(2)}) %collective-permute-start.11) | collective-permute-done | bytes 524320 | tf_op jit(solution)/shard_map/ppermute | solution.py:221
  34.8 1.9 %collective-permute-start.16 = (f32[256,256]{1,0:T(8,128)S(1)}, f32[256,256]{1,0:T(8,128)}, u32[]{:S(2)}, u32[]{:S(2)}) collective-permute-start(f32[256,256]{1,0:T(8,128)S(1)} %slice.67), channel_id=1, source_target_pairs={{0,4},{2,6},{4,0},{6,2},{8,12},{10,14},{12,8},{14,10},{17,21},{19,... | collective-permute-start | bytes 786440 | tf_op jit(solution)/shard_map/ppermute | solution.py:221
  36.8 0.1 pad_add_fusion
  36.9 0.1 pad_add_fusion.5
  37.0 13.0 %collective-permute-done.15.refs_7_ = f32[256,256]{1,0:T(8,128)S(1)} collective-permute-done((f32[256,256]{1,0:T(8,128)S(1)}, f32[256,256]{1,0:T(8,128)S(1)}, u32[]{:S(2)}, u32[]{:S(2)}) %collective-permute-start.15) | collective-permute-done | bytes 262176 | tf_op jit(solution)/shard_map/ppermute | solution.py:221
  50.0 0.5 collective-permute-start.14
  50.5 0.7 multiply_add_fusion.1
  51.2 0.4 collective-permute-start.18
  51.7 0.1 pad_add_fusion.3
  51.8 0.2 compare_reduce_fusion.1
  52.0 0.2 compare_reduce_fusion.3
  52.2 0.1 collective-permute-start.28
  52.4 0.8 collective-permute-done.17.refs_9_
  53.1 0.4 collective-permute-done.18.refs_10_
  53.5 0.5 collective-permute-start.25
  54.1 0.5 collective-permute-start.30
  54.6 0.1 pad_add_fusion.6.table
  54.6 0.1 pad_add_fusion.4.table
  54.7 1.0 copy-done.1
  55.7 3.4 %shard_map.134 = (f32[512,256]{1,0:T(8,128)}, f32[256,256]{1,0:T(8,128)S(1)}) custom-call(s32[35]{0:T(128)S(1)} %get-tuple-element.24.table, f32[512,4096]{1,0:T(8,128)} %refs_0_.7, f32[512,256]{1,0:T(8,128)} %refs_11_.1, f32[512,256]{1,0:T(8,128)S(1)} %collective-permute-done.10.refs_2_, f32[512,256]{1,0:T(8,128)S(1)} %collective-permute-done.11.refs_3_, ...), custom_call_target="tpu_custom_call" | custom-call | flops 805306368 | bytes 4194304 | tf_op jit(solution)/shard_map/pallas_call | solution.py:169
  59.1 2.4 %collective-permute-done.23.refs_1_ = f32[256,256]{1,0:T(8,128)S(1)} collective-permute-done((f32[256,256]{1,0:T(8,128)S(1)}, f32[256,256]{1,0:T(8,128)S(1)}, u32[]{:S(2)}, u32[]{:S(2)}) %collective-permute-start.23) | collective-permute-done | bytes 262176 | tf_op jit(solution)/shard_map/ppermute | solution.py:221
  61.5 1.5 %collective-permute-start.26 = (f32[256,256]{1,0:T(8,128)S(1)}, f32[256,256]{1,0:T(8,128)S(1)}, u32[]{:S(2)}, u32[]{:S(2)}) collective-permute-start(f32[256,256]{1,0:T(8,128)S(1)} %collective-permute-done.23.refs_1_), channel_id=1, source_target_pairs={{0,2},{1,3},{2,0},{3,1},{4,6},{5,7},{6,4},{7,5},{8,10},{9,11},{10,... | collective-permute-start | bytes 786440 | tf_op jit(solution)/shard_map/ppermute | solution.py:221
  63.0 0.1 collective-permute-start.27
  63.2 1.3 collective-permute-start
  64.5 3.9 %shard_map.136.refs_5_ = f32[512,256]{1,0:T(8,128)S(1)} custom-call(s32[27]{0:T(128)S(1)} %pad_add_fusion.6.table, f32[512,4096]{1,0:T(8,128)} %refs_0_.7, f32[512,256]{1,0:T(8,128)S(1)} %broadcast_select_fusion.refs_1_, f32[512,256]{1,0:T(8,128)S(1)} %collective-permute-done.22.refs_2_, f32[512,256]{1,0:T(8,128)S(1)} %collective-permute-done.24.refs_3_, ...), custom_call_target="tpu_custom_call" | custom-call | flops 603979776 | bytes 3145728 | tf_op jit(solution)/shard_map/pallas_call | solution.py:169
  68.5 3.4 %shard_map.137 = (f32[512,256]{1,0:T(8,128)}, f32[256,256]{1,0:T(8,128)S(1)}) custom-call(s32[11]{0:T(128)S(1)} %pad_add_fusion.4.table, f32[512,4096]{1,0:T(8,128)} %refs_0_.7, f32[256,256]{1,0:T(8,128)S(1)} %collective-permute-done.23.refs_1_, f32[256,256]{1,0:T(8,128)S(1)} %collective-permute-done.25.refs_2_, ...), custom_call_target="tpu_custom_call" | custom-call | flops 201326592 | bytes 1048576 | tf_op jit(solution)/shard_map/pallas_call | solution.py:169
  71.9 1.9 %collective-permute-start.32 = (f32[256,256]{1,0:T(8,128)S(1)}, f32[256,256]{1,0:T(8,128)S(1)}, u32[]{:S(2)}, u32[]{:S(2)}) collective-permute-start(f32[256,256]{1,0:T(8,128)S(1)} %pad_maximum_fusion), channel_id=1, source_target_pairs={{0,2},{1,3},{2,0},{3,1},{4,6},{5,7},{6,4},{7,5},{8,10},{9,11},{10,... | collective-permute-start | bytes 786440 | tf_op jit(solution)/shard_map/ppermute | solution.py:221
  73.8 3.0 %collective-permute-done.refs_1_ = f32[512,256]{1,0:T(8,128)S(1)} collective-permute-done((f32[512,256]{1,0:T(8,128)}, f32[512,256]{1,0:T(8,128)S(1)}, u32[]{:S(2)}, u32[]{:S(2)}) %collective-permute-start) | collective-permute-done | bytes 524320 | tf_op jit(solution)/shard_map/ppermute | solution.py:221
  76.9 0.7 collective-permute-start.1
  77.5 0.7 collective-permute-start.2
  78.4 19.6 %collective-permute-start.34 = (f32[64,256]{1,0:T(8,128)S(1)}, f32[64,256]{1,0:T(8,128)S(1)}, u32[]{:S(2)}, u32[]{:S(2)}) collective-permute-start(f32[64,256]{1,0:T(8,128)S(1)} %get-tuple-element.16), channel_id=1, source_target_pairs={{0,1},{1,0},{2,3},{3,2},{4,5},{5,4},{6,7},{7,6},{8,9},{9,8},{10,11... | collective-permute-start | bytes 196616 | tf_op jit(solution)/shard_map/ppermute | solution.py:221
  98.0 1.1 collective-permute-start.35
  99.2 0.6 collective-permute-start.33
  99.7 0.7 collective-permute-start.6
  100.5 1.0 collective-permute-done.34
  101.4 0.7 collective-permute-start.7
  102.1 8.1 %collective-permute-done.35 = f32[64,256]{1,0:T(8,128)S(1)} collective-permute-done((f32[64,256]{1,0:T(8,128)S(1)}, f32[64,256]{1,0:T(8,128)S(1)}, u32[]{:S(2)}, u32[]{:S(2)}) %collective-permute-start.35) | collective-permute-done | bytes 65568 | tf_op jit(solution)/shard_map/ppermute | solution.py:221
  110.2 0.5 collective-permute-start.5
  110.8 7.4 %collective-permute-start.37 = (f32[64,256]{1,0:T(8,128)S(1)}, f32[64,256]{1,0:T(8,128)S(1)}, u32[]{:S(2)}, u32[]{:S(2)}) collective-permute-start(f32[64,256]{1,0:T(8,128)S(1)} %add_add_fusion.1), channel_id=1, source_target_pairs={{0,16},{1,17},{2,18},{3,19},{4,20},{5,21},{6,22},{7,23},{8,24},{9,... | collective-permute-start | bytes 196616 | tf_op jit(solution)/shard_map/ppermute | solution.py:221
  118.3 0.5 collective-permute-start.9
  118.8 2.2 %collective-permute-done.37 = f32[64,256]{1,0:T(8,128)S(1)} collective-permute-done((f32[64,256]{1,0:T(8,128)S(1)}, f32[64,256]{1,0:T(8,128)S(1)}, u32[]{:S(2)}, u32[]{:S(2)}) %collective-permute-start.37) | collective-permute-done | bytes 65568 | tf_op jit(solution)/shard_map/ppermute | solution.py:221
  121.0 4.0 %collective-permute-start.38 = (f32[64,256]{1,0:T(8,128)S(1)}, f32[64,256]{1,0:T(8,128)S(1)}, u32[]{:S(2)}, u32[]{:S(2)}) collective-permute-start(f32[64,256]{1,0:T(8,128)S(1)} %add_add_fusion.1), channel_id=1, source_target_pairs={{0,24},{1,25},{2,26},{3,27},{4,28},{5,29},{6,30},{7,31},{8,16},{9,... | collective-permute-start | bytes 196616 | tf_op jit(solution)/shard_map/ppermute | solution.py:221
  125.0 0.1 compare_reduce_fusion
  125.1 2.1 %collective-permute-done.38 = f32[64,256]{1,0:T(8,128)S(1)} collective-permute-done((f32[64,256]{1,0:T(8,128)S(1)}, f32[64,256]{1,0:T(8,128)S(1)}, u32[]{:S(2)}, u32[]{:S(2)}) %collective-permute-start.38) | collective-permute-done | bytes 65568 | tf_op jit(solution)/shard_map/ppermute | solution.py:221
  127.2 4.9 %collective-permute-start.31 = (f32[512,256]{1,0:T(8,128)}, f32[512,256]{1,0:T(8,128)S(1)}, u32[]{:S(2)}, u32[]{:S(2)}) collective-permute-start(f32[512,256]{1,0:T(8,128)} %get-tuple-element.7), channel_id=1, source_target_pairs={{0,1},{1,0},{2,3},{3,2},{4,5},{5,4},{6,7},{7,6},{8,9},{9,8},{10,11... | collective-permute-start | bytes 1572872 | tf_op jit(solution)/shard_map/ppermute | solution.py:221
  132.2 2.0 %collective-permute-start.39 = (f32[64,256]{1,0:T(8,128)S(1)}, f32[64,256]{1,0:T(8,128)S(1)}, u32[]{:S(2)}, u32[]{:S(2)}) collective-permute-start(f32[64,256]{1,0:T(8,128)S(1)} %add_add_fusion), channel_id=1, source_target_pairs={{0,4},{1,5},{2,6},{3,7},{4,0},{5,1},{6,2},{7,3},{8,12},{9,13},{10,... | collective-permute-start | bytes 196616 | tf_op jit(solution)/shard_map/ppermute | solution.py:221
  134.2 2.0 %shard_map.135 = f32[512,256]{1,0:T(8,128)S(1)} custom-call(s32[35]{0:T(128)S(1)} %get-tuple-element.25.table, f32[512,4096]{1,0:T(8,128)} %refs_0_.7, f32[512,256]{1,0:T(8,128)S(1)} %collective-permute-done.refs_1_, f32[512,256]{1,0:T(8,128)S(1)} %collective-permute-done.1.refs_2_, f32[512,256]{1,0:T(8,128)S(1)} %collective-permute-done.2.refs_3_, ...), custom_call_target="tpu_custom_call" | custom-call | flops 805306368 | bytes 4194304 | tf_op jit(solution)/shard_map/pallas_call | solution.py:169
  136.2 0.3 collective-permute-done.39
  136.6 4.5 %collective-permute-done.31 = f32[512,256]{1,0:T(8,128)S(1)} collective-permute-done((f32[512,256]{1,0:T(8,128)}, f32[512,256]{1,0:T(8,128)S(1)}, u32[]{:S(2)}, u32[]{:S(2)}) %collective-permute-start.31) | collective-permute-done | bytes 524320 | tf_op jit(solution)/shard_map/ppermute | solution.py:221
  141.1 0.9 negate_select_fusion
  142.1 0.7 maximum_add_fusion
  (68 shorter events, 0.9 us)
Async XLA Ops:
  0.6 15.7 %collective-permute-start.20 = (f32[512,256]{1,0:T(8,128)}, f32[512,256]{1,0:T(8,128)S(1)}, u32[]{:S(2)}, u32[]{:S(2)}) collective-permute-start(f32[512,256]{1,0:T(8,128)} %refs_11_.1), channel_id=1, source_target_pairs={{0,1},{1,0},{2,3},{3,2},{4,5},{5,4},{6,7},{7,6},{8,9},{9,8},{10,11... | collective-permute-start | bytes 1572872 | tf_op jit(solution)/shard_map/ppermute | solution.py:221
  3.7 12.6 %collective-permute-start.21 = (f32[512,256]{1,0:T(8,128)}, f32[512,256]{1,0:T(8,128)S(1)}, u32[]{:S(2)}, u32[]{:S(2)}) collective-permute-start(f32[512,256]{1,0:T(8,128)} %refs_11_.1), channel_id=1, source_target_pairs={{1,16},{3,18},{5,20},{7,22},{9,24},{11,26},{13,28},{15,30},{16,1},... | collective-permute-start | bytes 1572872 | tf_op jit(solution)/shard_map/ppermute | solution.py:221
  4.4 25.3 %collective-permute-start.10 = (f32[512,256]{1,0:T(8,128)}, f32[512,256]{1,0:T(8,128)S(1)}, u32[]{:S(2)}, u32[]{:S(2)}) collective-permute-start(f32[512,256]{1,0:T(8,128)} %refs_11_.1), channel_id=1, source_target_pairs={{0,4},{2,6},{4,0},{6,2},{8,12},{10,14},{12,8},{14,10},{17,21},{19,... | collective-permute-start | bytes 1572872 | tf_op jit(solution)/shard_map/ppermute | solution.py:221
  7.8 27.0 %collective-permute-start.11 = (f32[512,256]{1,0:T(8,128)}, f32[512,256]{1,0:T(8,128)S(1)}, u32[]{:S(2)}, u32[]{:S(2)}) collective-permute-start(f32[512,256]{1,0:T(8,128)} %refs_11_.1), channel_id=1, source_target_pairs={{0,8},{2,10},{4,12},{6,14},{8,0},{10,2},{12,4},{14,6},{17,25},{19,... | collective-permute-start | bytes 1572872 | tf_op jit(solution)/shard_map/ppermute | solution.py:221
  11.3 25.7 %collective-permute-start.19 = (s32[1,16]{1,0:T(1,128)}, s32[1,16]{1,0:T(1,128)S(1)}, u32[]{:S(2)}, u32[]{:S(2)}) collective-permute-start(s32[1,16]{1,0:T(1,128)} %param.14), channel_id=1, source_target_pairs={{0,1},{1,0},{2,3},{3,2},{4,5},{5,4},{6,7},{7,6},{8,9},{9,8},{10,11... | collective-permute-start | bytes 200 | tf_op jit(solution)/shard_map/ppermute | solution.py:221
  16.4 34.8 %collective-permute-start.22 = (f32[512,256]{1,0:T(8,128)S(1)}, f32[512,256]{1,0:T(8,128)S(1)}, u32[]{:S(2)}, u32[]{:S(2)}) collective-permute-start(f32[512,256]{1,0:T(8,128)S(1)} %broadcast_select_fusion.refs_1_), channel_id=1, source_target_pairs={{0,4},{1,5},{2,6},{3,7},{4,0},{5,1},{6,2},{7,3},{8,12},{9,13},{10,... | collective-permute-start | bytes 1572872 | tf_op jit(solution)/shard_map/ppermute | solution.py:221
  17.9 33.3 %collective-permute-start.24 = (f32[512,256]{1,0:T(8,128)S(1)}, f32[512,256]{1,0:T(8,128)S(1)}, u32[]{:S(2)}, u32[]{:S(2)}) collective-permute-start(f32[512,256]{1,0:T(8,128)S(1)} %broadcast_select_fusion.refs_1_), channel_id=1, source_target_pairs={{0,8},{1,9},{2,10},{3,11},{4,12},{5,13},{6,14},{7,15},{8,0},{9,1},... | collective-permute-start | bytes 1572872 | tf_op jit(solution)/shard_map/ppermute | solution.py:221
  29.7 20.3 %collective-permute-start.15 = (f32[256,256]{1,0:T(8,128)S(1)}, f32[256,256]{1,0:T(8,128)S(1)}, u32[]{:S(2)}, u32[]{:S(2)}) collective-permute-start(f32[256,256]{1,0:T(8,128)S(1)} %slice.66), channel_id=1, source_target_pairs={{0,8},{2,10},{4,12},{6,14},{8,0},{10,2},{12,4},{14,6},{17,25},{19,... | collective-permute-start | bytes 786440 | tf_op jit(solution)/shard_map/ppermute | solution.py:221
  34.8 15.1 %collective-permute-start.16 = (f32[256,256]{1,0:T(8,128)S(1)}, f32[256,256]{1,0:T(8,128)}, u32[]{:S(2)}, u32[]{:S(2)}) collective-permute-start(f32[256,256]{1,0:T(8,128)S(1)} %slice.67), channel_id=1, source_target_pairs={{0,4},{2,6},{4,0},{6,2},{8,12},{10,14},{12,8},{14,10},{17,21},{19,... | collective-permute-start | bytes 786440 | tf_op jit(solution)/shard_map/ppermute | solution.py:221
  36.9 15.3 %collective-permute-start.12 = (f32[512,256]{1,0:T(8,128)}, f32[512,256]{1,0:T(8,128)}, u32[]{:S(2)}, u32[]{:S(2)}) collective-permute-start(f32[512,256]{1,0:T(8,128)} %refs_11_.1), channel_id=1, source_target_pairs={{0,2},{1,3},{2,0},{3,1},{4,6},{5,7},{6,4},{7,5},{8,10},{9,11},{10,... | collective-permute-start | bytes 1572872 | tf_op jit(solution)/shard_map/ppermute | solution.py:221
  50.0 4.8 %copy-start = (f32[256,256]{1,0:T(8,128)}, f32[256,256]{1,0:T(8,128)S(1)}, u32[]{:S(2)}) copy-start(f32[256,256]{1,0:T(8,128)S(1)} %collective-permute-done.15.refs_7_) | copy-start | bytes 786436
  50.0 4.1 %collective-permute-start.13 = (f32[512,256]{1,0:T(8,128)S(1)}, f32[512,256]{1,0:T(8,128)}, u32[]{:S(2)}, u32[]{:S(2)}) collective-permute-start(f32[512,256]{1,0:T(8,128)S(1)} %collective-permute-done.10.refs_2_), channel_id=1, source_target_pairs={{0,2},{1,3},{2,0},{3,1},{4,6},{5,7},{6,4},{7,5},{8,10},{9,11},{10,... | collective-permute-start | bytes 1572872 | tf_op jit(solution)/shard_map/ppermute | solution.py:221
  50.0 4.1 %collective-permute-start.14 = (f32[512,256]{1,0:T(8,128)S(1)}, f32[512,256]{1,0:T(8,128)}, u32[]{:S(2)}, u32[]{:S(2)}) collective-permute-start(f32[512,256]{1,0:T(8,128)S(1)} %collective-permute-done.11.refs_3_), channel_id=1, source_target_pairs={{0,2},{1,3},{2,0},{3,1},{4,6},{5,7},{6,4},{7,5},{8,10},{9,11},{10,... | collective-permute-start | bytes 1572872 | tf_op jit(solution)/shard_map/ppermute | solution.py:221
  51.2 2.0 %collective-permute-start.17 = (f32[256,256]{1,0:T(8,128)S(1)}, f32[256,256]{1,0:T(8,128)}, u32[]{:S(2)}, u32[]{:S(2)}) collective-permute-start(f32[256,256]{1,0:T(8,128)S(1)} %collective-permute-done.15.refs_7_), channel_id=1, source_target_pairs={{0,2},{1,3},{2,0},{3,1},{4,6},{5,7},{6,4},{7,5},{8,10},{9,11},{10,... | collective-permute-start | bytes 786440 | tf_op jit(solution)/shard_map/ppermute | solution.py:221
  51.2 2.3 %collective-permute-start.18 = (f32[256,256]{1,0:T(8,128)}, f32[256,256]{1,0:T(8,128)}, u32[]{:S(2)}, u32[]{:S(2)}) collective-permute-start(f32[256,256]{1,0:T(8,128)} %collective-permute-done.16.refs_8_), channel_id=1, source_target_pairs={{0,2},{1,3},{2,0},{3,1},{4,6},{5,7},{6,4},{7,5},{8,10},{9,11},{10,... | collective-permute-start | bytes 786440 | tf_op jit(solution)/shard_map/ppermute | solution.py:221
  52.2 10.9 %collective-permute-start.28 = (f32[512,256]{1,0:T(8,128)S(1)}, f32[512,256]{1,0:T(8,128)S(1)}, u32[]{:S(2)}, u32[]{:S(2)}) collective-permute-start(f32[512,256]{1,0:T(8,128)S(1)} %broadcast_select_fusion.refs_1_), channel_id=1, source_target_pairs={{0,2},{1,3},{2,0},{3,1},{4,6},{5,7},{6,4},{7,5},{8,10},{9,11},{10,... | collective-permute-start | bytes 1572872 | tf_op jit(solution)/shard_map/ppermute | solution.py:221
  53.1 8.3 %collective-permute-start.23 = (f32[256,256]{1,0:T(8,128)S(1)}, f32[256,256]{1,0:T(8,128)S(1)}, u32[]{:S(2)}, u32[]{:S(2)}) collective-permute-start(f32[256,256]{1,0:T(8,128)S(1)} %slice.68), channel_id=1, source_target_pairs={{0,8},{1,9},{2,10},{3,11},{4,12},{5,13},{6,14},{7,15},{8,0},{9,1},... | collective-permute-start | bytes 786440 | tf_op jit(solution)/shard_map/ppermute | solution.py:221
  53.5 9.5 %collective-permute-start.25 = (f32[256,256]{1,0:T(8,128)S(1)}, f32[256,256]{1,0:T(8,128)S(1)}, u32[]{:S(2)}, u32[]{:S(2)}) collective-permute-start(f32[256,256]{1,0:T(8,128)S(1)} %slice.69), channel_id=1, source_target_pairs={{0,4},{1,5},{2,6},{3,7},{4,0},{5,1},{6,2},{7,3},{8,12},{9,13},{10,... | collective-permute-start | bytes 786440 | tf_op jit(solution)/shard_map/ppermute | solution.py:221
  54.1 10.4 %collective-permute-start.29 = (f32[512,256]{1,0:T(8,128)S(1)}, f32[512,256]{1,0:T(8,128)S(1)}, u32[]{:S(2)}, u32[]{:S(2)}) collective-permute-start(f32[512,256]{1,0:T(8,128)S(1)} %collective-permute-done.22.refs_2_), channel_id=1, source_target_pairs={{0,2},{1,3},{2,0},{3,1},{4,6},{5,7},{6,4},{7,5},{8,10},{9,11},{10,... | collective-permute-start | bytes 1572872 | tf_op jit(solution)/shard_map/ppermute | solution.py:221
  54.1 10.4 %collective-permute-start.30 = (f32[512,256]{1,0:T(8,128)S(1)}, f32[512,256]{1,0:T(8,128)S(1)}, u32[]{:S(2)}, u32[]{:S(2)}) collective-permute-start(f32[512,256]{1,0:T(8,128)S(1)} %collective-permute-done.24.refs_3_), channel_id=1, source_target_pairs={{0,2},{1,3},{2,0},{3,1},{4,6},{5,7},{6,4},{7,5},{8,10},{9,11},{10,... | collective-permute-start | bytes 1572872 | tf_op jit(solution)/shard_map/ppermute | solution.py:221
  54.7 1.0 copy-start.1
  61.5 7.0 %collective-permute-start.26 = (f32[256,256]{1,0:T(8,128)S(1)}, f32[256,256]{1,0:T(8,128)S(1)}, u32[]{:S(2)}, u32[]{:S(2)}) collective-permute-start(f32[256,256]{1,0:T(8,128)S(1)} %collective-permute-done.23.refs_1_), channel_id=1, source_target_pairs={{0,2},{1,3},{2,0},{3,1},{4,6},{5,7},{6,4},{7,5},{8,10},{9,11},{10,... | collective-permute-start | bytes 786440 | tf_op jit(solution)/shard_map/ppermute | solution.py:221
  63.0 5.4 %collective-permute-start.27 = (f32[256,256]{1,0:T(8,128)S(1)}, f32[256,256]{1,0:T(8,128)S(1)}, u32[]{:S(2)}, u32[]{:S(2)}) collective-permute-start(f32[256,256]{1,0:T(8,128)S(1)} %collective-permute-done.25.refs_2_), channel_id=1, source_target_pairs={{0,2},{1,3},{2,0},{3,1},{4,6},{5,7},{6,4},{7,5},{8,10},{9,11},{10,... | collective-permute-start | bytes 786440 | tf_op jit(solution)/shard_map/ppermute | solution.py:221
  63.2 13.7 %collective-permute-start = (f32[512,256]{1,0:T(8,128)}, f32[512,256]{1,0:T(8,128)S(1)}, u32[]{:S(2)}, u32[]{:S(2)}) collective-permute-start(f32[512,256]{1,0:T(8,128)} %refs_11_.1), channel_id=1, source_target_pairs={{0,16},{2,18},{4,20},{6,22},{8,24},{10,26},{12,28},{14,30},{17,1},... | collective-permute-start | bytes 1572872 | tf_op jit(solution)/shard_map/ppermute | solution.py:221
  68.4 56.6 %copy-start.3 = (s32[1,16]{1,0:T(1,128)S(1)}, s32[1,16]{1,0:T(1,128)}, u32[]{:S(2)}) copy-start(s32[1,16]{1,0:T(1,128)} %param.14) | copy-start | bytes 196
  71.9 6.4 %collective-permute-start.32 = (f32[256,256]{1,0:T(8,128)S(1)}, f32[256,256]{1,0:T(8,128)S(1)}, u32[]{:S(2)}, u32[]{:S(2)}) collective-permute-start(f32[256,256]{1,0:T(8,128)S(1)} %pad_maximum_fusion), channel_id=1, source_target_pairs={{0,2},{1,3},{2,0},{3,1},{4,6},{5,7},{6,4},{7,5},{8,10},{9,11},{10,... | collective-permute-start | bytes 786440 | tf_op jit(solution)/shard_map/ppermute | solution.py:221
  76.9 22.3 %collective-permute-start.1 = (f32[512,256]{1,0:T(8,128)S(1)}, f32[512,256]{1,0:T(8,128)S(1)}, u32[]{:S(2)}, u32[]{:S(2)}) collective-permute-start(f32[512,256]{1,0:T(8,128)S(1)} %collective-permute-done.refs_1_), channel_id=1, source_target_pairs={{1,5},{3,7},{5,1},{7,3},{9,13},{11,15},{13,9},{15,11},{16,20},{18,... | collective-permute-start | bytes 1572872 | tf_op jit(solution)/shard_map/ppermute | solution.py:221
  77.5 22.2 %collective-permute-start.2 = (f32[512,256]{1,0:T(8,128)S(1)}, f32[512,256]{1,0:T(8,128)S(1)}, u32[]{:S(2)}, u32[]{:S(2)}) collective-permute-start(f32[512,256]{1,0:T(8,128)S(1)} %collective-permute-done.refs_1_), channel_id=1, source_target_pairs={{1,9},{3,11},{5,13},{7,15},{9,1},{11,3},{13,5},{15,7},{16,24},{18,... | collective-permute-start | bytes 1572872 | tf_op jit(solution)/shard_map/ppermute | solution.py:221
  78.2 32.5 %collective-permute-start.3 = (f32[512,256]{1,0:T(8,128)S(1)}, f32[512,256]{1,0:T(8,128)S(1)}, u32[]{:S(2)}, u32[]{:S(2)}) collective-permute-start(f32[512,256]{1,0:T(8,128)S(1)} %collective-permute-done.refs_1_), channel_id=1, source_target_pairs={{0,2},{1,3},{2,0},{3,1},{4,6},{5,7},{6,4},{7,5},{8,10},{9,11},{10,... | collective-permute-start | bytes 1572872 | tf_op jit(solution)/shard_map/ppermute | solution.py:221
  78.4 23.0 %collective-permute-start.34 = (f32[64,256]{1,0:T(8,128)S(1)}, f32[64,256]{1,0:T(8,128)S(1)}, u32[]{:S(2)}, u32[]{:S(2)}) collective-permute-start(f32[64,256]{1,0:T(8,128)S(1)} %get-tuple-element.16), channel_id=1, source_target_pairs={{0,1},{1,0},{2,3},{3,2},{4,5},{5,4},{6,7},{7,6},{8,9},{9,8},{10,11... | collective-permute-start | bytes 196616 | tf_op jit(solution)/shard_map/ppermute | solution.py:221
  98.0 12.2 %collective-permute-start.35 = (f32[64,256]{1,0:T(8,128)S(1)}, f32[64,256]{1,0:T(8,128)S(1)}, u32[]{:S(2)}, u32[]{:S(2)}) collective-permute-start(f32[64,256]{1,0:T(8,128)S(1)} %get-tuple-element.17), channel_id=1, source_target_pairs={{0,5},{1,4},{2,7},{3,6},{4,1},{5,0},{6,3},{7,2},{8,13},{9,12},{10,... | collective-permute-start | bytes 196616 | tf_op jit(solution)/shard_map/ppermute | solution.py:221
  99.2 11.0 %collective-permute-start.33 = (f32[64,256]{1,0:T(8,128)S(1)}, f32[64,256]{1,0:T(8,128)S(1)}, u32[]{:S(2)}, u32[]{:S(2)}) collective-permute-start(f32[64,256]{1,0:T(8,128)S(1)} %slice_select_fusion.4), channel_id=1, source_target_pairs={{0,4},{1,5},{2,6},{3,7},{4,0},{5,1},{6,2},{7,3},{8,12},{9,13},{10,... | collective-permute-start | bytes 196616 | tf_op jit(solution)/shard_map/ppermute | solution.py:221
  99.7 11.1 %collective-permute-start.6 = (f32[256,256]{1,0:T(8,128)S(1)}, f32[256,256]{1,0:T(8,128)S(1)}, u32[]{:S(2)}, u32[]{:S(2)}) collective-permute-start(f32[256,256]{1,0:T(8,128)S(1)} %slice.64), channel_id=1, source_target_pairs={{1,9},{3,11},{5,13},{7,15},{9,1},{11,3},{13,5},{15,7},{16,24},{18,... | collective-permute-start | bytes 786440 | tf_op jit(solution)/shard_map/ppermute | solution.py:221
  101.4 16.8 %collective-permute-start.7 = (f32[256,256]{1,0:T(8,128)S(1)}, f32[256,256]{1,0:T(8,128)S(1)}, u32[]{:S(2)}, u32[]{:S(2)}) collective-permute-start(f32[256,256]{1,0:T(8,128)S(1)} %slice.65), channel_id=1, source_target_pairs={{1,5},{3,7},{5,1},{7,3},{9,13},{11,15},{13,9},{15,11},{16,20},{18,... | collective-permute-start | bytes 786440 | tf_op jit(solution)/shard_map/ppermute | solution.py:221
  110.2 22.0 %collective-permute-start.4 = (f32[512,256]{1,0:T(8,128)S(1)}, f32[512,256]{1,0:T(8,128)S(1)}, u32[]{:S(2)}, u32[]{:S(2)}) collective-permute-start(f32[512,256]{1,0:T(8,128)S(1)} %collective-permute-done.1.refs_2_), channel_id=1, source_target_pairs={{0,2},{1,3},{2,0},{3,1},{4,6},{5,7},{6,4},{7,5},{8,10},{9,11},{10,... | collective-permute-start | bytes 1572872 | tf_op jit(solution)/shard_map/ppermute | solution.py:221
  110.2 24.0 %collective-permute-start.5 = (f32[512,256]{1,0:T(8,128)S(1)}, f32[512,256]{1,0:T(8,128)S(1)}, u32[]{:S(2)}, u32[]{:S(2)}) collective-permute-start(f32[512,256]{1,0:T(8,128)S(1)} %collective-permute-done.2.refs_3_), channel_id=1, source_target_pairs={{0,2},{1,3},{2,0},{3,1},{4,6},{5,7},{6,4},{7,5},{8,10},{9,11},{10,... | collective-permute-start | bytes 1572872 | tf_op jit(solution)/shard_map/ppermute | solution.py:221
  110.7 31.4 %copy-start.2 = (f32[256,256]{1,0:T(8,128)S(1)}, f32[256,256]{1,0:T(8,128)}, u32[]{:S(2)}) copy-start(f32[256,256]{1,0:T(8,128)} %param.15) | copy-start | bytes 786436
  110.7 7.6 %collective-permute-start.36 = (f32[64,256]{1,0:T(8,128)S(1)}, f32[64,256]{1,0:T(8,128)S(1)}, u32[]{:S(2)}, u32[]{:S(2)}) collective-permute-start(f32[64,256]{1,0:T(8,128)S(1)} %add_add_fusion.1), channel_id=1, source_target_pairs={{0,8},{1,9},{2,10},{3,11},{4,12},{5,13},{6,14},{7,15},{8,0},{9,1},... | collective-permute-start | bytes 196616 | tf_op jit(solution)/shard_map/ppermute | solution.py:221
  110.8 10.2 %collective-permute-start.37 = (f32[64,256]{1,0:T(8,128)S(1)}, f32[64,256]{1,0:T(8,128)S(1)}, u32[]{:S(2)}, u32[]{:S(2)}) collective-permute-start(f32[64,256]{1,0:T(8,128)S(1)} %add_add_fusion.1), channel_id=1, source_target_pairs={{0,16},{1,17},{2,18},{3,19},{4,20},{5,21},{6,22},{7,23},{8,24},{9,... | collective-permute-start | bytes 196616 | tf_op jit(solution)/shard_map/ppermute | solution.py:221
  118.2 15.9 %collective-permute-start.8 = (f32[256,256]{1,0:T(8,128)S(1)}, f32[256,256]{1,0:T(8,128)S(1)}, u32[]{:S(2)}, u32[]{:S(2)}) collective-permute-start(f32[256,256]{1,0:T(8,128)S(1)} %collective-permute-done.6.refs_7_), channel_id=1, source_target_pairs={{0,2},{1,3},{2,0},{3,1},{4,6},{5,7},{6,4},{7,5},{8,10},{9,11},{10,... | collective-permute-start | bytes 786440 | tf_op jit(solution)/shard_map/ppermute | solution.py:221
  118.3 15.8 %collective-permute-start.9 = (f32[256,256]{1,0:T(8,128)S(1)}, f32[256,256]{1,0:T(8,128)S(1)}, u32[]{:S(2)}, u32[]{:S(2)}) collective-permute-start(f32[256,256]{1,0:T(8,128)S(1)} %collective-permute-done.7.refs_8_), channel_id=1, source_target_pairs={{0,2},{1,3},{2,0},{3,1},{4,6},{5,7},{6,4},{7,5},{8,10},{9,11},{10,... | collective-permute-start | bytes 786440 | tf_op jit(solution)/shard_map/ppermute | solution.py:221
  121.0 6.2 %collective-permute-start.38 = (f32[64,256]{1,0:T(8,128)S(1)}, f32[64,256]{1,0:T(8,128)S(1)}, u32[]{:S(2)}, u32[]{:S(2)}) collective-permute-start(f32[64,256]{1,0:T(8,128)S(1)} %add_add_fusion.1), channel_id=1, source_target_pairs={{0,24},{1,25},{2,26},{3,27},{4,28},{5,29},{6,30},{7,31},{8,16},{9,... | collective-permute-start | bytes 196616 | tf_op jit(solution)/shard_map/ppermute | solution.py:221
  127.2 13.9 %collective-permute-start.31 = (f32[512,256]{1,0:T(8,128)}, f32[512,256]{1,0:T(8,128)S(1)}, u32[]{:S(2)}, u32[]{:S(2)}) collective-permute-start(f32[512,256]{1,0:T(8,128)} %get-tuple-element.7), channel_id=1, source_target_pairs={{0,1},{1,0},{2,3},{3,2},{4,5},{5,4},{6,7},{7,6},{8,9},{9,8},{10,11... | collective-permute-start | bytes 1572872 | tf_op jit(solution)/shard_map/ppermute | solution.py:221
  132.2 4.3 %collective-permute-start.39 = (f32[64,256]{1,0:T(8,128)S(1)}, f32[64,256]{1,0:T(8,128)S(1)}, u32[]{:S(2)}, u32[]{:S(2)}) collective-permute-start(f32[64,256]{1,0:T(8,128)S(1)} %add_add_fusion), channel_id=1, source_target_pairs={{0,4},{1,5},{2,6},{3,7},{4,0},{5,1},{6,2},{7,3},{8,12},{9,13},{10,... | collective-permute-start | bytes 196616 | tf_op jit(solution)/shard_map/ppermute | solution.py:221
  136.5 5.5 %collective-permute-start.40 = (f32[128,256]{1,0:T(8,128)S(1)}, f32[128,256]{1,0:T(8,128)S(1)}, u32[]{:S(2)}, u32[]{:S(2)}) collective-permute-start(f32[128,256]{1,0:T(8,128)S(1)} %pad_maximum_fusion.1), channel_id=1, source_target_pairs={{0,2},{1,3},{2,0},{3,1},{4,6},{5,7},{6,4},{7,5},{8,10},{9,11},{10,... | collective-permute-start | bytes 393224 | tf_op jit(solution)/shard_map/ppermute | solution.py:221

commit v8 on v7

--- a/solution.py
+++ b/solution.py
@@ -49,13 +49,31 @@
     return dot(a[0], b[0]) + (dot(a[0], b[1]) + dot(a[1], b[0]))
 
 
-def product_kernel(slots, blocks, width, has_acc, final, table, *refs):
+def product_kernel(slots, blocks, width, mode, final, table, *refs):
+    active = table[2 * len(slots) + blocks + 1] > 0
+
+    @pl.when(active)
+    def _():
+        product_body(slots, blocks, width, mode, final, table, *refs)
+
+    if mode == "keep":
+        arrays = 1 + max(slot[0] for slot in slots)
+
+        @pl.when(jnp.logical_not(active))
+        def _():
+            copy = pltpu.make_async_copy(refs[1 + arrays], refs[2 + arrays], refs[-1].at[0])
+            copy.start()
+            copy.wait()
+
+
+def product_body(slots, blocks, width, mode, final, table, *refs):
     count = len(slots)
     narrays = 1 + max(s[0] for s in slots)
     refs = list(refs)
     a_hbm = refs.pop(0)
     arrays = [refs.pop(0) for _ in range(narrays)]
-    acc_in = refs.pop(0) if has_acc else None
+    acc_in = refs.pop(0) if mode else None
+    has_acc = mode == "sum"
     extra_in = refs.pop(0) if final else None
     out = refs.pop(0)
     terms = refs.pop(0) if final else None
@@ -150,7 +168,7 @@
             terms[...] += terms[...].T
 
 
-def product(table, inverse_anc, arrays, slots, width, acc=None, extra=None, kind=jax.ShapeDtypeStruct):
+def product(table, inverse_anc, arrays, slots, width, acc=None, extra=None, kind=jax.ShapeDtypeStruct, mode=None):
     rows = inverse_anc.shape[0]
     blocks = rows // width
     count = len(slots)
@@ -167,7 +185,7 @@
     if extra is not None:
         shapes.append(jax.ShapeDtypeStruct((width, width), jnp.float32))
     return pl.pallas_call(
-        functools.partial(product_kernel, slots, blocks, width, acc is not None, extra is not None),
+        functools.partial(product_kernel, slots, blocks, width, mode, extra is not None),
         out_shape=shapes,
         grid_spec=pltpu.PrefetchScalarGridSpec(
             num_scalar_prefetch=1,
@@ -197,6 +215,8 @@
 SECOND = tuple((Z | X | c, h) for c in (0, 1) for h in (0, 1))
 SLOTS1 = tuple((i, h) for i in range(6) for h in (0, 1))
 SLOTS2 = tuple((i, 0) for i in range(4))
+WHOLE = FIRST + tuple((Z | X | c, h) for c in (0, 1) for h in (0, 1))
+SLOTSW = SLOTS1 + tuple((6 + i, h) for i in range(2) for h in (0, 1))
 SLOTS12 = SLOTS1 + tuple((6 + i, 0) for i in range(4))
 
 
@@ -228,7 +248,9 @@
         if who is not None:
             on = on & (near == who)
         far = jnp.logical_not(near) if who is None else jnp.zeros((), jnp.bool_)
-        return jnp.concatenate([block, on.astype(jnp.int32), far.astype(jnp.int32)[None]])
+        active = near == who if who is not None else jnp.ones((), jnp.bool_)
+        flags = jnp.concatenate([on, far[None], active[None]])
+        return jnp.concatenate([block, flags.astype(jnp.int32)])
 
     def step_one(q, who):
         return move(q, X, 0, who), move(q, Z, 0, who)
@@ -256,7 +278,7 @@
     o_first = with_sibling([q_other, *o_one], None)
     o_second = with_sibling(o_two, None)
     f_one = step_one(q_far, False)
-    f_two = step_two(f_one, False)
+    f_two = [move(q_far, Z | X, 0, False)]
     f_first = with_sibling([q_far, *f_one], None)
     f_second = with_sibling(f_two, None)
 
@@ -267,12 +289,12 @@
     (part,) = product(table(other_structure, FIRST, None), inverse_anc, o_first, SLOTS1, width)
     part, other_terms = product(
         table(other_structure, SECOND, None), inverse_anc, o_second, SLOTS2, width,
-        acc=part, extra=lower_other, kind=pltpu.HBM,
+        acc=part, extra=lower_other, kind=pltpu.HBM, mode="sum",
     )
     recv = move(part, 0, 1)
     (own,) = product(
-        table(structure, FIRST + SECOND, False), inverse_anc, f_first + f_second, SLOTS12, width,
-        acc=in_hbm(own),
+        table(structure, WHOLE, False), inverse_anc, f_first + f_second, SLOTSW, width,
+        acc=in_hbm(own), mode="keep",
     )
     keep = keep_rows(structure, row * rows, rows, width)
     panel = jnp.where(keep, -(own + recv), jnp.float32(0.0))
@@ -288,7 +310,7 @@
         got = move(value, mask, 0)
         return jnp.concatenate([jnp.where(bit, got, value), jnp.where(bit, value, got)])
 
-    u_keep, u_send = parts(own_terms, CORE)
+    u_keep, u_send = parts(jnp.where(near, own_terms, jnp.float32(0.0)), CORE)
     v_keep, v_send = parts(other_terms, CORE)
     size = u_keep.shape[0]
     got = move(jnp.concatenate([u_send, v_send]), CORE, 0)

time: 143 us -> 152 us (1.063)
  waiting for transfers between devices: 43.8 us -> 48.9 us
  starting transfers between devices: 78.4 us -> 81.7 us
    ppermute x41 -> x39, waiting for transfers between devices: 43.8 us -> 48.9 us  [move(): return lax.ppermute(value, BOTH, pairs)]
    ppermute x41 -> x39, starting transfers between devices: 78.4 us -> 81.7 us  [move(): return lax.ppermute(value, BOTH, pairs)]
  transfers between devices with their start and end apart: 41 -> 39, of which waited for: 13 -> 14; matrix products, arithmetic and copies ran while one was open for 4% -> 4% of each run, Pallas kernels for 9% -> 8%
where the time goes in v8:
time: 152 us
  starting transfers between devices  81.7 us (54%)
  waiting for transfers between devices  48.9 us (32%)
  Pallas kernels  12.5 us (8%)
  other arithmetic  5.99 us (4%)
    ppermute x39, starting transfers between devices, move(): return lax.ppermute(value, BOTH, pairs)  81.7 us
    ppermute x39, waiting for transfers between devices, move(): return lax.ppermute(value, BOTH, pairs)  48.9 us
    pallas_call x4, Pallas kernels, product(): pl.pallas_call(functools.partial(product_kernel, slots, blocks, width, mo...  12.5 us
  transfers between devices with their start and end apart: 39, of which 14 were waited for; matrix products, arithmetic and copies ran while one was open for 4% of the time, Pallas kernels for 8%

profile of v8, /device:TPU:0, one launch (start us, length us, event | category | flops | bytes accessed | tf_op | source)
XLA Modules:
  0.0 151.7 jit_solution(2623810537227233556)
XLA Ops:
  0.6 3.1 %collective-permute-start.18 = (f32[512,256]{1,0:T(8,128)}, f32[512,256]{1,0:T(8,128)S(1)}, u32[]{:S(2)}, u32[]{:S(2)}) collective-permute-start(f32[512,256]{1,0:T(8,128)} %refs_11_.1), channel_id=1, source_target_pairs={{0,1},{1,0},{2,3},{3,2},{4,5},{5,4},{6,7},{7,6},{8,9},{9,8},{10,11... | collective-permute-start | bytes 1572872 | tf_op jit(solution)/shard_map/ppermute | solution.py:241
  3.7 0.7 collective-permute-start.19
  4.4 3.4 %collective-permute-start.8 = (f32[512,256]{1,0:T(8,128)}, f32[512,256]{1,0:T(8,128)S(1)}, u32[]{:S(2)}, u32[]{:S(2)}) collective-permute-start(f32[512,256]{1,0:T(8,128)} %refs_11_.1), channel_id=1, source_target_pairs={{0,4},{2,6},{4,0},{6,2},{8,12},{10,14},{12,8},{14,10},{17,21},{19,... | collective-permute-start | bytes 1572872 | tf_op jit(solution)/shard_map/ppermute | solution.py:241
  7.8 3.5 %collective-permute-start.9 = (f32[512,256]{1,0:T(8,128)}, f32[512,256]{1,0:T(8,128)S(1)}, u32[]{:S(2)}, u32[]{:S(2)}) collective-permute-start(f32[512,256]{1,0:T(8,128)} %refs_11_.1), channel_id=1, source_target_pairs={{0,8},{2,10},{4,12},{6,14},{8,0},{10,2},{12,4},{14,6},{17,25},{19,... | collective-permute-start | bytes 1572872 | tf_op jit(solution)/shard_map/ppermute | solution.py:241
  11.4 0.7 multiply_add_fusion
  12.1 0.7 multiply_add_fusion.1
  12.8 0.7 multiply_add_fusion.2
  13.4 0.1 pad_add_fusion.2
  13.5 0.7 compare_reduce_fusion.2
  14.3 0.1 pad_add_fusion.7
  14.4 0.1 fusion.6
  14.5 1.8 %collective-permute-done.18.refs_6_ = f32[512,256]{1,0:T(8,128)S(1)} collective-permute-done((f32[512,256]{1,0:T(8,128)}, f32[512,256]{1,0:T(8,128)S(1)}, u32[]{:S(2)}, u32[]{:S(2)}) %collective-permute-start.18) | collective-permute-done | bytes 524320 | tf_op jit(solution)/shard_map/ppermute | solution.py:241
  16.4 1.6 %collective-permute-start.20 = (f32[512,256]{1,0:T(8,128)S(1)}, f32[512,256]{1,0:T(8,128)S(1)}, u32[]{:S(2)}, u32[]{:S(2)}) collective-permute-start(f32[512,256]{1,0:T(8,128)S(1)} %broadcast_select_fusion.refs_1_), channel_id=1, source_target_pairs={{0,4},{1,5},{2,6},{3,7},{4,0},{5,1},{6,2},{7,3},{8,12},{9,13},{10,... | collective-permute-start | bytes 1572872 | tf_op jit(solution)/shard_map/ppermute | solution.py:241
  17.9 11.7 %collective-permute-start.22 = (f32[512,256]{1,0:T(8,128)S(1)}, f32[512,256]{1,0:T(8,128)S(1)}, u32[]{:S(2)}, u32[]{:S(2)}) collective-permute-start(f32[512,256]{1,0:T(8,128)S(1)} %broadcast_select_fusion.refs_1_), channel_id=1, source_target_pairs={{0,8},{1,9},{2,10},{3,11},{4,12},{5,13},{6,14},{7,15},{8,0},{9,1},... | collective-permute-start | bytes 1572872 | tf_op jit(solution)/shard_map/ppermute | solution.py:241
  29.6 0.7 slice.56
  30.4 1.9 %collective-permute-start.13 = (f32[256,256]{1,0:T(8,128)}, f32[256,256]{1,0:T(8,128)S(1)}, u32[]{:S(2)}, u32[]{:S(2)}) collective-permute-start(f32[256,256]{1,0:T(8,128)} %slice.56), channel_id=1, source_target_pairs={{0,8},{2,10},{4,12},{6,14},{8,0},{10,2},{12,4},{14,6},{17,25},{19,... | collective-permute-start | bytes 786440 | tf_op jit(solution)/shard_map/ppermute | solution.py:241
  32.3 2.5 %collective-permute-done.9.refs_3_ = f32[512,256]{1,0:T(8,128)S(1)} collective-permute-done((f32[512,256]{1,0:T(8,128)}, f32[512,256]{1,0:T(8,128)S(1)}, u32[]{:S(2)}, u32[]{:S(2)}) %collective-permute-start.9) | collective-permute-done | bytes 524320 | tf_op jit(solution)/shard_map/ppermute | solution.py:241
  34.8 0.7 slice.57
  35.5 1.9 %collective-permute-start.14 = (f32[256,256]{1,0:T(8,128)}, f32[256,256]{1,0:T(8,128)}, u32[]{:S(2)}, u32[]{:S(2)}) collective-permute-start(f32[256,256]{1,0:T(8,128)} %slice.57), channel_id=1, source_target_pairs={{0,4},{2,6},{4,0},{6,2},{8,12},{10,14},{12,8},{14,10},{17,21},{19,... | collective-permute-start | bytes 786440 | tf_op jit(solution)/shard_map/ppermute | solution.py:241
  37.5 0.1 fusion.5
  37.5 0.1 pad_add_fusion.4
  37.6 0.2 compare_reduce_fusion.1
  37.8 12.1 %collective-permute-done.13.refs_7_ = f32[256,256]{1,0:T(8,128)S(1)} collective-permute-done((f32[256,256]{1,0:T(8,128)}, f32[256,256]{1,0:T(8,128)S(1)}, u32[]{:S(2)}, u32[]{:S(2)}) %collective-permute-start.13) | collective-permute-done | bytes 262176 | tf_op jit(solution)/shard_map/ppermute | solution.py:241
  50.0 0.5 collective-permute-start.12
  50.5 0.1 add_convert_fusion.1
  50.6 0.2 compare_reduce_fusion.3
  50.8 0.5 collective-permute-start.16
  51.3 0.1 add_convert_fusion
  51.5 0.1 pad_add_fusion.6.table
  51.6 0.2 collective-permute-start.26
  51.8 1.2 collective-permute-done.15.refs_9_
  53.0 0.4 collective-permute-done.16.refs_10_
  53.4 0.5 collective-permute-start.23
  53.9 0.5 collective-permute-start.28
  54.4 3.1 %shard_map.134 = (f32[512,256]{1,0:T(8,128)}, f32[256,256]{1,0:T(8,128)S(1)}) custom-call(s32[36]{0:T(128)S(1)} %get-tuple-element.24.table, f32[512,4096]{1,0:T(8,128)} %refs_0_.7, f32[512,256]{1,0:T(8,128)} %refs_11_.1, f32[512,256]{1,0:T(8,128)S(1)} %collective-permute-done.8.refs_2_, f32[512,256]{1,0:T(8,128)S(1)} %collective-permute-done.9.refs_3_, ...), custom_call_target="tpu_custom_call" | custom-call | flops 805306368 | bytes 4194304 | tf_op jit(solution)/shard_map/pallas_call | solution.py:187
  57.6 3.7 %collective-permute-done.21.refs_1_ = f32[256,256]{1,0:T(8,128)S(1)} collective-permute-done((f32[256,256]{1,0:T(8,128)S(1)}, f32[256,256]{1,0:T(8,128)S(1)}, u32[]{:S(2)}, u32[]{:S(2)}) %collective-permute-start.21) | collective-permute-done | bytes 262176 | tf_op jit(solution)/shard_map/ppermute | solution.py:241
  61.4 0.4 collective-permute-start.24
  61.8 0.1 collective-permute-start.25
  61.9 1.3 collective-permute-start
  63.3 3.9 %shard_map.136.refs_5_ = f32[512,256]{1,0:T(8,128)S(1)} custom-call(s32[28]{0:T(128)S(1)} %pad_add_fusion.8.table, f32[512,4096]{1,0:T(8,128)} %refs_0_.7, f32[512,256]{1,0:T(8,128)S(1)} %broadcast_select_fusion.refs_1_, f32[512,256]{1,0:T(8,128)S(1)} %collective-permute-done.20.refs_2_, f32[512,256]{1,0:T(8,128)S(1)} %collective-permute-done.22.refs_3_, ...), custom_call_target="tpu_custom_call" | custom-call | flops 603979776 | bytes 3145728 | tf_op jit(solution)/shard_map/pallas_call | solution.py:187
  67.2 3.4 %shard_map.137 = (f32[512,256]{1,0:T(8,128)}, f32[256,256]{1,0:T(8,128)S(1)}) custom-call(s32[12]{0:T(128)S(1)} %pad_add_fusion.6.table, f32[512,4096]{1,0:T(8,128)} %refs_0_.7, f32[256,256]{1,0:T(8,128)S(1)} %collective-permute-done.21.refs_1_, f32[256,256]{1,0:T(8,128)S(1)} %collective-permute-done.23.refs_2_, ...), custom_call_target="tpu_custom_call" | custom-call | flops 201326592 | bytes 1048576 | tf_op jit(solution)/shard_map/pallas_call | solution.py:187
  70.7 1.9 %collective-permute-start.30 = (f32[256,256]{1,0:T(8,128)S(1)}, f32[256,256]{1,0:T(8,128)S(1)}, u32[]{:S(2)}, u32[]{:S(2)}) collective-permute-start(f32[256,256]{1,0:T(8,128)S(1)} %pad_maximum_fusion), channel_id=1, source_target_pairs={{0,2},{1,3},{2,0},{3,1},{4,6},{5,7},{6,4},{7,5},{8,10},{9,11},{10,... | collective-permute-start | bytes 786440 | tf_op jit(solution)/shard_map/ppermute | solution.py:241
  72.6 3.0 %collective-permute-done.refs_1_ = f32[512,256]{1,0:T(8,128)S(1)} collective-permute-done((f32[512,256]{1,0:T(8,128)}, f32[512,256]{1,0:T(8,128)S(1)}, u32[]{:S(2)}, u32[]{:S(2)}) %collective-permute-start) | collective-permute-done | bytes 524320 | tf_op jit(solution)/shard_map/ppermute | solution.py:241
  75.6 0.7 collective-permute-start.1
  76.3 0.7 collective-permute-start.2
  77.0 0.7 collective-permute-start.6
  77.8 23.9 %collective-permute-start.32 = (f32[64,256]{1,0:T(8,128)S(1)}, f32[64,256]{1,0:T(8,128)S(1)}, u32[]{:S(2)}, u32[]{:S(2)}) collective-permute-start(f32[64,256]{1,0:T(8,128)S(1)} %get-tuple-element.16), channel_id=1, source_target_pairs={{0,1},{1,0},{2,3},{3,2},{4,5},{5,4},{6,7},{7,6},{8,9},{9,8},{10,11... | collective-permute-start | bytes 196616 | tf_op jit(solution)/shard_map/ppermute | solution.py:241
  101.7 1.6 %collective-permute-start.31 = (f32[64,256]{1,0:T(8,128)S(1)}, f32[64,256]{1,0:T(8,128)S(1)}, u32[]{:S(2)}, u32[]{:S(2)}) collective-permute-start(f32[64,256]{1,0:T(8,128)S(1)} %slice_select_fusion.4), channel_id=1, source_target_pairs={{0,4},{1,5},{2,6},{3,7},{4,0},{5,1},{6,2},{7,3},{8,12},{9,13},{10,... | collective-permute-start | bytes 196616 | tf_op jit(solution)/shard_map/ppermute | solution.py:241
  103.3 0.5 collective-permute-start.4
  103.8 0.1 collective-permute-done.32
  103.9 5.0 %collective-permute-done.33 = f32[64,256]{1,0:T(8,128)S(1)} collective-permute-done((f32[64,256]{1,0:T(8,128)S(1)}, f32[64,256]{1,0:T(8,128)S(1)}, u32[]{:S(2)}, u32[]{:S(2)}) %collective-permute-start.33) | collective-permute-done | bytes 65568 | tf_op jit(solution)/shard_map/ppermute | solution.py:241
  109.1 4.5 %collective-permute-done.34 = f32[64,256]{1,0:T(8,128)S(1)} collective-permute-done((f32[64,256]{1,0:T(8,128)S(1)}, f32[64,256]{1,0:T(8,128)S(1)}, u32[]{:S(2)}, u32[]{:S(2)}) %collective-permute-start.34) | collective-permute-done | bytes 65568 | tf_op jit(solution)/shard_map/ppermute | solution.py:241
  113.6 11.6 %collective-permute-start.35 = (f32[64,256]{1,0:T(8,128)S(1)}, f32[64,256]{1,0:T(8,128)S(1)}, u32[]{:S(2)}, u32[]{:S(2)}) collective-permute-start(f32[64,256]{1,0:T(8,128)S(1)} %add_add_fusion.1), channel_id=1, source_target_pairs={{0,16},{1,17},{2,18},{3,19},{4,20},{5,21},{6,22},{7,23},{8,24},{9,... | collective-permute-start | bytes 196616 | tf_op jit(solution)/shard_map/ppermute | solution.py:241
  125.2 3.6 %collective-permute-done.35 = f32[64,256]{1,0:T(8,128)S(1)} collective-permute-done((f32[64,256]{1,0:T(8,128)S(1)}, f32[64,256]{1,0:T(8,128)S(1)}, u32[]{:S(2)}, u32[]{:S(2)}) %collective-permute-start.35) | collective-permute-done | bytes 65568 | tf_op jit(solution)/shard_map/ppermute | solution.py:241
  128.8 3.2 %collective-permute-start.36 = (f32[64,256]{1,0:T(8,128)S(1)}, f32[64,256]{1,0:T(8,128)S(1)}, u32[]{:S(2)}, u32[]{:S(2)}) collective-permute-start(f32[64,256]{1,0:T(8,128)S(1)} %add_add_fusion.1), channel_id=1, source_target_pairs={{0,24},{1,25},{2,26},{3,27},{4,28},{5,29},{6,30},{7,31},{8,16},{9,... | collective-permute-start | bytes 196616 | tf_op jit(solution)/shard_map/ppermute | solution.py:241
  132.1 0.1 compare_reduce_fusion
  132.1 2.7 %collective-permute-done.36 = f32[64,256]{1,0:T(8,128)S(1)} collective-permute-done((f32[64,256]{1,0:T(8,128)S(1)}, f32[64,256]{1,0:T(8,128)S(1)}, u32[]{:S(2)}, u32[]{:S(2)}) %collective-permute-start.36) | collective-permute-done | bytes 65568 | tf_op jit(solution)/shard_map/ppermute | solution.py:241
  134.9 4.5 %collective-permute-start.29 = (f32[512,256]{1,0:T(8,128)}, f32[512,256]{1,0:T(8,128)S(1)}, u32[]{:S(2)}, u32[]{:S(2)}) collective-permute-start(f32[512,256]{1,0:T(8,128)} %get-tuple-element.7), channel_id=1, source_target_pairs={{0,1},{1,0},{2,3},{3,2},{4,5},{5,4},{6,7},{7,6},{8,9},{9,8},{10,11... | collective-permute-start | bytes 1572872 | tf_op jit(solution)/shard_map/ppermute | solution.py:241
  139.5 0.4 collective-permute-start.37
  139.8 2.0 %shard_map.135 = f32[512,256]{1,0:T(8,128)S(1)} custom-call(s32[36]{0:T(128)S(1)} %get-tuple-element.25.table, f32[512,4096]{1,0:T(8,128)} %refs_0_.7, f32[512,256]{1,0:T(8,128)S(1)} %collective-permute-done.refs_1_, f32[512,256]{1,0:T(8,128)S(1)} %collective-permute-done.1.refs_2_, f32[512,256]{1,0:T(8,128)S(1)} %collective-permute-done.2.refs_3_, ...), custom_call_target="tpu_custom_call" | custom-call | flops 805306368 | bytes 4194304 | tf_op jit(solution)/shard_map/pallas_call | solution.py:187
  141.9 1.9 %collective-permute-done.37 = f32[64,256]{1,0:T(8,128)S(1)} collective-permute-done((f32[64,256]{1,0:T(8,128)S(1)}, f32[64,256]{1,0:T(8,128)S(1)}, u32[]{:S(2)}, u32[]{:S(2)}) %collective-permute-start.37) | collective-permute-done | bytes 65568 | tf_op jit(solution)/shard_map/ppermute | solution.py:241
  143.9 6.1 %collective-permute-done.29 = f32[512,256]{1,0:T(8,128)S(1)} collective-permute-done((f32[512,256]{1,0:T(8,128)}, f32[512,256]{1,0:T(8,128)S(1)}, u32[]{:S(2)}, u32[]{:S(2)}) %collective-permute-start.29) | collective-permute-done | bytes 524320 | tf_op jit(solution)/shard_map/ppermute | solution.py:241
  150.0 0.9 negate_select_fusion
  151.0 0.7 maximum_add_fusion
  (61 shorter events, 0.9 us)
Async XLA Ops:
  0.6 15.7 %collective-permute-start.18 = (f32[512,256]{1,0:T(8,128)}, f32[512,256]{1,0:T(8,128)S(1)}, u32[]{:S(2)}, u32[]{:S(2)}) collective-permute-start(f32[512,256]{1,0:T(8,128)} %refs_11_.1), channel_id=1, source_target_pairs={{0,1},{1,0},{2,3},{3,2},{4,5},{5,4},{6,7},{7,6},{8,9},{9,8},{10,11... | collective-permute-start | bytes 1572872 | tf_op jit(solution)/shard_map/ppermute | solution.py:241
  3.7 12.6 %collective-permute-start.19 = (f32[512,256]{1,0:T(8,128)}, f32[512,256]{1,0:T(8,128)S(1)}, u32[]{:S(2)}, u32[]{:S(2)}) collective-permute-start(f32[512,256]{1,0:T(8,128)} %refs_11_.1), channel_id=1, source_target_pairs={{1,16},{3,18},{5,20},{7,22},{9,24},{11,26},{13,28},{15,30},{16,1},... | collective-permute-start | bytes 1572872 | tf_op jit(solution)/shard_map/ppermute | solution.py:241
  4.4 25.3 %collective-permute-start.8 = (f32[512,256]{1,0:T(8,128)}, f32[512,256]{1,0:T(8,128)S(1)}, u32[]{:S(2)}, u32[]{:S(2)}) collective-permute-start(f32[512,256]{1,0:T(8,128)} %refs_11_.1), channel_id=1, source_target_pairs={{0,4},{2,6},{4,0},{6,2},{8,12},{10,14},{12,8},{14,10},{17,21},{19,... | collective-permute-start | bytes 1572872 | tf_op jit(solution)/shard_map/ppermute | solution.py:241
  7.8 27.0 %collective-permute-start.9 = (f32[512,256]{1,0:T(8,128)}, f32[512,256]{1,0:T(8,128)S(1)}, u32[]{:S(2)}, u32[]{:S(2)}) collective-permute-start(f32[512,256]{1,0:T(8,128)} %refs_11_.1), channel_id=1, source_target_pairs={{0,8},{2,10},{4,12},{6,14},{8,0},{10,2},{12,4},{14,6},{17,25},{19,... | collective-permute-start | bytes 1572872 | tf_op jit(solution)/shard_map/ppermute | solution.py:241
  11.3 26.3 %collective-permute-start.17 = (s32[1,16]{1,0:T(1,128)}, s32[1,16]{1,0:T(1,128)S(1)}, u32[]{:S(2)}, u32[]{:S(2)}) collective-permute-start(s32[1,16]{1,0:T(1,128)} %param.14), channel_id=1, source_target_pairs={{0,1},{1,0},{2,3},{3,2},{4,5},{5,4},{6,7},{7,6},{8,9},{9,8},{10,11... | collective-permute-start | bytes 200 | tf_op jit(solution)/shard_map/ppermute | solution.py:241
  16.4 34.4 %collective-permute-start.20 = (f32[512,256]{1,0:T(8,128)S(1)}, f32[512,256]{1,0:T(8,128)S(1)}, u32[]{:S(2)}, u32[]{:S(2)}) collective-permute-start(f32[512,256]{1,0:T(8,128)S(1)} %broadcast_select_fusion.refs_1_), channel_id=1, source_target_pairs={{0,4},{1,5},{2,6},{3,7},{4,0},{5,1},{6,2},{7,3},{8,12},{9,13},{10,... | collective-permute-start | bytes 1572872 | tf_op jit(solution)/shard_map/ppermute | solution.py:241
  17.9 32.9 %collective-permute-start.22 = (f32[512,256]{1,0:T(8,128)S(1)}, f32[512,256]{1,0:T(8,128)S(1)}, u32[]{:S(2)}, u32[]{:S(2)}) collective-permute-start(f32[512,256]{1,0:T(8,128)S(1)} %broadcast_select_fusion.refs_1_), channel_id=1, source_target_pairs={{0,8},{1,9},{2,10},{3,11},{4,12},{5,13},{6,14},{7,15},{8,0},{9,1},... | collective-permute-start | bytes 1572872 | tf_op jit(solution)/shard_map/ppermute | solution.py:241
  30.4 19.6 %collective-permute-start.13 = (f32[256,256]{1,0:T(8,128)}, f32[256,256]{1,0:T(8,128)S(1)}, u32[]{:S(2)}, u32[]{:S(2)}) collective-permute-start(f32[256,256]{1,0:T(8,128)} %slice.56), channel_id=1, source_target_pairs={{0,8},{2,10},{4,12},{6,14},{8,0},{10,2},{12,4},{14,6},{17,25},{19,... | collective-permute-start | bytes 786440 | tf_op jit(solution)/shard_map/ppermute | solution.py:241
  35.5 14.4 %collective-permute-start.14 = (f32[256,256]{1,0:T(8,128)}, f32[256,256]{1,0:T(8,128)}, u32[]{:S(2)}, u32[]{:S(2)}) collective-permute-start(f32[256,256]{1,0:T(8,128)} %slice.57), channel_id=1, source_target_pairs={{0,4},{2,6},{4,0},{6,2},{8,12},{10,14},{12,8},{14,10},{17,21},{19,... | collective-permute-start | bytes 786440 | tf_op jit(solution)/shard_map/ppermute | solution.py:241
  37.6 14.0 %collective-permute-start.10 = (f32[512,256]{1,0:T(8,128)}, f32[512,256]{1,0:T(8,128)S(1)}, u32[]{:S(2)}, u32[]{:S(2)}) collective-permute-start(f32[512,256]{1,0:T(8,128)} %refs_11_.1), channel_id=1, source_target_pairs={{0,2},{1,3},{2,0},{3,1},{4,6},{5,7},{6,4},{7,5},{8,10},{9,11},{10,... | collective-permute-start | bytes 1572872 | tf_op jit(solution)/shard_map/ppermute | solution.py:241
  50.0 3.9 %collective-permute-start.11 = (f32[512,256]{1,0:T(8,128)S(1)}, f32[512,256]{1,0:T(8,128)S(1)}, u32[]{:S(2)}, u32[]{:S(2)}) collective-permute-start(f32[512,256]{1,0:T(8,128)S(1)} %collective-permute-done.8.refs_2_), channel_id=1, source_target_pairs={{0,2},{1,3},{2,0},{3,1},{4,6},{5,7},{6,4},{7,5},{8,10},{9,11},{10,... | collective-permute-start | bytes 1572872 | tf_op jit(solution)/shard_map/ppermute | solution.py:241
  50.0 3.9 %collective-permute-start.12 = (f32[512,256]{1,0:T(8,128)S(1)}, f32[512,256]{1,0:T(8,128)S(1)}, u32[]{:S(2)}, u32[]{:S(2)}) collective-permute-start(f32[512,256]{1,0:T(8,128)S(1)} %collective-permute-done.9.refs_3_), channel_id=1, source_target_pairs={{0,2},{1,3},{2,0},{3,1},{4,6},{5,7},{6,4},{7,5},{8,10},{9,11},{10,... | collective-permute-start | bytes 1572872 | tf_op jit(solution)/shard_map/ppermute | solution.py:241
  50.8 2.3 %collective-permute-start.15 = (f32[256,256]{1,0:T(8,128)S(1)}, f32[256,256]{1,0:T(8,128)S(1)}, u32[]{:S(2)}, u32[]{:S(2)}) collective-permute-start(f32[256,256]{1,0:T(8,128)S(1)} %collective-permute-done.13.refs_7_), channel_id=1, source_target_pairs={{0,2},{1,3},{2,0},{3,1},{4,6},{5,7},{6,4},{7,5},{8,10},{9,11},{10,... | collective-permute-start | bytes 786440 | tf_op jit(solution)/shard_map/ppermute | solution.py:241
  50.8 2.5 %collective-permute-start.16 = (f32[256,256]{1,0:T(8,128)}, f32[256,256]{1,0:T(8,128)S(1)}, u32[]{:S(2)}, u32[]{:S(2)}) collective-permute-start(f32[256,256]{1,0:T(8,128)} %collective-permute-done.14.refs_8_), channel_id=1, source_target_pairs={{0,2},{1,3},{2,0},{3,1},{4,6},{5,7},{6,4},{7,5},{8,10},{9,11},{10,... | collective-permute-start | bytes 786440 | tf_op jit(solution)/shard_map/ppermute | solution.py:241
  51.6 10.3 %collective-permute-start.26 = (f32[512,256]{1,0:T(8,128)S(1)}, f32[512,256]{1,0:T(8,128)S(1)}, u32[]{:S(2)}, u32[]{:S(2)}) collective-permute-start(f32[512,256]{1,0:T(8,128)S(1)} %broadcast_select_fusion.refs_1_), channel_id=1, source_target_pairs={{0,2},{1,3},{2,0},{3,1},{4,6},{5,7},{6,4},{7,5},{8,10},{9,11},{10,... | collective-permute-start | bytes 1572872 | tf_op jit(solution)/shard_map/ppermute | solution.py:241
  53.0 8.3 %collective-permute-start.21 = (f32[256,256]{1,0:T(8,128)S(1)}, f32[256,256]{1,0:T(8,128)S(1)}, u32[]{:S(2)}, u32[]{:S(2)}) collective-permute-start(f32[256,256]{1,0:T(8,128)S(1)} %slice.58), channel_id=1, source_target_pairs={{0,8},{1,9},{2,10},{3,11},{4,12},{5,13},{6,14},{7,15},{8,0},{9,1},... | collective-permute-start | bytes 786440 | tf_op jit(solution)/shard_map/ppermute | solution.py:241
  53.4 8.4 %collective-permute-start.23 = (f32[256,256]{1,0:T(8,128)S(1)}, f32[256,256]{1,0:T(8,128)S(1)}, u32[]{:S(2)}, u32[]{:S(2)}) collective-permute-start(f32[256,256]{1,0:T(8,128)S(1)} %slice.59), channel_id=1, source_target_pairs={{0,4},{1,5},{2,6},{3,7},{4,0},{5,1},{6,2},{7,3},{8,12},{9,13},{10,... | collective-permute-start | bytes 786440 | tf_op jit(solution)/shard_map/ppermute | solution.py:241
  53.9 9.3 %collective-permute-start.27 = (f32[512,256]{1,0:T(8,128)S(1)}, f32[512,256]{1,0:T(8,128)S(1)}, u32[]{:S(2)}, u32[]{:S(2)}) collective-permute-start(f32[512,256]{1,0:T(8,128)S(1)} %collective-permute-done.20.refs_2_), channel_id=1, source_target_pairs={{0,2},{1,3},{2,0},{3,1},{4,6},{5,7},{6,4},{7,5},{8,10},{9,11},{10,... | collective-permute-start | bytes 1572872 | tf_op jit(solution)/shard_map/ppermute | solution.py:241
  53.9 9.3 %collective-permute-start.28 = (f32[512,256]{1,0:T(8,128)S(1)}, f32[512,256]{1,0:T(8,128)S(1)}, u32[]{:S(2)}, u32[]{:S(2)}) collective-permute-start(f32[512,256]{1,0:T(8,128)S(1)} %collective-permute-done.22.refs_3_), channel_id=1, source_target_pairs={{0,2},{1,3},{2,0},{3,1},{4,6},{5,7},{6,4},{7,5},{8,10},{9,11},{10,... | collective-permute-start | bytes 1572872 | tf_op jit(solution)/shard_map/ppermute | solution.py:241
  61.4 5.8 %collective-permute-start.24 = (f32[256,256]{1,0:T(8,128)S(1)}, f32[256,256]{1,0:T(8,128)S(1)}, u32[]{:S(2)}, u32[]{:S(2)}) collective-permute-start(f32[256,256]{1,0:T(8,128)S(1)} %collective-permute-done.21.refs_1_), channel_id=1, source_target_pairs={{0,2},{1,3},{2,0},{3,1},{4,6},{5,7},{6,4},{7,5},{8,10},{9,11},{10,... | collective-permute-start | bytes 786440 | tf_op jit(solution)/shard_map/ppermute | solution.py:241
  61.8 5.4 %collective-permute-start.25 = (f32[256,256]{1,0:T(8,128)S(1)}, f32[256,256]{1,0:T(8,128)S(1)}, u32[]{:S(2)}, u32[]{:S(2)}) collective-permute-start(f32[256,256]{1,0:T(8,128)S(1)} %collective-permute-done.23.refs_2_), channel_id=1, source_target_pairs={{0,2},{1,3},{2,0},{3,1},{4,6},{5,7},{6,4},{7,5},{8,10},{9,11},{10,... | collective-permute-start | bytes 786440 | tf_op jit(solution)/shard_map/ppermute | solution.py:241
  61.9 13.7 %collective-permute-start = (f32[512,256]{1,0:T(8,128)}, f32[512,256]{1,0:T(8,128)S(1)}, u32[]{:S(2)}, u32[]{:S(2)}) collective-permute-start(f32[512,256]{1,0:T(8,128)} %refs_11_.1), channel_id=1, source_target_pairs={{0,16},{2,18},{4,20},{6,22},{8,24},{10,26},{12,28},{14,30},{17,1},... | collective-permute-start | bytes 1572872 | tf_op jit(solution)/shard_map/ppermute | solution.py:241
  67.2 64.9 %copy-start.1 = (s32[1,16]{1,0:T(1,128)S(1)}, s32[1,16]{1,0:T(1,128)}, u32[]{:S(2)}) copy-start(s32[1,16]{1,0:T(1,128)} %param.14) | copy-start | bytes 196
  70.7 7.0 %collective-permute-start.30 = (f32[256,256]{1,0:T(8,128)S(1)}, f32[256,256]{1,0:T(8,128)S(1)}, u32[]{:S(2)}, u32[]{:S(2)}) collective-permute-start(f32[256,256]{1,0:T(8,128)S(1)} %pad_maximum_fusion), channel_id=1, source_target_pairs={{0,2},{1,3},{2,0},{3,1},{4,6},{5,7},{6,4},{7,5},{8,10},{9,11},{10,... | collective-permute-start | bytes 786440 | tf_op jit(solution)/shard_map/ppermute | solution.py:241
  75.6 26.1 %collective-permute-start.1 = (f32[512,256]{1,0:T(8,128)S(1)}, f32[512,256]{1,0:T(8,128)S(1)}, u32[]{:S(2)}, u32[]{:S(2)}) collective-permute-start(f32[512,256]{1,0:T(8,128)S(1)} %collective-permute-done.refs_1_), channel_id=1, source_target_pairs={{1,5},{3,7},{5,1},{7,3},{9,13},{11,15},{13,9},{15,11},{16,20},{18,... | collective-permute-start | bytes 1572872 | tf_op jit(solution)/shard_map/ppermute | solution.py:241
  76.3 27.0 %collective-permute-start.2 = (f32[512,256]{1,0:T(8,128)S(1)}, f32[512,256]{1,0:T(8,128)S(1)}, u32[]{:S(2)}, u32[]{:S(2)}) collective-permute-start(f32[512,256]{1,0:T(8,128)S(1)} %collective-permute-done.refs_1_), channel_id=1, source_target_pairs={{1,9},{3,11},{5,13},{7,15},{9,1},{11,3},{13,5},{15,7},{16,24},{18,... | collective-permute-start | bytes 1572872 | tf_op jit(solution)/shard_map/ppermute | solution.py:241
  77.0 26.3 %collective-permute-start.6 = (f32[512,256]{1,0:T(8,128)S(1)}, f32[512,256]{1,0:T(8,128)S(1)}, u32[]{:S(2)}, u32[]{:S(2)}) collective-permute-start(f32[512,256]{1,0:T(8,128)S(1)} %collective-permute-done.refs_1_), channel_id=1, source_target_pairs={{1,13},{3,15},{5,9},{7,11},{9,5},{11,7},{13,1},{15,3},{16,28},{18,... | collective-permute-start | bytes 1572872 | tf_op jit(solution)/shard_map/ppermute | solution.py:241
  77.8 26.1 %collective-permute-start.32 = (f32[64,256]{1,0:T(8,128)S(1)}, f32[64,256]{1,0:T(8,128)S(1)}, u32[]{:S(2)}, u32[]{:S(2)}) collective-permute-start(f32[64,256]{1,0:T(8,128)S(1)} %get-tuple-element.16), channel_id=1, source_target_pairs={{0,1},{1,0},{2,3},{3,2},{4,5},{5,4},{6,7},{7,6},{8,9},{9,8},{10,11... | collective-permute-start | bytes 196616 | tf_op jit(solution)/shard_map/ppermute | solution.py:241
  101.7 7.3 %collective-permute-start.33 = (f32[64,256]{1,0:T(8,128)S(1)}, f32[64,256]{1,0:T(8,128)S(1)}, u32[]{:S(2)}, u32[]{:S(2)}) collective-permute-start(f32[64,256]{1,0:T(8,128)S(1)} %get-tuple-element.17), channel_id=1, source_target_pairs={{0,5},{1,4},{2,7},{3,6},{4,1},{5,0},{6,3},{7,2},{8,13},{9,12},{10,... | collective-permute-start | bytes 196616 | tf_op jit(solution)/shard_map/ppermute | solution.py:241
  101.7 7.2 %collective-permute-start.31 = (f32[64,256]{1,0:T(8,128)S(1)}, f32[64,256]{1,0:T(8,128)S(1)}, u32[]{:S(2)}, u32[]{:S(2)}) collective-permute-start(f32[64,256]{1,0:T(8,128)S(1)} %slice_select_fusion.4), channel_id=1, source_target_pairs={{0,4},{1,5},{2,6},{3,7},{4,0},{5,1},{6,2},{7,3},{8,12},{9,13},{10,... | collective-permute-start | bytes 196616 | tf_op jit(solution)/shard_map/ppermute | solution.py:241
  103.3 36.1 %collective-permute-start.3 = (f32[512,256]{1,0:T(8,128)S(1)}, f32[512,256]{1,0:T(8,128)S(1)}, u32[]{:S(2)}, u32[]{:S(2)}) collective-permute-start(f32[512,256]{1,0:T(8,128)S(1)} %collective-permute-done.refs_1_), channel_id=1, source_target_pairs={{0,2},{1,3},{2,0},{3,1},{4,6},{5,7},{6,4},{7,5},{8,10},{9,11},{10,... | collective-permute-start | bytes 1572872 | tf_op jit(solution)/shard_map/ppermute | solution.py:241
  103.3 36.5 %collective-permute-start.4 = (f32[512,256]{1,0:T(8,128)S(1)}, f32[512,256]{1,0:T(8,128)}, u32[]{:S(2)}, u32[]{:S(2)}) collective-permute-start(f32[512,256]{1,0:T(8,128)S(1)} %collective-permute-done.1.refs_2_), channel_id=1, source_target_pairs={{0,2},{1,3},{2,0},{3,1},{4,6},{5,7},{6,4},{7,5},{8,10},{9,11},{10,... | collective-permute-start | bytes 1572872 | tf_op jit(solution)/shard_map/ppermute | solution.py:241
  103.9 35.9 %collective-permute-start.5 = (f32[512,256]{1,0:T(8,128)S(1)}, f32[512,256]{1,0:T(8,128)}, u32[]{:S(2)}, u32[]{:S(2)}) collective-permute-start(f32[512,256]{1,0:T(8,128)S(1)} %collective-permute-done.2.refs_3_), channel_id=1, source_target_pairs={{0,2},{1,3},{2,0},{3,1},{4,6},{5,7},{6,4},{7,5},{8,10},{9,11},{10,... | collective-permute-start | bytes 1572872 | tf_op jit(solution)/shard_map/ppermute | solution.py:241
  108.9 30.9 %collective-permute-start.7 = (f32[512,256]{1,0:T(8,128)S(1)}, f32[512,256]{1,0:T(8,128)}, u32[]{:S(2)}, u32[]{:S(2)}) collective-permute-start(f32[512,256]{1,0:T(8,128)S(1)} %collective-permute-done.6.refs_7_), channel_id=1, source_target_pairs={{0,2},{1,3},{2,0},{3,1},{4,6},{5,7},{6,4},{7,5},{8,10},{9,11},{10,... | collective-permute-start | bytes 1572872 | tf_op jit(solution)/shard_map/ppermute | solution.py:241
  109.0 42.0 %copy-start = (f32[256,256]{1,0:T(8,128)S(1)}, f32[256,256]{1,0:T(8,128)}, u32[]{:S(2)}) copy-start(f32[256,256]{1,0:T(8,128)} %param.15) | copy-start | bytes 786436
  109.0 4.6 %collective-permute-start.34 = (f32[64,256]{1,0:T(8,128)S(1)}, f32[64,256]{1,0:T(8,128)S(1)}, u32[]{:S(2)}, u32[]{:S(2)}) collective-permute-start(f32[64,256]{1,0:T(8,128)S(1)} %add_add_fusion.1), channel_id=1, source_target_pairs={{0,8},{1,9},{2,10},{3,11},{4,12},{5,13},{6,14},{7,15},{8,0},{9,1},... | collective-permute-start | bytes 196616 | tf_op jit(solution)/shard_map/ppermute | solution.py:241
  113.6 15.3 %collective-permute-start.35 = (f32[64,256]{1,0:T(8,128)S(1)}, f32[64,256]{1,0:T(8,128)S(1)}, u32[]{:S(2)}, u32[]{:S(2)}) collective-permute-start(f32[64,256]{1,0:T(8,128)S(1)} %add_add_fusion.1), channel_id=1, source_target_pairs={{0,16},{1,17},{2,18},{3,19},{4,20},{5,21},{6,22},{7,23},{8,24},{9,... | collective-permute-start | bytes 196616 | tf_op jit(solution)/shard_map/ppermute | solution.py:241
  128.8 6.1 %collective-permute-start.36 = (f32[64,256]{1,0:T(8,128)S(1)}, f32[64,256]{1,0:T(8,128)S(1)}, u32[]{:S(2)}, u32[]{:S(2)}) collective-permute-start(f32[64,256]{1,0:T(8,128)S(1)} %add_add_fusion.1), channel_id=1, source_target_pairs={{0,24},{1,25},{2,26},{3,27},{4,28},{5,29},{6,30},{7,31},{8,16},{9,... | collective-permute-start | bytes 196616 | tf_op jit(solution)/shard_map/ppermute | solution.py:241
  134.9 15.1 %collective-permute-start.29 = (f32[512,256]{1,0:T(8,128)}, f32[512,256]{1,0:T(8,128)S(1)}, u32[]{:S(2)}, u32[]{:S(2)}) collective-permute-start(f32[512,256]{1,0:T(8,128)} %get-tuple-element.7), channel_id=1, source_target_pairs={{0,1},{1,0},{2,3},{3,2},{4,5},{5,4},{6,7},{7,6},{8,9},{9,8},{10,11... | collective-permute-start | bytes 1572872 | tf_op jit(solution)/shard_map/ppermute | solution.py:241
  139.5 4.3 %collective-permute-start.37 = (f32[64,256]{1,0:T(8,128)S(1)}, f32[64,256]{1,0:T(8,128)S(1)}, u32[]{:S(2)}, u32[]{:S(2)}) collective-permute-start(f32[64,256]{1,0:T(8,128)S(1)} %add_add_fusion), channel_id=1, source_target_pairs={{0,4},{1,5},{2,6},{3,7},{4,0},{5,1},{6,2},{7,3},{8,12},{9,13},{10,... | collective-permute-start | bytes 196616 | tf_op jit(solution)/shard_map/ppermute | solution.py:241
  143.8 7.1 %collective-permute-start.38 = (f32[128,256]{1,0:T(8,128)S(1)}, f32[128,256]{1,0:T(8,128)S(1)}, u32[]{:S(2)}, u32[]{:S(2)}) collective-permute-start(f32[128,256]{1,0:T(8,128)S(1)} %pad_maximum_fusion.1), channel_id=1, source_target_pairs={{0,2},{1,3},{2,0},{3,1},{4,6},{5,7},{6,4},{7,5},{8,10},{9,11},{10,... | collective-permute-start | bytes 393224 | tf_op jit(solution)/shard_map/ppermute | solution.py:241

commit v9 on v8

--- a/solution.py
+++ b/solution.py
@@ -76,7 +76,7 @@
     has_acc = mode == "sum"
     extra_in = refs.pop(0) if final else None
     out = refs.pop(0)
-    terms = refs.pop(0) if final else None
+    terms = refs.pop(0) if final == "terms" else None
     a_buf, p_buf, extra, a_sem, p_sem, one_sem = refs
     row_on = [table[2 * count + rb] > 0 for rb in range(blocks)]
     all_on = functools.reduce(jnp.logical_and, row_on)
@@ -155,6 +155,11 @@
             step(p, 0)
     if final:
         extra_copy.wait()
+    if final == "panel":
+        for rb in range(blocks):
+            rows = pl.ds(rb * width, width)
+            out[rows, :] = jnp.where(row_on[rb], -(out[rows, :] + extra[rows, :]), jnp.float32(0.0))
+    if final == "terms":
         terms[...] = jnp.zeros_like(terms)
         for rb in range(blocks):
             rows = pl.ds(rb * width, width)
@@ -168,7 +173,7 @@
             terms[...] += terms[...].T
 
 
-def product(table, inverse_anc, arrays, slots, width, acc=None, extra=None, kind=jax.ShapeDtypeStruct, mode=None):
+def product(table, inverse_anc, arrays, slots, width, acc=None, extra=None, kind=jax.ShapeDtypeStruct, mode=None, final=None):
     rows = inverse_anc.shape[0]
     blocks = rows // width
     count = len(slots)
@@ -182,10 +187,10 @@
             operands.append(more)
             specs.append(any_spec)
     shapes = [kind((rows, width), jnp.float32)]
-    if extra is not None:
+    if final == "terms":
         shapes.append(jax.ShapeDtypeStruct((width, width), jnp.float32))
     return pl.pallas_call(
-        functools.partial(product_kernel, slots, blocks, width, mode, extra is not None),
+        functools.partial(product_kernel, slots, blocks, width, mode, final),
         out_shape=shapes,
         grid_spec=pltpu.PrefetchScalarGridSpec(
             num_scalar_prefetch=1,
@@ -215,9 +220,7 @@
 SECOND = tuple((Z | X | c, h) for c in (0, 1) for h in (0, 1))
 SLOTS1 = tuple((i, h) for i in range(6) for h in (0, 1))
 SLOTS2 = tuple((i, 0) for i in range(4))
-WHOLE = FIRST + tuple((Z | X | c, h) for c in (0, 1) for h in (0, 1))
-SLOTSW = SLOTS1 + tuple((6 + i, h) for i in range(2) for h in (0, 1))
-SLOTS12 = SLOTS1 + tuple((6 + i, 0) for i in range(4))
+SLOTS2B = tuple((i, h) for i in range(2) for h in (0, 1))
 
 
 def local_two(n_row, inverse_anc, lower_panel, structure, diag_inverse):
@@ -240,15 +243,17 @@
         ]
         return lax.ppermute(value, BOTH, pairs)
 
-    def table(listed, order, who):
+    def table(listed, order, who, everywhere=False):
         block = ((row % FAR) ^ jnp.array([m for m, _ in order], jnp.int32)) * 2
         block = block + jnp.array([h for _, h in order], jnp.int32)
         ids = jnp.concatenate([block + col * 2 * FAR, row * 2 + jnp.arange(2, dtype=jnp.int32)])
         on = jnp.any(ids[:, None] == listed[0][None, :], axis=1)
+        count = len(order)
         if who is not None:
-            on = on & (near == who)
-        far = jnp.logical_not(near) if who is None else jnp.zeros((), jnp.bool_)
-        active = near == who if who is not None else jnp.ones((), jnp.bool_)
+            served = (near == who) | (everywhere & (jnp.arange(count + 2) >= count))
+            on = on & served
+        far = jnp.logical_not(near) & jnp.bool_(who is None and order == SECOND)
+        active = near == who if who is not None and not everywhere else jnp.ones((), jnp.bool_)
         flags = jnp.concatenate([on, far[None], active[None]])
         return jnp.concatenate([block, flags.astype(jnp.int32)])
 
@@ -274,6 +279,7 @@
     n_second = with_sibling(n_two, None)
     q_other = jnp.where(near, lower_other, got_far)
     o_one = step_one(q_other, None)
+    other_structure, _ = lax.optimization_barrier((other_structure, o_one[0]))
     o_two = step_two(o_one, None)
     o_first = with_sibling([q_other, *o_one], None)
     o_second = with_sibling(o_two, None)
@@ -282,22 +288,26 @@
     f_first = with_sibling([q_far, *f_one], None)
     f_second = with_sibling(f_two, None)
 
+    (own,) = product(table(structure, FIRST, True), inverse_anc, n_first, SLOTS1, width)
+    (part,) = product(table(other_structure, FIRST, None), inverse_anc, o_first, SLOTS1, width)
+    own, part = lax.optimization_barrier((own, part))
     own, own_terms = product(
-        table(structure, FIRST + SECOND, True), inverse_anc, n_first + n_second, SLOTS12, width,
-        extra=n_first[0], kind=pltpu.HBM,
-    )
-    (part,) = product(table(other_structure, FIRST, None), inverse_anc, o_first, SLOTS1, width)
+        table(structure, SECOND, True), inverse_anc, n_second, SLOTS2, width,
+        acc=own, extra=n_first[0], kind=pltpu.HBM, mode="sum", final="terms",
+    )
     part, other_terms = product(
         table(other_structure, SECOND, None), inverse_anc, o_second, SLOTS2, width,
-        acc=part, extra=lower_other, kind=pltpu.HBM, mode="sum",
+        acc=part, extra=lower_other, kind=pltpu.HBM, mode="sum", final="terms",
     )
     recv = move(part, 0, 1)
     (own,) = product(
-        table(structure, WHOLE, False), inverse_anc, f_first + f_second, SLOTSW, width,
+        table(structure, FIRST, False), inverse_anc, f_first, SLOTS1, width,
         acc=in_hbm(own), mode="keep",
     )
-    keep = keep_rows(structure, row * rows, rows, width)
-    panel = jnp.where(keep, -(own + recv), jnp.float32(0.0))
+    (panel,) = product(
+        table(structure, SECOND, False, True), inverse_anc, f_second, SLOTS2B, width,
+        acc=own, extra=recv, mode="sum", final="panel",
+    )
 
     def parts(value, mask):
         size = value.shape[0] // 2

time: 152 us -> 160 us (1.053)
  starting transfers between devices: 81.7 us -> 99.2 us
  waiting for transfers between devices: 48.9 us -> 38.2 us
  Pallas kernels: 12.5 us -> 15.4 us
    ppermute x39, starting transfers between devices: 81.7 us -> 99.2 us  [move(): return lax.ppermute(value, BOTH, pairs)]
    ppermute x39, waiting for transfers between devices: 48.9 us -> 38.2 us  [move(): return lax.ppermute(value, BOTH, pairs)]
    pallas_call x4 -> x6, Pallas kernels: 12.5 us -> 15.4 us  [product(): pl.pallas_call(functools.partial(product_kernel, slots, blocks, width, mo...]
  transfers between devices with their start and end apart: 39 -> 39, of which waited for: 14 -> 9; matrix products, arithmetic and copies ran while one was open for 4% -> 3% of each run, Pallas kernels for 8% -> 7%
where the time goes in v9:
time: 160 us; the launch traced here: 159 us
  starting transfers between devices  99.2 us (62%)
  waiting for transfers between devices  38.2 us (24%)
  Pallas kernels  15.4 us (10%)
  other arithmetic  4.76 us (3%)
    ppermute x39, starting transfers between devices, move(): return lax.ppermute(value, BOTH, pairs)  99.2 us
    ppermute x39, waiting for transfers between devices, move(): return lax.ppermute(value, BOTH, pairs)  38.2 us
    pallas_call x6, Pallas kernels, product(): pl.pallas_call(functools.partial(product_kernel, slots, blocks, width, mo...  15.4 us
  transfers between devices with their start and end apart: 39, of which 9 were waited for; matrix products, arithmetic and copies ran while one was open for 3% of the time, Pallas kernels for 7%

profile of v9, /device:TPU:0, one launch (start us, length us, event | category | flops | bytes accessed | tf_op | source)
XLA Modules:
  0.0 158.7 jit_solution(17653024891286894964)
XLA Ops:
  0.6 3.1 %collective-permute-start.18 = (f32[512,256]{1,0:T(8,128)}, f32[512,256]{1,0:T(8,128)S(1)}, u32[]{:S(2)}, u32[]{:S(2)}) collective-permute-start(f32[512,256]{1,0:T(8,128)} %refs_6_.1), channel_id=1, source_target_pairs={{0,1},{1,0},{2,3},{3,2},{4,5},{5,4},{6,7},{7,6},{8,9},{9,8},{10,11... | collective-permute-start | bytes 1572872 | tf_op jit(solution)/shard_map/ppermute | solution.py:244
  3.7 0.7 collective-permute-start.19
  4.4 3.4 %collective-permute-start.8 = (f32[512,256]{1,0:T(8,128)}, f32[512,256]{1,0:T(8,128)S(1)}, u32[]{:S(2)}, u32[]{:S(2)}) collective-permute-start(f32[512,256]{1,0:T(8,128)} %refs_6_.1), channel_id=1, source_target_pairs={{0,4},{2,6},{4,0},{6,2},{8,12},{10,14},{12,8},{14,10},{17,21},{19,... | collective-permute-start | bytes 1572872 | tf_op jit(solution)/shard_map/ppermute | solution.py:244
  7.8 3.5 %collective-permute-start.10 = (f32[512,256]{1,0:T(8,128)}, f32[512,256]{1,0:T(8,128)S(1)}, u32[]{:S(2)}, u32[]{:S(2)}) collective-permute-start(f32[512,256]{1,0:T(8,128)} %refs_6_.1), channel_id=1, source_target_pairs={{0,8},{2,10},{4,12},{6,14},{8,0},{10,2},{12,4},{14,6},{17,25},{19,... | collective-permute-start | bytes 1572872 | tf_op jit(solution)/shard_map/ppermute | solution.py:244
  11.3 0.1 collective-permute-start.14
  11.4 0.7 multiply_add_fusion
  12.1 4.2 %collective-permute-done.18.refs_6_ = f32[512,256]{1,0:T(8,128)S(1)} collective-permute-done((f32[512,256]{1,0:T(8,128)}, f32[512,256]{1,0:T(8,128)S(1)}, u32[]{:S(2)}, u32[]{:S(2)}) %collective-permute-start.18) | collective-permute-done | bytes 524320 | tf_op jit(solution)/shard_map/ppermute | solution.py:244
  16.3 2.4 %collective-permute-start.17 = (s32[1,16]{1,0:T(1,128)}, s32[1,16]{1,0:T(1,128)S(1)}, u32[]{:S(2)}, u32[]{:S(2)}) collective-permute-start(s32[1,16]{1,0:T(1,128)} %param.18), channel_id=1, source_target_pairs={{0,1},{1,0},{2,3},{3,2},{4,5},{5,4},{6,7},{7,6},{8,9},{9,8},{10,11... | collective-permute-start | bytes 200 | tf_op jit(solution)/shard_map/ppermute | solution.py:244
  18.7 0.1 broadcast_select_fusion.refs_1_
  18.8 1.6 collective-permute-start.20
  20.3 0.1 pad_add_fusion.9
  20.4 0.7 multiply_add_fusion.1
  21.1 0.1 pad_add_fusion.7
  21.1 11.7 %collective-permute-start.21 = (f32[512,256]{1,0:T(8,128)S(1)}, f32[512,256]{1,0:T(8,128)S(1)}, u32[]{:S(2)}, u32[]{:S(2)}) collective-permute-start(f32[512,256]{1,0:T(8,128)S(1)} %broadcast_select_fusion.refs_1_), channel_id=1, source_target_pairs={{0,8},{1,9},{2,10},{3,11},{4,12},{5,13},{6,14},{7,15},{8,0},{9,1},... | collective-permute-start | bytes 1572872 | tf_op jit(solution)/shard_map/ppermute | solution.py:244
  32.9 1.2 collective-permute-done.10.refs_3_
  34.1 1.9 %collective-permute-start.9 = (f32[256,256]{1,0:T(8,128)S(1)}, f32[256,256]{1,0:T(8,128)S(1)}, u32[]{:S(2)}, u32[]{:S(2)}) collective-permute-start(f32[256,256]{1,0:T(8,128)S(1)} %slice.56), channel_id=1, source_target_pairs={{0,8},{2,10},{4,12},{6,14},{8,0},{10,2},{12,4},{14,6},{17,25},{19,... | collective-permute-start | bytes 786440 | tf_op jit(solution)/shard_map/ppermute | solution.py:244
  36.1 0.6 collective-permute-start.15
  36.7 0.8 compare_reduce_fusion
  37.5 0.9 compare_reduce_fusion.2
  38.4 2.3 %collective-permute-start.11 = (f32[256,256]{1,0:T(8,128)S(1)}, f32[256,256]{1,0:T(8,128)S(1)}, u32[]{:S(2)}, u32[]{:S(2)}) collective-permute-start(f32[256,256]{1,0:T(8,128)S(1)} %slice.57), channel_id=1, source_target_pairs={{0,4},{2,6},{4,0},{6,2},{8,12},{10,14},{12,8},{14,10},{17,21},{19,... | collective-permute-start | bytes 786440 | tf_op jit(solution)/shard_map/ppermute | solution.py:244
  40.7 9.3 %collective-permute-done.9.refs_1_ = f32[256,256]{1,0:T(8,128)S(1)} collective-permute-done((f32[256,256]{1,0:T(8,128)S(1)}, f32[256,256]{1,0:T(8,128)S(1)}, u32[]{:S(2)}, u32[]{:S(2)}) %collective-permute-start.9) | collective-permute-done | bytes 262176 | tf_op jit(solution)/shard_map/ppermute | solution.py:244
  50.0 0.1 fusion.6
  50.1 0.5 collective-permute-start.23
  50.6 0.1 collective-permute-start.24
  50.7 0.1 fusion.1
  50.8 5.3 %collective-permute-start.25 = (f32[256,256]{1,0:T(8,128)S(1)}, f32[256,256]{1,0:T(8,128)S(1)}, u32[]{:S(2)}, u32[]{:S(2)}) collective-permute-start(f32[256,256]{1,0:T(8,128)S(1)} %slice.58), channel_id=1, source_target_pairs={{0,8},{1,9},{2,10},{3,11},{4,12},{5,13},{6,14},{7,15},{8,0},{9,1},... | collective-permute-start | bytes 786440 | tf_op jit(solution)/shard_map/ppermute | solution.py:244
  56.1 0.1 fusion.7
  56.2 0.1 pad_add_fusion.13
  56.3 1.5 collective-permute-start.26
  57.8 1.6 %shard_map.167.refs_5_ = f32[512,256]{1,0:T(8,128)S(1)} custom-call(s32[28]{0:T(128)S(1)} %get-tuple-element.37.table, f32[512,4096]{1,0:T(8,128)} %refs_0_.11, f32[512,256]{1,0:T(8,128)} %refs_6_.1, f32[512,256]{1,0:T(8,128)S(1)} %collective-permute-done.8.refs_2_, f32[512,256]{1,0:T(8,128)S(1)} %collective-permute-done.10.refs_3_, ...), custom_call_target="tpu_custom_call" | custom-call | flops 603979776 | bytes 3145728 | tf_op jit(solution)/shard_map/pallas_call | solution.py:192
  59.4 2.6 %collective-permute-start.12 = (f32[256,256]{1,0:T(8,128)S(1)}, f32[256,256]{1,0:T(8,128)S(1)}, u32[]{:S(2)}, u32[]{:S(2)}) collective-permute-start(f32[256,256]{1,0:T(8,128)S(1)} %collective-permute-done.9.refs_1_), channel_id=1, source_target_pairs={{0,2},{1,3},{2,0},{3,1},{4,6},{5,7},{6,4},{7,5},{8,10},{9,11},{10,... | collective-permute-start | bytes 786440 | tf_op jit(solution)/shard_map/ppermute | solution.py:244
  62.0 0.5 collective-permute-done.25.refs_1_
  62.6 0.1 fusion.9
  62.7 0.1 pad_add_fusion.14
  62.7 1.5 collective-permute-done.26.refs_2_
  64.2 0.5 collective-permute-start.28
  64.7 3.9 %shard_map.168.refs_5_ = f32[512,256]{1,0:T(8,128)S(1)} custom-call(s32[28]{0:T(128)S(1)} %get-tuple-element.35.table, f32[512,4096]{1,0:T(8,128)} %refs_0_.11, f32[512,256]{1,0:T(8,128)S(1)} %broadcast_select_fusion.refs_1_, f32[512,256]{1,0:T(8,128)S(1)} %collective-permute-done.20.refs_2_, f32[512,256]{1,0:T(8,128)S(1)} %collective-permute-done.21.refs_3_, ...), custom_call_target="tpu_custom_call" | custom-call | flops 603979776 | bytes 3145728 | tf_op jit(solution)/shard_map/pallas_call | solution.py:192
  68.6 2.6 %shard_map.169 = (f32[512,256]{1,0:T(8,128)}, f32[256,256]{1,0:T(8,128)S(1)}) custom-call(s32[12]{0:T(128)S(1)} %get-tuple-element.34.table, f32[512,4096]{1,0:T(8,128)} %refs_0_.11, f32[256,256]{1,0:T(8,128)S(1)} %collective-permute-done.9.refs_1_, f32[256,256]{1,0:T(8,128)S(1)} %collective-permute-done.11.refs_2_, ...), custom_call_target="tpu_custom_call" | custom-call | flops 201326592 | bytes 1048576 | tf_op jit(solution)/shard_map/pallas_call | solution.py:192
  71.3 0.0 copy-start
  71.4 3.6 %shard_map.171 = (f32[512,256]{1,0:T(8,128)}, f32[256,256]{1,0:T(8,128)S(1)}) custom-call(s32[12]{0:T(128)S(1)} %get-tuple-element.32.table, f32[512,4096]{1,0:T(8,128)} %refs_0_.11, f32[256,256]{1,0:T(8,128)S(1)} %collective-permute-done.25.refs_1_, f32[256,256]{1,0:T(8,128)S(1)} %collective-permute-done.26.refs_2_, ...), custom_call_target="tpu_custom_call" | custom-call | flops 201326592 | bytes 1048576 | tf_op jit(solution)/shard_map/pallas_call | solution.py:192
  75.0 2.8 %collective-permute-start.30 = (f32[256,256]{1,0:T(8,128)S(1)}, f32[256,256]{1,0:T(8,128)S(1)}, u32[]{:S(2)}, u32[]{:S(2)}) collective-permute-start(f32[256,256]{1,0:T(8,128)S(1)} %pad_maximum_fusion), channel_id=1, source_target_pairs={{0,2},{1,3},{2,0},{3,1},{4,6},{5,7},{6,4},{7,5},{8,10},{9,11},{10,... | collective-permute-start | bytes 786440 | tf_op jit(solution)/shard_map/ppermute | solution.py:244
  77.9 1.3 collective-permute-start
  79.2 0.1 slice_add_fusion.1
  79.3 0.1 collective-permute-start.32
  79.4 2.3 %collective-permute-start.33 = (f32[64,256]{1,0:T(8,128)S(1)}, f32[64,256]{1,0:T(8,128)S(1)}, u32[]{:S(2)}, u32[]{:S(2)}) collective-permute-start(f32[64,256]{1,0:T(8,128)S(1)} %get-tuple-element.27), channel_id=1, source_target_pairs={{0,5},{1,4},{2,7},{3,6},{4,1},{5,0},{6,3},{7,2},{8,13},{9,12},{10,... | collective-permute-start | bytes 196616 | tf_op jit(solution)/shard_map/ppermute | solution.py:244
  81.7 1.2 collective-permute-start.31
  82.9 7.9 %collective-permute-done.refs_1_ = f32[512,256]{1,0:T(8,128)S(1)} collective-permute-done((f32[512,256]{1,0:T(8,128)S(1)}, f32[512,256]{1,0:T(8,128)S(1)}, u32[]{:S(2)}, u32[]{:S(2)}) %collective-permute-start) | collective-permute-done | bytes 524320 | tf_op jit(solution)/shard_map/ppermute | solution.py:244
  90.9 0.7 collective-permute-start.3
  91.6 0.7 collective-permute-start.4
  92.3 0.7 collective-permute-start.1
  93.0 10.7 %collective-permute-start.34 = (f32[64,256]{1,0:T(8,128)S(1)}, f32[64,256]{1,0:T(8,128)S(1)}, u32[]{:S(2)}, u32[]{:S(2)}) collective-permute-start(f32[64,256]{1,0:T(8,128)S(1)} %add_add_fusion.1), channel_id=1, source_target_pairs={{0,8},{1,9},{2,10},{3,11},{4,12},{5,13},{6,14},{7,15},{8,0},{9,1},... | collective-permute-start | bytes 196616 | tf_op jit(solution)/shard_map/ppermute | solution.py:244
  103.7 10.5 %collective-permute-start.35 = (f32[64,256]{1,0:T(8,128)S(1)}, f32[64,256]{1,0:T(8,128)S(1)}, u32[]{:S(2)}, u32[]{:S(2)}) collective-permute-start(f32[64,256]{1,0:T(8,128)S(1)} %add_add_fusion.1), channel_id=1, source_target_pairs={{0,16},{1,17},{2,18},{3,19},{4,20},{5,21},{6,22},{7,23},{8,24},{9,... | collective-permute-start | bytes 196616 | tf_op jit(solution)/shard_map/ppermute | solution.py:244
  114.2 21.9 %collective-permute-start.36 = (f32[64,256]{1,0:T(8,128)S(1)}, f32[64,256]{1,0:T(8,128)S(1)}, u32[]{:S(2)}, u32[]{:S(2)}) collective-permute-start(f32[64,256]{1,0:T(8,128)S(1)} %add_add_fusion.1), channel_id=1, source_target_pairs={{0,24},{1,25},{2,26},{3,27},{4,28},{5,29},{6,30},{7,31},{8,16},{9,... | collective-permute-start | bytes 196616 | tf_op jit(solution)/shard_map/ppermute | solution.py:244
  136.1 2.2 %collective-permute-done.36 = f32[64,256]{1,0:T(8,128)S(1)} collective-permute-done((f32[64,256]{1,0:T(8,128)S(1)}, f32[64,256]{1,0:T(8,128)S(1)}, u32[]{:S(2)}, u32[]{:S(2)}) %collective-permute-start.36) | collective-permute-done | bytes 65568 | tf_op jit(solution)/shard_map/ppermute | solution.py:244
  138.4 1.1 collective-permute-start.37
  139.5 0.5 collective-permute-start.7
  140.0 0.1 collective-permute-start.2
  140.1 2.6 %collective-permute-done.37 = f32[64,256]{1,0:T(8,128)S(1)} collective-permute-done((f32[64,256]{1,0:T(8,128)S(1)}, f32[64,256]{1,0:T(8,128)S(1)}, u32[]{:S(2)}, u32[]{:S(2)}) %collective-permute-start.37) | collective-permute-done | bytes 65568 | tf_op jit(solution)/shard_map/ppermute | solution.py:244
  142.7 2.9 %collective-permute-start.29 = (f32[512,256]{1,0:T(8,128)}, f32[512,256]{1,0:T(8,128)S(1)}, u32[]{:S(2)}, u32[]{:S(2)}) collective-permute-start(f32[512,256]{1,0:T(8,128)} %get-tuple-element.13), channel_id=1, source_target_pairs={{0,1},{1,0},{2,3},{3,2},{4,5},{5,4},{6,7},{7,6},{8,9},{9,8},{10,11... | collective-permute-start | bytes 1572872 | tf_op jit(solution)/shard_map/ppermute | solution.py:244
  145.6 0.1 collective-permute-start.38
  145.7 1.9 %shard_map.170.refs_3_ = f32[512,256]{1,0:T(8,128)S(1)} custom-call(s32[28]{0:T(128)S(1)} %get-tuple-element.36.table, f32[512,4096]{1,0:T(8,128)} %refs_0_.11, f32[512,256]{1,0:T(8,128)S(1)} %collective-permute-done.refs_1_, f32[512,256]{1,0:T(8,128)S(1)} %collective-permute-done.3.refs_2_, f32[512,256]{1,0:T(8,128)S(1)} %collective-permute-done.4.refs_3_, ...), custom_call_target="tpu_custom_call" | custom-call | flops 603979776 | bytes 3145728 | tf_op jit(solution)/shard_map/pallas_call | solution.py:192
  147.7 8.5 %collective-permute-done.29.refs_4_ = f32[512,256]{1,0:T(8,128)S(1)} collective-permute-done((f32[512,256]{1,0:T(8,128)}, f32[512,256]{1,0:T(8,128)S(1)}, u32[]{:S(2)}, u32[]{:S(2)}) %collective-permute-start.29) | collective-permute-done | bytes 524320 | tf_op jit(solution)/shard_map/ppermute | solution.py:244
  156.2 1.7 %shard_map.172 = f32[512,256]{1,0:T(8,128)} custom-call(s32[12]{0:T(128)S(1)} %get-tuple-element.33.table, f32[512,4096]{1,0:T(8,128)} %refs_0_.11, f32[512,256]{1,0:T(8,128)S(1)} %collective-permute-done.1.refs_1_, f32[512,256]{1,0:T(8,128)S(1)} %collective-permute-done.2.refs_2_, f32[512,256]{1,0:T(8,128)S(1)} %shard_map.170.refs_3_, ...), custom_call_target="tpu_custom_call" | custom-call | flops 201326592 | bytes 1048576 | tf_op jit(solution)/shard_map/pallas_call | solution.py:192
  158.0 0.7 maximum_add_fusion
  (57 shorter events, 0.4 us)
Async XLA Ops:
  0.6 15.7 %collective-permute-start.18 = (f32[512,256]{1,0:T(8,128)}, f32[512,256]{1,0:T(8,128)S(1)}, u32[]{:S(2)}, u32[]{:S(2)}) collective-permute-start(f32[512,256]{1,0:T(8,128)} %refs_6_.1), channel_id=1, source_target_pairs={{0,1},{1,0},{2,3},{3,2},{4,5},{5,4},{6,7},{7,6},{8,9},{9,8},{10,11... | collective-permute-start | bytes 1572872 | tf_op jit(solution)/shard_map/ppermute | solution.py:244
  3.7 15.0 %collective-permute-start.19 = (f32[512,256]{1,0:T(8,128)}, f32[512,256]{1,0:T(8,128)S(1)}, u32[]{:S(2)}, u32[]{:S(2)}) collective-permute-start(f32[512,256]{1,0:T(8,128)} %refs_6_.1), channel_id=1, source_target_pairs={{1,16},{3,18},{5,20},{7,22},{9,24},{11,26},{13,28},{15,30},{16,1},... | collective-permute-start | bytes 1572872 | tf_op jit(solution)/shard_map/ppermute | solution.py:244
  4.4 16.8 %collective-permute-start.8 = (f32[512,256]{1,0:T(8,128)}, f32[512,256]{1,0:T(8,128)S(1)}, u32[]{:S(2)}, u32[]{:S(2)}) collective-permute-start(f32[512,256]{1,0:T(8,128)} %refs_6_.1), channel_id=1, source_target_pairs={{0,4},{2,6},{4,0},{6,2},{8,12},{10,14},{12,8},{14,10},{17,21},{19,... | collective-permute-start | bytes 1572872 | tf_op jit(solution)/shard_map/ppermute | solution.py:244
  7.8 26.3 %collective-permute-start.10 = (f32[512,256]{1,0:T(8,128)}, f32[512,256]{1,0:T(8,128)S(1)}, u32[]{:S(2)}, u32[]{:S(2)}) collective-permute-start(f32[512,256]{1,0:T(8,128)} %refs_6_.1), channel_id=1, source_target_pairs={{0,8},{2,10},{4,12},{6,14},{8,0},{10,2},{12,4},{14,6},{17,25},{19,... | collective-permute-start | bytes 1572872 | tf_op jit(solution)/shard_map/ppermute | solution.py:244
  11.3 27.1 %collective-permute-start.14 = (f32[512,256]{1,0:T(8,128)}, f32[512,256]{1,0:T(8,128)S(1)}, u32[]{:S(2)}, u32[]{:S(2)}) collective-permute-start(f32[512,256]{1,0:T(8,128)} %refs_6_.1), channel_id=1, source_target_pairs={{0,2},{1,3},{2,0},{3,1},{4,6},{5,7},{6,4},{7,5},{8,10},{9,11},{10,... | collective-permute-start | bytes 1572872 | tf_op jit(solution)/shard_map/ppermute | solution.py:244
  16.3 17.8 %collective-permute-start.17 = (s32[1,16]{1,0:T(1,128)}, s32[1,16]{1,0:T(1,128)S(1)}, u32[]{:S(2)}, u32[]{:S(2)}) collective-permute-start(s32[1,16]{1,0:T(1,128)} %param.18), channel_id=1, source_target_pairs={{0,1},{1,0},{2,3},{3,2},{4,5},{5,4},{6,7},{7,6},{8,9},{9,8},{10,11... | collective-permute-start | bytes 200 | tf_op jit(solution)/shard_map/ppermute | solution.py:244
  18.8 17.3 %collective-permute-start.20 = (f32[512,256]{1,0:T(8,128)S(1)}, f32[512,256]{1,0:T(8,128)S(1)}, u32[]{:S(2)}, u32[]{:S(2)}) collective-permute-start(f32[512,256]{1,0:T(8,128)S(1)} %broadcast_select_fusion.refs_1_), channel_id=1, source_target_pairs={{0,4},{1,5},{2,6},{3,7},{4,0},{5,1},{6,2},{7,3},{8,12},{9,13},{10,... | collective-permute-start | bytes 1572872 | tf_op jit(solution)/shard_map/ppermute | solution.py:244
  21.1 29.4 %collective-permute-start.21 = (f32[512,256]{1,0:T(8,128)S(1)}, f32[512,256]{1,0:T(8,128)S(1)}, u32[]{:S(2)}, u32[]{:S(2)}) collective-permute-start(f32[512,256]{1,0:T(8,128)S(1)} %broadcast_select_fusion.refs_1_), channel_id=1, source_target_pairs={{0,8},{1,9},{2,10},{3,11},{4,12},{5,13},{6,14},{7,15},{8,0},{9,1},... | collective-permute-start | bytes 1572872 | tf_op jit(solution)/shard_map/ppermute | solution.py:244
  34.1 25.3 %collective-permute-start.22 = (f32[512,256]{1,0:T(8,128)S(1)}, f32[512,256]{1,0:T(8,128)S(1)}, u32[]{:S(2)}, u32[]{:S(2)}) collective-permute-start(f32[512,256]{1,0:T(8,128)S(1)} %broadcast_select_fusion.refs_1_), channel_id=1, source_target_pairs={{0,2},{1,3},{2,0},{3,1},{4,6},{5,7},{6,4},{7,5},{8,10},{9,11},{10,... | collective-permute-start | bytes 1572872 | tf_op jit(solution)/shard_map/ppermute | solution.py:244
  34.1 15.8 %collective-permute-start.9 = (f32[256,256]{1,0:T(8,128)S(1)}, f32[256,256]{1,0:T(8,128)S(1)}, u32[]{:S(2)}, u32[]{:S(2)}) collective-permute-start(f32[256,256]{1,0:T(8,128)S(1)} %slice.56), channel_id=1, source_target_pairs={{0,8},{2,10},{4,12},{6,14},{8,0},{10,2},{12,4},{14,6},{17,25},{19,... | collective-permute-start | bytes 786440 | tf_op jit(solution)/shard_map/ppermute | solution.py:244
  36.1 14.7 %collective-permute-start.15 = (f32[512,256]{1,0:T(8,128)S(1)}, f32[512,256]{1,0:T(8,128)S(1)}, u32[]{:S(2)}, u32[]{:S(2)}) collective-permute-start(f32[512,256]{1,0:T(8,128)S(1)} %collective-permute-done.8.refs_2_), channel_id=1, source_target_pairs={{0,2},{1,3},{2,0},{3,1},{4,6},{5,7},{6,4},{7,5},{8,10},{9,11},{10,... | collective-permute-start | bytes 1572872 | tf_op jit(solution)/shard_map/ppermute | solution.py:244
  38.4 11.7 %collective-permute-start.11 = (f32[256,256]{1,0:T(8,128)S(1)}, f32[256,256]{1,0:T(8,128)S(1)}, u32[]{:S(2)}, u32[]{:S(2)}) collective-permute-start(f32[256,256]{1,0:T(8,128)S(1)} %slice.57), channel_id=1, source_target_pairs={{0,4},{2,6},{4,0},{6,2},{8,12},{10,14},{12,8},{14,10},{17,21},{19,... | collective-permute-start | bytes 786440 | tf_op jit(solution)/shard_map/ppermute | solution.py:244
  50.0 6.3 %collective-permute-start.16 = (f32[512,256]{1,0:T(8,128)S(1)}, f32[512,256]{1,0:T(8,128)S(1)}, u32[]{:S(2)}, u32[]{:S(2)}) collective-permute-start(f32[512,256]{1,0:T(8,128)S(1)} %collective-permute-done.10.refs_3_), channel_id=1, source_target_pairs={{0,2},{1,3},{2,0},{3,1},{4,6},{5,7},{6,4},{7,5},{8,10},{9,11},{10,... | collective-permute-start | bytes 1572872 | tf_op jit(solution)/shard_map/ppermute | solution.py:244
  50.1 14.1 %collective-permute-start.23 = (f32[512,256]{1,0:T(8,128)S(1)}, f32[512,256]{1,0:T(8,128)S(1)}, u32[]{:S(2)}, u32[]{:S(2)}) collective-permute-start(f32[512,256]{1,0:T(8,128)S(1)} %collective-permute-done.20.refs_2_), channel_id=1, source_target_pairs={{0,2},{1,3},{2,0},{3,1},{4,6},{5,7},{6,4},{7,5},{8,10},{9,11},{10,... | collective-permute-start | bytes 1572872 | tf_op jit(solution)/shard_map/ppermute | solution.py:244
  50.6 14.1 %collective-permute-start.24 = (f32[512,256]{1,0:T(8,128)S(1)}, f32[512,256]{1,0:T(8,128)S(1)}, u32[]{:S(2)}, u32[]{:S(2)}) collective-permute-start(f32[512,256]{1,0:T(8,128)S(1)} %collective-permute-done.21.refs_3_), channel_id=1, source_target_pairs={{0,2},{1,3},{2,0},{3,1},{4,6},{5,7},{6,4},{7,5},{8,10},{9,11},{10,... | collective-permute-start | bytes 1572872 | tf_op jit(solution)/shard_map/ppermute | solution.py:244
  50.8 11.8 %collective-permute-start.25 = (f32[256,256]{1,0:T(8,128)S(1)}, f32[256,256]{1,0:T(8,128)S(1)}, u32[]{:S(2)}, u32[]{:S(2)}) collective-permute-start(f32[256,256]{1,0:T(8,128)S(1)} %slice.58), channel_id=1, source_target_pairs={{0,8},{1,9},{2,10},{3,11},{4,12},{5,13},{6,14},{7,15},{8,0},{9,1},... | collective-permute-start | bytes 786440 | tf_op jit(solution)/shard_map/ppermute | solution.py:244
  56.3 7.9 %collective-permute-start.26 = (f32[256,256]{1,0:T(8,128)S(1)}, f32[256,256]{1,0:T(8,128)S(1)}, u32[]{:S(2)}, u32[]{:S(2)}) collective-permute-start(f32[256,256]{1,0:T(8,128)S(1)} %slice.59), channel_id=1, source_target_pairs={{0,4},{1,5},{2,6},{3,7},{4,0},{5,1},{6,2},{7,3},{8,12},{9,13},{10,... | collective-permute-start | bytes 786440 | tf_op jit(solution)/shard_map/ppermute | solution.py:244
  59.4 9.2 %collective-permute-start.12 = (f32[256,256]{1,0:T(8,128)S(1)}, f32[256,256]{1,0:T(8,128)S(1)}, u32[]{:S(2)}, u32[]{:S(2)}) collective-permute-start(f32[256,256]{1,0:T(8,128)S(1)} %collective-permute-done.9.refs_1_), channel_id=1, source_target_pairs={{0,2},{1,3},{2,0},{3,1},{4,6},{5,7},{6,4},{7,5},{8,10},{9,11},{10,... | collective-permute-start | bytes 786440 | tf_op jit(solution)/shard_map/ppermute | solution.py:244
  62.6 6.0 %collective-permute-start.13 = (f32[256,256]{1,0:T(8,128)S(1)}, f32[256,256]{1,0:T(8,128)S(1)}, u32[]{:S(2)}, u32[]{:S(2)}) collective-permute-start(f32[256,256]{1,0:T(8,128)S(1)} %collective-permute-done.11.refs_2_), channel_id=1, source_target_pairs={{0,2},{1,3},{2,0},{3,1},{4,6},{5,7},{6,4},{7,5},{8,10},{9,11},{10,... | collective-permute-start | bytes 786440 | tf_op jit(solution)/shard_map/ppermute | solution.py:244
  64.2 7.2 %collective-permute-start.27 = (f32[256,256]{1,0:T(8,128)S(1)}, f32[256,256]{1,0:T(8,128)S(1)}, u32[]{:S(2)}, u32[]{:S(2)}) collective-permute-start(f32[256,256]{1,0:T(8,128)S(1)} %collective-permute-done.25.refs_1_), channel_id=1, source_target_pairs={{0,2},{1,3},{2,0},{3,1},{4,6},{5,7},{6,4},{7,5},{8,10},{9,11},{10,... | collective-permute-start | bytes 786440 | tf_op jit(solution)/shard_map/ppermute | solution.py:244
  64.2 7.2 %collective-permute-start.28 = (f32[256,256]{1,0:T(8,128)S(1)}, f32[256,256]{1,0:T(8,128)S(1)}, u32[]{:S(2)}, u32[]{:S(2)}) collective-permute-start(f32[256,256]{1,0:T(8,128)S(1)} %collective-permute-done.26.refs_2_), channel_id=1, source_target_pairs={{0,2},{1,3},{2,0},{3,1},{4,6},{5,7},{6,4},{7,5},{8,10},{9,11},{10,... | collective-permute-start | bytes 786440 | tf_op jit(solution)/shard_map/ppermute | solution.py:244
  71.3 6.6 %copy-start = (f32[512,256]{1,0:T(8,128)S(1)}, f32[512,256]{1,0:T(8,128)}, u32[]{:S(2)}) copy-start(f32[512,256]{1,0:T(8,128)} %refs_6_.1) | copy-start | bytes 1572868
  75.0 4.2 %collective-permute-start.30 = (f32[256,256]{1,0:T(8,128)S(1)}, f32[256,256]{1,0:T(8,128)S(1)}, u32[]{:S(2)}, u32[]{:S(2)}) collective-permute-start(f32[256,256]{1,0:T(8,128)S(1)} %pad_maximum_fusion), channel_id=1, source_target_pairs={{0,2},{1,3},{2,0},{3,1},{4,6},{5,7},{6,4},{7,5},{8,10},{9,11},{10,... | collective-permute-start | bytes 786440 | tf_op jit(solution)/shard_map/ppermute | solution.py:244
  77.9 13.0 %collective-permute-start = (f32[512,256]{1,0:T(8,128)S(1)}, f32[512,256]{1,0:T(8,128)S(1)}, u32[]{:S(2)}, u32[]{:S(2)}) collective-permute-start(f32[512,256]{1,0:T(8,128)S(1)} %copy-done), channel_id=1, source_target_pairs={{0,16},{2,18},{4,20},{6,22},{8,24},{10,26},{12,28},{14,30},{17,1},... | collective-permute-start | bytes 1572872 | tf_op jit(solution)/shard_map/ppermute | solution.py:244
  79.3 13.0 %collective-permute-start.32 = (f32[64,256]{1,0:T(8,128)S(1)}, f32[64,256]{1,0:T(8,128)S(1)}, u32[]{:S(2)}, u32[]{:S(2)}) collective-permute-start(f32[64,256]{1,0:T(8,128)S(1)} %get-tuple-element.26), channel_id=1, source_target_pairs={{0,1},{1,0},{2,3},{3,2},{4,5},{5,4},{6,7},{7,6},{8,9},{9,8},{10,11... | collective-permute-start | bytes 196616 | tf_op jit(solution)/shard_map/ppermute | solution.py:244
  79.4 13.6 %collective-permute-start.33 = (f32[64,256]{1,0:T(8,128)S(1)}, f32[64,256]{1,0:T(8,128)S(1)}, u32[]{:S(2)}, u32[]{:S(2)}) collective-permute-start(f32[64,256]{1,0:T(8,128)S(1)} %get-tuple-element.27), channel_id=1, source_target_pairs={{0,5},{1,4},{2,7},{3,6},{4,1},{5,0},{6,3},{7,2},{8,13},{9,12},{10,... | collective-permute-start | bytes 196616 | tf_op jit(solution)/shard_map/ppermute | solution.py:244
  81.7 11.3 %collective-permute-start.31 = (f32[64,256]{1,0:T(8,128)S(1)}, f32[64,256]{1,0:T(8,128)S(1)}, u32[]{:S(2)}, u32[]{:S(2)}) collective-permute-start(f32[64,256]{1,0:T(8,128)S(1)} %slice_select_fusion.4), channel_id=1, source_target_pairs={{0,4},{1,5},{2,6},{3,7},{4,0},{5,1},{6,2},{7,3},{8,12},{9,13},{10,... | collective-permute-start | bytes 196616 | tf_op jit(solution)/shard_map/ppermute | solution.py:244
  90.9 48.6 %collective-permute-start.3 = (f32[512,256]{1,0:T(8,128)S(1)}, f32[512,256]{1,0:T(8,128)S(1)}, u32[]{:S(2)}, u32[]{:S(2)}) collective-permute-start(f32[512,256]{1,0:T(8,128)S(1)} %collective-permute-done.refs_1_), channel_id=1, source_target_pairs={{1,5},{3,7},{5,1},{7,3},{9,13},{11,15},{13,9},{15,11},{16,20},{18,... | collective-permute-start | bytes 1572872 | tf_op jit(solution)/shard_map/ppermute | solution.py:244
  91.6 47.9 %collective-permute-start.4 = (f32[512,256]{1,0:T(8,128)S(1)}, f32[512,256]{1,0:T(8,128)S(1)}, u32[]{:S(2)}, u32[]{:S(2)}) collective-permute-start(f32[512,256]{1,0:T(8,128)S(1)} %collective-permute-done.refs_1_), channel_id=1, source_target_pairs={{1,9},{3,11},{5,13},{7,15},{9,1},{11,3},{13,5},{15,7},{16,24},{18,... | collective-permute-start | bytes 1572872 | tf_op jit(solution)/shard_map/ppermute | solution.py:244
  92.3 47.7 %collective-permute-start.1 = (f32[512,256]{1,0:T(8,128)S(1)}, f32[512,256]{1,0:T(8,128)S(1)}, u32[]{:S(2)}, u32[]{:S(2)}) collective-permute-start(f32[512,256]{1,0:T(8,128)S(1)} %collective-permute-done.refs_1_), channel_id=1, source_target_pairs={{1,13},{3,15},{5,9},{7,11},{9,5},{11,7},{13,1},{15,3},{16,28},{18,... | collective-permute-start | bytes 1572872 | tf_op jit(solution)/shard_map/ppermute | solution.py:244
  93.0 21.2 %collective-permute-start.34 = (f32[64,256]{1,0:T(8,128)S(1)}, f32[64,256]{1,0:T(8,128)S(1)}, u32[]{:S(2)}, u32[]{:S(2)}) collective-permute-start(f32[64,256]{1,0:T(8,128)S(1)} %add_add_fusion.1), channel_id=1, source_target_pairs={{0,8},{1,9},{2,10},{3,11},{4,12},{5,13},{6,14},{7,15},{8,0},{9,1},... | collective-permute-start | bytes 196616 | tf_op jit(solution)/shard_map/ppermute | solution.py:244
  103.7 32.4 %collective-permute-start.35 = (f32[64,256]{1,0:T(8,128)S(1)}, f32[64,256]{1,0:T(8,128)S(1)}, u32[]{:S(2)}, u32[]{:S(2)}) collective-permute-start(f32[64,256]{1,0:T(8,128)S(1)} %add_add_fusion.1), channel_id=1, source_target_pairs={{0,16},{1,17},{2,18},{3,19},{4,20},{5,21},{6,22},{7,23},{8,24},{9,... | collective-permute-start | bytes 196616 | tf_op jit(solution)/shard_map/ppermute | solution.py:244
  114.2 24.2 %collective-permute-start.36 = (f32[64,256]{1,0:T(8,128)S(1)}, f32[64,256]{1,0:T(8,128)S(1)}, u32[]{:S(2)}, u32[]{:S(2)}) collective-permute-start(f32[64,256]{1,0:T(8,128)S(1)} %add_add_fusion.1), channel_id=1, source_target_pairs={{0,24},{1,25},{2,26},{3,27},{4,28},{5,29},{6,30},{7,31},{8,16},{9,... | collective-permute-start | bytes 196616 | tf_op jit(solution)/shard_map/ppermute | solution.py:244
  136.1 9.5 %collective-permute-start.5 = (f32[512,256]{1,0:T(8,128)S(1)}, f32[512,256]{1,0:T(8,128)S(1)}, u32[]{:S(2)}, u32[]{:S(2)}) collective-permute-start(f32[512,256]{1,0:T(8,128)S(1)} %collective-permute-done.refs_1_), channel_id=1, source_target_pairs={{0,2},{1,3},{2,0},{3,1},{4,6},{5,7},{6,4},{7,5},{8,10},{9,11},{10,... | collective-permute-start | bytes 1572872 | tf_op jit(solution)/shard_map/ppermute | solution.py:244
  138.4 4.3 %collective-permute-start.37 = (f32[64,256]{1,0:T(8,128)S(1)}, f32[64,256]{1,0:T(8,128)S(1)}, u32[]{:S(2)}, u32[]{:S(2)}) collective-permute-start(f32[64,256]{1,0:T(8,128)S(1)} %add_add_fusion), channel_id=1, source_target_pairs={{0,4},{1,5},{2,6},{3,7},{4,0},{5,1},{6,2},{7,3},{8,12},{9,13},{10,... | collective-permute-start | bytes 196616 | tf_op jit(solution)/shard_map/ppermute | solution.py:244
  139.5 6.2 %collective-permute-start.6 = (f32[512,256]{1,0:T(8,128)S(1)}, f32[512,256]{1,0:T(8,128)S(1)}, u32[]{:S(2)}, u32[]{:S(2)}) collective-permute-start(f32[512,256]{1,0:T(8,128)S(1)} %collective-permute-done.3.refs_2_), channel_id=1, source_target_pairs={{0,2},{1,3},{2,0},{3,1},{4,6},{5,7},{6,4},{7,5},{8,10},{9,11},{10,... | collective-permute-start | bytes 1572872 | tf_op jit(solution)/shard_map/ppermute | solution.py:244
  139.5 6.2 %collective-permute-start.7 = (f32[512,256]{1,0:T(8,128)S(1)}, f32[512,256]{1,0:T(8,128)S(1)}, u32[]{:S(2)}, u32[]{:S(2)}) collective-permute-start(f32[512,256]{1,0:T(8,128)S(1)} %collective-permute-done.4.refs_3_), channel_id=1, source_target_pairs={{0,2},{1,3},{2,0},{3,1},{4,6},{5,7},{6,4},{7,5},{8,10},{9,11},{10,... | collective-permute-start | bytes 1572872 | tf_op jit(solution)/shard_map/ppermute | solution.py:244
  140.0 7.7 %collective-permute-start.2 = (f32[512,256]{1,0:T(8,128)S(1)}, f32[512,256]{1,0:T(8,128)S(1)}, u32[]{:S(2)}, u32[]{:S(2)}) collective-permute-start(f32[512,256]{1,0:T(8,128)S(1)} %collective-permute-done.1.refs_1_), channel_id=1, source_target_pairs={{0,2},{1,3},{2,0},{3,1},{4,6},{5,7},{6,4},{7,5},{8,10},{9,11},{10,... | collective-permute-start | bytes 1572872 | tf_op jit(solution)/shard_map/ppermute | solution.py:244
  142.7 13.5 %collective-permute-start.29 = (f32[512,256]{1,0:T(8,128)}, f32[512,256]{1,0:T(8,128)S(1)}, u32[]{:S(2)}, u32[]{:S(2)}) collective-permute-start(f32[512,256]{1,0:T(8,128)} %get-tuple-element.13), channel_id=1, source_target_pairs={{0,1},{1,0},{2,3},{3,2},{4,5},{5,4},{6,7},{7,6},{8,9},{9,8},{10,11... | collective-permute-start | bytes 1572872 | tf_op jit(solution)/shard_map/ppermute | solution.py:244
  145.6 12.3 %collective-permute-start.38 = (f32[128,256]{1,0:T(8,128)S(1)}, f32[128,256]{1,0:T(8,128)S(1)}, u32[]{:S(2)}, u32[]{:S(2)}) collective-permute-start(f32[128,256]{1,0:T(8,128)S(1)} %pad_maximum_fusion.1), channel_id=1, source_target_pairs={{0,2},{1,3},{2,0},{3,1},{4,6},{5,7},{6,4},{7,5},{8,10},{9,11},{10,... | collective-permute-start | bytes 393224 | tf_op jit(solution)/shard_map/ppermute | solution.py:244
  147.7 10.3 %copy-start.1 = (f32[256,256]{1,0:T(8,128)S(1)}, f32[256,256]{1,0:T(8,128)}, u32[]{:S(2)}) copy-start(f32[256,256]{1,0:T(8,128)} %param.19) | copy-start | bytes 786436
